TPU v7x, 128 devices: a whole 4x4x4 slice. The times are simulated.
128 devices in a mesh: grp: 8 (over x, y_lo), blk: 16 (over z, y_hi, core).
Axes of the slice: x: 4, y: 4 (y_hi: 2, y_lo: 2; y = y_hi * 2 + y_lo), z: 4, core: 2. Of those that a mesh axis runs over, the one named last changes fastest.
Arguments:
- source_emb: bfloat16 [24576, 768], P('blk'), may hold values from -32 to 32
- target_emb: bfloat16 [24576, 768], P(('grp', 'blk')), may hold values from -16 to 16
- hard_pool: bfloat16 [24576, 768], P(('grp', 'blk')), may hold values from -16 to 16
- hard_index: int32 [24576], P('blk'), may hold values from 0 to 24575, as said below
- language: int32 [24576], P('blk'), may hold values from 0 to 108
- margin: float32 [109], replicated, may hold values from 0.5 to 3
Outputs:
- row_loss: float32 [24576], P('blk')
- source_grad: float32 [24576, 768], P('blk')
- target_grad: float32 [24576, 768], P(('grp', 'blk'))
- pool_grad: float32 [24576, 768], P(('grp', 'blk'))
Inputs may be any that keep to these rules, and one draw needn't show every extreme that they name: `hard_index`: each entry is a row of hard_pool; an entry's owner is its value // 192. Within each aligned block of 192 entries no owner is named more than 3 times, and one owner, the same for all blocks, is named exactly 3 times in every block.
All inputs are finite; a program needn't handle non-finite values.
Results may differ from a plain program's by a relative error of at most 0.0025.
Values may be sent and summed in bfloat16 or wider, within the bound.
No kernel may reach another device: no remote copies, remote signals or barrier semaphores. Data moves between devices by JAX's collectives and lax.ppermute only.
A program may use at most 64 MiB of HBM per device.

v0:
```python
import jax
import jax.numpy as jnp
from jax import lax
from jax.experimental import pallas as pl
from jax.experimental.pallas import tpu as pltpu
from jax.sharding import PartitionSpec as P

BF, F32 = jnp.bfloat16, jnp.float32
NEG = -1e30
LOW = -3e38
TILE = 768
PART = 384
CHUNKS = tuple(((dz, 0), (dz, 1)) for dz in (0, 1, 3, 2))


def hop_blk(value, dz, dy, dc):
    route = []
    for i in range(16):
        z, y, c = i // 4, (i // 2) % 2, i % 2
        route.append((i, ((z + dz) % 4) * 4 + (y ^ dy) * 2 + (c ^ dc)))
    return lax.ppermute(value, "blk", route)


def hop_grp(value, dx, dy):
    return lax.ppermute(value, "grp", [(i, ((i // 2 + dx) % 4) * 2 + ((i % 2) ^ dy)) for i in range(8)])


def dot_f32(a, b, dims):
    return lax.dot_general(a, b, (dims, ((), ())), preferred_element_type=F32)


def columns_of(rows):
    pad = jnp.zeros((120, rows.shape[1]), F32)
    return jnp.transpose(jnp.concatenate([rows, pad], axis=0))


def score_kernel(place, src, near_pair, away_pair, *refs):
    e_out, stat_out, tgt_out, a_ref = refs[-4:]
    half = near_pair.shape[0]
    rows = half // 2
    step = pl.program_id(0)

    @pl.when(step == 0)
    def _():
        top = jnp.zeros((1, 1), F32)
        for q, pair in enumerate((near_pair, away_pair)):
            block = pair[...]
            tgt_out[0, q * half : (q + 1) * half, :] = block
            top = jnp.maximum(top, jnp.max(jnp.abs(block).astype(F32), keepdims=True))
        a_ref[...] = jnp.broadcast_to(top, a_ref.shape)

    tgt = tgt_out[0]
    lane = lax.broadcasted_iota(jnp.int32, (PART, 128), 1)
    column = lax.broadcasted_iota(jnp.int32, (PART, 2 * half), 1)
    line = lax.broadcasted_iota(jnp.int32, (PART, 1), 0)
    parts = []
    for first in range(0, src.shape[0], PART):
        ats = []
        for sub in range(2):
            k = step * (src.shape[0] // rows) + first // rows + sub
            at = jnp.int32(-(1 << 20))
            for q in range(4):
                at = jnp.where(place[q] == k, (q - sub) * rows, at)
            ats.append(at)
        hole = line + jnp.where(line < rows, ats[0], ats[1])
        here = pl.ds(first, PART)
        s = dot_f32(src[here, :], tgt, ((1,), (1,)))
        s = jnp.where(column == hole, NEG, s)
        top = jnp.max(s, axis=1, keepdims=True)
        e = jnp.exp(s - top)
        total = jnp.sum(e, axis=1, keepdims=True)
        e_out[0, here, :] = e.astype(BF)
        parts.append(jnp.where(lane == 0, top, jnp.where(lane == 1, total, a_ref[0:1, :])))
    stat_out[...] = jnp.transpose(jnp.concatenate(parts, axis=0))[0:8, :]


def score_call(place, src, near_pair, away_pair, n, so_far):
    half, width = near_pair.shape
    total = src.shape[0]
    cols = 2 * half
    so_far = list(so_far)
    vmem = pl.BlockSpec((half, width), lambda i, p: (0, 0))
    return pl.pallas_call(
        score_kernel,
        out_shape=(
            pltpu.HBM((4, total, cols), BF),
            jax.ShapeDtypeStruct((8, total), F32),
            pltpu.HBM((4, cols, width), BF),
        ),
        grid_spec=pltpu.PrefetchScalarGridSpec(
            num_scalar_prefetch=1,
            grid=(total // TILE,),
            in_specs=[pl.BlockSpec((TILE, width), lambda i, p: (i, 0)), vmem, vmem]
            + [pl.BlockSpec(memory_space=pl.ANY)] * len(so_far),
            out_specs=(
                pl.BlockSpec((1, TILE, cols), lambda i, p: (n, i, 0)),
                pl.BlockSpec((8, TILE), lambda i, p: (0, i)),
                pl.BlockSpec((1, cols, width), lambda i, p: (n, 0, 0)),
            ),
            scratch_shapes=[pltpu.VMEM((8, 128), F32)],
        ),
        input_output_aliases={4: 0, 5: 2} if so_far else {},
        compiler_params=pltpu.CompilerParams(vmem_limit_bytes=24 << 20),
        cost_estimate=pl.CostEstimate(
            flops=2 * total * cols * width, bytes_accessed=total * (width + cols) * 2, transcendentals=total * cols
        ),
        name="scores",
    )(place, src, near_pair, away_pair, *so_far)


def source_kernel(w_ref, e_ref, tgt_ref, out, acc):
    c, i = pl.program_id(0), pl.program_id(1)
    lane = lax.broadcasted_iota(jnp.int32, (PART, 128), 1)
    weight = jnp.sum(jnp.where(lane == c, columns_of(w_ref[...]), 0.0), axis=1, keepdims=True)
    part = dot_f32(e_ref[0], tgt_ref[0], ((1,), (0,))) * weight
    total = jnp.where(c == 0, 0.0, acc[i]) + part
    acc[i] = total
    out[...] = total.astype(BF)


def source_call(weights, e_all, tgt_all):
    _, total, cols = e_all.shape
    width = tgt_all.shape[2]
    return pl.pallas_call(
        source_kernel,
        out_shape=jax.ShapeDtypeStruct((total, width), BF),
        grid=(4, total // PART),
        in_specs=[
            pl.BlockSpec((8, PART), lambda c, i: (0, i)),
            pl.BlockSpec((1, PART, cols), lambda c, i: (c, i, 0)),
            pl.BlockSpec((1, cols, width), lambda c, i: (c, 0, 0)),
        ],
        out_specs=pl.BlockSpec((PART, width), lambda c, i: (jnp.where(c == 3, i, 0), 0)),
        scratch_shapes=[pltpu.VMEM((total // PART, PART, width), F32)],
        cost_estimate=pl.CostEstimate(
            flops=8 * total * cols * width, bytes_accessed=total * (8 * cols + 2 * width), transcendentals=0
        ),
        name="source_terms",
    )(weights, e_all, tgt_all)


def target_kernel(place, w_ref, e_ref, src_ref, _, keep, give, acc, scaled, column):
    rows = acc.shape[0] // 4
    total = src_ref.shape[0]
    chunk = pl.program_id(0)

    @pl.when(chunk == 0)
    def _():
        for first in range(0, total, PART):
            here = slice(first, first + PART)
            column[here, :] = columns_of(w_ref[:, here])

    lane = lax.broadcasted_iota(jnp.int32, (PART, 128), 1)
    for first in range(0, total, PART):
        here = slice(first, first + PART)
        weight = jnp.sum(jnp.where(lane == chunk, column[here, :], 0.0), axis=1, keepdims=True)
        scaled[here, :] = (src_ref[here, :].astype(F32) * weight).astype(BF)
    acc[...] = dot_f32(e_ref[0], scaled[...], ((0,), (0,)))
    for q in range(4):
        at = place[chunk * 4 + q]

        @pl.when(at >= 0)
        def _():
            there = slice(q * rows, (q + 1) * rows)
            here = pl.ds(pl.multiple_of(at * rows, rows), rows)
            acc[there, :] = acc[there, :] + column[here, 4:5] * src_ref[here, :].astype(F32)

    keep[0] = acc[0 : 2 * rows, :]
    give[0] = acc[2 * rows : 4 * rows, :].astype(BF)


def target_call(place, weights, e_all, src, after):
    _, total, cols = e_all.shape
    width = src.shape[1]
    half = (4, cols // 2, width)
    half_spec = pl.BlockSpec((1, cols // 2, width), lambda i, p: (i, 0, 0))
    return pl.pallas_call(
        target_kernel,
        out_shape=(jax.ShapeDtypeStruct(half, F32), jax.ShapeDtypeStruct(half, BF)),
        grid_spec=pltpu.PrefetchScalarGridSpec(
            num_scalar_prefetch=1,
            grid=(4,),
            in_specs=[
                pl.BlockSpec((8, total), lambda i, p: (0, 0)),
                pl.BlockSpec((1, total, cols), lambda i, p: (i, 0, 0)),
                pl.BlockSpec((total, width), lambda i, p: (0, 0)),
                pl.BlockSpec(memory_space=pl.ANY),
            ],
            out_specs=(half_spec, half_spec),
            scratch_shapes=[
                pltpu.VMEM((cols, width), F32),
                pltpu.VMEM((total, width), BF),
                pltpu.VMEM((total, 128), F32),
            ],
        ),
        cost_estimate=pl.CostEstimate(
            flops=8 * total * cols * width, bytes_accessed=total * (width + 4 * cols) * 2 + cols * width * 12, transcendentals=0
        ),
        name="target_terms",
    )(place, weights, e_all, src, after)


def code_kernel(parts, hard, tgt, col, _, out, high):
    total = hard[...] * col[:, 0:1] + tgt[...].astype(F32) * col[:, 1:2]
    for g in range(parts.shape[0]):
        total = total + parts[g].astype(F32) * col[:, 3 + g : 4 + g]
    scaled = jnp.clip(total * col[:, 2:3], -32767.0, 32767.0)
    coded = jnp.round(scaled).astype(jnp.int32).astype(jnp.int16)
    out[...] = coded
    high[...] = coded


def line_kernel(keep, got, m1, m2, m3, mine, other):
    rows = mine.shape[0]
    total = keep[0] + got[0].astype(F32)
    for part in (m1, m2, m3):
        total = total + part[...].astype(F32)
    mine[...] = total[:rows, :]
    other[...] = total[rows:, :].astype(BF)


def decode_kernel(order, scale, own, side, far1, far2, far3, pairs1, pairs2, pairs3, far_side, out):
    step = pl.program_id(0)
    half = own.shape[0] // 2
    far, pairs = (None, far1, far2, far3), (None, pairs1, pairs2, pairs3)
    for dx in range(4):
        for dy in range(2):

            @pl.when(step == dx * 2 + dy)
            def _():
                if dx == 0:
                    whole = (own if dy == 0 else side)[...]
                    out[...] = whole.astype(jnp.int32).astype(F32) * scale[...]
                else:
                    low = pairs[dx][dy]
                    high = far[dx][...] if dy == 0 else far_side[dx - 1]
                    out[0:half, :] = low.astype(jnp.int32).astype(F32) * scale[0:half, :]
                    out[half:, :] = high.astype(jnp.int32).astype(F32) * scale[half:, :]


def decode_call(order, scale, pieces):
    rows, width = pieces[0].shape
    total = scale.shape[0]
    return pl.pallas_call(
        decode_kernel,
        out_shape=jax.ShapeDtypeStruct((total, width), F32),
        grid_spec=pltpu.PrefetchScalarGridSpec(
            num_scalar_prefetch=1,
            grid=(total // rows,),
            in_specs=[pl.BlockSpec((rows, 1), lambda i, p: (p[i], 0))]
            + [pl.BlockSpec(x.shape, lambda i, p, n=x.ndim: (0,) * n) for x in pieces],
            out_specs=pl.BlockSpec((rows, width), lambda i, p: (p[i], 0)),
        ),
        cost_estimate=pl.CostEstimate(flops=total * width, bytes_accessed=total * width * 6, transcendentals=0),
        name="decode",
    )(order, scale, *pieces)


def shards(source_emb, target_emb, hard_pool, hard_index, language, margin):
    total, width = source_emb.shape
    rows = target_emb.shape[0]
    blk, grp = lax.axis_index("blk"), lax.axis_index("grp")
    owners = 128
    cap = max(2, (2 * rows + owners - 1) // owners)
    slots = owners * cap
    z, y, c = blk // 4, (blk // 2) % 2, blk % 2

    start = grp * rows
    own_index = lax.dynamic_slice_in_dim(hard_index, start, rows, 0)
    own_source = lax.dynamic_slice_in_dim(source_emb, start, rows, 0)
    owner, pool_row = own_index // rows, own_index % rows
    position = jnp.arange(rows, dtype=jnp.int32)
    same = (owner[:, None] == owner[None, :]) & (position[None, :] < position[:, None])
    slot = owner * cap + jnp.sum(same.astype(jnp.int32), axis=1)
    at_slot = slot[:, None] == jnp.arange(slots, dtype=jnp.int32)[None, :]
    requests = jnp.sum(jnp.where(at_slot, pool_row[:, None] + 1, 0), axis=0) - 1
    wanted = lax.all_to_all(requests.reshape(owners, cap), ("grp", "blk"), 0, 0, tiled=True)
    lang_match = language[:, None] == jnp.arange(margin.shape[0], dtype=jnp.int32)[None, :]
    margin_row = jnp.sum(jnp.where(lang_match, margin[None, :], 0.0), axis=1)

    across = hop_blk(target_emb, 0, 1, 0)
    line = {0: target_emb, **{dz: hop_blk(target_emb, -dz, 0, 0) for dz in (1, 3, 2)}}
    lines = {0: across, **{dz: hop_blk(across, -dz, 0, 0) for dz in (1, 3, 2)}}
    near = {dz: jnp.concatenate([line[dz], lines[dz]]) for dz in (0, 1, 3, 2)}
    away = {dz: hop_blk(near[dz], 0, 0, 1) for dz in (0, 1, 3, 2)}

    own_target = lax.ppermute(
        target_emb, ("grp", "blk"), [(16 * i + j, (j % 8) * 16 + 2 * i + j // 8) for i in range(8) for j in range(16)]
    )

    holds = grp == blk // 2
    place = {}
    for dz in range(4):
        for dy in range(2):
            for dc in range(2):
                zz = (z + dz) % 4
                k = (zz % 2) * 4 + (y ^ dy) * 2 + (c ^ dc)
                place[dz, dy, dc] = jnp.where(holds & (zz // 2 == c), k, -1)
    order = [[(dz, dy, dc) for dc in (0, 1) for dz, dy in chunk] for chunk in CHUNKS]
    places = [jnp.stack([place[key] for key in chunk]) for chunk in order]
    flat = jnp.concatenate(places)

    stats, so_far = [], ()

    def add_chunk(n):
        nonlocal so_far
        e, stat, tgt = score_call(places[n], source_emb, near[CHUNKS[n][0][0]], away[CHUNKS[n][0][0]], n, so_far)
        so_far = (e, tgt)
        stats.append(stat)

    add_chunk(0)
    wanted, stats[0] = lax.optimization_barrier((wanted, stats[0]))
    serve = (wanted.reshape(slots)[:, None] == position[None, :]).astype(BF)
    served = dot_f32(serve, hard_pool, ((1,), (0,))).astype(BF).reshape(owners, cap, width)
    served, places[1] = lax.optimization_barrier((served, places[1]))
    fetched = lax.all_to_all(served, ("grp", "blk"), 0, 0, tiled=True).reshape(slots, width)
    add_chunk(1)
    add_chunk(2)
    fetched, stats[2] = lax.optimization_barrier((fetched, stats[2]))
    pick = at_slot.astype(BF)
    hard_rows = dot_f32(pick, fetched, ((1,), (0,)))
    hard_score = jnp.sum(own_source.astype(F32) * hard_rows, axis=1)
    add_chunk(3)

    tops = jnp.stack([stat[0] for stat in stats])
    sums = jnp.stack([stat[1] for stat in stats])
    reach = jnp.maximum(jnp.max(jnp.stack([stat[2] for stat in stats]), axis=0), jnp.max(jnp.abs(hard_rows)))
    own_margin = lax.dynamic_slice_in_dim(margin_row, start, rows, 0)
    own_pos = jnp.sum(own_source.astype(F32) * own_target.astype(F32), axis=1) - own_margin
    pos = lax.dynamic_update_slice_in_dim(jnp.zeros((total,), F32), own_pos, start, 0)
    hard_all = lax.dynamic_update_slice_in_dim(jnp.full((total,), LOW, F32), hard_score, start, 0)
    soft_top = jnp.max(tops, axis=0)
    soft = jnp.sum(sums * jnp.exp(tops - soft_top), axis=0)
    mine = jnp.stack([soft_top, soft, pos, hard_all, reach] + [jnp.zeros((total,), F32)] * 3)
    everyone = lax.all_to_all(jnp.broadcast_to(mine[None], (8, 8, total)), "grp", 0, 0, tiled=True)
    source_part = source_call(jnp.concatenate([jnp.exp(tops - soft_top), jnp.zeros((4, total), F32)]), *so_far)
    everyone, source_part = lax.optimization_barrier((everyone, source_part))
    source_parts = lax.all_to_all(source_part.reshape(8, rows, width), "grp", 0, 0, tiled=True)
    token = hop_blk(source_part[:16, :128], 0, 0, 1)
    pos = jnp.sum(everyone[:, 2], axis=0)
    hard_all = jnp.max(everyone[:, 3], axis=0)
    reach = jnp.max(everyone[:, 4], axis=0)
    top = jnp.maximum(jnp.max(everyone[:, 0], axis=0), jnp.maximum(pos, hard_all))
    off = jnp.sum(everyone[:, 1] * jnp.exp(everyone[:, 0] - top), axis=0) + jnp.exp(hard_all - top)
    log_total = top + jnp.log(off + jnp.exp(pos - top))
    row_loss = log_total - pos
    less = jnp.exp(pos - log_total) - 1.0
    diag_weight = jnp.where(holds, less, 0.0)

    x_at, y_at = grp // 2, grp % 2
    mass = jnp.abs(less) + off * jnp.exp(top - log_total)
    bound = jnp.maximum(1.01 * reach * mass, 1e-30)
    col = jnp.concatenate(
        [jnp.stack([jnp.exp(hard_all - log_total), less, 32767.0 / bound]), jnp.exp(everyone[:, 0] - log_total[None])]
    )
    col = lax.dynamic_slice_in_dim(col, start, rows, 1)
    hard_prob = col[0]
    col = jnp.transpose(col)
    half = rows // 2

    weights = jnp.concatenate([jnp.exp(tops - log_total), diag_weight[None], jnp.zeros((3, total), F32)])
    keep, give = target_call(flat, weights, so_far[0], source_emb, token)
    got = hop_blk(give, 0, 0, 1)
    moved = []
    for n in (1, 2, 3):
        dz = CHUNKS[n][0][0]
        moved.append(hop_blk((keep[n] + got[n].astype(F32)).astype(BF), dz, 0, 0))
    whole = [pl.BlockSpec((1, 2 * rows, width), lambda i: (0, 0, 0))] * 2
    whole += [pl.BlockSpec((2 * rows, width), lambda i: (0, 0))] * 3
    mine, other = pl.pallas_call(
        line_kernel,
        out_shape=(jax.ShapeDtypeStruct((rows, width), F32), jax.ShapeDtypeStruct((rows, width), BF)),
        grid=(1,),
        in_specs=whole,
        out_specs=[pl.BlockSpec((rows, width), lambda i: (0, 0))] * 2,
        cost_estimate=pl.CostEstimate(flops=10 * rows * width, bytes_accessed=30 * rows * width, transcendentals=0),
        name="lines",
    )(keep, got, *moved)
    target_grad = mine + hop_blk(other, 0, 1, 0).astype(F32)

    coded, coded_high = pl.pallas_call(
        code_kernel,
        out_shape=(jax.ShapeDtypeStruct((rows, width), jnp.int16), jax.ShapeDtypeStruct((half, width), jnp.int16)),
        grid=(2,),
        in_specs=[
            pl.BlockSpec((8, half, width), lambda i: (0, i, 0)),
            pl.BlockSpec((half, width), lambda i: (i, 0)),
            pl.BlockSpec((half, width), lambda i: (i, 0)),
            pl.BlockSpec((half, col.shape[1]), lambda i: (i, 0)),
            pl.BlockSpec(memory_space=pl.ANY),
        ],
        out_specs=(pl.BlockSpec((half, width), lambda i: (i, 0)), pl.BlockSpec((half, width), lambda i: (0, 0))),
        cost_estimate=pl.CostEstimate(flops=10 * rows * width, bytes_accessed=22 * rows * width, transcendentals=0),
        name="code",
    )(source_parts, hard_rows, own_target, col, other)
    hard_gate = hard_prob + 0.0 * coded[0, 0].astype(F32)
    side = hop_grp(coded, 0, 1)
    far = [hop_grp(coded_high, -dx, 0) for dx in (1, 2, 3)]
    low = jnp.stack([coded[:half], side[:half]])
    pairs = [hop_grp(low, -dx, 0) for dx in (1, 2, 3)]
    far_side = hop_grp(jnp.stack(far), 0, 1)
    blocks = jnp.stack([((x_at + dx) % 4) * 2 + (y_at ^ dy) for dx in range(4) for dy in range(2)])
    source_grad = decode_call(
        blocks, (bound * (1.0 / 32767.0))[:, None], [coded, side, *far, *pairs, far_side]
    )

    contribution = (hard_gate[:, None] * own_source.astype(F32)).astype(BF)
    outgoing = dot_f32(pick, contribution, ((0,), (0,))).astype(BF).reshape(owners, cap, width)
    incoming = lax.all_to_all(outgoing, ("grp", "blk"), 0, 0, tiled=True).reshape(slots, width)
    pool_grad = dot_f32(serve, incoming, ((0,), (0,)))
    return (row_loss, source_grad, target_grad, pool_grad)


def solution(mesh):
    in_specs = (P("blk", None), P(("grp", "blk"), None), P(("grp", "blk"), None), P("blk"), P("blk"), P())
    out_specs = (P("blk"), P("blk", None), P(("grp", "blk"), None), P(("grp", "blk"), None))
    return jax.shard_map(shards, mesh=mesh, in_specs=in_specs, out_specs=out_specs, check_vma=False)
```

profile of v0, /device:TPU:0, one launch (start us, length us, event | category | flops | bytes accessed | tf_op | source)
XLA Modules:
  0.0 241.4 jit_solution(4767614802307850243)
XLA Ops:
  0.6 3.4 %collective-permute-start = (bf16[192,768]{1,0:T(8,128)(2,1)}, bf16[192,768]{1,0:T(8,128)(2,1)S(1)}, u32[]{:S(2)}, u32[]{:S(2)}) collective-permute-start(bf16[192,768]{1,0:T(8,128)(2,1)} %param.7), channel_id=1, source_target_pairs={{0,2},{1,3},{2,0},{3,1},{4,6},{5,7},{6,4},{7,5},{8,10},{9,11},{10,... | collective-permute-start | bytes 884744 | tf_op jit(solution)/shard_map/ppermute | solution.py:21
  4.0 4.0 %collective-permute-start.2 = (bf16[192,768]{1,0:T(8,128)(2,1)}, bf16[192,768]{1,0:T(8,128)(2,1)}, u32[]{:S(2)}, u32[]{:S(2)}) collective-permute-start(bf16[192,768]{1,0:T(8,128)(2,1)} %param.7), channel_id=1, source_target_pairs={{0,12},{1,13},{2,14},{3,15},{4,0},{5,1},{6,2},{7,3},{8,4},{9,5},{1... | collective-permute-start | bytes 884744 | tf_op jit(solution)/shard_map/ppermute | solution.py:21
  8.0 3.7 %collective-permute-start.11 = (bf16[192,768]{1,0:T(8,128)(2,1)}, bf16[192,768]{1,0:T(8,128)(2,1)}, u32[]{:S(2)}, u32[]{:S(2)}) collective-permute-start(bf16[192,768]{1,0:T(8,128)(2,1)} %param.7), channel_id=1, source_target_pairs={{0,0},{1,16},{2,32},{3,48},{4,64},{5,80},{6,96},{7,112},{8,1},{9,1... | collective-permute-start | bytes 884744 | tf_op jit(solution)/shard_map/ppermute | solution.py:287
  14.4 12.2 %all-to-all-start = ((s32[128,1,3]{2,1,0:T(1,128)}), s32[128,1,3]{2,1,0:T(1,128)}, u32[]{:S(2)}, u32[]{:S(2)}) async-start(s32[128,1,3]{2,1,0:T(1,128)} %bitcast), calls=%async_computation | async-start | bytes 131072 | tf_op jit(solution)/shard_map/all_to_all | solution.py:277
  32.4 2.9 %collective-permute-start.3 = (bf16[192,768]{1,0:T(8,128)(2,1)S(1)}, bf16[192,768]{1,0:T(8,128)(2,1)S(1)}, u32[]{:S(2)}, u32[]{:S(2)}) collective-permute-start(bf16[192,768]{1,0:T(8,128)(2,1)S(1)} %collective-permute-done), channel_id=1, source_target_pairs={{0,12},{1,13},{2,14},{3,15},{4,0},{5,1},{6,2},{7,3},{8,4},{9,5},{1... | collective-permute-start | bytes 884744 | tf_op jit(solution)/shard_map/ppermute | solution.py:21
  38.5 2.0 collective-permute-start.9
  42.9 10.6 %collective-permute-done.6 = bf16[192,768]{1,0:T(8,128)(2,1)S(1)} collective-permute-done((bf16[192,768]{1,0:T(8,128)(2,1)S(1)}, bf16[192,768]{1,0:T(8,128)(2,1)S(1)}, u32[]{:S(2)}, u32[]{:S(2)}) %collective-permute-start.6) | collective-permute-done | bytes 294944 | tf_op jit(solution)/shard_map/ppermute | solution.py:21
  54.9 6.5 %scores.4 = (bf16[4,1536,768]{2,1,0:T(8,128)(2,1)}, f32[8,1536]{1,0:T(8,128)S(1)}, bf16[4,768,768]{2,1,0:T(8,128)(2,1)}) custom-call(s32[4]{0:T(128)S(1)} %pad_add_fusion.2.place, bf16[1536,768]{1,0:T(8,128)(2,1)S(1)} %copy-done.1, bf16[384,768]{1,0:T(8,128)(2,1)} %constant_dynamic-update-slice_fusion.near_pair, ...), custom_call_target="tpu_custom_call" | custom-call | flops 1811939328 | bytes 4718592 | tf_op jit(solution)/shard_map/scores/pallas_call | solution.py:83
  63.6 2.0 reshape.342
  65.6 8.1 %all-to-all-start.1 = ((bf16[128,3,768]{2,1,0:T(4,128)(2,1)}), bf16[128,3,768]{2,1,0:T(4,128)(2,1)}, u32[]{:S(2)}, u32[]{:S(2)}) async-start(bf16[128,3,768]{2,1,0:T(4,128)(2,1)} %reshape.342), calls=%async_computation.1 | async-start | bytes 1572864 | tf_op jit(solution)/shard_map/all_to_all | solution.py:316
  73.8 6.7 %scores.5 = (bf16[4,1536,768]{2,1,0:T(8,128)(2,1)}, f32[8,1536]{1,0:T(8,128)S(1)}, bf16[4,768,768]{2,1,0:T(8,128)(2,1)}) custom-call(s32[4]{0:T(128)S(1)} %pad_add_fusion.3.place, bf16[1536,768]{1,0:T(8,128)(2,1)S(1)} %copy-done.1, bf16[384,768]{1,0:T(8,128)(2,1)} %constant_dynamic-update-slice_fusion.2.near_pair, ...), custom_call_target="tpu_custom_call", output_to_operand_aliasing={{0}: (4, {}), {2}: (5, {})} | custom-call | flops 1811939328 | bytes 4718592 | tf_op jit(solution)/shard_map/scores/pallas_call | solution.py:83
  80.5 6.7 %scores.6 = (bf16[4,1536,768]{2,1,0:T(8,128)(2,1)}, f32[8,1536]{1,0:T(8,128)S(1)}, bf16[4,768,768]{2,1,0:T(8,128)(2,1)}) custom-call(s32[4]{0:T(128)S(1)} %pad_add_fusion.4.place, bf16[1536,768]{1,0:T(8,128)(2,1)S(1)} %copy-done.1, bf16[384,768]{1,0:T(8,128)(2,1)} %constant_dynamic-update-slice_fusion.4.near_pair, ...), custom_call_target="tpu_custom_call", output_to_operand_aliasing={{0}: (4, {}), {2}: (5, {})} | custom-call | flops 1811939328 | bytes 4718592 | tf_op jit(solution)/shard_map/scores/pallas_call | solution.py:83
  87.2 6.5 %scores.7 = (bf16[4,1536,768]{2,1,0:T(8,128)(2,1)}, f32[8,1536]{1,0:T(8,128)S(1)}, bf16[4,768,768]{2,1,0:T(8,128)(2,1)}) custom-call(s32[4]{0:T(128)S(1)} %pad_add_fusion.5.place, bf16[1536,768]{1,0:T(8,128)(2,1)S(1)} %copy-done.1, bf16[384,768]{1,0:T(8,128)(2,1)S(1)} %constant_dynamic-update-slice_fusion.6.near_pair, ...), custom_call_target="tpu_custom_call", output_to_operand_aliasing={{0}: (4, {}), {2}: (5, {})} | custom-call | flops 1811939328 | bytes 4718592 | tf_op jit(solution)/shard_map/scores/pallas_call | solution.py:83
  95.2 2.7 %fusion.3 = (f32[192]{0:T(256)S(1)}, f32[192]{0:T(256)S(1)}, f32[]{:T(128)}, f32[192,768]{1,0:T(8,128)}) fusion(bf16[1536,768]{1,0:T(8,128)(2,1)S(1)} %copy-done.1, s32[]{:T(128)S(6)} %select_n.245, bf16[192,768]{1,0:T(8,128)(2,1)} %collective-permute-done.11.tgt, bf16[384,768]{1,0:T(8,128)(2,1)S(1)} %reshape.343, s32[192]{0:T(256)S(1)} %multiply_add_fusion), kind=kOutput, calls=%fused_computation.16 | convolution fusion | flops 114499200 | bytes 1771784 | tf_op jit(solution)/shard_map/dot_general | solution.py:29
  100.7 4.6 %all-to-all-start.2 = ((f32[8,8,1536]{2,1,0:T(8,128)}), f32[8,8,1536]{2,1,0:T(8,128)S(1)}, u32[]{:S(2)}, u32[]{:S(2)}) async-start(f32[8,8,1536]{2,1,0:T(8,128)} %broadcast_in_dim.40), calls=%async_computation.2 | async-start | bytes 786432 | tf_op jit(solution)/shard_map/all_to_all | solution.py:335
  106.0 17.2 %source_terms.1 = bf16[1536,768]{1,0:T(8,128)(2,1)} custom-call(f32[8,1536]{1,0:T(8,128)} %concatenate.29.w_ref, bf16[4,1536,768]{2,1,0:T(8,128)(2,1)} %get-tuple-element.46.e_ref, bf16[4,768,768]{2,1,0:T(8,128)(2,1)} %get-tuple-element.47.tgt_ref), custom_call_target="tpu_custom_call" | custom-call | flops 7247757312 | bytes 11796480 | tf_op jit(solution)/shard_map/source_terms/pallas_call | solution.py:124
  126.9 15.4 %target_terms.1 = (f32[4,384,768]{2,1,0:T(8,128)}, bf16[4,384,768]{2,1,0:T(8,128)(2,1)}) custom-call(s32[16]{0:T(128)} %concatenate.31.place, f32[8,1536]{1,0:T(8,128)} %maximum_maximum_fusion.w_ref, bf16[4,1536,768]{2,1,0:T(8,128)(2,1)} %get-tuple-element.46.e_ref, bf16[1536,768]{1,0:T(8,128)(2,1)} %src_ref.1, bf16[16,128]{1,0:T(8,128)(2,1)} %copy-done.13), custom_call_target="tpu_custom_call" | custom-call | flops 7247757312 | bytes 18874368 | tf_op jit(solution)/shard_map/target_terms/pallas_call | solution.py:177
  143.1 4.7 %all-to-all-start.3 = ((bf16[8,192,768]{2,1,0:T(8,128)(2,1)}), bf16[8,192,768]{2,1,0:T(8,128)(2,1)S(1)}, u32[]{:S(2)}, u32[]{:S(2)}) async-start(bf16[8,192,768]{2,1,0:T(8,128)(2,1)} %bitcast.60), calls=%async_computation.3 | async-start | bytes 4718592 | tf_op jit(solution)/shard_map/all_to_all | solution.py:338
  147.9 3.9 %fusion.7 = (bf16[384,768]{1,0:T(8,128)(2,1)}, bf16[384,768]{1,0:T(8,128)(2,1)}, bf16[384,768]{1,0:T(8,128)(2,1)}) fusion(f32[4,384,768]{2,1,0:T(8,128)} %get-tuple-element.50.keep, bf16[4,384,768]{2,1,0:T(8,128)(2,1)} %collective-permute-done.13.got), kind=kLoop, calls=%fused_computation.20 | loop fusion | flops 2654208 | bytes 7077888 | tf_op jit(solution)/shard_map/convert_element_type | solution.py:367
  155.2 2.1 collective-permute-start.16
  160.9 3.0 %fusion.1.scale = f32[1536,1]{1,0:T(8,128)} fusion(f32[1536]{0:T(1024)S(1)} %get-tuple-element.89, f32[1536,1]{1,0:T(8,128)} %copy.69, f32[1536]{0:T(1024)S(1)} %fusion.19, f32[1536,1]{1,0:T(8,128)} %copy.66, f32[1536,1]{1,0:T(8,128)S(1)} %copy.65, f32[1536]{0:T(1024)S(1)} %slice_reduce_fusion.3), kind=kLoop, calls=%fused_computation.12 | loop fusion | flops 23040 | bytes 43008 | tf_op jit(solution)/shard_map/mul | solution.py:404
  163.9 5.2 %collective-permute-done.14.m1 = bf16[384,768]{1,0:T(8,128)(2,1)} collective-permute-done((bf16[384,768]{1,0:T(8,128)(2,1)}, bf16[384,768]{1,0:T(8,128)(2,1)}, u32[]{:S(2)}, u32[]{:S(2)}) %collective-permute-start.14) | collective-permute-done | bytes 589856 | tf_op jit(solution)/shard_map/ppermute | solution.py:21
  169.1 11.9 %collective-permute-done.15.m2 = bf16[384,768]{1,0:T(8,128)(2,1)} collective-permute-done((bf16[384,768]{1,0:T(8,128)(2,1)}, bf16[384,768]{1,0:T(8,128)(2,1)}, u32[]{:S(2)}, u32[]{:S(2)}) %collective-permute-start.15) | collective-permute-done | bytes 589856 | tf_op jit(solution)/shard_map/ppermute | solution.py:21
  181.0 1.9 collective-permute-done.16.m3
  182.9 3.0 %lines.1 = (f32[192,768]{1,0:T(8,128)}, bf16[192,768]{1,0:T(8,128)(2,1)}) custom-call(f32[4,384,768]{2,1,0:T(8,128)} %get-tuple-element.50.keep, bf16[4,384,768]{2,1,0:T(8,128)(2,1)} %collective-permute-done.13.got, bf16[384,768]{1,0:T(8,128)(2,1)} %collective-permute-done.14.m1, bf16[384,768]{1,0:T(8,128)(2,1)} %collective-permute-done.15.m2, ...), custom_call_target="tpu_custom_call" | custom-call | flops 1474560 | bytes 4423680 | tf_op jit(solution)/shard_map/lines/pallas_call | solution.py:370
  185.9 3.5 %collective-permute-start.25 = (bf16[192,768]{1,0:T(8,128)(2,1)}, bf16[192,768]{1,0:T(8,128)(2,1)}, u32[]{:S(2)}, u32[]{:S(2)}) collective-permute-start(bf16[192,768]{1,0:T(8,128)(2,1)} %get-tuple-element.52._), channel_id=1, source_target_pairs={{0,2},{1,3},{2,0},{3,1},{4,6},{5,7},{6,4},{7,5},{8,10},{9,11},{10,... | collective-permute-start | bytes 884744 | tf_op jit(solution)/shard_map/ppermute | solution.py:21
  190.8 3.0 %code.1 = (s16[192,768]{1,0:T(8,128)(2,1)}, s16[96,768]{1,0:T(8,128)(2,1)}) custom-call(bf16[8,192,768]{2,1,0:T(8,128)(2,1)} %copy-done.2, f32[192,768]{1,0:T(8,128)} %get-tuple-element.88.hard, bf16[192,768]{1,0:T(8,128)(2,1)} %collective-permute-done.11.tgt, f32[192,11]{1,0:T(8,128)} %bitcast.61, bf16[192,768]{1,0:T(8,128)(2,1)} %get-tuple-element.52._), custom_call_target="tpu_custom_call" | custom-call | flops 1474560 | bytes 3244032 | tf_op jit(solution)/shard_map/code/pallas_call | solution.py:381
  193.8 3.0 %collective-permute-start.18 = (s16[96,768]{1,0:T(8,128)(2,1)}, s16[96,768]{1,0:T(8,128)(2,1)S(1)}, u32[]{:S(2)}, u32[]{:S(2)}) collective-permute-start(s16[96,768]{1,0:T(8,128)(2,1)} %get-tuple-element.54), channel_id=1, source_target_pairs={{0,96},{16,112},{32,0},{48,16},{64,32},{80,48},{96,64},{112,80},{1... | collective-permute-start | bytes 442376 | tf_op jit(solution)/shard_map/ppermute | solution.py:25
  203.9 6.2 %all-to-all-start.4 = ((bf16[128,3,768]{2,1,0:T(4,128)(2,1)}), bf16[128,3,768]{2,1,0:T(4,128)(2,1)S(1)}, u32[]{:S(2)}, u32[]{:S(2)}) async-start(bf16[128,3,768]{2,1,0:T(4,128)(2,1)} %reshape.345), calls=%async_computation.4 | async-start | bytes 1572864 | tf_op jit(solution)/shard_map/all_to_all | solution.py:409
  212.9 2.7 %collective-permute-start.21 = (s16[2,96,768]{2,1,0:T(8,128)(2,1)}, s16[2,96,768]{2,1,0:T(8,128)(2,1)S(1)}, u32[]{:S(2)}, u32[]{:S(2)}) collective-permute-start(s16[2,96,768]{2,1,0:T(8,128)(2,1)} %pad_add_fusion.1), channel_id=1, source_target_pairs={{0,96},{16,112},{32,0},{48,16},{64,32},{80,48},{96,64},{112,80},{1... | collective-permute-start | bytes 884744 | tf_op jit(solution)/shard_map/ppermute | solution.py:25
  219.1 12.0 %all-to-all-done.4 = bf16[128,3,768]{2,1,0:T(4,128)(2,1)S(1)} async-done(((bf16[128,3,768]{2,1,0:T(4,128)(2,1)}), bf16[128,3,768]{2,1,0:T(4,128)(2,1)S(1)}, u32[]{:S(2)}, u32[]{:S(2)}) %all-to-all-start.4) | async-done | bytes 589856 | tf_op jit(solution)/shard_map/all_to_all | solution.py:409
  233.8 7.6 %decode.1 = f32[1536,768]{1,0:T(8,128)} custom-call(s32[8]{0:T(128)} %stack.170.order, f32[1536,1]{1,0:T(8,128)} %fusion.1.scale, s16[192,768]{1,0:T(8,128)(2,1)} %get-tuple-element.53.own, s16[192,768]{1,0:T(8,128)(2,1)} %copy-done.5, s16[96,768]{1,0:T(8,128)(2,1)} %copy-done.7, s16[96,768]{1,0:T(8,128)(2,1)} %copy-done.8, s16[96,768]{1,0:T(8,128)(2,1)} %copy-done.9, ...), custom_call_target="tpu_custom_call" | custom-call | flops 1179648 | bytes 7077888 | tf_op jit(solution)/shard_map/decode/pallas_call | solution.py:244
  (141 shorter events, 50.4 us)
Async XLA Ops:
  0.6 61.8 %copy-start = (bf16[192,768]{1,0:T(8,128)(2,1)S(1)}, bf16[192,768]{1,0:T(8,128)(2,1)}, u32[]{:S(2)}) copy-start(bf16[192,768]{1,0:T(8,128)(2,1)} %param.8) | copy-start | bytes 884740
  0.6 31.0 %collective-permute-start = (bf16[192,768]{1,0:T(8,128)(2,1)}, bf16[192,768]{1,0:T(8,128)(2,1)S(1)}, u32[]{:S(2)}, u32[]{:S(2)}) collective-permute-start(bf16[192,768]{1,0:T(8,128)(2,1)} %param.7), channel_id=1, source_target_pairs={{0,2},{1,3},{2,0},{3,1},{4,6},{5,7},{6,4},{7,5},{8,10},{9,11},{10,... | collective-permute-start | bytes 884744 | tf_op jit(solution)/shard_map/ppermute | solution.py:21
  4.0 28.4 %collective-permute-start.2 = (bf16[192,768]{1,0:T(8,128)(2,1)}, bf16[192,768]{1,0:T(8,128)(2,1)}, u32[]{:S(2)}, u32[]{:S(2)}) collective-permute-start(bf16[192,768]{1,0:T(8,128)(2,1)} %param.7), channel_id=1, source_target_pairs={{0,12},{1,13},{2,14},{3,15},{4,0},{5,1},{6,2},{7,3},{8,4},{9,5},{1... | collective-permute-start | bytes 884744 | tf_op jit(solution)/shard_map/ppermute | solution.py:21
  8.0 29.0 %collective-permute-start.5 = (bf16[192,768]{1,0:T(8,128)(2,1)}, bf16[192,768]{1,0:T(8,128)(2,1)S(1)}, u32[]{:S(2)}, u32[]{:S(2)}) collective-permute-start(bf16[192,768]{1,0:T(8,128)(2,1)} %param.7), channel_id=1, source_target_pairs={{0,4},{1,5},{2,6},{3,7},{4,8},{5,9},{6,10},{7,11},{8,12},{9,13},{1... | collective-permute-start | bytes 884744 | tf_op jit(solution)/shard_map/ppermute | solution.py:21
  8.0 87.2 %collective-permute-start.11 = (bf16[192,768]{1,0:T(8,128)(2,1)}, bf16[192,768]{1,0:T(8,128)(2,1)}, u32[]{:S(2)}, u32[]{:S(2)}) collective-permute-start(bf16[192,768]{1,0:T(8,128)(2,1)} %param.7), channel_id=1, source_target_pairs={{0,0},{1,16},{2,32},{3,48},{4,64},{5,80},{6,96},{7,112},{8,1},{9,1... | collective-permute-start | bytes 884744 | tf_op jit(solution)/shard_map/ppermute | solution.py:287
  11.8 26.0 %collective-permute-start.8 = (bf16[192,768]{1,0:T(8,128)(2,1)}, bf16[192,768]{1,0:T(8,128)(2,1)S(1)}, u32[]{:S(2)}, u32[]{:S(2)}) collective-permute-start(bf16[192,768]{1,0:T(8,128)(2,1)} %param.7), channel_id=1, source_target_pairs={{0,8},{1,9},{2,10},{3,11},{4,12},{5,13},{6,14},{7,15},{8,0},{9,1},... | collective-permute-start | bytes 884744 | tf_op jit(solution)/shard_map/ppermute | solution.py:21
  14.4 47.0 %all-to-all-start = ((s32[128,1,3]{2,1,0:T(1,128)}), s32[128,1,3]{2,1,0:T(1,128)}, u32[]{:S(2)}, u32[]{:S(2)}) async-start(s32[128,1,3]{2,1,0:T(1,128)} %bitcast), calls=%async_computation | async-start | bytes 131072 | tf_op jit(solution)/shard_map/all_to_all | solution.py:277
  32.4 22.5 %collective-permute-start.1 = (bf16[384,768]{1,0:T(8,128)(2,1)}, bf16[384,768]{1,0:T(8,128)(2,1)S(1)}, u32[]{:S(2)}, u32[]{:S(2)}) collective-permute-start(bf16[384,768]{1,0:T(8,128)(2,1)} %constant_dynamic-update-slice_fusion.near_pair), channel_id=1, source_target_pairs={{0,1},{1,0},{2,3},{3,2},{4,5},{5,4},{6,7},{7,6},{8,9},{9,8},{10,11... | collective-permute-start | bytes 1769480 | tf_op jit(solution)/shard_map/ppermute | solution.py:21
  32.4 9.7 %collective-permute-start.3 = (bf16[192,768]{1,0:T(8,128)(2,1)S(1)}, bf16[192,768]{1,0:T(8,128)(2,1)S(1)}, u32[]{:S(2)}, u32[]{:S(2)}) collective-permute-start(bf16[192,768]{1,0:T(8,128)(2,1)S(1)} %collective-permute-done), channel_id=1, source_target_pairs={{0,12},{1,13},{2,14},{3,15},{4,0},{5,1},{6,2},{7,3},{8,4},{9,5},{1... | collective-permute-start | bytes 884744 | tf_op jit(solution)/shard_map/ppermute | solution.py:21
  37.0 16.5 %collective-permute-start.6 = (bf16[192,768]{1,0:T(8,128)(2,1)S(1)}, bf16[192,768]{1,0:T(8,128)(2,1)S(1)}, u32[]{:S(2)}, u32[]{:S(2)}) collective-permute-start(bf16[192,768]{1,0:T(8,128)(2,1)S(1)} %collective-permute-done), channel_id=1, source_target_pairs={{0,4},{1,5},{2,6},{3,7},{4,8},{5,9},{6,10},{7,11},{8,12},{9,13},{1... | collective-permute-start | bytes 884744 | tf_op jit(solution)/shard_map/ppermute | solution.py:21
  38.5 15.8 %collective-permute-start.9 = (bf16[192,768]{1,0:T(8,128)(2,1)S(1)}, bf16[192,768]{1,0:T(8,128)(2,1)S(1)}, u32[]{:S(2)}, u32[]{:S(2)}) collective-permute-start(bf16[192,768]{1,0:T(8,128)(2,1)S(1)} %collective-permute-done), channel_id=1, source_target_pairs={{0,8},{1,9},{2,10},{3,11},{4,12},{5,13},{6,14},{7,15},{8,0},{9,1},... | collective-permute-start | bytes 884744 | tf_op jit(solution)/shard_map/ppermute | solution.py:21
  42.9 31.0 %collective-permute-start.4 = (bf16[384,768]{1,0:T(8,128)(2,1)}, bf16[384,768]{1,0:T(8,128)(2,1)}, u32[]{:S(2)}, u32[]{:S(2)}) collective-permute-start(bf16[384,768]{1,0:T(8,128)(2,1)} %constant_dynamic-update-slice_fusion.2.near_pair), channel_id=1, source_target_pairs={{0,1},{1,0},{2,3},{3,2},{4,5},{5,4},{6,7},{7,6},{8,9},{9,8},{10,11... | collective-permute-start | bytes 1769480 | tf_op jit(solution)/shard_map/ppermute | solution.py:21
  54.3 26.2 %collective-permute-start.7 = (bf16[384,768]{1,0:T(8,128)(2,1)}, bf16[384,768]{1,0:T(8,128)(2,1)}, u32[]{:S(2)}, u32[]{:S(2)}) collective-permute-start(bf16[384,768]{1,0:T(8,128)(2,1)} %constant_dynamic-update-slice_fusion.4.near_pair), channel_id=1, source_target_pairs={{0,1},{1,0},{2,3},{3,2},{4,5},{5,4},{6,7},{7,6},{8,9},{9,8},{10,11... | collective-permute-start | bytes 1769480 | tf_op jit(solution)/shard_map/ppermute | solution.py:21
  54.3 32.9 %collective-permute-start.10 = (bf16[384,768]{1,0:T(8,128)(2,1)S(1)}, bf16[384,768]{1,0:T(8,128)(2,1)}, u32[]{:S(2)}, u32[]{:S(2)}) collective-permute-start(bf16[384,768]{1,0:T(8,128)(2,1)S(1)} %constant_dynamic-update-slice_fusion.6.near_pair), channel_id=1, source_target_pairs={{0,1},{1,0},{2,3},{3,2},{4,5},{5,4},{6,7},{7,6},{8,9},{9,8},{10,11... | collective-permute-start | bytes 1769480 | tf_op jit(solution)/shard_map/ppermute | solution.py:21
  65.6 28.0 %all-to-all-start.1 = ((bf16[128,3,768]{2,1,0:T(4,128)(2,1)}), bf16[128,3,768]{2,1,0:T(4,128)(2,1)}, u32[]{:S(2)}, u32[]{:S(2)}) async-start(bf16[128,3,768]{2,1,0:T(4,128)(2,1)} %reshape.342), calls=%async_computation.1 | async-start | bytes 1572864 | tf_op jit(solution)/shard_map/all_to_all | solution.py:316
  100.7 22.4 %all-to-all-start.2 = ((f32[8,8,1536]{2,1,0:T(8,128)}), f32[8,8,1536]{2,1,0:T(8,128)S(1)}, u32[]{:S(2)}, u32[]{:S(2)}) async-start(f32[8,8,1536]{2,1,0:T(8,128)} %broadcast_in_dim.40), calls=%async_computation.2 | async-start | bytes 786432 | tf_op jit(solution)/shard_map/all_to_all | solution.py:335
  125.1 1.2 collective-permute-start.12
  142.2 5.7 %collective-permute-start.13 = (bf16[4,384,768]{2,1,0:T(8,128)(2,1)}, bf16[4,384,768]{2,1,0:T(8,128)(2,1)}, u32[]{:S(2)}, u32[]{:S(2)}) collective-permute-start(bf16[4,384,768]{2,1,0:T(8,128)(2,1)} %get-tuple-element.51), channel_id=1, source_target_pairs={{0,1},{1,0},{2,3},{3,2},{4,5},{5,4},{6,7},{7,6},{8,9},{9,8},{10,11... | collective-permute-start | bytes 7077896 | tf_op jit(solution)/shard_map/ppermute | solution.py:21
  143.1 46.3 %all-to-all-start.3 = ((bf16[8,192,768]{2,1,0:T(8,128)(2,1)}), bf16[8,192,768]{2,1,0:T(8,128)(2,1)S(1)}, u32[]{:S(2)}, u32[]{:S(2)}) async-start(bf16[8,192,768]{2,1,0:T(8,128)(2,1)} %bitcast.60), calls=%async_computation.3 | async-start | bytes 4718592 | tf_op jit(solution)/shard_map/all_to_all | solution.py:338
  151.8 17.3 %collective-permute-start.14 = (bf16[384,768]{1,0:T(8,128)(2,1)}, bf16[384,768]{1,0:T(8,128)(2,1)}, u32[]{:S(2)}, u32[]{:S(2)}) collective-permute-start(bf16[384,768]{1,0:T(8,128)(2,1)} %get-tuple-element.73), channel_id=1, source_target_pairs={{0,4},{1,5},{2,6},{3,7},{4,8},{5,9},{6,10},{7,11},{8,12},{9,13},{1... | collective-permute-start | bytes 1769480 | tf_op jit(solution)/shard_map/ppermute | solution.py:21
  153.5 27.6 %collective-permute-start.15 = (bf16[384,768]{1,0:T(8,128)(2,1)}, bf16[384,768]{1,0:T(8,128)(2,1)}, u32[]{:S(2)}, u32[]{:S(2)}) collective-permute-start(bf16[384,768]{1,0:T(8,128)(2,1)} %get-tuple-element.72), channel_id=1, source_target_pairs={{0,12},{1,13},{2,14},{3,15},{4,0},{5,1},{6,2},{7,3},{8,4},{9,5},{1... | collective-permute-start | bytes 1769480 | tf_op jit(solution)/shard_map/ppermute | solution.py:21
  155.2 27.7 %collective-permute-start.16 = (bf16[384,768]{1,0:T(8,128)(2,1)}, bf16[384,768]{1,0:T(8,128)(2,1)}, u32[]{:S(2)}, u32[]{:S(2)}) collective-permute-start(bf16[384,768]{1,0:T(8,128)(2,1)} %get-tuple-element.71), channel_id=1, source_target_pairs={{0,8},{1,9},{2,10},{3,11},{4,12},{5,13},{6,14},{7,15},{8,0},{9,1},... | collective-permute-start | bytes 1769480 | tf_op jit(solution)/shard_map/ppermute | solution.py:21
  185.9 31.3 %collective-permute-start.25 = (bf16[192,768]{1,0:T(8,128)(2,1)}, bf16[192,768]{1,0:T(8,128)(2,1)}, u32[]{:S(2)}, u32[]{:S(2)}) collective-permute-start(bf16[192,768]{1,0:T(8,128)(2,1)} %get-tuple-element.52._), channel_id=1, source_target_pairs={{0,2},{1,3},{2,0},{3,1},{4,6},{5,7},{6,4},{7,5},{8,10},{9,11},{10,... | collective-permute-start | bytes 884744 | tf_op jit(solution)/shard_map/ppermute | solution.py:21
  193.8 16.3 %collective-permute-start.18 = (s16[96,768]{1,0:T(8,128)(2,1)}, s16[96,768]{1,0:T(8,128)(2,1)S(1)}, u32[]{:S(2)}, u32[]{:S(2)}) collective-permute-start(s16[96,768]{1,0:T(8,128)(2,1)} %get-tuple-element.54), channel_id=1, source_target_pairs={{0,96},{16,112},{32,0},{48,16},{64,32},{80,48},{96,64},{112,80},{1... | collective-permute-start | bytes 442376 | tf_op jit(solution)/shard_map/ppermute | solution.py:25
  196.8 13.3 %collective-permute-start.19 = (s16[96,768]{1,0:T(8,128)(2,1)}, s16[96,768]{1,0:T(8,128)(2,1)S(1)}, u32[]{:S(2)}, u32[]{:S(2)}) collective-permute-start(s16[96,768]{1,0:T(8,128)(2,1)} %get-tuple-element.54), channel_id=1, source_target_pairs={{0,64},{16,80},{32,96},{48,112},{64,0},{80,16},{96,32},{112,48},{1... | collective-permute-start | bytes 442376 | tf_op jit(solution)/shard_map/ppermute | solution.py:25
  197.7 12.5 %collective-permute-start.20 = (s16[96,768]{1,0:T(8,128)(2,1)}, s16[96,768]{1,0:T(8,128)(2,1)S(1)}, u32[]{:S(2)}, u32[]{:S(2)}) collective-permute-start(s16[96,768]{1,0:T(8,128)(2,1)} %get-tuple-element.54), channel_id=1, source_target_pairs={{0,32},{16,48},{32,64},{48,80},{64,96},{80,112},{96,0},{112,16},{1... | collective-permute-start | bytes 442376 | tf_op jit(solution)/shard_map/ppermute | solution.py:25
  199.7 12.3 %collective-permute-start.17 = (s16[192,768]{1,0:T(8,128)(2,1)}, s16[192,768]{1,0:T(8,128)(2,1)S(1)}, u32[]{:S(2)}, u32[]{:S(2)}) collective-permute-start(s16[192,768]{1,0:T(8,128)(2,1)} %get-tuple-element.53.own), channel_id=1, source_target_pairs={{0,16},{16,0},{32,48},{48,32},{64,80},{80,64},{96,112},{112,96},{1... | collective-permute-start | bytes 884744 | tf_op jit(solution)/shard_map/ppermute | solution.py:25
  203.9 27.2 %all-to-all-start.4 = ((bf16[128,3,768]{2,1,0:T(4,128)(2,1)}), bf16[128,3,768]{2,1,0:T(4,128)(2,1)S(1)}, u32[]{:S(2)}, u32[]{:S(2)}) async-start(bf16[128,3,768]{2,1,0:T(4,128)(2,1)} %reshape.345), calls=%async_computation.4 | async-start | bytes 1572864 | tf_op jit(solution)/shard_map/all_to_all | solution.py:409
  211.1 21.8 %collective-permute-start.24 = (s16[3,96,768]{2,1,0:T(8,128)(2,1)}, s16[3,96,768]{2,1,0:T(8,128)(2,1)}, u32[]{:S(2)}, u32[]{:S(2)}) collective-permute-start(s16[3,96,768]{2,1,0:T(8,128)(2,1)} %pad_add_fusion), channel_id=1, source_target_pairs={{0,16},{16,0},{32,48},{48,32},{64,80},{80,64},{96,112},{112,96},{1... | collective-permute-start | bytes 1327112 | tf_op jit(solution)/shard_map/ppermute | solution.py:25
  212.9 20.0 %collective-permute-start.21 = (s16[2,96,768]{2,1,0:T(8,128)(2,1)}, s16[2,96,768]{2,1,0:T(8,128)(2,1)S(1)}, u32[]{:S(2)}, u32[]{:S(2)}) collective-permute-start(s16[2,96,768]{2,1,0:T(8,128)(2,1)} %pad_add_fusion.1), channel_id=1, source_target_pairs={{0,96},{16,112},{32,0},{48,16},{64,32},{80,48},{96,64},{112,80},{1... | collective-permute-start | bytes 884744 | tf_op jit(solution)/shard_map/ppermute | solution.py:25
  215.5 17.4 %collective-permute-start.22 = (s16[2,96,768]{2,1,0:T(8,128)(2,1)}, s16[2,96,768]{2,1,0:T(8,128)(2,1)}, u32[]{:S(2)}, u32[]{:S(2)}) collective-permute-start(s16[2,96,768]{2,1,0:T(8,128)(2,1)} %pad_add_fusion.1), channel_id=1, source_target_pairs={{0,64},{16,80},{32,96},{48,112},{64,0},{80,16},{96,32},{112,48},{1... | collective-permute-start | bytes 884744 | tf_op jit(solution)/shard_map/ppermute | solution.py:25
  216.4 17.4 %collective-permute-start.23 = (s16[2,96,768]{2,1,0:T(8,128)(2,1)}, s16[2,96,768]{2,1,0:T(8,128)(2,1)}, u32[]{:S(2)}, u32[]{:S(2)}) collective-permute-start(s16[2,96,768]{2,1,0:T(8,128)(2,1)} %pad_add_fusion.1), channel_id=1, source_target_pairs={{0,32},{16,48},{32,64},{48,80},{64,96},{80,112},{96,0},{112,16},{1... | collective-permute-start | bytes 884744 | tf_op jit(solution)/shard_map/ppermute | solution.py:25
  (13 other events, 185.8 us)
where the time goes:
time: 244 us; the launch traced here: 241 us
  starting transfers between devices  73.4 us (30%)
  Pallas kernels  72.5 us (30%)
  waiting for transfers between devices  43.7 us (18%)
  local copies, waits for them, and re-layouts  26.5 us (11%)
  other arithmetic  16.8 us (7%)
  matrix products  6.65 us (3%)
    ppermute x17, waiting for transfers between devices, hop_blk(): return lax.ppermute(value, 'blk', route)  30.8 us
    pallas_call x4, Pallas kernels, score_call(): pl.pallas_call(score_kernel, out_shape=(pltpu.HBM((4, total, cols), BF),...  26.3 us
    ppermute x17, starting transfers between devices, hop_blk(): return lax.ppermute(value, 'blk', route)  22.8 us
    pallas_call x1, Pallas kernels, source_call(): pl.pallas_call(source_kernel, out_shape=jax.ShapeDtypeStruct((total, widt...  17.2 us
    pallas_call x1, Pallas kernels, target_call(): pl.pallas_call(target_kernel, out_shape=(jax.ShapeDtypeStruct(half, F32),...  15.4 us
    all_to_all x1, starting transfers between devices, shards(): lax.all_to_all(requests.reshape(owners, cap), ('grp', 'blk'), 0, 0, tiled...  12.2 us
    all_to_all x1, waiting for transfers between devices, shards(): lax.all_to_all(outgoing, ('grp', 'blk'), 0, 0, tiled=True)  12 us
    ppermute x8, starting transfers between devices, hop_grp(): lax.ppermute(value, 'grp', [(i, (i // 2 + dx) % 4 * 2 + (i % 2 ^ dy)) for...  10.9 us
  transfers between devices with their start and end apart: 31, of which 8 were waited for; matrix products, arithmetic and copies ran while one was open for 16% of the time, Pallas kernels for 21%

commit v1 on v0

--- a/solution.py
+++ b/solution.py
@@ -108,13 +108,12 @@
     )(place, src, near_pair, away_pair, *so_far)
 
 
-def source_kernel(w_ref, e_ref, tgt_ref, out, acc):
-    c, i = pl.program_id(0), pl.program_id(1)
-    lane = lax.broadcasted_iota(jnp.int32, (PART, 128), 1)
-    weight = jnp.sum(jnp.where(lane == c, columns_of(w_ref[...]), 0.0), axis=1, keepdims=True)
-    part = dot_f32(e_ref[0], tgt_ref[0], ((1,), (0,))) * weight
-    total = jnp.where(c == 0, 0.0, acc[i]) + part
-    acc[i] = total
+def source_kernel(w_ref, e_ref, tgt_ref, out):
+    weights = columns_of(w_ref[...])
+    total = None
+    for c in range(4):
+        part = dot_f32(e_ref[c], tgt_ref[c], ((1,), (0,))) * weights[:, c : c + 1]
+        total = part if total is None else total + part
     out[...] = total.astype(BF)
 
 
@@ -124,14 +123,13 @@
     return pl.pallas_call(
         source_kernel,
         out_shape=jax.ShapeDtypeStruct((total, width), BF),
-        grid=(4, total // PART),
+        grid=(total // PART,),
         in_specs=[
-            pl.BlockSpec((8, PART), lambda c, i: (0, i)),
-            pl.BlockSpec((1, PART, cols), lambda c, i: (c, i, 0)),
-            pl.BlockSpec((1, cols, width), lambda c, i: (c, 0, 0)),
+            pl.BlockSpec((8, PART), lambda i: (0, i)),
+            pl.BlockSpec((4, PART, cols), lambda i: (0, i, 0)),
+            pl.BlockSpec((4, cols, width), lambda i: (0, 0, 0), pipeline_mode=pl.Buffered(1)),
         ],
-        out_specs=pl.BlockSpec((PART, width), lambda c, i: (jnp.where(c == 3, i, 0), 0)),
-        scratch_shapes=[pltpu.VMEM((total // PART, PART, width), F32)],
+        out_specs=pl.BlockSpec((PART, width), lambda i: (i, 0)),
         cost_estimate=pl.CostEstimate(
             flops=8 * total * cols * width, bytes_accessed=total * (8 * cols + 2 * width), transcendentals=0
         ),
@@ -200,60 +198,44 @@
     )(place, weights, e_all, src, after)
 
 
-def code_kernel(parts, hard, tgt, col, _, out, high):
+def code_kernel(parts, hard, tgt, col, *refs):
+    out = refs[-1]
     total = hard[...] * col[:, 0:1] + tgt[...].astype(F32) * col[:, 1:2]
     for g in range(parts.shape[0]):
         total = total + parts[g].astype(F32) * col[:, 3 + g : 4 + g]
     scaled = jnp.clip(total * col[:, 2:3], -32767.0, 32767.0)
     coded = jnp.round(scaled).astype(jnp.int32).astype(jnp.int16)
-    out[...] = coded
-    high[...] = coded
-
-
-def line_kernel(keep, got, m1, m2, m3, mine, other):
+    for g in range(parts.shape[0]):
+        out[g] = coded
+
+
+def code_call(parts, hard, tgt, col, after):
+    groups, rows, width = parts.shape
+    half = rows // 2
+    return pl.pallas_call(
+        code_kernel,
+        out_shape=jax.ShapeDtypeStruct((groups, rows, width), jnp.int16),
+        grid=(2,),
+        in_specs=[
+            pl.BlockSpec((groups, half, width), lambda i: (0, i, 0)),
+            pl.BlockSpec((half, width), lambda i: (i, 0)),
+            pl.BlockSpec((half, width), lambda i: (i, 0)),
+            pl.BlockSpec((half, col.shape[1]), lambda i: (i, 0)),
+        ]
+        + [pl.BlockSpec(memory_space=pl.ANY)] * len(after),
+        out_specs=pl.BlockSpec((groups, half, width), lambda i: (0, i, 0)),
+        cost_estimate=pl.CostEstimate(flops=30 * rows * width, bytes_accessed=40 * rows * width, transcendentals=0),
+        name="code",
+    )(parts, hard, tgt, col, *after)
+
+
+def line_kernel(keep, got, m1, m2, m3, _, mine, other):
     rows = mine.shape[0]
     total = keep[0] + got[0].astype(F32)
     for part in (m1, m2, m3):
         total = total + part[...].astype(F32)
     mine[...] = total[:rows, :]
     other[...] = total[rows:, :].astype(BF)
-
-
-def decode_kernel(order, scale, own, side, far1, far2, far3, pairs1, pairs2, pairs3, far_side, out):
-    step = pl.program_id(0)
-    half = own.shape[0] // 2
-    far, pairs = (None, far1, far2, far3), (None, pairs1, pairs2, pairs3)
-    for dx in range(4):
-        for dy in range(2):
-
-            @pl.when(step == dx * 2 + dy)
-            def _():
-                if dx == 0:
-                    whole = (own if dy == 0 else side)[...]
-                    out[...] = whole.astype(jnp.int32).astype(F32) * scale[...]
-                else:
-                    low = pairs[dx][dy]
-                    high = far[dx][...] if dy == 0 else far_side[dx - 1]
-                    out[0:half, :] = low.astype(jnp.int32).astype(F32) * scale[0:half, :]
-                    out[half:, :] = high.astype(jnp.int32).astype(F32) * scale[half:, :]
-
-
-def decode_call(order, scale, pieces):
-    rows, width = pieces[0].shape
-    total = scale.shape[0]
-    return pl.pallas_call(
-        decode_kernel,
-        out_shape=jax.ShapeDtypeStruct((total, width), F32),
-        grid_spec=pltpu.PrefetchScalarGridSpec(
-            num_scalar_prefetch=1,
-            grid=(total // rows,),
-            in_specs=[pl.BlockSpec((rows, 1), lambda i, p: (p[i], 0))]
-            + [pl.BlockSpec(x.shape, lambda i, p, n=x.ndim: (0,) * n) for x in pieces],
-            out_specs=pl.BlockSpec((rows, width), lambda i, p: (p[i], 0)),
-        ),
-        cost_estimate=pl.CostEstimate(flops=total * width, bytes_accessed=total * width * 6, transcendentals=0),
-        name="decode",
-    )(order, scale, *pieces)
 
 
 def shards(source_emb, target_emb, hard_pool, hard_index, language, margin):
@@ -272,22 +254,20 @@
     position = jnp.arange(rows, dtype=jnp.int32)
     same = (owner[:, None] == owner[None, :]) & (position[None, :] < position[:, None])
     slot = owner * cap + jnp.sum(same.astype(jnp.int32), axis=1)
-    at_slot = slot[:, None] == jnp.arange(slots, dtype=jnp.int32)[None, :]
-    requests = jnp.sum(jnp.where(at_slot, pool_row[:, None] + 1, 0), axis=0) - 1
-    wanted = lax.all_to_all(requests.reshape(owners, cap), ("grp", "blk"), 0, 0, tiled=True)
+    pick = (slot[:, None] == jnp.arange(slots, dtype=jnp.int32)[None, :]).astype(BF)
+    lane = jnp.arange(128, dtype=jnp.int32)[None, :]
+    note = jnp.where(lane == 0, pool_row[:, None] + 1, jnp.where(lane == 1, position[:, None], 0)).astype(BF)
+    sent = dot_f32(pick, jnp.concatenate([own_source, note], axis=1), ((0,), (0,))).astype(BF)
+    sent = sent.reshape(owners, cap, width + 128)
+
     lang_match = language[:, None] == jnp.arange(margin.shape[0], dtype=jnp.int32)[None, :]
     margin_row = jnp.sum(jnp.where(lang_match, margin[None, :], 0.0), axis=1)
 
     across = hop_blk(target_emb, 0, 1, 0)
+    sent, across = lax.optimization_barrier((sent, across))
+    asked = lax.all_to_all(sent, ("grp", "blk"), 0, 0, tiled=True)
     line = {0: target_emb, **{dz: hop_blk(target_emb, -dz, 0, 0) for dz in (1, 3, 2)}}
     lines = {0: across, **{dz: hop_blk(across, -dz, 0, 0) for dz in (1, 3, 2)}}
-    near = {dz: jnp.concatenate([line[dz], lines[dz]]) for dz in (0, 1, 3, 2)}
-    away = {dz: hop_blk(near[dz], 0, 0, 1) for dz in (0, 1, 3, 2)}
-
-    own_target = lax.ppermute(
-        target_emb, ("grp", "blk"), [(16 * i + j, (j % 8) * 16 + 2 * i + j // 8) for i in range(8) for j in range(16)]
-    )
-
     holds = grp == blk // 2
     place = {}
     for dz in range(4):
@@ -302,25 +282,43 @@
 
     stats, so_far = [], ()
 
-    def add_chunk(n):
+    def pair_of(n):
+        dz = CHUNKS[n][0][0]
+        near = jnp.concatenate([line[dz], lines[dz]])
+        return near, hop_blk(near, 0, 0, 1)
+
+    def add_chunk(n, pair):
         nonlocal so_far
-        e, stat, tgt = score_call(places[n], source_emb, near[CHUNKS[n][0][0]], away[CHUNKS[n][0][0]], n, so_far)
+        e, stat, tgt = score_call(places[n], source_emb, *pair, n, so_far)
         so_far = (e, tgt)
         stats.append(stat)
 
-    add_chunk(0)
-    wanted, stats[0] = lax.optimization_barrier((wanted, stats[0]))
-    serve = (wanted.reshape(slots)[:, None] == position[None, :]).astype(BF)
-    served = dot_f32(serve, hard_pool, ((1,), (0,))).astype(BF).reshape(owners, cap, width)
+    add_chunk(0, pair_of(0))
+    asked, line[1], lines[1], line[3], lines[3], stats[0] = lax.optimization_barrier(
+        (asked, line[1], lines[1], line[3], lines[3], stats[0])
+    )
+    asked = asked.reshape(slots, width + 128)
+    asker_rows = asked[:, :width]
+    pool_at = asked[:, width].astype(jnp.int32) - 1
+    asker_at = asked[:, width + 1].astype(jnp.int32)
+    serve = (pool_at[:, None] == position[None, :]).astype(BF)
+    served = dot_f32(serve, hard_pool, ((1,), (0,))).astype(BF)
+    first_pair = pair_of(1)
+    second_pair = pair_of(2)
     served, places[1] = lax.optimization_barrier((served, places[1]))
-    fetched = lax.all_to_all(served, ("grp", "blk"), 0, 0, tiled=True).reshape(slots, width)
-    add_chunk(1)
-    add_chunk(2)
+    fetched = lax.all_to_all(served.reshape(owners, cap, width), ("grp", "blk"), 0, 0, tiled=True)
+    asked_score = jnp.sum(asker_rows.astype(F32) * served.astype(F32), axis=1)
+    add_chunk(1, first_pair)
+    early_target, line[2], lines[2], stats[1] = lax.optimization_barrier((target_emb, line[2], lines[2], stats[1]))
+    own_target = lax.ppermute(
+        early_target, ("grp", "blk"), [(16 * i + j, (j % 8) * 16 + 2 * i + j // 8) for i in range(8) for j in range(16)]
+    )
+    last_pair = pair_of(2 + 1)
+    add_chunk(2, second_pair)
     fetched, stats[2] = lax.optimization_barrier((fetched, stats[2]))
-    pick = at_slot.astype(BF)
-    hard_rows = dot_f32(pick, fetched, ((1,), (0,)))
+    hard_rows = dot_f32(pick, fetched.reshape(slots, width), ((1,), (0,)))
     hard_score = jnp.sum(own_source.astype(F32) * hard_rows, axis=1)
-    add_chunk(3)
+    add_chunk(3, last_pair)
 
     tops = jnp.stack([stat[0] for stat in stats])
     sums = jnp.stack([stat[1] for stat in stats])
@@ -336,7 +334,6 @@
     source_part = source_call(jnp.concatenate([jnp.exp(tops - soft_top), jnp.zeros((4, total), F32)]), *so_far)
     everyone, source_part = lax.optimization_barrier((everyone, source_part))
     source_parts = lax.all_to_all(source_part.reshape(8, rows, width), "grp", 0, 0, tiled=True)
-    token = hop_blk(source_part[:16, :128], 0, 0, 1)
     pos = jnp.sum(everyone[:, 2], axis=0)
     hard_all = jnp.max(everyone[:, 3], axis=0)
     reach = jnp.max(everyone[:, 4], axis=0)
@@ -347,26 +344,38 @@
     less = jnp.exp(pos - log_total) - 1.0
     diag_weight = jnp.where(holds, less, 0.0)
 
-    x_at, y_at = grp // 2, grp % 2
     mass = jnp.abs(less) + off * jnp.exp(top - log_total)
     bound = jnp.maximum(1.01 * reach * mass, 1e-30)
     col = jnp.concatenate(
         [jnp.stack([jnp.exp(hard_all - log_total), less, 32767.0 / bound]), jnp.exp(everyone[:, 0] - log_total[None])]
     )
     col = lax.dynamic_slice_in_dim(col, start, rows, 1)
-    hard_prob = col[0]
     col = jnp.transpose(col)
-    half = rows // 2
+
+    all_logs = jnp.concatenate([log_total[None], hop_blk(log_total[None], 0, 0, 1)])
+    all_logs = jnp.concatenate([all_logs] + [hop_blk(all_logs, -dz, 0, 0) for dz in (1, 2, 3)])
+    all_logs = jnp.concatenate([all_logs, hop_blk(all_logs, 0, 1, 0)])
+    asker = jnp.arange(owners, dtype=jnp.int32)
+    asker_blk = asker % 16
+    log_at = ((asker_blk // 2 % 2) ^ y) * 8 + (asker_blk // 4 - z) % 4 * 2 + ((asker_blk % 2) ^ c)
+    log_rows = jnp.take(all_logs, jnp.repeat(log_at, cap), axis=0, mode="clip")
+    row_in_block = jnp.repeat(asker // 16 * rows, cap) + asker_at
+    match = row_in_block[:, None] == jnp.arange(total, dtype=jnp.int32)[None, :]
+    asked_log = jnp.sum(jnp.where(match, log_rows, 0.0), axis=1)
+    asked_prob = jnp.where(pool_at >= 0, jnp.exp(jnp.where(pool_at >= 0, asked_score - asked_log, LOW)), 0.0)
+    pool_terms = (asked_prob[:, None] * asker_rows.astype(F32)).astype(BF)
+    pool_grad = dot_f32(serve, pool_terms, ((0,), (0,)))
 
     weights = jnp.concatenate([jnp.exp(tops - log_total), diag_weight[None], jnp.zeros((3, total), F32)])
-    keep, give = target_call(flat, weights, so_far[0], source_emb, token)
+    keep, give = target_call(flat, weights, so_far[0], source_emb, all_logs)
     got = hop_blk(give, 0, 0, 1)
-    moved = []
-    for n in (1, 2, 3):
-        dz = CHUNKS[n][0][0]
-        moved.append(hop_blk((keep[n] + got[n].astype(F32)).astype(BF), dz, 0, 0))
+    leave = [(keep[n] + got[n].astype(F32)).astype(BF) for n in (1, 2, 3)]
+    coded = code_call(source_parts, hard_rows, own_target, col, [])
+    source_codes = lax.all_to_all(coded, "grp", 0, 0, tiled=True).reshape(total, width)
+    source_grad = source_codes.astype(F32) * (bound * (1.0 / 32767.0))[:, None]
+    moved = [hop_blk(leave[n - 1], CHUNKS[n][0][0], 0, 0) for n in (1, 2, 3)]
     whole = [pl.BlockSpec((1, 2 * rows, width), lambda i: (0, 0, 0))] * 2
-    whole += [pl.BlockSpec((2 * rows, width), lambda i: (0, 0))] * 3
+    whole += [pl.BlockSpec((2 * rows, width), lambda i: (0, 0))] * 3 + [pl.BlockSpec(memory_space=pl.ANY)]
     mine, other = pl.pallas_call(
         line_kernel,
         out_shape=(jax.ShapeDtypeStruct((rows, width), F32), jax.ShapeDtypeStruct((rows, width), BF)),
@@ -375,39 +384,8 @@
         out_specs=[pl.BlockSpec((rows, width), lambda i: (0, 0))] * 2,
         cost_estimate=pl.CostEstimate(flops=10 * rows * width, bytes_accessed=30 * rows * width, transcendentals=0),
         name="lines",
-    )(keep, got, *moved)
+    )(keep, got, *moved, coded)
     target_grad = mine + hop_blk(other, 0, 1, 0).astype(F32)
-
-    coded, coded_high = pl.pallas_call(
-        code_kernel,
-        out_shape=(jax.ShapeDtypeStruct((rows, width), jnp.int16), jax.ShapeDtypeStruct((half, width), jnp.int16)),
-        grid=(2,),
-        in_specs=[
-            pl.BlockSpec((8, half, width), lambda i: (0, i, 0)),
-            pl.BlockSpec((half, width), lambda i: (i, 0)),
-            pl.BlockSpec((half, width), lambda i: (i, 0)),
-            pl.BlockSpec((half, col.shape[1]), lambda i: (i, 0)),
-            pl.BlockSpec(memory_space=pl.ANY),
-        ],
-        out_specs=(pl.BlockSpec((half, width), lambda i: (i, 0)), pl.BlockSpec((half, width), lambda i: (0, 0))),
-        cost_estimate=pl.CostEstimate(flops=10 * rows * width, bytes_accessed=22 * rows * width, transcendentals=0),
-        name="code",
-    )(source_parts, hard_rows, own_target, col, other)
-    hard_gate = hard_prob + 0.0 * coded[0, 0].astype(F32)
-    side = hop_grp(coded, 0, 1)
-    far = [hop_grp(coded_high, -dx, 0) for dx in (1, 2, 3)]
-    low = jnp.stack([coded[:half], side[:half]])
-    pairs = [hop_grp(low, -dx, 0) for dx in (1, 2, 3)]
-    far_side = hop_grp(jnp.stack(far), 0, 1)
-    blocks = jnp.stack([((x_at + dx) % 4) * 2 + (y_at ^ dy) for dx in range(4) for dy in range(2)])
-    source_grad = decode_call(
-        blocks, (bound * (1.0 / 32767.0))[:, None], [coded, side, *far, *pairs, far_side]
-    )
-
-    contribution = (hard_gate[:, None] * own_source.astype(F32)).astype(BF)
-    outgoing = dot_f32(pick, contribution, ((0,), (0,))).astype(BF).reshape(owners, cap, width)
-    incoming = lax.all_to_all(outgoing, ("grp", "blk"), 0, 0, tiled=True).reshape(slots, width)
-    pool_grad = dot_f32(serve, incoming, ((0,), (0,)))
     return (row_loss, source_grad, target_grad, pool_grad)
 
 

time: 244 us -> 256 us (1.049)
  starting transfers between devices: 73.4 us -> 92.1 us
  Pallas kernels: 72.5 us -> 60.1 us
  waiting for transfers between devices: 43.7 us -> 47.5 us
  local copies, waits for them, and re-layouts: 26.5 us -> 29.2 us
    ppermute x17 -> x21, waiting for transfers between devices: 30.8 us -> 47.5 us  [hop_blk(): return lax.ppermute(value, 'blk', route)]
    all_to_all x3, starting transfers between devices: 26.6 us -> 39.5 us  [the longest x1 18.9 us: shards(): lax.all_to_all(served.reshape(owners, cap, width), ('grp', 'blk'), 0, 0,...]
    all_to_all x3, waiting for transfers between devices: 12 us -> 0.01 us  [the longest x1 0.01 us: shards(): asked = lax.all_to_all(sent, ('grp', 'blk'), 0, 0, tiled=True)]
    ppermute x9 -> x1, starting transfers between devices: 14.7 us -> 3.75 us  [shards(): lax.ppermute(early_target, ('grp', 'blk'), [(16 * i + j, j % 8 * 16 + 2 *...]
    ppermute x17 -> x21, starting transfers between devices: 22.8 us -> 32.6 us  [hop_blk(): return lax.ppermute(value, 'blk', route)]
    pallas_call x2 -> x1, Pallas kernels: 10.6 us -> 3.33 us  [code_call(): pl.pallas_call(code_kernel, out_shape=jax.ShapeDtypeStruct((groups, rows,...]
    all_to_all x1, starting transfers between devices: 4.61 us -> 10.8 us  [shards(): lax.all_to_all(jnp.broadcast_to(mine[None], (8, 8, total)), 'grp', 0, 0,...]
    pallas_call x1, Pallas kernels: 17.2 us -> 12.2 us  [source_call(): pl.pallas_call(source_kernel, out_shape=jax.ShapeDtypeStruct((total, widt...]
  transfers between devices with their start and end apart: 31 -> 27, of which waited for: 8 -> 10; matrix products, arithmetic and copies ran while one was open for 16% -> 18% of each run, Pallas kernels for 21% -> 21%
where the time goes in v1:
time: 256 us; the launch traced here: 254 us
  starting transfers between devices  92.1 us (36%)
  Pallas kernels  60.1 us (23%)
  waiting for transfers between devices  47.5 us (19%)
  local copies, waits for them, and re-layouts  29.2 us (11%)
  other arithmetic  18 us (7%)
  matrix products  6 us (2%)
    ppermute x21, waiting for transfers between devices, hop_blk(): return lax.ppermute(value, 'blk', route)  47.5 us
    ppermute x21, starting transfers between devices, hop_blk(): return lax.ppermute(value, 'blk', route)  32.6 us
    pallas_call x4, Pallas kernels, score_call(): pl.pallas_call(score_kernel, out_shape=(pltpu.HBM((4, total, cols), BF),...  26.1 us
    all_to_all x1, starting transfers between devices, shards(): lax.all_to_all(served.reshape(owners, cap, width), ('grp', 'blk'), 0, 0,...  18.9 us
    pallas_call x1, Pallas kernels, target_call(): pl.pallas_call(target_kernel, out_shape=(jax.ShapeDtypeStruct(half, F32),...  15.4 us
    pallas_call x1, Pallas kernels, source_call(): pl.pallas_call(source_kernel, out_shape=jax.ShapeDtypeStruct((total, widt...  12.2 us
    all_to_all x1, starting transfers between devices, shards(): lax.all_to_all(jnp.broadcast_to(mine[None], (8, 8, total)), 'grp', 0, 0,...  10.8 us
    all_to_all x1, starting transfers between devices, shards(): asked = lax.all_to_all(sent, ('grp', 'blk'), 0, 0, tiled=True)  10.7 us
  transfers between devices with their start and end apart: 27, of which 10 were waited for; matrix products, arithmetic and copies ran while one was open for 18% of the time, Pallas kernels for 21%

profile of v1, /device:TPU:0, one launch (start us, length us, event | category | flops | bytes accessed | tf_op | source)
XLA Modules:
  0.0 254.1 jit_solution(14260124615204863162)
XLA Ops:
  0.6 3.4 %collective-permute-start = (bf16[192,768]{1,0:T(8,128)(2,1)}, bf16[192,768]{1,0:T(8,128)(2,1)}, u32[]{:S(2)}, u32[]{:S(2)}) collective-permute-start(bf16[192,768]{1,0:T(8,128)(2,1)} %param.7), channel_id=1, source_target_pairs={{0,2},{1,3},{2,0},{3,1},{4,6},{5,7},{6,4},{7,5},{8,10},{9,11},{10,... | collective-permute-start | bytes 884744 | tf_op jit(solution)/shard_map/ppermute | solution.py:21
  12.4 4.2 %collective-permute-start.1 = (bf16[192,768]{1,0:T(8,128)(2,1)}, bf16[192,768]{1,0:T(8,128)(2,1)}, u32[]{:S(2)}, u32[]{:S(2)}) collective-permute-start(bf16[192,768]{1,0:T(8,128)(2,1)} %param.7), channel_id=1, source_target_pairs={{0,12},{1,13},{2,14},{3,15},{4,0},{5,1},{6,2},{7,3},{8,4},{9,5},{1... | collective-permute-start | bytes 884744 | tf_op jit(solution)/shard_map/ppermute | solution.py:21
  16.6 10.7 %all-to-all-start = ((bf16[128,3,896]{2,1,0:T(4,128)(2,1)}), bf16[128,3,896]{2,1,0:T(4,128)(2,1)}, u32[]{:S(2)}, u32[]{:S(2)}) async-start(bf16[128,3,896]{2,1,0:T(4,128)(2,1)} %reshape.298), calls=%async_computation | async-start | bytes 1835008 | tf_op jit(solution)/shard_map/all_to_all | solution.py:268
  28.6 2.8 %collective-permute-start.2 = (bf16[192,768]{1,0:T(8,128)(2,1)}, bf16[192,768]{1,0:T(8,128)(2,1)}, u32[]{:S(2)}, u32[]{:S(2)}) collective-permute-start(bf16[192,768]{1,0:T(8,128)(2,1)} %collective-permute-done), channel_id=1, source_target_pairs={{0,12},{1,13},{2,14},{3,15},{4,0},{5,1},{6,2},{7,3},{8,4},{9,5},{1... | collective-permute-start | bytes 884744 | tf_op jit(solution)/shard_map/ppermute | solution.py:21
  33.7 6.5 %scores.4 = (bf16[4,1536,768]{2,1,0:T(8,128)(2,1)}, f32[8,1536]{1,0:T(8,128)S(1)}, bf16[4,768,768]{2,1,0:T(8,128)(2,1)}) custom-call(s32[4]{0:T(128)S(1)} %pad_add_fusion.place, bf16[1536,768]{1,0:T(8,128)(2,1)S(1)} %copy-done.1, bf16[384,768]{1,0:T(8,128)(2,1)S(1)} %constant_dynamic-update-slice_fusion.near_pair, ...), custom_call_target="tpu_custom_call" | custom-call | flops 1811939328 | bytes 4718592 | tf_op jit(solution)/shard_map/scores/pallas_call | solution.py:83
  41.7 4.6 %collective-permute-done.2 = bf16[192,768]{1,0:T(8,128)(2,1)} collective-permute-done((bf16[192,768]{1,0:T(8,128)(2,1)}, bf16[192,768]{1,0:T(8,128)(2,1)}, u32[]{:S(2)}, u32[]{:S(2)}) %collective-permute-start.2) | collective-permute-done | bytes 294944 | tf_op jit(solution)/shard_map/ppermute | solution.py:21
  47.9 3.0 %reshape.299 = bf16[384,896]{1,0:T(8,128)(2,1)} reshape(bf16[128,3,896]{2,1,0:T(4,128)(2,1)} %all-to-all-done) | data formatting | bytes 1376256 | tf_op jit(solution)/shard_map/reshape | solution.py:300
  61.4 18.9 %all-to-all-start.1 = ((bf16[128,3,768]{2,1,0:T(4,128)(2,1)}), bf16[128,3,768]{2,1,0:T(4,128)(2,1)}, u32[]{:S(2)}, u32[]{:S(2)}) async-start(bf16[128,3,768]{2,1,0:T(4,128)(2,1)} %reshape.300), calls=%async_computation.1 | async-start | bytes 1572864 | tf_op jit(solution)/shard_map/all_to_all | solution.py:309
  81.1 6.5 %scores.5 = (bf16[4,1536,768]{2,1,0:T(8,128)(2,1)}, f32[8,1536]{1,0:T(8,128)S(1)}, bf16[4,768,768]{2,1,0:T(8,128)(2,1)}) custom-call(s32[4]{0:T(128)S(1)} %pad_add_fusion.1.place, bf16[1536,768]{1,0:T(8,128)(2,1)S(1)} %copy-done.1, bf16[384,768]{1,0:T(8,128)(2,1)S(1)} %constant_dynamic-update-slice_fusion.2.near_pair, ...), custom_call_target="tpu_custom_call", output_to_operand_aliasing={{0}: (4, {}), {2}: (5, {})} | custom-call | flops 1811939328 | bytes 4718592 | tf_op jit(solution)/shard_map/scores/pallas_call | solution.py:83
  87.6 3.8 %collective-permute-start.11 = (bf16[192,768]{1,0:T(8,128)(2,1)}, bf16[192,768]{1,0:T(8,128)(2,1)}, u32[]{:S(2)}, u32[]{:S(2)}) collective-permute-start(bf16[192,768]{1,0:T(8,128)(2,1)} %param.7), channel_id=1, source_target_pairs={{0,0},{1,16},{2,32},{3,48},{4,64},{5,80},{6,96},{7,112},{8,1},{9,1... | collective-permute-start | bytes 884744 | tf_op jit(solution)/shard_map/ppermute | solution.py:313
  93.6 6.7 %scores.6 = (bf16[4,1536,768]{2,1,0:T(8,128)(2,1)}, f32[8,1536]{1,0:T(8,128)S(1)}, bf16[4,768,768]{2,1,0:T(8,128)(2,1)}) custom-call(s32[4]{0:T(128)S(1)} %pad_add_fusion.2.place, bf16[1536,768]{1,0:T(8,128)(2,1)S(1)} %copy-done.1, bf16[384,768]{1,0:T(8,128)(2,1)} %constant_dynamic-update-slice_fusion.4.near_pair, ...), custom_call_target="tpu_custom_call", output_to_operand_aliasing={{0}: (4, {}), {2}: (5, {})} | custom-call | flops 1811939328 | bytes 4718592 | tf_op jit(solution)/shard_map/scores/pallas_call | solution.py:83
  102.5 3.0 %abs_reduce_fusion = (f32[]{:T(128)}, f32[192]{0:T(256)S(1)}, f32[192]{0:T(256)S(1)}, f32[192,768]{1,0:T(8,128)}) fusion(bf16[192,768]{1,0:T(8,128)(2,1)} %copy-done.6, bf16[192,768]{1,0:T(8,128)(2,1)} %collective-permute-done.11.tgt, bf16[384,768]{1,0:T(8,128)(2,1)} %reshape.301, s32[192]{0:T(256)S(1)} %multiply_add_fusion), kind=kOutput, calls=%fused_computation.25 | convolution fusion | flops 114499200 | bytes 1771780 | tf_op jit(solution)/shard_map/dot_general | solution.py:29
  105.9 6.5 %scores.7 = (bf16[4,1536,768]{2,1,0:T(8,128)(2,1)}, f32[8,1536]{1,0:T(8,128)S(1)}, bf16[4,768,768]{2,1,0:T(8,128)(2,1)}) custom-call(s32[4]{0:T(128)S(1)} %pad_add_fusion.3.place, bf16[1536,768]{1,0:T(8,128)(2,1)S(1)} %copy-done.1, bf16[384,768]{1,0:T(8,128)(2,1)S(1)} %constant_dynamic-update-slice_fusion.6.near_pair, ...), custom_call_target="tpu_custom_call", output_to_operand_aliasing={{0}: (4, {}), {2}: (5, {})} | custom-call | flops 1811939328 | bytes 4718592 | tf_op jit(solution)/shard_map/scores/pallas_call | solution.py:83
  114.1 10.8 %all-to-all-start.2 = ((f32[8,8,1536]{2,1,0:T(8,128)}), f32[8,8,1536]{2,1,0:T(8,128)S(1)}, u32[]{:S(2)}, u32[]{:S(2)}) async-start(f32[8,8,1536]{2,1,0:T(8,128)} %broadcast_in_dim.122), calls=%async_computation.2 | async-start | bytes 786432 | tf_op jit(solution)/shard_map/all_to_all | solution.py:333
  125.5 12.2 %source_terms.1 = bf16[1536,768]{1,0:T(8,128)(2,1)} custom-call(f32[8,1536]{1,0:T(8,128)} %concatenate.44.w_ref, bf16[4,1536,768]{2,1,0:T(8,128)(2,1)} %get-tuple-element.64.e_ref, bf16[4,768,768]{2,1,0:T(8,128)(2,1)} %get-tuple-element.65.tgt_ref), custom_call_target="tpu_custom_call" | custom-call | flops 7247757312 | bytes 11796480 | tf_op jit(solution)/shard_map/source_terms/pallas_call | solution.py:123
  139.0 5.4 %all-to-all-start.3 = ((bf16[8,192,768]{2,1,0:T(8,128)(2,1)}), bf16[8,192,768]{2,1,0:T(8,128)(2,1)S(1)}, u32[]{:S(2)}, u32[]{:S(2)}) async-start(bf16[8,192,768]{2,1,0:T(8,128)(2,1)} %bitcast.44), calls=%async_computation.3 | async-start | bytes 4718592 | tf_op jit(solution)/shard_map/all_to_all | solution.py:336
  144.4 3.1 %collective-permute-start.13 = (f32[2,1536]{1,0:T(2,128)S(1)}, f32[2,1536]{1,0:T(2,128)S(1)}, u32[]{:S(2)}, u32[]{:S(2)}) collective-permute-start(f32[2,1536]{1,0:T(2,128)S(1)} %pad_maximum_fusion.1), channel_id=1, source_target_pairs={{0,12},{1,13},{2,14},{3,15},{4,0},{5,1},{6,2},{7,3},{8,4},{9,5},{1... | collective-permute-start | bytes 36872 | tf_op jit(solution)/shard_map/ppermute | solution.py:21
  148.9 3.8 %collective-permute-done.14 = f32[2,1536]{1,0:T(2,128)S(1)} collective-permute-done((f32[2,1536]{1,0:T(2,128)S(1)}, f32[2,1536]{1,0:T(2,128)S(1)}, u32[]{:S(2)}, u32[]{:S(2)}) %collective-permute-start.14) | collective-permute-done | bytes 12320 | tf_op jit(solution)/shard_map/ppermute | solution.py:21
  152.8 3.6 %collective-permute-start.16 = (f32[8,1536]{1,0:T(8,128)S(1)}, f32[8,1536]{1,0:T(8,128)S(1)}, u32[]{:S(2)}, u32[]{:S(2)}) collective-permute-start(f32[8,1536]{1,0:T(8,128)S(1)} %concatenate.49), channel_id=1, source_target_pairs={{0,2},{1,3},{2,0},{3,1},{4,6},{5,7},{6,4},{7,5},{8,10},{9,11},{10,... | collective-permute-start | bytes 147464 | tf_op jit(solution)/shard_map/ppermute | solution.py:21
  157.1 9.6 %collective-permute-done.16 = f32[8,1536]{1,0:T(8,128)S(1)} collective-permute-done((f32[8,1536]{1,0:T(8,128)S(1)}, f32[8,1536]{1,0:T(8,128)S(1)}, u32[]{:S(2)}, u32[]{:S(2)}) %collective-permute-start.16) | collective-permute-done | bytes 49184 | tf_op jit(solution)/shard_map/ppermute | solution.py:21
  168.0 15.4 %target_terms.1 = (f32[4,384,768]{2,1,0:T(8,128)}, bf16[4,384,768]{2,1,0:T(8,128)(2,1)}) custom-call(s32[16]{0:T(128)} %concatenate.46.place, f32[8,1536]{1,0:T(8,128)} %maximum_maximum_fusion.w_ref, bf16[4,1536,768]{2,1,0:T(8,128)(2,1)} %get-tuple-element.64.e_ref, bf16[1536,768]{1,0:T(8,128)(2,1)} %src_ref.1, f32[16,1536]{1,0:T(8,128)} %concatenate.50._), custom_call_target="tpu_custom_call" | custom-call | flops 7247757312 | bytes 18874368 | tf_op jit(solution)/shard_map/target_terms/pallas_call | solution.py:175
  185.7 3.3 %code.1._ = s16[8,192,768]{2,1,0:T(8,128)(2,1)} custom-call(bf16[8,192,768]{2,1,0:T(8,128)(2,1)} %copy-done.3, f32[192,768]{1,0:T(8,128)} %get-tuple-element.107.hard, bf16[192,768]{1,0:T(8,128)(2,1)} %collective-permute-done.11.tgt, f32[192,11]{1,0:T(8,128)} %bitcast.45), custom_call_target="tpu_custom_call" | custom-call | flops 4423680 | bytes 5898240 | tf_op jit(solution)/shard_map/code/pallas_call | solution.py:215
  189.1 9.9 %all-to-all-start.4 = ((s16[8,192,768]{2,1,0:T(8,128)(2,1)}), s16[8,192,768]{2,1,0:T(8,128)(2,1)S(1)}, u32[]{:S(2)}, u32[]{:S(2)}) async-start(s16[8,192,768]{2,1,0:T(8,128)(2,1)} %code.1._), calls=%async_computation.4 | async-start | bytes 4718592 | tf_op jit(solution)/shard_map/all_to_all | solution.py:374
  199.0 3.9 %fusion.6 = (bf16[384,768]{1,0:T(8,128)(2,1)}, bf16[384,768]{1,0:T(8,128)(2,1)}, bf16[384,768]{1,0:T(8,128)(2,1)}) fusion(f32[4,384,768]{2,1,0:T(8,128)} %get-tuple-element.68.keep, bf16[4,384,768]{2,1,0:T(8,128)(2,1)} %collective-permute-done.17.got), kind=kLoop, calls=%fused_computation.21 | loop fusion | flops 2654208 | bytes 7077888 | tf_op jit(solution)/shard_map/convert_element_type | solution.py:372
  202.9 3.3 %collective-permute-start.18 = (bf16[384,768]{1,0:T(8,128)(2,1)}, bf16[384,768]{1,0:T(8,128)(2,1)}, u32[]{:S(2)}, u32[]{:S(2)}) collective-permute-start(bf16[384,768]{1,0:T(8,128)(2,1)} %get-tuple-element.91), channel_id=1, source_target_pairs={{0,4},{1,5},{2,6},{3,7},{4,8},{5,9},{6,10},{7,11},{8,12},{9,13},{1... | collective-permute-start | bytes 1769480 | tf_op jit(solution)/shard_map/ppermute | solution.py:21
  212.3 2.7 %gather_fusion = f32[384,1536]{1,0:T(8,128)} fusion(f32[16,1536]{1,0:T(8,128)S(1)} %copy-done.2, s32[1024]{0:T(1024)S(1)} %pad_clamp_fusion), kind=kCustom, calls=%fused_computation | custom fusion | bytes 4720128 | tf_op jit(solution)/shard_map/jit(_take)/gather | solution.py:361
  217.1 5.3 %collective-permute-done.18.m1 = bf16[384,768]{1,0:T(8,128)(2,1)} collective-permute-done((bf16[384,768]{1,0:T(8,128)(2,1)}, bf16[384,768]{1,0:T(8,128)(2,1)}, u32[]{:S(2)}, u32[]{:S(2)}) %collective-permute-start.18) | collective-permute-done | bytes 589856 | tf_op jit(solution)/shard_map/ppermute | solution.py:21
  222.4 12.0 %collective-permute-done.19.m2 = bf16[384,768]{1,0:T(8,128)(2,1)} collective-permute-done((bf16[384,768]{1,0:T(8,128)(2,1)}, bf16[384,768]{1,0:T(8,128)(2,1)}, u32[]{:S(2)}, u32[]{:S(2)}) %collective-permute-start.19) | collective-permute-done | bytes 589856 | tf_op jit(solution)/shard_map/ppermute | solution.py:21
  236.2 3.0 %lines.1 = (f32[192,768]{1,0:T(8,128)}, bf16[192,768]{1,0:T(8,128)(2,1)}) custom-call(f32[4,384,768]{2,1,0:T(8,128)} %get-tuple-element.68.keep, bf16[4,384,768]{2,1,0:T(8,128)(2,1)} %collective-permute-done.17.got, bf16[384,768]{1,0:T(8,128)(2,1)} %collective-permute-done.18.m1, bf16[384,768]{1,0:T(8,128)(2,1)} %collective-permute-done.19.m2, ...), custom_call_target="tpu_custom_call" | custom-call | flops 1474560 | bytes 4423680 | tf_op jit(solution)/shard_map/lines/pallas_call | solution.py:379
  239.2 2.3 collective-permute-start.21
  243.1 6.2 %collective-permute-done.21 = bf16[192,768]{1,0:T(8,128)(2,1)S(1)} collective-permute-done((bf16[192,768]{1,0:T(8,128)(2,1)}, bf16[192,768]{1,0:T(8,128)(2,1)S(1)}, u32[]{:S(2)}, u32[]{:S(2)}) %collective-permute-start.21) | collective-permute-done | bytes 294944 | tf_op jit(solution)/shard_map/ppermute | solution.py:21
  251.1 3.0 %convert_multiply_fusion = f32[1536,768]{1,0:T(8,128)} fusion(s16[8,192,768]{2,1,0:T(8,128)(2,1)S(1)} %all-to-all-done.4, f32[1536]{0:T(1024)S(1)} %get-tuple-element.83), kind=kLoop, calls=%fused_computation.1 | loop fusion | flops 2359296 | bytes 7084032 | tf_op jit(solution)/shard_map/mul | solution.py:375
  (123 shorter events, 53.7 us)
Async XLA Ops:
  0.6 57.6 %copy-start = (bf16[192,768]{1,0:T(8,128)(2,1)S(1)}, bf16[192,768]{1,0:T(8,128)(2,1)}, u32[]{:S(2)}) copy-start(bf16[192,768]{1,0:T(8,128)(2,1)} %param.8) | copy-start | bytes 884740
  0.6 10.7 %collective-permute-start = (bf16[192,768]{1,0:T(8,128)(2,1)}, bf16[192,768]{1,0:T(8,128)(2,1)}, u32[]{:S(2)}, u32[]{:S(2)}) collective-permute-start(bf16[192,768]{1,0:T(8,128)(2,1)} %param.7), channel_id=1, source_target_pairs={{0,2},{1,3},{2,0},{3,1},{4,6},{5,7},{6,4},{7,5},{8,10},{9,11},{10,... | collective-permute-start | bytes 884744 | tf_op jit(solution)/shard_map/ppermute | solution.py:21
  7.0 24.4 %copy-start.7 = (s32[1536]{0:T(1024)S(1)}, s32[1536]{0:T(1024)}, u32[]{:S(2)}) copy-start(s32[1536]{0:T(1024)} %param.10) | copy-start | bytes 18436
  7.0 24.4 %copy-start.8 = (f32[109]{0:T(128)S(1)}, f32[109]{0:T(128)}, u32[]{:S(2)}) copy-start(f32[109]{0:T(128)} %param.11) | copy-start | bytes 1312
  7.0 26.7 %copy-start.1 = (bf16[1536,768]{1,0:T(8,128)(2,1)S(1)}, bf16[1536,768]{1,0:T(8,128)(2,1)}, u32[]{:S(2)}) copy-start(bf16[1536,768]{1,0:T(8,128)(2,1)} %src_ref.1) | copy-start | bytes 7077892
  12.3 19.3 %collective-permute-start.5 = (bf16[384,768]{1,0:T(8,128)(2,1)S(1)}, bf16[384,768]{1,0:T(8,128)(2,1)}, u32[]{:S(2)}, u32[]{:S(2)}) collective-permute-start(bf16[384,768]{1,0:T(8,128)(2,1)S(1)} %constant_dynamic-update-slice_fusion.near_pair), channel_id=1, source_target_pairs={{0,1},{1,0},{2,3},{3,2},{4,5},{5,4},{6,7},{7,6},{8,9},{9,8},{10,11... | collective-permute-start | bytes 1769480 | tf_op jit(solution)/shard_map/ppermute | solution.py:21
  12.4 27.8 %collective-permute-start.1 = (bf16[192,768]{1,0:T(8,128)(2,1)}, bf16[192,768]{1,0:T(8,128)(2,1)}, u32[]{:S(2)}, u32[]{:S(2)}) collective-permute-start(bf16[192,768]{1,0:T(8,128)(2,1)} %param.7), channel_id=1, source_target_pairs={{0,12},{1,13},{2,14},{3,15},{4,0},{5,1},{6,2},{7,3},{8,4},{9,5},{1... | collective-permute-start | bytes 884744 | tf_op jit(solution)/shard_map/ppermute | solution.py:21
  16.6 25.1 %collective-permute-start.3 = (bf16[192,768]{1,0:T(8,128)(2,1)}, bf16[192,768]{1,0:T(8,128)(2,1)}, u32[]{:S(2)}, u32[]{:S(2)}) collective-permute-start(bf16[192,768]{1,0:T(8,128)(2,1)} %param.7), channel_id=1, source_target_pairs={{0,4},{1,5},{2,6},{3,7},{4,8},{5,9},{6,10},{7,11},{8,12},{9,13},{1... | collective-permute-start | bytes 884744 | tf_op jit(solution)/shard_map/ppermute | solution.py:21
  16.6 31.4 %all-to-all-start = ((bf16[128,3,896]{2,1,0:T(4,128)(2,1)}), bf16[128,3,896]{2,1,0:T(4,128)(2,1)}, u32[]{:S(2)}, u32[]{:S(2)}) async-start(bf16[128,3,896]{2,1,0:T(4,128)(2,1)} %reshape.298), calls=%async_computation | async-start | bytes 1835008 | tf_op jit(solution)/shard_map/all_to_all | solution.py:268
  28.6 17.6 %collective-permute-start.2 = (bf16[192,768]{1,0:T(8,128)(2,1)}, bf16[192,768]{1,0:T(8,128)(2,1)}, u32[]{:S(2)}, u32[]{:S(2)}) collective-permute-start(bf16[192,768]{1,0:T(8,128)(2,1)} %collective-permute-done), channel_id=1, source_target_pairs={{0,12},{1,13},{2,14},{3,15},{4,0},{5,1},{6,2},{7,3},{8,4},{9,5},{1... | collective-permute-start | bytes 884744 | tf_op jit(solution)/shard_map/ppermute | solution.py:21
  31.4 16.5 %collective-permute-start.4 = (bf16[192,768]{1,0:T(8,128)(2,1)}, bf16[192,768]{1,0:T(8,128)(2,1)}, u32[]{:S(2)}, u32[]{:S(2)}) collective-permute-start(bf16[192,768]{1,0:T(8,128)(2,1)} %collective-permute-done), channel_id=1, source_target_pairs={{0,4},{1,5},{2,6},{3,7},{4,8},{5,9},{6,10},{7,11},{8,12},{9,13},{1... | collective-permute-start | bytes 884744 | tf_op jit(solution)/shard_map/ppermute | solution.py:21
  31.6 56.0 %collective-permute-start.6 = (bf16[192,768]{1,0:T(8,128)(2,1)}, bf16[192,768]{1,0:T(8,128)(2,1)}, u32[]{:S(2)}, u32[]{:S(2)}) collective-permute-start(bf16[192,768]{1,0:T(8,128)(2,1)} %param.7), channel_id=1, source_target_pairs={{0,8},{1,9},{2,10},{3,11},{4,12},{5,13},{6,14},{7,15},{8,0},{9,1},... | collective-permute-start | bytes 884744 | tf_op jit(solution)/shard_map/ppermute | solution.py:21
  40.2 47.4 %collective-permute-start.7 = (bf16[192,768]{1,0:T(8,128)(2,1)}, bf16[192,768]{1,0:T(8,128)(2,1)}, u32[]{:S(2)}, u32[]{:S(2)}) collective-permute-start(bf16[192,768]{1,0:T(8,128)(2,1)} %collective-permute-done), channel_id=1, source_target_pairs={{0,8},{1,9},{2,10},{3,11},{4,12},{5,13},{6,14},{7,15},{8,0},{9,1},... | collective-permute-start | bytes 884744 | tf_op jit(solution)/shard_map/ppermute | solution.py:21
  52.9 28.2 %collective-permute-start.8 = (bf16[384,768]{1,0:T(8,128)(2,1)S(1)}, bf16[384,768]{1,0:T(8,128)(2,1)}, u32[]{:S(2)}, u32[]{:S(2)}) collective-permute-start(bf16[384,768]{1,0:T(8,128)(2,1)S(1)} %constant_dynamic-update-slice_fusion.2.near_pair), channel_id=1, source_target_pairs={{0,1},{1,0},{2,3},{3,2},{4,5},{5,4},{6,7},{7,6},{8,9},{9,8},{10,11... | collective-permute-start | bytes 1769480 | tf_op jit(solution)/shard_map/ppermute | solution.py:21
  56.4 37.2 %collective-permute-start.9 = (bf16[384,768]{1,0:T(8,128)(2,1)}, bf16[384,768]{1,0:T(8,128)(2,1)}, u32[]{:S(2)}, u32[]{:S(2)}) collective-permute-start(bf16[384,768]{1,0:T(8,128)(2,1)} %constant_dynamic-update-slice_fusion.4.near_pair), channel_id=1, source_target_pairs={{0,1},{1,0},{2,3},{3,2},{4,5},{5,4},{6,7},{7,6},{8,9},{9,8},{10,11... | collective-permute-start | bytes 1769480 | tf_op jit(solution)/shard_map/ppermute | solution.py:21
  61.4 38.8 %all-to-all-start.1 = ((bf16[128,3,768]{2,1,0:T(4,128)(2,1)}), bf16[128,3,768]{2,1,0:T(4,128)(2,1)}, u32[]{:S(2)}, u32[]{:S(2)}) async-start(bf16[128,3,768]{2,1,0:T(4,128)(2,1)} %reshape.300), calls=%async_computation.1 | async-start | bytes 1572864 | tf_op jit(solution)/shard_map/all_to_all | solution.py:309
  87.6 14.9 %collective-permute-start.11 = (bf16[192,768]{1,0:T(8,128)(2,1)}, bf16[192,768]{1,0:T(8,128)(2,1)}, u32[]{:S(2)}, u32[]{:S(2)}) collective-permute-start(bf16[192,768]{1,0:T(8,128)(2,1)} %param.7), channel_id=1, source_target_pairs={{0,0},{1,16},{2,32},{3,48},{4,64},{5,80},{6,96},{7,112},{8,1},{9,1... | collective-permute-start | bytes 884744 | tf_op jit(solution)/shard_map/ppermute | solution.py:313
  93.3 12.6 %collective-permute-start.10 = (bf16[384,768]{1,0:T(8,128)(2,1)S(1)}, bf16[384,768]{1,0:T(8,128)(2,1)}, u32[]{:S(2)}, u32[]{:S(2)}) collective-permute-start(bf16[384,768]{1,0:T(8,128)(2,1)S(1)} %constant_dynamic-update-slice_fusion.6.near_pair), channel_id=1, source_target_pairs={{0,1},{1,0},{2,3},{3,2},{4,5},{5,4},{6,7},{7,6},{8,9},{9,8},{10,11... | collective-permute-start | bytes 1769480 | tf_op jit(solution)/shard_map/ppermute | solution.py:21
  114.1 23.6 %all-to-all-start.2 = ((f32[8,8,1536]{2,1,0:T(8,128)}), f32[8,8,1536]{2,1,0:T(8,128)S(1)}, u32[]{:S(2)}, u32[]{:S(2)}) async-start(f32[8,8,1536]{2,1,0:T(8,128)} %broadcast_in_dim.122), calls=%async_computation.2 | async-start | bytes 786432 | tf_op jit(solution)/shard_map/all_to_all | solution.py:333
  138.3 6.1 %collective-permute-start.12 = (f32[1,1536]{1,0:T(1,128)S(1)}, f32[1,1536]{1,0:T(1,128)S(1)}, u32[]{:S(2)}, u32[]{:S(2)}) collective-permute-start(f32[1,1536]{1,0:T(1,128)S(1)} %get-tuple-element.82), channel_id=1, source_target_pairs={{0,1},{1,0},{2,3},{3,2},{4,5},{5,4},{6,7},{7,6},{8,9},{9,8},{10,11... | collective-permute-start | bytes 18440 | tf_op jit(solution)/shard_map/ppermute | solution.py:21
  139.0 45.3 %all-to-all-start.3 = ((bf16[8,192,768]{2,1,0:T(8,128)(2,1)}), bf16[8,192,768]{2,1,0:T(8,128)(2,1)S(1)}, u32[]{:S(2)}, u32[]{:S(2)}) async-start(bf16[8,192,768]{2,1,0:T(8,128)(2,1)} %bitcast.44), calls=%async_computation.3 | async-start | bytes 4718592 | tf_op jit(solution)/shard_map/all_to_all | solution.py:336
  144.4 4.5 %collective-permute-start.13 = (f32[2,1536]{1,0:T(2,128)S(1)}, f32[2,1536]{1,0:T(2,128)S(1)}, u32[]{:S(2)}, u32[]{:S(2)}) collective-permute-start(f32[2,1536]{1,0:T(2,128)S(1)} %pad_maximum_fusion.1), channel_id=1, source_target_pairs={{0,12},{1,13},{2,14},{3,15},{4,0},{5,1},{6,2},{7,3},{8,4},{9,5},{1... | collective-permute-start | bytes 36872 | tf_op jit(solution)/shard_map/ppermute | solution.py:21
  147.5 5.2 %collective-permute-start.14 = (f32[2,1536]{1,0:T(2,128)S(1)}, f32[2,1536]{1,0:T(2,128)S(1)}, u32[]{:S(2)}, u32[]{:S(2)}) collective-permute-start(f32[2,1536]{1,0:T(2,128)S(1)} %pad_maximum_fusion.1), channel_id=1, source_target_pairs={{0,8},{1,9},{2,10},{3,11},{4,12},{5,13},{6,14},{7,15},{8,0},{9,1},... | collective-permute-start | bytes 36872 | tf_op jit(solution)/shard_map/ppermute | solution.py:21
  147.5 5.2 %collective-permute-start.15 = (f32[2,1536]{1,0:T(2,128)S(1)}, f32[2,1536]{1,0:T(2,128)S(1)}, u32[]{:S(2)}, u32[]{:S(2)}) collective-permute-start(f32[2,1536]{1,0:T(2,128)S(1)} %pad_maximum_fusion.1), channel_id=1, source_target_pairs={{0,4},{1,5},{2,6},{3,7},{4,8},{5,9},{6,10},{7,11},{8,12},{9,13},{1... | collective-permute-start | bytes 36872 | tf_op jit(solution)/shard_map/ppermute | solution.py:21
  152.8 13.9 %collective-permute-start.16 = (f32[8,1536]{1,0:T(8,128)S(1)}, f32[8,1536]{1,0:T(8,128)S(1)}, u32[]{:S(2)}, u32[]{:S(2)}) collective-permute-start(f32[8,1536]{1,0:T(8,128)S(1)} %concatenate.49), channel_id=1, source_target_pairs={{0,2},{1,3},{2,0},{3,1},{4,6},{5,7},{6,4},{7,5},{8,10},{9,11},{10,... | collective-permute-start | bytes 147464 | tf_op jit(solution)/shard_map/ppermute | solution.py:21
  183.4 15.6 %collective-permute-start.17 = (bf16[4,384,768]{2,1,0:T(8,128)(2,1)}, bf16[4,384,768]{2,1,0:T(8,128)(2,1)}, u32[]{:S(2)}, u32[]{:S(2)}) collective-permute-start(bf16[4,384,768]{2,1,0:T(8,128)(2,1)} %get-tuple-element.69), channel_id=1, source_target_pairs={{0,1},{1,0},{2,3},{3,2},{4,5},{5,4},{6,7},{7,6},{8,9},{9,8},{10,11... | collective-permute-start | bytes 7077896 | tf_op jit(solution)/shard_map/ppermute | solution.py:21
  189.1 62.1 %all-to-all-start.4 = ((s16[8,192,768]{2,1,0:T(8,128)(2,1)}), s16[8,192,768]{2,1,0:T(8,128)(2,1)S(1)}, u32[]{:S(2)}, u32[]{:S(2)}) async-start(s16[8,192,768]{2,1,0:T(8,128)(2,1)} %code.1._), calls=%async_computation.4 | async-start | bytes 4718592 | tf_op jit(solution)/shard_map/all_to_all | solution.py:374
  202.9 19.4 %collective-permute-start.18 = (bf16[384,768]{1,0:T(8,128)(2,1)}, bf16[384,768]{1,0:T(8,128)(2,1)}, u32[]{:S(2)}, u32[]{:S(2)}) collective-permute-start(bf16[384,768]{1,0:T(8,128)(2,1)} %get-tuple-element.91), channel_id=1, source_target_pairs={{0,4},{1,5},{2,6},{3,7},{4,8},{5,9},{6,10},{7,11},{8,12},{9,13},{1... | collective-permute-start | bytes 1769480 | tf_op jit(solution)/shard_map/ppermute | solution.py:21
  206.2 28.1 %collective-permute-start.19 = (bf16[384,768]{1,0:T(8,128)(2,1)}, bf16[384,768]{1,0:T(8,128)(2,1)}, u32[]{:S(2)}, u32[]{:S(2)}) collective-permute-start(bf16[384,768]{1,0:T(8,128)(2,1)} %get-tuple-element.90), channel_id=1, source_target_pairs={{0,12},{1,13},{2,14},{3,15},{4,0},{5,1},{6,2},{7,3},{8,4},{9,5},{1... | collective-permute-start | bytes 1769480 | tf_op jit(solution)/shard_map/ppermute | solution.py:21
  208.4 27.7 %collective-permute-start.20 = (bf16[384,768]{1,0:T(8,128)(2,1)}, bf16[384,768]{1,0:T(8,128)(2,1)}, u32[]{:S(2)}, u32[]{:S(2)}) collective-permute-start(bf16[384,768]{1,0:T(8,128)(2,1)} %get-tuple-element.89), channel_id=1, source_target_pairs={{0,8},{1,9},{2,10},{3,11},{4,12},{5,13},{6,14},{7,15},{8,0},{9,1},... | collective-permute-start | bytes 1769480 | tf_op jit(solution)/shard_map/ppermute | solution.py:21
  217.1 24.4 %copy-start.5 = (bf16[384,896]{1,0:T(8,128)(2,1)S(1)}, bf16[384,896]{1,0:T(8,128)(2,1)}, u32[]{:S(2)}) copy-start(bf16[384,896]{1,0:T(8,128)(2,1)} %reshape.299) | copy-start | bytes 2064388
  239.2 10.0 %collective-permute-start.21 = (bf16[192,768]{1,0:T(8,128)(2,1)}, bf16[192,768]{1,0:T(8,128)(2,1)S(1)}, u32[]{:S(2)}, u32[]{:S(2)}) collective-permute-start(bf16[192,768]{1,0:T(8,128)(2,1)} %get-tuple-element.71), channel_id=1, source_target_pairs={{0,2},{1,3},{2,0},{3,1},{4,6},{5,7},{6,4},{7,5},{8,10},{9,11},{10,... | collective-permute-start | bytes 884744 | tf_op jit(solution)/shard_map/ppermute | solution.py:21
  (4 other events, 22.9 us)

commit v2 on v0

--- a/solution.py
+++ b/solution.py
@@ -10,7 +10,7 @@
 LOW = -3e38
 TILE = 768
 PART = 384
-CHUNKS = tuple(((dz, 0), (dz, 1)) for dz in (0, 1, 3, 2))
+CHUNKS = (((0, 0), (0, 1)), ((1, 0), (3, 0)), ((2, 0), (1, 1)), ((3, 1), (2, 1)))
 
 
 def hop_blk(value, dz, dy, dc):
@@ -34,18 +34,18 @@
     return jnp.transpose(jnp.concatenate([rows, pad], axis=0))
 
 
-def score_kernel(place, src, near_pair, away_pair, *refs):
+def score_kernel(place, src, t0, t1, t2, t3, *refs):
     e_out, stat_out, tgt_out, a_ref = refs[-4:]
-    half = near_pair.shape[0]
-    rows = half // 2
+    rows = t0.shape[0]
+    half = 2 * rows
     step = pl.program_id(0)
 
     @pl.when(step == 0)
     def _():
         top = jnp.zeros((1, 1), F32)
-        for q, pair in enumerate((near_pair, away_pair)):
-            block = pair[...]
-            tgt_out[0, q * half : (q + 1) * half, :] = block
+        for q, t in enumerate((t0, t1, t2, t3)):
+            block = t[...]
+            tgt_out[0, q * rows : (q + 1) * rows, :] = block
             top = jnp.maximum(top, jnp.max(jnp.abs(block).astype(F32), keepdims=True))
         a_ref[...] = jnp.broadcast_to(top, a_ref.shape)
 
@@ -74,12 +74,12 @@
     stat_out[...] = jnp.transpose(jnp.concatenate(parts, axis=0))[0:8, :]
 
 
-def score_call(place, src, near_pair, away_pair, n, so_far):
-    half, width = near_pair.shape
+def score_call(place, src, blocks, n, so_far):
+    rows, width = blocks[0].shape
     total = src.shape[0]
-    cols = 2 * half
+    cols = 4 * rows
     so_far = list(so_far)
-    vmem = pl.BlockSpec((half, width), lambda i, p: (0, 0))
+    whole = pl.BlockSpec((rows, width), lambda i, p: (0, 0))
     return pl.pallas_call(
         score_kernel,
         out_shape=(
@@ -90,7 +90,8 @@
         grid_spec=pltpu.PrefetchScalarGridSpec(
             num_scalar_prefetch=1,
             grid=(total // TILE,),
-            in_specs=[pl.BlockSpec((TILE, width), lambda i, p: (i, 0)), vmem, vmem]
+            in_specs=[pl.BlockSpec((TILE, width), lambda i, p: (i, 0))]
+            + [whole] * 4
             + [pl.BlockSpec(memory_space=pl.ANY)] * len(so_far),
             out_specs=(
                 pl.BlockSpec((1, TILE, cols), lambda i, p: (n, i, 0)),
@@ -99,22 +100,21 @@
             ),
             scratch_shapes=[pltpu.VMEM((8, 128), F32)],
         ),
-        input_output_aliases={4: 0, 5: 2} if so_far else {},
+        input_output_aliases={6: 0, 7: 2} if so_far else {},
         compiler_params=pltpu.CompilerParams(vmem_limit_bytes=24 << 20),
         cost_estimate=pl.CostEstimate(
             flops=2 * total * cols * width, bytes_accessed=total * (width + cols) * 2, transcendentals=total * cols
         ),
         name="scores",
-    )(place, src, near_pair, away_pair, *so_far)
-
-
-def source_kernel(w_ref, e_ref, tgt_ref, out, acc):
-    c, i = pl.program_id(0), pl.program_id(1)
-    lane = lax.broadcasted_iota(jnp.int32, (PART, 128), 1)
-    weight = jnp.sum(jnp.where(lane == c, columns_of(w_ref[...]), 0.0), axis=1, keepdims=True)
-    part = dot_f32(e_ref[0], tgt_ref[0], ((1,), (0,))) * weight
-    total = jnp.where(c == 0, 0.0, acc[i]) + part
-    acc[i] = total
+    )(place, src, *blocks, *so_far)
+
+
+def source_kernel(w_ref, e_ref, tgt_ref, out):
+    weights = columns_of(w_ref[...])
+    total = None
+    for c in range(4):
+        part = dot_f32(e_ref[c], tgt_ref[c], ((1,), (0,))) * weights[:, c : c + 1]
+        total = part if total is None else total + part
     out[...] = total.astype(BF)
 
 
@@ -124,14 +124,13 @@
     return pl.pallas_call(
         source_kernel,
         out_shape=jax.ShapeDtypeStruct((total, width), BF),
-        grid=(4, total // PART),
+        grid=(total // PART,),
         in_specs=[
-            pl.BlockSpec((8, PART), lambda c, i: (0, i)),
-            pl.BlockSpec((1, PART, cols), lambda c, i: (c, i, 0)),
-            pl.BlockSpec((1, cols, width), lambda c, i: (c, 0, 0)),
+            pl.BlockSpec((8, PART), lambda i: (0, i)),
+            pl.BlockSpec((4, PART, cols), lambda i: (0, i, 0)),
+            pl.BlockSpec((4, cols, width), lambda i: (0, 0, 0), pipeline_mode=pl.Buffered(1)),
         ],
-        out_specs=pl.BlockSpec((PART, width), lambda c, i: (jnp.where(c == 3, i, 0), 0)),
-        scratch_shapes=[pltpu.VMEM((total // PART, PART, width), F32)],
+        out_specs=pl.BlockSpec((PART, width), lambda i: (i, 0)),
         cost_estimate=pl.CostEstimate(
             flops=8 * total * cols * width, bytes_accessed=total * (8 * cols + 2 * width), transcendentals=0
         ),
@@ -278,15 +277,14 @@
     lang_match = language[:, None] == jnp.arange(margin.shape[0], dtype=jnp.int32)[None, :]
     margin_row = jnp.sum(jnp.where(lang_match, margin[None, :], 0.0), axis=1)
 
-    across = hop_blk(target_emb, 0, 1, 0)
-    line = {0: target_emb, **{dz: hop_blk(target_emb, -dz, 0, 0) for dz in (1, 3, 2)}}
-    lines = {0: across, **{dz: hop_blk(across, -dz, 0, 0) for dz in (1, 3, 2)}}
-    near = {dz: jnp.concatenate([line[dz], lines[dz]]) for dz in (0, 1, 3, 2)}
-    away = {dz: hop_blk(near[dz], 0, 0, 1) for dz in (0, 1, 3, 2)}
-
-    own_target = lax.ppermute(
-        target_emb, ("grp", "blk"), [(16 * i + j, (j % 8) * 16 + 2 * i + j // 8) for i in range(8) for j in range(16)]
-    )
+    have = {(0, 0, 0): target_emb}
+    have[0, 1, 0] = hop_blk(target_emb, 0, 1, 0)
+    for dz in (1, 3, 2):
+        have[dz, 0, 0] = hop_blk(target_emb, -dz, 0, 0)
+    for dz in (1, 3, 2):
+        have[dz, 1, 0] = hop_blk(have[0, 1, 0], -dz, 0, 0)
+    for dz, dy in [pair for chunk in CHUNKS for pair in chunk]:
+        have[dz, dy, 1] = hop_blk(have[dz, dy, 0], 0, 0, 1)
 
     holds = grp == blk // 2
     place = {}
@@ -304,7 +302,7 @@
 
     def add_chunk(n):
         nonlocal so_far
-        e, stat, tgt = score_call(places[n], source_emb, near[CHUNKS[n][0][0]], away[CHUNKS[n][0][0]], n, so_far)
+        e, stat, tgt = score_call(places[n], source_emb, [have[key] for key in order[n]], n, so_far)
         so_far = (e, tgt)
         stats.append(stat)
 
@@ -315,6 +313,10 @@
     served, places[1] = lax.optimization_barrier((served, places[1]))
     fetched = lax.all_to_all(served, ("grp", "blk"), 0, 0, tiled=True).reshape(slots, width)
     add_chunk(1)
+    early_target, stats[1] = lax.optimization_barrier((target_emb, stats[1]))
+    own_target = lax.ppermute(
+        early_target, ("grp", "blk"), [(16 * i + j, (j % 8) * 16 + 2 * i + j // 8) for i in range(8) for j in range(16)]
+    )
     add_chunk(2)
     fetched, stats[2] = lax.optimization_barrier((fetched, stats[2]))
     pick = at_slot.astype(BF)
@@ -361,10 +363,14 @@
     weights = jnp.concatenate([jnp.exp(tops - log_total), diag_weight[None], jnp.zeros((3, total), F32)])
     keep, give = target_call(flat, weights, so_far[0], source_emb, token)
     got = hop_blk(give, 0, 0, 1)
-    moved = []
-    for n in (1, 2, 3):
-        dz = CHUNKS[n][0][0]
-        moved.append(hop_blk((keep[n] + got[n].astype(F32)).astype(BF), dz, 0, 0))
+    where_at = {pair: (n, j) for n, chunk in enumerate(CHUNKS) for j, pair in enumerate(chunk)}
+
+    def both(dz, dy):
+        n, j = where_at[dz, dy]
+        here = slice(j * rows, (j + 1) * rows)
+        return (keep[n, here] + got[n, here].astype(F32)).astype(BF)
+
+    moved = [hop_blk(jnp.concatenate([both(dz, 0), both(dz, 1)]), dz, 0, 0) for dz in (1, 3, 2)]
     whole = [pl.BlockSpec((1, 2 * rows, width), lambda i: (0, 0, 0))] * 2
     whole += [pl.BlockSpec((2 * rows, width), lambda i: (0, 0))] * 3
     mine, other = pl.pallas_call(

time: 244 us -> 224 us (0.918)
  waiting for transfers between devices: 43.7 us -> 30.8 us
  Pallas kernels: 72.5 us -> 66.9 us
  local copies, waits for them, and re-layouts: 26.5 us -> 21.5 us
  other arithmetic: 16.8 us -> 19.4 us
    ppermute x17 -> x21, waiting for transfers between devices: 30.8 us -> 17.8 us  [hop_blk(): return lax.ppermute(value, 'blk', route)]
    all_to_all x1, starting transfers between devices: 4.61 us -> 9.67 us  [shards(): lax.all_to_all(jnp.broadcast_to(mine[None], (8, 8, total)), 'grp', 0, 0,...]
    pallas_call x1, Pallas kernels: 17.2 us -> 12.2 us  [source_call(): pl.pallas_call(source_kernel, out_shape=jax.ShapeDtypeStruct((total, widt...]
    all_to_all x1, starting transfers between devices: 12.2 us -> 7.64 us  [shards(): lax.all_to_all(requests.reshape(owners, cap), ('grp', 'blk'), 0, 0, tiled...]
    unnamed x33 -> x35, local copies, waits for them, and re-layouts: 8.76 us -> 5.09 us
    concatenate x0 -> x3, other arithmetic: none -> 2.6 us  [shards(): jnp.concatenate([both(dz, 0), both(dz, 1)])]
    ppermute x17 -> x21, starting transfers between devices: 22.8 us -> 24.1 us  [hop_blk(): return lax.ppermute(value, 'blk', route)]
  transfers between devices with their start and end apart: 31 -> 35, of which waited for: 8 -> 6; matrix products, arithmetic and copies ran while one was open for 16% -> 16% of each run, Pallas kernels for 21% -> 20%
where the time goes in v2:
time: 224 us; the launch traced here: 222 us
  starting transfers between devices  74.4 us (33%)
  Pallas kernels  66.9 us (30%)
  waiting for transfers between devices  30.8 us (14%)
  local copies, waits for them, and re-layouts  21.5 us (10%)
  other arithmetic  19.4 us (9%)
  matrix products  6.96 us (3%)
    pallas_call x4, Pallas kernels, score_call(): pl.pallas_call(score_kernel, out_shape=(pltpu.HBM((4, total, cols), BF),...  25.8 us
    ppermute x21, starting transfers between devices, hop_blk(): return lax.ppermute(value, 'blk', route)  24.1 us
    ppermute x21, waiting for transfers between devices, hop_blk(): return lax.ppermute(value, 'blk', route)  17.8 us
    pallas_call x1, Pallas kernels, target_call(): pl.pallas_call(target_kernel, out_shape=(jax.ShapeDtypeStruct(half, F32),...  15.4 us
    pallas_call x1, Pallas kernels, source_call(): pl.pallas_call(source_kernel, out_shape=jax.ShapeDtypeStruct((total, widt...  12.2 us
    all_to_all x1, waiting for transfers between devices, shards(): lax.all_to_all(outgoing, ('grp', 'blk'), 0, 0, tiled=True)  12 us
    ppermute x8, starting transfers between devices, hop_grp(): lax.ppermute(value, 'grp', [(i, (i // 2 + dx) % 4 * 2 + (i % 2 ^ dy)) for...  10.9 us
    all_to_all x1, starting transfers between devices, shards(): lax.all_to_all(jnp.broadcast_to(mine[None], (8, 8, total)), 'grp', 0, 0,...  9.67 us
  transfers between devices with their start and end apart: 35, of which 6 were waited for; matrix products, arithmetic and copies ran while one was open for 16% of the time, Pallas kernels for 20%

profile of v2, /device:TPU:0, one launch (start us, length us, event | category | flops | bytes accessed | tf_op | source)
XLA Modules:
  0.0 221.9 jit_solution(2670923603396046)
XLA Ops:
  0.6 3.4 %collective-permute-start = (bf16[192,768]{1,0:T(8,128)(2,1)}, bf16[192,768]{1,0:T(8,128)(2,1)}, u32[]{:S(2)}, u32[]{:S(2)}) collective-permute-start(bf16[192,768]{1,0:T(8,128)(2,1)} %t0.1), channel_id=1, source_target_pairs={{0,2},{1,3},{2,0},{3,1},{4,6},{5,7},{6,4},{7,5},{8,10},{9,11},{10,... | collective-permute-start | bytes 884744 | tf_op jit(solution)/shard_map/ppermute | solution.py:21
  4.0 4.0 %collective-permute-start.3 = (bf16[192,768]{1,0:T(8,128)(2,1)}, bf16[192,768]{1,0:T(8,128)(2,1)S(1)}, u32[]{:S(2)}, u32[]{:S(2)}) collective-permute-start(bf16[192,768]{1,0:T(8,128)(2,1)} %t0.1), channel_id=1, source_target_pairs={{0,12},{1,13},{2,14},{3,15},{4,0},{5,1},{6,2},{7,3},{8,4},{9,5},{1... | collective-permute-start | bytes 884744 | tf_op jit(solution)/shard_map/ppermute | solution.py:21
  8.0 1.9 collective-permute-start.7
  11.9 7.6 %all-to-all-start = ((s32[128,1,3]{2,1,0:T(1,128)}), s32[128,1,3]{2,1,0:T(1,128)}, u32[]{:S(2)}, u32[]{:S(2)}) async-start(s32[128,1,3]{2,1,0:T(1,128)} %bitcast), calls=%async_computation | async-start | bytes 131072 | tf_op jit(solution)/shard_map/all_to_all | solution.py:276
  21.4 2.9 %collective-permute-start.8 = (bf16[192,768]{1,0:T(8,128)(2,1)}, bf16[192,768]{1,0:T(8,128)(2,1)}, u32[]{:S(2)}, u32[]{:S(2)}) collective-permute-start(bf16[192,768]{1,0:T(8,128)(2,1)} %collective-permute-done.t1), channel_id=1, source_target_pairs={{0,12},{1,13},{2,14},{3,15},{4,0},{5,1},{6,2},{7,3},{8,4},{9,5},{1... | collective-permute-start | bytes 884744 | tf_op jit(solution)/shard_map/ppermute | solution.py:21
  27.6 6.4 %scores.4 = (bf16[4,1536,768]{2,1,0:T(8,128)(2,1)}, f32[8,1536]{1,0:T(8,128)S(1)}, bf16[4,768,768]{2,1,0:T(8,128)(2,1)}) custom-call(s32[4]{0:T(128)S(1)} %pad_add_fusion.2.place, bf16[1536,768]{1,0:T(8,128)(2,1)S(1)} %copy-done.1, bf16[192,768]{1,0:T(8,128)(2,1)} %t0.1, bf16[192,768]{1,0:T(8,128)(2,1)} %collective-permute-done.t1, ...), custom_call_target="tpu_custom_call" | custom-call | flops 1811939328 | bytes 4718592 | tf_op jit(solution)/shard_map/scores/pallas_call | solution.py:83
  35.8 2.6 %collective-permute-start.12 = (bf16[192,768]{1,0:T(8,128)(2,1)}, bf16[192,768]{1,0:T(8,128)(2,1)}, u32[]{:S(2)}, u32[]{:S(2)}) collective-permute-start(bf16[192,768]{1,0:T(8,128)(2,1)} %collective-permute-done.t1), channel_id=1, source_target_pairs={{0,8},{1,9},{2,10},{3,11},{4,12},{5,13},{6,14},{7,15},{8,0},{9,1},... | collective-permute-start | bytes 884744 | tf_op jit(solution)/shard_map/ppermute | solution.py:21
  40.2 2.0 reshape.351
  42.2 9.0 %all-to-all-start.1 = ((bf16[128,3,768]{2,1,0:T(4,128)(2,1)}), bf16[128,3,768]{2,1,0:T(4,128)(2,1)}, u32[]{:S(2)}, u32[]{:S(2)}) async-start(bf16[128,3,768]{2,1,0:T(4,128)(2,1)} %reshape.351), calls=%async_computation.1 | async-start | bytes 1572864 | tf_op jit(solution)/shard_map/all_to_all | solution.py:314
  51.8 6.4 %scores.5 = (bf16[4,1536,768]{2,1,0:T(8,128)(2,1)}, f32[8,1536]{1,0:T(8,128)S(1)}, bf16[4,768,768]{2,1,0:T(8,128)(2,1)}) custom-call(s32[4]{0:T(128)S(1)} %pad_add_fusion.3.place, bf16[1536,768]{1,0:T(8,128)(2,1)S(1)} %copy-done.2, bf16[192,768]{1,0:T(8,128)(2,1)S(1)} %collective-permute-done.3.t0, ...), custom_call_target="tpu_custom_call", output_to_operand_aliasing={{0}: (6, {}), {2}: (7, {})} | custom-call | flops 1811939328 | bytes 4718592 | tf_op jit(solution)/shard_map/scores/pallas_call | solution.py:83
  59.9 6.5 %scores.6 = (bf16[4,1536,768]{2,1,0:T(8,128)(2,1)}, f32[8,1536]{1,0:T(8,128)S(1)}, bf16[4,768,768]{2,1,0:T(8,128)(2,1)}) custom-call(s32[4]{0:T(128)S(1)} %pad_add_fusion.4.place, bf16[1536,768]{1,0:T(8,128)(2,1)S(1)} %copy-done.2, bf16[192,768]{1,0:T(8,128)(2,1)S(1)} %collective-permute-done.7.t0, ...), custom_call_target="tpu_custom_call", output_to_operand_aliasing={{0}: (6, {}), {2}: (7, {})} | custom-call | flops 1811939328 | bytes 4718592 | tf_op jit(solution)/shard_map/scores/pallas_call | solution.py:83
  66.4 6.4 %scores.7 = (bf16[4,1536,768]{2,1,0:T(8,128)(2,1)}, f32[8,1536]{1,0:T(8,128)S(1)}, bf16[4,768,768]{2,1,0:T(8,128)(2,1)}) custom-call(s32[4]{0:T(128)S(1)} %pad_add_fusion.5.place, bf16[1536,768]{1,0:T(8,128)(2,1)S(1)} %copy-done.2, bf16[192,768]{1,0:T(8,128)(2,1)} %collective-permute-done.11.t0, ...), custom_call_target="tpu_custom_call", output_to_operand_aliasing={{0}: (6, {}), {2}: (7, {})} | custom-call | flops 1811939328 | bytes 4718592 | tf_op jit(solution)/shard_map/scores/pallas_call | solution.py:83
  72.8 2.2 reshape.352
  75.1 3.1 %fusion.3 = (f32[192]{0:T(256)S(1)}, f32[192]{0:T(256)S(1)}, f32[]{:T(128)}, f32[192,768]{1,0:T(8,128)}) fusion(bf16[1536,768]{1,0:T(8,128)(2,1)S(1)} %copy-done.2, s32[]{:T(128)S(6)} %select_n.245, bf16[192,768]{1,0:T(8,128)(2,1)S(1)} %collective-permute-done.15.tgt, bf16[384,768]{1,0:T(8,128)(2,1)} %reshape.352, s32[192]{0:T(256)S(1)} %multiply_add_fusion), kind=kOutput, calls=%fused_computation.13 | convolution fusion | flops 114499200 | bytes 1771784 | tf_op jit(solution)/shard_map/dot_general | solution.py:29
  81.9 9.7 %all-to-all-start.2 = ((f32[8,8,1536]{2,1,0:T(8,128)}), f32[8,8,1536]{2,1,0:T(8,128)S(1)}, u32[]{:S(2)}, u32[]{:S(2)}) async-start(f32[8,8,1536]{2,1,0:T(8,128)} %broadcast_in_dim.40), calls=%async_computation.2 | async-start | bytes 786432 | tf_op jit(solution)/shard_map/all_to_all | solution.py:337
  92.2 12.2 %source_terms.1 = bf16[1536,768]{1,0:T(8,128)(2,1)} custom-call(f32[8,1536]{1,0:T(8,128)} %concatenate.22.w_ref, bf16[4,1536,768]{2,1,0:T(8,128)(2,1)} %get-tuple-element.50.e_ref, bf16[4,768,768]{2,1,0:T(8,128)(2,1)} %get-tuple-element.51.tgt_ref), custom_call_target="tpu_custom_call" | custom-call | flops 7247757312 | bytes 11796480 | tf_op jit(solution)/shard_map/source_terms/pallas_call | solution.py:124
  108.3 15.4 %target_terms.1 = (f32[4,384,768]{2,1,0:T(8,128)}, bf16[4,384,768]{2,1,0:T(8,128)(2,1)}) custom-call(s32[16]{0:T(128)} %concatenate.24.place, f32[8,1536]{1,0:T(8,128)} %maximum_maximum_fusion.w_ref, bf16[4,1536,768]{2,1,0:T(8,128)(2,1)} %get-tuple-element.50.e_ref, bf16[1536,768]{1,0:T(8,128)(2,1)} %src_ref.1, bf16[16,128]{1,0:T(8,128)(2,1)} %copy-done.16), custom_call_target="tpu_custom_call" | custom-call | flops 7247757312 | bytes 18874368 | tf_op jit(solution)/shard_map/target_terms/pallas_call | solution.py:176
  124.7 4.4 %all-to-all-start.3 = ((bf16[8,192,768]{2,1,0:T(8,128)(2,1)}), bf16[8,192,768]{2,1,0:T(8,128)(2,1)S(1)}, u32[]{:S(2)}, u32[]{:S(2)}) async-start(bf16[8,192,768]{2,1,0:T(8,128)(2,1)} %bitcast.66), calls=%async_computation.3 | async-start | bytes 4718592 | tf_op jit(solution)/shard_map/all_to_all | solution.py:340
  129.2 2.9 %fusion.10 = (bf16[192,768]{1,0:T(8,128)(2,1)S(1)}, bf16[192,768]{1,0:T(8,128)(2,1)S(1)}, bf16[192,768]{1,0:T(8,128)(2,1)S(1)}, bf16[192,768]{1,0:T(8,128)(2,1)S...) fusion(f32[4,384,768]{2,1,0:T(8,128)} %get-tuple-element.54.keep, ...), kind=kLoop, calls=%fused_computation.33 | loop fusion | flops 2654208 | bytes 7077888 | tf_op jit(solution)/shard_map/convert_element_type | solution.py:371
  135.6 1.8 collective-permute-start.19
  142.0 3.0 %fusion.1.scale = f32[1536,1]{1,0:T(8,128)} fusion(f32[1536]{0:T(1024)S(1)} %get-tuple-element.96, f32[1536,1]{1,0:T(8,128)} %copy.69, f32[1536]{0:T(1024)S(1)} %fusion.22, f32[1536,1]{1,0:T(8,128)} %copy.66, f32[1536,1]{1,0:T(8,128)S(1)} %copy.65, f32[1536]{0:T(1024)S(1)} %slice_reduce_fusion.3), kind=kLoop, calls=%fused_computation.9 | loop fusion | flops 23040 | bytes 43008 | tf_op jit(solution)/shard_map/mul | solution.py:410
  145.0 6.0 %collective-permute-done.20.m3 = bf16[384,768]{1,0:T(8,128)(2,1)} collective-permute-done((bf16[384,768]{1,0:T(8,128)(2,1)}, bf16[384,768]{1,0:T(8,128)(2,1)}, u32[]{:S(2)}, u32[]{:S(2)}) %collective-permute-start.20) | collective-permute-done | bytes 589856 | tf_op jit(solution)/shard_map/ppermute | solution.py:21
  151.0 11.4 %collective-permute-done.19.m2 = bf16[384,768]{1,0:T(8,128)(2,1)} collective-permute-done((bf16[384,768]{1,0:T(8,128)(2,1)}, bf16[384,768]{1,0:T(8,128)(2,1)}, u32[]{:S(2)}, u32[]{:S(2)}) %collective-permute-start.19) | collective-permute-done | bytes 589856 | tf_op jit(solution)/shard_map/ppermute | solution.py:21
  162.7 3.0 %lines.1 = (f32[192,768]{1,0:T(8,128)}, bf16[192,768]{1,0:T(8,128)(2,1)}) custom-call(f32[4,384,768]{2,1,0:T(8,128)} %get-tuple-element.54.keep, bf16[4,384,768]{2,1,0:T(8,128)(2,1)} %collective-permute-done.17.got, bf16[384,768]{1,0:T(8,128)(2,1)} %collective-permute-done.18.m1, bf16[384,768]{1,0:T(8,128)(2,1)} %collective-permute-done.19.m2, ...), custom_call_target="tpu_custom_call" | custom-call | flops 1474560 | bytes 4423680 | tf_op jit(solution)/shard_map/lines/pallas_call | solution.py:376
  165.7 3.5 %collective-permute-start.29 = (bf16[192,768]{1,0:T(8,128)(2,1)}, bf16[192,768]{1,0:T(8,128)(2,1)}, u32[]{:S(2)}, u32[]{:S(2)}) collective-permute-start(bf16[192,768]{1,0:T(8,128)(2,1)} %get-tuple-element.56._), channel_id=1, source_target_pairs={{0,2},{1,3},{2,0},{3,1},{4,6},{5,7},{6,4},{7,5},{8,10},{9,11},{10,... | collective-permute-start | bytes 884744 | tf_op jit(solution)/shard_map/ppermute | solution.py:21
  170.6 3.0 %code.1 = (s16[192,768]{1,0:T(8,128)(2,1)}, s16[96,768]{1,0:T(8,128)(2,1)}) custom-call(bf16[8,192,768]{2,1,0:T(8,128)(2,1)} %copy-done.5, f32[192,768]{1,0:T(8,128)} %get-tuple-element.95.hard, bf16[192,768]{1,0:T(8,128)(2,1)} %copy-done.6, f32[192,11]{1,0:T(8,128)} %bitcast.67, bf16[192,768]{1,0:T(8,128)(2,1)} %get-tuple-element.56._), custom_call_target="tpu_custom_call" | custom-call | flops 1474560 | bytes 3244032 | tf_op jit(solution)/shard_map/code/pallas_call | solution.py:387
  173.6 3.0 %collective-permute-start.22 = (s16[96,768]{1,0:T(8,128)(2,1)}, s16[96,768]{1,0:T(8,128)(2,1)S(1)}, u32[]{:S(2)}, u32[]{:S(2)}) collective-permute-start(s16[96,768]{1,0:T(8,128)(2,1)} %get-tuple-element.58), channel_id=1, source_target_pairs={{0,96},{16,112},{32,0},{48,16},{64,32},{80,48},{96,64},{112,80},{1... | collective-permute-start | bytes 442376 | tf_op jit(solution)/shard_map/ppermute | solution.py:25
  183.7 7.0 %all-to-all-start.4 = ((bf16[128,3,768]{2,1,0:T(4,128)(2,1)}), bf16[128,3,768]{2,1,0:T(4,128)(2,1)S(1)}, u32[]{:S(2)}, u32[]{:S(2)}) async-start(bf16[128,3,768]{2,1,0:T(4,128)(2,1)} %reshape.354), calls=%async_computation.4 | async-start | bytes 1572864 | tf_op jit(solution)/shard_map/all_to_all | solution.py:415
  193.4 2.7 %collective-permute-start.25 = (s16[2,96,768]{2,1,0:T(8,128)(2,1)}, s16[2,96,768]{2,1,0:T(8,128)(2,1)S(1)}, u32[]{:S(2)}, u32[]{:S(2)}) collective-permute-start(s16[2,96,768]{2,1,0:T(8,128)(2,1)} %pad_add_fusion.1), channel_id=1, source_target_pairs={{0,96},{16,112},{32,0},{48,16},{64,32},{80,48},{96,64},{112,80},{1... | collective-permute-start | bytes 884744 | tf_op jit(solution)/shard_map/ppermute | solution.py:25
  197.8 1.8 convert_add_fusion
  199.6 12.0 %all-to-all-done.4 = bf16[128,3,768]{2,1,0:T(4,128)(2,1)S(1)} async-done(((bf16[128,3,768]{2,1,0:T(4,128)(2,1)}), bf16[128,3,768]{2,1,0:T(4,128)(2,1)S(1)}, u32[]{:S(2)}, u32[]{:S(2)}) %all-to-all-start.4) | async-done | bytes 589856 | tf_op jit(solution)/shard_map/all_to_all | solution.py:415
  214.4 7.6 %decode.1 = f32[1536,768]{1,0:T(8,128)} custom-call(s32[8]{0:T(128)} %stack.170.order, f32[1536,1]{1,0:T(8,128)} %fusion.1.scale, s16[192,768]{1,0:T(8,128)(2,1)} %get-tuple-element.57.own, s16[192,768]{1,0:T(8,128)(2,1)} %copy-done.9, s16[96,768]{1,0:T(8,128)(2,1)} %copy-done.11, s16[96,768]{1,0:T(8,128)(2,1)} %copy-done.12, s16[96,768]{1,0:T(8,128)(2,1)} %copy-done.13, ...), custom_call_target="tpu_custom_call" | custom-call | flops 1179648 | bytes 7077888 | tf_op jit(solution)/shard_map/decode/pallas_call | solution.py:243
  (150 shorter events, 45.0 us)
Async XLA Ops:
  0.6 19.2 %collective-permute-start = (bf16[192,768]{1,0:T(8,128)(2,1)}, bf16[192,768]{1,0:T(8,128)(2,1)}, u32[]{:S(2)}, u32[]{:S(2)}) collective-permute-start(bf16[192,768]{1,0:T(8,128)(2,1)} %t0.1), channel_id=1, source_target_pairs={{0,2},{1,3},{2,0},{3,1},{4,6},{5,7},{6,4},{7,5},{8,10},{9,11},{10,... | collective-permute-start | bytes 884744 | tf_op jit(solution)/shard_map/ppermute | solution.py:21
  4.0 17.4 %collective-permute-start.1 = (bf16[192,768]{1,0:T(8,128)(2,1)}, bf16[192,768]{1,0:T(8,128)(2,1)S(1)}, u32[]{:S(2)}, u32[]{:S(2)}) collective-permute-start(bf16[192,768]{1,0:T(8,128)(2,1)} %t0.1), channel_id=1, source_target_pairs={{0,1},{1,0},{2,3},{3,2},{4,5},{5,4},{6,7},{7,6},{8,9},{9,8},{10,11... | collective-permute-start | bytes 884744 | tf_op jit(solution)/shard_map/ppermute | solution.py:21
  4.0 20.3 %collective-permute-start.3 = (bf16[192,768]{1,0:T(8,128)(2,1)}, bf16[192,768]{1,0:T(8,128)(2,1)S(1)}, u32[]{:S(2)}, u32[]{:S(2)}) collective-permute-start(bf16[192,768]{1,0:T(8,128)(2,1)} %t0.1), channel_id=1, source_target_pairs={{0,12},{1,13},{2,14},{3,15},{4,0},{5,1},{6,2},{7,3},{8,4},{9,5},{1... | collective-permute-start | bytes 884744 | tf_op jit(solution)/shard_map/ppermute | solution.py:21
  8.0 27.8 %collective-permute-start.4 = (bf16[192,768]{1,0:T(8,128)(2,1)}, bf16[192,768]{1,0:T(8,128)(2,1)S(1)}, u32[]{:S(2)}, u32[]{:S(2)}) collective-permute-start(bf16[192,768]{1,0:T(8,128)(2,1)} %t0.1), channel_id=1, source_target_pairs={{0,4},{1,5},{2,6},{3,7},{4,8},{5,9},{6,10},{7,11},{8,12},{9,13},{1... | collective-permute-start | bytes 884744 | tf_op jit(solution)/shard_map/ppermute | solution.py:21
  8.0 30.3 %collective-permute-start.7 = (bf16[192,768]{1,0:T(8,128)(2,1)}, bf16[192,768]{1,0:T(8,128)(2,1)S(1)}, u32[]{:S(2)}, u32[]{:S(2)}) collective-permute-start(bf16[192,768]{1,0:T(8,128)(2,1)} %t0.1), channel_id=1, source_target_pairs={{0,8},{1,9},{2,10},{3,11},{4,12},{5,13},{6,14},{7,15},{8,0},{9,1},... | collective-permute-start | bytes 884744 | tf_op jit(solution)/shard_map/ppermute | solution.py:21
  11.9 22.7 %all-to-all-start = ((s32[128,1,3]{2,1,0:T(1,128)}), s32[128,1,3]{2,1,0:T(1,128)}, u32[]{:S(2)}, u32[]{:S(2)}) async-start(s32[128,1,3]{2,1,0:T(1,128)} %bitcast), calls=%async_computation | async-start | bytes 131072 | tf_op jit(solution)/shard_map/all_to_all | solution.py:276
  21.4 17.5 %collective-permute-start.8 = (bf16[192,768]{1,0:T(8,128)(2,1)}, bf16[192,768]{1,0:T(8,128)(2,1)}, u32[]{:S(2)}, u32[]{:S(2)}) collective-permute-start(bf16[192,768]{1,0:T(8,128)(2,1)} %collective-permute-done.t1), channel_id=1, source_target_pairs={{0,12},{1,13},{2,14},{3,15},{4,0},{5,1},{6,2},{7,3},{8,4},{9,5},{1... | collective-permute-start | bytes 884744 | tf_op jit(solution)/shard_map/ppermute | solution.py:21
  24.3 14.1 %collective-permute-start.5 = (bf16[192,768]{1,0:T(8,128)(2,1)S(1)}, bf16[192,768]{1,0:T(8,128)(2,1)}, u32[]{:S(2)}, u32[]{:S(2)}) collective-permute-start(bf16[192,768]{1,0:T(8,128)(2,1)S(1)} %collective-permute-done.3.t0), channel_id=1, source_target_pairs={{0,1},{1,0},{2,3},{3,2},{4,5},{5,4},{6,7},{7,6},{8,9},{9,8},{10,11... | collective-permute-start | bytes 884744 | tf_op jit(solution)/shard_map/ppermute | solution.py:21
  25.9 25.4 %collective-permute-start.11 = (bf16[192,768]{1,0:T(8,128)(2,1)}, bf16[192,768]{1,0:T(8,128)(2,1)}, u32[]{:S(2)}, u32[]{:S(2)}) collective-permute-start(bf16[192,768]{1,0:T(8,128)(2,1)} %collective-permute-done.t1), channel_id=1, source_target_pairs={{0,4},{1,5},{2,6},{3,7},{4,8},{5,9},{6,10},{7,11},{8,12},{9,13},{1... | collective-permute-start | bytes 884744 | tf_op jit(solution)/shard_map/ppermute | solution.py:21
  35.8 15.5 %collective-permute-start.12 = (bf16[192,768]{1,0:T(8,128)(2,1)}, bf16[192,768]{1,0:T(8,128)(2,1)}, u32[]{:S(2)}, u32[]{:S(2)}) collective-permute-start(bf16[192,768]{1,0:T(8,128)(2,1)} %collective-permute-done.t1), channel_id=1, source_target_pairs={{0,8},{1,9},{2,10},{3,11},{4,12},{5,13},{6,14},{7,15},{8,0},{9,1},... | collective-permute-start | bytes 884744 | tf_op jit(solution)/shard_map/ppermute | solution.py:21
  38.4 13.5 %collective-permute-start.6 = (bf16[192,768]{1,0:T(8,128)(2,1)S(1)}, bf16[192,768]{1,0:T(8,128)(2,1)}, u32[]{:S(2)}, u32[]{:S(2)}) collective-permute-start(bf16[192,768]{1,0:T(8,128)(2,1)S(1)} %collective-permute-done.4.t1), channel_id=1, source_target_pairs={{0,1},{1,0},{2,3},{3,2},{4,5},{5,4},{6,7},{7,6},{8,9},{9,8},{10,11... | collective-permute-start | bytes 884744 | tf_op jit(solution)/shard_map/ppermute | solution.py:21
  38.4 21.5 %collective-permute-start.9 = (bf16[192,768]{1,0:T(8,128)(2,1)S(1)}, bf16[192,768]{1,0:T(8,128)(2,1)}, u32[]{:S(2)}, u32[]{:S(2)}) collective-permute-start(bf16[192,768]{1,0:T(8,128)(2,1)S(1)} %collective-permute-done.7.t0), channel_id=1, source_target_pairs={{0,1},{1,0},{2,3},{3,2},{4,5},{5,4},{6,7},{7,6},{8,9},{9,8},{10,11... | collective-permute-start | bytes 884744 | tf_op jit(solution)/shard_map/ppermute | solution.py:21
  38.9 21.0 %collective-permute-start.10 = (bf16[192,768]{1,0:T(8,128)(2,1)}, bf16[192,768]{1,0:T(8,128)(2,1)}, u32[]{:S(2)}, u32[]{:S(2)}) collective-permute-start(bf16[192,768]{1,0:T(8,128)(2,1)} %collective-permute-done.8.t1), channel_id=1, source_target_pairs={{0,1},{1,0},{2,3},{3,2},{4,5},{5,4},{6,7},{7,6},{8,9},{9,8},{10,11... | collective-permute-start | bytes 884744 | tf_op jit(solution)/shard_map/ppermute | solution.py:21
  42.2 30.7 %all-to-all-start.1 = ((bf16[128,3,768]{2,1,0:T(4,128)(2,1)}), bf16[128,3,768]{2,1,0:T(4,128)(2,1)}, u32[]{:S(2)}, u32[]{:S(2)}) async-start(bf16[128,3,768]{2,1,0:T(4,128)(2,1)} %reshape.351), calls=%async_computation.1 | async-start | bytes 1572864 | tf_op jit(solution)/shard_map/all_to_all | solution.py:314
  51.3 15.1 %collective-permute-start.13 = (bf16[192,768]{1,0:T(8,128)(2,1)}, bf16[192,768]{1,0:T(8,128)(2,1)S(1)}, u32[]{:S(2)}, u32[]{:S(2)}) collective-permute-start(bf16[192,768]{1,0:T(8,128)(2,1)} %collective-permute-done.11.t0), channel_id=1, source_target_pairs={{0,1},{1,0},{2,3},{3,2},{4,5},{5,4},{6,7},{7,6},{8,9},{9,8},{10,11... | collective-permute-start | bytes 884744 | tf_op jit(solution)/shard_map/ppermute | solution.py:21
  51.4 15.0 %collective-permute-start.14 = (bf16[192,768]{1,0:T(8,128)(2,1)}, bf16[192,768]{1,0:T(8,128)(2,1)S(1)}, u32[]{:S(2)}, u32[]{:S(2)}) collective-permute-start(bf16[192,768]{1,0:T(8,128)(2,1)} %collective-permute-done.12.t1), channel_id=1, source_target_pairs={{0,1},{1,0},{2,3},{3,2},{4,5},{5,4},{6,7},{7,6},{8,9},{9,8},{10,11... | collective-permute-start | bytes 884744 | tf_op jit(solution)/shard_map/ppermute | solution.py:21
  58.3 16.8 %collective-permute-start.15 = (bf16[192,768]{1,0:T(8,128)(2,1)}, bf16[192,768]{1,0:T(8,128)(2,1)S(1)}, u32[]{:S(2)}, u32[]{:S(2)}) collective-permute-start(bf16[192,768]{1,0:T(8,128)(2,1)} %t0.1), channel_id=1, source_target_pairs={{0,0},{1,16},{2,32},{3,48},{4,64},{5,80},{6,96},{7,112},{8,1},{9,1... | collective-permute-start | bytes 884744 | tf_op jit(solution)/shard_map/ppermute | solution.py:317
  81.9 22.5 %all-to-all-start.2 = ((f32[8,8,1536]{2,1,0:T(8,128)}), f32[8,8,1536]{2,1,0:T(8,128)S(1)}, u32[]{:S(2)}, u32[]{:S(2)}) async-start(f32[8,8,1536]{2,1,0:T(8,128)} %broadcast_in_dim.40), calls=%async_computation.2 | async-start | bytes 786432 | tf_op jit(solution)/shard_map/all_to_all | solution.py:337
  124.7 44.5 %all-to-all-start.3 = ((bf16[8,192,768]{2,1,0:T(8,128)(2,1)}), bf16[8,192,768]{2,1,0:T(8,128)(2,1)S(1)}, u32[]{:S(2)}, u32[]{:S(2)}) async-start(bf16[8,192,768]{2,1,0:T(8,128)(2,1)} %bitcast.66), calls=%async_computation.3 | async-start | bytes 4718592 | tf_op jit(solution)/shard_map/all_to_all | solution.py:340
  133.0 18.1 %collective-permute-start.20 = (bf16[384,768]{1,0:T(8,128)(2,1)}, bf16[384,768]{1,0:T(8,128)(2,1)}, u32[]{:S(2)}, u32[]{:S(2)}) collective-permute-start(bf16[384,768]{1,0:T(8,128)(2,1)} %pad_maximum_fusion.2), channel_id=1, source_target_pairs={{0,8},{1,9},{2,10},{3,11},{4,12},{5,13},{6,14},{7,15},{8,0},{9,1},... | collective-permute-start | bytes 1769480 | tf_op jit(solution)/shard_map/ppermute | solution.py:21
  135.6 26.9 %collective-permute-start.19 = (bf16[384,768]{1,0:T(8,128)(2,1)}, bf16[384,768]{1,0:T(8,128)(2,1)}, u32[]{:S(2)}, u32[]{:S(2)}) collective-permute-start(bf16[384,768]{1,0:T(8,128)(2,1)} %pad_maximum_fusion.1), channel_id=1, source_target_pairs={{0,12},{1,13},{2,14},{3,15},{4,0},{5,1},{6,2},{7,3},{8,4},{9,5},{1... | collective-permute-start | bytes 1769480 | tf_op jit(solution)/shard_map/ppermute | solution.py:21
  138.2 24.5 %collective-permute-start.18 = (bf16[384,768]{1,0:T(8,128)(2,1)}, bf16[384,768]{1,0:T(8,128)(2,1)}, u32[]{:S(2)}, u32[]{:S(2)}) collective-permute-start(bf16[384,768]{1,0:T(8,128)(2,1)} %pad_maximum_fusion), channel_id=1, source_target_pairs={{0,4},{1,5},{2,6},{3,7},{4,8},{5,9},{6,10},{7,11},{8,12},{9,13},{1... | collective-permute-start | bytes 1769480 | tf_op jit(solution)/shard_map/ppermute | solution.py:21
  165.7 32.1 %collective-permute-start.29 = (bf16[192,768]{1,0:T(8,128)(2,1)}, bf16[192,768]{1,0:T(8,128)(2,1)}, u32[]{:S(2)}, u32[]{:S(2)}) collective-permute-start(bf16[192,768]{1,0:T(8,128)(2,1)} %get-tuple-element.56._), channel_id=1, source_target_pairs={{0,2},{1,3},{2,0},{3,1},{4,6},{5,7},{6,4},{7,5},{8,10},{9,11},{10,... | collective-permute-start | bytes 884744 | tf_op jit(solution)/shard_map/ppermute | solution.py:21
  173.6 17.1 %collective-permute-start.22 = (s16[96,768]{1,0:T(8,128)(2,1)}, s16[96,768]{1,0:T(8,128)(2,1)S(1)}, u32[]{:S(2)}, u32[]{:S(2)}) collective-permute-start(s16[96,768]{1,0:T(8,128)(2,1)} %get-tuple-element.58), channel_id=1, source_target_pairs={{0,96},{16,112},{32,0},{48,16},{64,32},{80,48},{96,64},{112,80},{1... | collective-permute-start | bytes 442376 | tf_op jit(solution)/shard_map/ppermute | solution.py:25
  176.6 14.1 %collective-permute-start.23 = (s16[96,768]{1,0:T(8,128)(2,1)}, s16[96,768]{1,0:T(8,128)(2,1)S(1)}, u32[]{:S(2)}, u32[]{:S(2)}) collective-permute-start(s16[96,768]{1,0:T(8,128)(2,1)} %get-tuple-element.58), channel_id=1, source_target_pairs={{0,64},{16,80},{32,96},{48,112},{64,0},{80,16},{96,32},{112,48},{1... | collective-permute-start | bytes 442376 | tf_op jit(solution)/shard_map/ppermute | solution.py:25
  177.5 13.3 %collective-permute-start.24 = (s16[96,768]{1,0:T(8,128)(2,1)}, s16[96,768]{1,0:T(8,128)(2,1)S(1)}, u32[]{:S(2)}, u32[]{:S(2)}) collective-permute-start(s16[96,768]{1,0:T(8,128)(2,1)} %get-tuple-element.58), channel_id=1, source_target_pairs={{0,32},{16,48},{32,64},{48,80},{64,96},{80,112},{96,0},{112,16},{1... | collective-permute-start | bytes 442376 | tf_op jit(solution)/shard_map/ppermute | solution.py:25
  179.5 13.0 %collective-permute-start.21 = (s16[192,768]{1,0:T(8,128)(2,1)}, s16[192,768]{1,0:T(8,128)(2,1)S(1)}, u32[]{:S(2)}, u32[]{:S(2)}) collective-permute-start(s16[192,768]{1,0:T(8,128)(2,1)} %get-tuple-element.57.own), channel_id=1, source_target_pairs={{0,16},{16,0},{32,48},{48,32},{64,80},{80,64},{96,112},{112,96},{1... | collective-permute-start | bytes 884744 | tf_op jit(solution)/shard_map/ppermute | solution.py:25
  183.7 28.0 %all-to-all-start.4 = ((bf16[128,3,768]{2,1,0:T(4,128)(2,1)}), bf16[128,3,768]{2,1,0:T(4,128)(2,1)S(1)}, u32[]{:S(2)}, u32[]{:S(2)}) async-start(bf16[128,3,768]{2,1,0:T(4,128)(2,1)} %reshape.354), calls=%async_computation.4 | async-start | bytes 1572864 | tf_op jit(solution)/shard_map/all_to_all | solution.py:415
  191.6 21.8 %collective-permute-start.28 = (s16[3,96,768]{2,1,0:T(8,128)(2,1)}, s16[3,96,768]{2,1,0:T(8,128)(2,1)}, u32[]{:S(2)}, u32[]{:S(2)}) collective-permute-start(s16[3,96,768]{2,1,0:T(8,128)(2,1)} %pad_add_fusion), channel_id=1, source_target_pairs={{0,16},{16,0},{32,48},{48,32},{64,80},{80,64},{96,112},{112,96},{1... | collective-permute-start | bytes 1327112 | tf_op jit(solution)/shard_map/ppermute | solution.py:25
  193.4 20.0 %collective-permute-start.25 = (s16[2,96,768]{2,1,0:T(8,128)(2,1)}, s16[2,96,768]{2,1,0:T(8,128)(2,1)S(1)}, u32[]{:S(2)}, u32[]{:S(2)}) collective-permute-start(s16[2,96,768]{2,1,0:T(8,128)(2,1)} %pad_add_fusion.1), channel_id=1, source_target_pairs={{0,96},{16,112},{32,0},{48,16},{64,32},{80,48},{96,64},{112,80},{1... | collective-permute-start | bytes 884744 | tf_op jit(solution)/shard_map/ppermute | solution.py:25
  196.1 17.4 %collective-permute-start.26 = (s16[2,96,768]{2,1,0:T(8,128)(2,1)}, s16[2,96,768]{2,1,0:T(8,128)(2,1)}, u32[]{:S(2)}, u32[]{:S(2)}) collective-permute-start(s16[2,96,768]{2,1,0:T(8,128)(2,1)} %pad_add_fusion.1), channel_id=1, source_target_pairs={{0,64},{16,80},{32,96},{48,112},{64,0},{80,16},{96,32},{112,48},{1... | collective-permute-start | bytes 884744 | tf_op jit(solution)/shard_map/ppermute | solution.py:25
  196.9 17.4 %collective-permute-start.27 = (s16[2,96,768]{2,1,0:T(8,128)(2,1)}, s16[2,96,768]{2,1,0:T(8,128)(2,1)}, u32[]{:S(2)}, u32[]{:S(2)}) collective-permute-start(s16[2,96,768]{2,1,0:T(8,128)(2,1)} %pad_add_fusion.1), channel_id=1, source_target_pairs={{0,32},{16,48},{32,64},{48,80},{64,96},{80,112},{96,0},{112,16},{1... | collective-permute-start | bytes 884744 | tf_op jit(solution)/shard_map/ppermute | solution.py:25
  (20 other events, 262.4 us)

commit v3 on v2

--- a/solution.py
+++ b/solution.py
@@ -35,7 +35,7 @@
 
 
 def score_kernel(place, src, t0, t1, t2, t3, *refs):
-    e_out, stat_out, tgt_out, a_ref = refs[-4:]
+    e_out, stat_out, tgt_ref, a_ref = refs[-4:]
     rows = t0.shape[0]
     half = 2 * rows
     step = pl.program_id(0)
@@ -45,11 +45,11 @@
         top = jnp.zeros((1, 1), F32)
         for q, t in enumerate((t0, t1, t2, t3)):
             block = t[...]
-            tgt_out[0, q * rows : (q + 1) * rows, :] = block
+            tgt_ref[q * rows : (q + 1) * rows, :] = block
             top = jnp.maximum(top, jnp.max(jnp.abs(block).astype(F32), keepdims=True))
         a_ref[...] = jnp.broadcast_to(top, a_ref.shape)
 
-    tgt = tgt_out[0]
+    tgt = tgt_ref[...]
     lane = lax.broadcasted_iota(jnp.int32, (PART, 128), 1)
     column = lax.broadcasted_iota(jnp.int32, (PART, 2 * half), 1)
     line = lax.broadcasted_iota(jnp.int32, (PART, 1), 0)
@@ -85,7 +85,6 @@
         out_shape=(
             pltpu.HBM((4, total, cols), BF),
             jax.ShapeDtypeStruct((8, total), F32),
-            pltpu.HBM((4, cols, width), BF),
         ),
         grid_spec=pltpu.PrefetchScalarGridSpec(
             num_scalar_prefetch=1,
@@ -96,11 +95,10 @@
             out_specs=(
                 pl.BlockSpec((1, TILE, cols), lambda i, p: (n, i, 0)),
                 pl.BlockSpec((8, TILE), lambda i, p: (0, i)),
-                pl.BlockSpec((1, cols, width), lambda i, p: (n, 0, 0)),
             ),
-            scratch_shapes=[pltpu.VMEM((8, 128), F32)],
-        ),
-        input_output_aliases={6: 0, 7: 2} if so_far else {},
+            scratch_shapes=[pltpu.VMEM((cols, width), BF), pltpu.VMEM((8, 128), F32)],
+        ),
+        input_output_aliases={6: 0} if so_far else {},
         compiler_params=pltpu.CompilerParams(vmem_limit_bytes=24 << 20),
         cost_estimate=pl.CostEstimate(
             flops=2 * total * cols * width, bytes_accessed=total * (width + cols) * 2, transcendentals=total * cols
@@ -109,18 +107,27 @@
     )(place, src, *blocks, *so_far)
 
 
-def source_kernel(w_ref, e_ref, tgt_ref, out):
+def source_kernel(w_ref, e_ref, *refs):
+    blocks, out, tgt = refs[:-2], refs[-2], refs[-1]
+    rows = blocks[0].shape[0]
+
+    @pl.when(pl.program_id(0) == 0)
+    def _():
+        for n, block in enumerate(blocks):
+            tgt[n // 4, n % 4 * rows : (n % 4 + 1) * rows, :] = block[...]
+
     weights = columns_of(w_ref[...])
     total = None
     for c in range(4):
-        part = dot_f32(e_ref[c], tgt_ref[c], ((1,), (0,))) * weights[:, c : c + 1]
+        part = dot_f32(e_ref[c], tgt[c], ((1,), (0,))) * weights[:, c : c + 1]
         total = part if total is None else total + part
     out[...] = total.astype(BF)
 
 
-def source_call(weights, e_all, tgt_all):
+def source_call(weights, e_all, blocks):
     _, total, cols = e_all.shape
-    width = tgt_all.shape[2]
+    rows, width = blocks[0].shape
+    whole = pl.BlockSpec((rows, width), lambda i: (0, 0), pipeline_mode=pl.Buffered(1))
     return pl.pallas_call(
         source_kernel,
         out_shape=jax.ShapeDtypeStruct((total, width), BF),
@@ -128,14 +135,15 @@
         in_specs=[
             pl.BlockSpec((8, PART), lambda i: (0, i)),
             pl.BlockSpec((4, PART, cols), lambda i: (0, i, 0)),
-            pl.BlockSpec((4, cols, width), lambda i: (0, 0, 0), pipeline_mode=pl.Buffered(1)),
-        ],
+        ]
+        + [whole] * len(blocks),
         out_specs=pl.BlockSpec((PART, width), lambda i: (i, 0)),
+        scratch_shapes=[pltpu.VMEM((4, cols, width), BF)],
         cost_estimate=pl.CostEstimate(
             flops=8 * total * cols * width, bytes_accessed=total * (8 * cols + 2 * width), transcendentals=0
         ),
         name="source_terms",
-    )(weights, e_all, tgt_all)
+    )(weights, e_all, *blocks)
 
 
 def target_kernel(place, w_ref, e_ref, src_ref, _, keep, give, acc, scaled, column):
@@ -250,6 +258,7 @@
             + [pl.BlockSpec(x.shape, lambda i, p, n=x.ndim: (0,) * n) for x in pieces],
             out_specs=pl.BlockSpec((rows, width), lambda i, p: (p[i], 0)),
         ),
+        compiler_params=pltpu.CompilerParams(vmem_limit_bytes=24 << 20),
         cost_estimate=pl.CostEstimate(flops=total * width, bytes_accessed=total * width * 6, transcendentals=0),
         name="decode",
     )(order, scale, *pieces)
@@ -302,8 +311,8 @@
 
     def add_chunk(n):
         nonlocal so_far
-        e, stat, tgt = score_call(places[n], source_emb, [have[key] for key in order[n]], n, so_far)
-        so_far = (e, tgt)
+        e, stat = score_call(places[n], source_emb, [have[key] for key in order[n]], n, so_far)
+        so_far = (e,)
         stats.append(stat)
 
     add_chunk(0)
@@ -335,7 +344,8 @@
     soft = jnp.sum(sums * jnp.exp(tops - soft_top), axis=0)
     mine = jnp.stack([soft_top, soft, pos, hard_all, reach] + [jnp.zeros((total,), F32)] * 3)
     everyone = lax.all_to_all(jnp.broadcast_to(mine[None], (8, 8, total)), "grp", 0, 0, tiled=True)
-    source_part = source_call(jnp.concatenate([jnp.exp(tops - soft_top), jnp.zeros((4, total), F32)]), *so_far)
+    source_part = source_call(jnp.concatenate([jnp.exp(tops - soft_top), jnp.zeros((4, total), F32)]), so_far[0],
+        [have[key] for chunk in order for key in chunk])
     everyone, source_part = lax.optimization_barrier((everyone, source_part))
     source_parts = lax.all_to_all(source_part.reshape(8, rows, width), "grp", 0, 0, tiled=True)
     token = hop_blk(source_part[:16, :128], 0, 0, 1)

time: 224 us -> 225 us (level)
  local copies, waits for them, and re-layouts: 21.5 us -> 26.4 us
  Pallas kernels: 66.9 us -> 62.8 us
    pallas_call x1, Pallas kernels: 7.59 us -> 4.53 us  [decode_call(): pl.pallas_call(decode_kernel, out_shape=jax.ShapeDtypeStruct((total, widt...]
    unnamed x35 -> x37, local copies, waits for them, and re-layouts: 5.09 us -> 7.97 us
  transfers between devices with their start and end apart: 35 -> 35, of which waited for: 6 -> 5; matrix products, arithmetic and copies ran while one was open for 16% -> 17% of each run, Pallas kernels for 20% -> 18%
where the time goes in v3:
time: 225 us; the launch traced here: 224 us
  starting transfers between devices  75.6 us (34%)
  Pallas kernels  62.8 us (28%)
  waiting for transfers between devices  30.2 us (13%)
  local copies, waits for them, and re-layouts  26.4 us (12%)
  other arithmetic  18.9 us (8%)
  matrix products  7.94 us (4%)
    pallas_call x4, Pallas kernels, score_call(): pl.pallas_call(score_kernel, out_shape=(pltpu.HBM((4, total, cols), BF),...  24.3 us
    ppermute x21, starting transfers between devices, hop_blk(): return lax.ppermute(value, 'blk', route)  23.1 us
    ppermute x21, waiting for transfers between devices, hop_blk(): return lax.ppermute(value, 'blk', route)  18.5 us
    pallas_call x1, Pallas kernels, target_call(): pl.pallas_call(target_kernel, out_shape=(jax.ShapeDtypeStruct(half, F32),...  15.4 us
    pallas_call x1, Pallas kernels, source_call(): pl.pallas_call(source_kernel, out_shape=jax.ShapeDtypeStruct((total, widt...  12.6 us
    all_to_all x1, waiting for transfers between devices, shards(): lax.all_to_all(outgoing, ('grp', 'blk'), 0, 0, tiled=True)  11.6 us
    ppermute x8, starting transfers between devices, hop_grp(): lax.ppermute(value, 'grp', [(i, (i // 2 + dx) % 4 * 2 + (i % 2 ^ dy)) for...  10.6 us
    all_to_all x1, starting transfers between devices, shards(): lax.all_to_all(served, ('grp', 'blk'), 0, 0, tiled=True)  10.2 us
  transfers between devices with their start and end apart: 35, of which 5 were waited for; matrix products, arithmetic and copies ran while one was open for 17% of the time, Pallas kernels for 18%

profile of v3, /device:TPU:0, one launch (start us, length us, event | category | flops | bytes accessed | tf_op | source)
XLA Modules:
  0.0 223.9 jit_solution(1092509009817830145)
XLA Ops:
  0.6 3.4 %collective-permute-start = (bf16[192,768]{1,0:T(8,128)(2,1)}, bf16[192,768]{1,0:T(8,128)(2,1)}, u32[]{:S(2)}, u32[]{:S(2)}) collective-permute-start(bf16[192,768]{1,0:T(8,128)(2,1)} %refs_0_.1), channel_id=1, source_target_pairs={{0,2},{1,3},{2,0},{3,1},{4,6},{5,7},{6,4},{7,5},{8,10},{9,11},{10,... | collective-permute-start | bytes 884744 | tf_op jit(solution)/shard_map/ppermute | solution.py:21
  4.0 3.9 %collective-permute-start.7 = (bf16[192,768]{1,0:T(8,128)(2,1)}, bf16[192,768]{1,0:T(8,128)(2,1)S(1)}, u32[]{:S(2)}, u32[]{:S(2)}) collective-permute-start(bf16[192,768]{1,0:T(8,128)(2,1)} %refs_0_.1), channel_id=1, source_target_pairs={{0,8},{1,9},{2,10},{3,11},{4,12},{5,13},{6,14},{7,15},{8,0},{9,1},... | collective-permute-start | bytes 884744 | tf_op jit(solution)/shard_map/ppermute | solution.py:21
  11.9 7.3 %all-to-all-start = ((s32[128,1,3]{2,1,0:T(1,128)}), s32[128,1,3]{2,1,0:T(1,128)}, u32[]{:S(2)}, u32[]{:S(2)}) async-start(s32[128,1,3]{2,1,0:T(1,128)} %bitcast), calls=%async_computation | async-start | bytes 131072 | tf_op jit(solution)/shard_map/all_to_all | solution.py:285
  22.7 2.8 %collective-permute-start.8 = (bf16[192,768]{1,0:T(8,128)(2,1)}, bf16[192,768]{1,0:T(8,128)(2,1)}, u32[]{:S(2)}, u32[]{:S(2)}) collective-permute-start(bf16[192,768]{1,0:T(8,128)(2,1)} %collective-permute-done.t1.refs_1_), channel_id=1, source_target_pairs={{0,12},{1,13},{2,14},{3,15},{4,0},{5,1},{6,2},{7,3},{8,4},{9,5},{1... | collective-permute-start | bytes 884744 | tf_op jit(solution)/shard_map/ppermute | solution.py:21
  28.6 6.1 %scores.4 = (bf16[4,1536,768]{2,1,0:T(8,128)(2,1)}, f32[8,1536]{1,0:T(8,128)S(1)}) custom-call(s32[4]{0:T(128)S(1)} %pad_add_fusion.2.place, bf16[1536,768]{1,0:T(8,128)(2,1)S(1)} %copy-done.1, bf16[192,768]{1,0:T(8,128)(2,1)} %refs_0_.1, bf16[192,768]{1,0:T(8,128)(2,1)} %collective-permute-done.t1.refs_1_, ...), custom_call_target="tpu_custom_call" | custom-call | flops 1811939328 | bytes 4718592 | tf_op jit(solution)/shard_map/scores/pallas_call | solution.py:83
  40.9 2.0 reshape.351
  42.9 10.2 %all-to-all-start.1 = ((bf16[128,3,768]{2,1,0:T(4,128)(2,1)}), bf16[128,3,768]{2,1,0:T(4,128)(2,1)}, u32[]{:S(2)}, u32[]{:S(2)}) async-start(bf16[128,3,768]{2,1,0:T(4,128)(2,1)} %reshape.351), calls=%async_computation.1 | async-start | bytes 1572864 | tf_op jit(solution)/shard_map/all_to_all | solution.py:323
  53.8 6.0 %scores.5 = (bf16[4,1536,768]{2,1,0:T(8,128)(2,1)}, f32[8,1536]{1,0:T(8,128)S(1)}) custom-call(s32[4]{0:T(128)S(1)} %pad_add_fusion.3.place, bf16[1536,768]{1,0:T(8,128)(2,1)S(1)} %copy-done.2, bf16[192,768]{1,0:T(8,128)(2,1)S(1)} %collective-permute-done.3.t0.refs_4_, ...), custom_call_target="tpu_custom_call", output_to_operand_aliasing={{0}: (6, {})} | custom-call | flops 1811939328 | bytes 4718592 | tf_op jit(solution)/shard_map/scores/pallas_call | solution.py:83
  61.4 6.1 %scores.6 = (bf16[4,1536,768]{2,1,0:T(8,128)(2,1)}, f32[8,1536]{1,0:T(8,128)S(1)}) custom-call(s32[4]{0:T(128)S(1)} %pad_add_fusion.4.place, bf16[1536,768]{1,0:T(8,128)(2,1)S(1)} %copy-done.2, bf16[192,768]{1,0:T(8,128)(2,1)S(1)} %collective-permute-done.7.t0.refs_8_, ...), custom_call_target="tpu_custom_call", output_to_operand_aliasing={{0}: (6, {})} | custom-call | flops 1811939328 | bytes 4718592 | tf_op jit(solution)/shard_map/scores/pallas_call | solution.py:83
  67.6 6.1 %scores.7 = (bf16[4,1536,768]{2,1,0:T(8,128)(2,1)}, f32[8,1536]{1,0:T(8,128)S(1)}) custom-call(s32[4]{0:T(128)S(1)} %pad_add_fusion.5.place, bf16[1536,768]{1,0:T(8,128)(2,1)S(1)} %copy-done.2, bf16[192,768]{1,0:T(8,128)(2,1)} %collective-permute-done.11.t0.refs_12_, ...), custom_call_target="tpu_custom_call", output_to_operand_aliasing={{0}: (6, {})} | custom-call | flops 1811939328 | bytes 4718592 | tf_op jit(solution)/shard_map/scores/pallas_call | solution.py:83
  75.1 2.2 reshape.352
  77.4 3.0 %fusion.3 = (f32[192]{0:T(256)S(1)}, f32[192]{0:T(256)S(1)}, f32[]{:T(128)}, f32[192,768]{1,0:T(8,128)}) fusion(bf16[1536,768]{1,0:T(8,128)(2,1)S(1)} %copy-done.2, s32[]{:T(128)S(6)} %select_n.245, bf16[192,768]{1,0:T(8,128)(2,1)S(1)} %collective-permute-done.15.tgt, bf16[384,768]{1,0:T(8,128)(2,1)} %reshape.352, s32[192]{0:T(256)S(1)} %multiply_add_fusion), kind=kOutput, calls=%fused_computation.13 | convolution fusion | flops 114499200 | bytes 1771784 | tf_op jit(solution)/shard_map/dot_general | solution.py:29
  80.4 1.8 fusion.32
  84.2 9.7 %all-to-all-start.2 = ((f32[8,8,1536]{2,1,0:T(8,128)}), f32[8,8,1536]{2,1,0:T(8,128)S(1)}, u32[]{:S(2)}, u32[]{:S(2)}) async-start(f32[8,8,1536]{2,1,0:T(8,128)} %broadcast_in_dim.40), calls=%async_computation.2 | async-start | bytes 786432 | tf_op jit(solution)/shard_map/all_to_all | solution.py:346
  94.5 12.6 %source_terms.1 = bf16[1536,768]{1,0:T(8,128)(2,1)} custom-call(f32[8,1536]{1,0:T(8,128)} %concatenate.22.w_ref, bf16[4,1536,768]{2,1,0:T(8,128)(2,1)} %get-tuple-element.43.e_ref, bf16[192,768]{1,0:T(8,128)(2,1)} %refs_0_.1, bf16[192,768]{1,0:T(8,128)(2,1)} %collective-permute-done.t1.refs_1_, bf16[192,768]{1,0:T(8,128)(2,1)} %copy-done.11, ...), custom_call_target="tpu_custom_call" | custom-call | flops 7247757312 | bytes 11796480 | tf_op jit(solution)/shard_map/source_terms/pallas_call | solution.py:131
  111.0 15.4 %target_terms.1 = (f32[4,384,768]{2,1,0:T(8,128)}, bf16[4,384,768]{2,1,0:T(8,128)(2,1)}) custom-call(s32[16]{0:T(128)} %concatenate.24.place, f32[8,1536]{1,0:T(8,128)} %maximum_maximum_fusion.w_ref, bf16[4,1536,768]{2,1,0:T(8,128)(2,1)} %get-tuple-element.43.e_ref, bf16[1536,768]{1,0:T(8,128)(2,1)} %src_ref.1, bf16[16,128]{1,0:T(8,128)(2,1)} %copy-done.17), custom_call_target="tpu_custom_call" | custom-call | flops 7247757312 | bytes 18874368 | tf_op jit(solution)/shard_map/target_terms/pallas_call | solution.py:184
  126.8 4.4 %all-to-all-start.3 = ((bf16[8,192,768]{2,1,0:T(8,128)(2,1)}), bf16[8,192,768]{2,1,0:T(8,128)(2,1)S(1)}, u32[]{:S(2)}, u32[]{:S(2)}) async-start(bf16[8,192,768]{2,1,0:T(8,128)(2,1)} %bitcast.69), calls=%async_computation.3 | async-start | bytes 4718592 | tf_op jit(solution)/shard_map/all_to_all | solution.py:350
  131.4 2.9 %fusion.10 = (bf16[192,768]{1,0:T(8,128)(2,1)S(1)}, bf16[192,768]{1,0:T(8,128)(2,1)S(1)}, bf16[192,768]{1,0:T(8,128)(2,1)S(1)}, bf16[192,768]{1,0:T(8,128)(2,1)S...) fusion(f32[4,384,768]{2,1,0:T(8,128)} %get-tuple-element.46.keep, ...), kind=kLoop, calls=%fused_computation.33 | loop fusion | flops 2654208 | bytes 7077888 | tf_op jit(solution)/shard_map/convert_element_type | solution.py:381
  136.7 2.4 %collective-permute-start.19 = (bf16[384,768]{1,0:T(8,128)(2,1)}, bf16[384,768]{1,0:T(8,128)(2,1)}, u32[]{:S(2)}, u32[]{:S(2)}) collective-permute-start(bf16[384,768]{1,0:T(8,128)(2,1)} %pad_maximum_fusion.1), channel_id=1, source_target_pairs={{0,12},{1,13},{2,14},{3,15},{4,0},{5,1},{6,2},{7,3},{8,4},{9,5},{1... | collective-permute-start | bytes 1769480 | tf_op jit(solution)/shard_map/ppermute | solution.py:21
  144.5 2.4 %fusion.1.scale = f32[1536,1]{1,0:T(8,128)S(1)} fusion(f32[1536]{0:T(1024)S(1)} %get-tuple-element.88, f32[1536,1]{1,0:T(8,128)} %copy.66, f32[1536]{0:T(1024)S(1)} %fusion.22, f32[1536,1]{1,0:T(8,128)} %copy.63, f32[1536,1]{1,0:T(8,128)} %copy.62, f32[1536]{0:T(1024)S(1)} %slice_reduce_fusion.3), kind=kLoop, calls=%fused_computation.9 | loop fusion | flops 23040 | bytes 43008 | tf_op jit(solution)/shard_map/mul | solution.py:420
  146.9 17.8 %collective-permute-done.18.m1 = bf16[384,768]{1,0:T(8,128)(2,1)} collective-permute-done((bf16[384,768]{1,0:T(8,128)(2,1)}, bf16[384,768]{1,0:T(8,128)(2,1)}, u32[]{:S(2)}, u32[]{:S(2)}) %collective-permute-start.18) | collective-permute-done | bytes 589856 | tf_op jit(solution)/shard_map/ppermute | solution.py:21
  164.9 3.0 %lines.1 = (f32[192,768]{1,0:T(8,128)}, bf16[192,768]{1,0:T(8,128)(2,1)}) custom-call(f32[4,384,768]{2,1,0:T(8,128)} %get-tuple-element.46.keep, bf16[4,384,768]{2,1,0:T(8,128)(2,1)} %collective-permute-done.17.got, bf16[384,768]{1,0:T(8,128)(2,1)} %collective-permute-done.18.m1, bf16[384,768]{1,0:T(8,128)(2,1)} %collective-permute-done.19.m2, ...), custom_call_target="tpu_custom_call" | custom-call | flops 1474560 | bytes 4423680 | tf_op jit(solution)/shard_map/lines/pallas_call | solution.py:386
  169.3 3.0 %code.1 = (s16[192,768]{1,0:T(8,128)(2,1)}, s16[96,768]{1,0:T(8,128)(2,1)}) custom-call(bf16[8,192,768]{2,1,0:T(8,128)(2,1)} %copy-done.13, f32[192,768]{1,0:T(8,128)} %get-tuple-element.87.hard, bf16[192,768]{1,0:T(8,128)(2,1)} %copy-done.14, f32[192,11]{1,0:T(8,128)} %bitcast.70, bf16[192,768]{1,0:T(8,128)(2,1)} %get-tuple-element.48._), custom_call_target="tpu_custom_call" | custom-call | flops 1474560 | bytes 3244032 | tf_op jit(solution)/shard_map/code/pallas_call | solution.py:397
  172.3 2.8 %collective-permute-start.22 = (s16[96,768]{1,0:T(8,128)(2,1)}, s16[96,768]{1,0:T(8,128)(2,1)S(1)}, u32[]{:S(2)}, u32[]{:S(2)}) collective-permute-start(s16[96,768]{1,0:T(8,128)(2,1)} %get-tuple-element.50), channel_id=1, source_target_pairs={{0,96},{16,112},{32,0},{48,16},{64,32},{80,48},{96,64},{112,80},{1... | collective-permute-start | bytes 442376 | tf_op jit(solution)/shard_map/ppermute | solution.py:25
  176.8 3.5 %collective-permute-start.29 = (bf16[192,768]{1,0:T(8,128)(2,1)}, bf16[192,768]{1,0:T(8,128)(2,1)}, u32[]{:S(2)}, u32[]{:S(2)}) collective-permute-start(bf16[192,768]{1,0:T(8,128)(2,1)} %get-tuple-element.48._), channel_id=1, source_target_pairs={{0,2},{1,3},{2,0},{3,1},{4,6},{5,7},{6,4},{7,5},{8,10},{9,11},{10,... | collective-permute-start | bytes 884744 | tf_op jit(solution)/shard_map/ppermute | solution.py:21
  185.6 8.5 %all-to-all-start.4 = ((bf16[128,3,768]{2,1,0:T(4,128)(2,1)}), bf16[128,3,768]{2,1,0:T(4,128)(2,1)}, u32[]{:S(2)}, u32[]{:S(2)}) async-start(bf16[128,3,768]{2,1,0:T(4,128)(2,1)} %reshape.354), calls=%async_computation.4 | async-start | bytes 1572864 | tf_op jit(solution)/shard_map/all_to_all | solution.py:425
  196.8 2.7 %collective-permute-start.25 = (s16[2,96,768]{2,1,0:T(8,128)(2,1)}, s16[2,96,768]{2,1,0:T(8,128)(2,1)S(1)}, u32[]{:S(2)}, u32[]{:S(2)}) collective-permute-start(s16[2,96,768]{2,1,0:T(8,128)(2,1)} %pad_add_fusion.1), channel_id=1, source_target_pairs={{0,96},{16,112},{32,0},{48,16},{64,32},{80,48},{96,64},{112,80},{1... | collective-permute-start | bytes 884744 | tf_op jit(solution)/shard_map/ppermute | solution.py:25
  201.1 2.0 convert_add_fusion
  203.2 11.6 %all-to-all-done.4 = bf16[128,3,768]{2,1,0:T(4,128)(2,1)} async-done(((bf16[128,3,768]{2,1,0:T(4,128)(2,1)}), bf16[128,3,768]{2,1,0:T(4,128)(2,1)}, u32[]{:S(2)}, u32[]{:S(2)}) %all-to-all-start.4) | async-done | bytes 589856 | tf_op jit(solution)/shard_map/all_to_all | solution.py:425
  214.8 2.2 reshape.355
  217.0 2.3 %fusion.5 = f32[192,768]{1,0:T(8,128)} fusion(bf16[384,768]{1,0:T(8,128)(2,1)} %reshape.355, s32[384]{0:T(512)S(1)} %eq.135), kind=kOutput, calls=%fused_computation.28 | convolution fusion | flops 113319936 | bytes 1181184 | tf_op jit(solution)/shard_map/dot_general | solution.py:29
  219.4 4.5 %decode.1 = f32[1536,768]{1,0:T(8,128)} custom-call(s32[8]{0:T(128)S(1)} %stack.170.order, f32[1536,1]{1,0:T(8,128)S(1)} %fusion.1.scale, s16[192,768]{1,0:T(8,128)(2,1)S(1)} %copy-done.3, s16[192,768]{1,0:T(8,128)(2,1)S(1)} %collective-permute-done.21.side, s16[96,768]{1,0:T(8,128)(2,1)S(1)} %collective-permute-done.22.far1, ...), custom_call_target="tpu_custom_call" | custom-call | flops 1179648 | bytes 7077888 | tf_op jit(solution)/shard_map/decode/pallas_call | solution.py:251
  (152 shorter events, 47.2 us)
Async XLA Ops:
  0.6 20.2 %collective-permute-start = (bf16[192,768]{1,0:T(8,128)(2,1)}, bf16[192,768]{1,0:T(8,128)(2,1)}, u32[]{:S(2)}, u32[]{:S(2)}) collective-permute-start(bf16[192,768]{1,0:T(8,128)(2,1)} %refs_0_.1), channel_id=1, source_target_pairs={{0,2},{1,3},{2,0},{3,1},{4,6},{5,7},{6,4},{7,5},{8,10},{9,11},{10,... | collective-permute-start | bytes 884744 | tf_op jit(solution)/shard_map/ppermute | solution.py:21
  4.0 33.9 %collective-permute-start.7 = (bf16[192,768]{1,0:T(8,128)(2,1)}, bf16[192,768]{1,0:T(8,128)(2,1)S(1)}, u32[]{:S(2)}, u32[]{:S(2)}) collective-permute-start(bf16[192,768]{1,0:T(8,128)(2,1)} %refs_0_.1), channel_id=1, source_target_pairs={{0,8},{1,9},{2,10},{3,11},{4,12},{5,13},{6,14},{7,15},{8,0},{9,1},... | collective-permute-start | bytes 884744 | tf_op jit(solution)/shard_map/ppermute | solution.py:21
  7.9 13.2 %collective-permute-start.1 = (bf16[192,768]{1,0:T(8,128)(2,1)}, bf16[192,768]{1,0:T(8,128)(2,1)S(1)}, u32[]{:S(2)}, u32[]{:S(2)}) collective-permute-start(bf16[192,768]{1,0:T(8,128)(2,1)} %refs_0_.1), channel_id=1, source_target_pairs={{0,1},{1,0},{2,3},{3,2},{4,5},{5,4},{6,7},{7,6},{8,9},{9,8},{10,11... | collective-permute-start | bytes 884744 | tf_op jit(solution)/shard_map/ppermute | solution.py:21
  7.9 30.8 %collective-permute-start.3 = (bf16[192,768]{1,0:T(8,128)(2,1)}, bf16[192,768]{1,0:T(8,128)(2,1)S(1)}, u32[]{:S(2)}, u32[]{:S(2)}) collective-permute-start(bf16[192,768]{1,0:T(8,128)(2,1)} %refs_0_.1), channel_id=1, source_target_pairs={{0,12},{1,13},{2,14},{3,15},{4,0},{5,1},{6,2},{7,3},{8,4},{9,5},{1... | collective-permute-start | bytes 884744 | tf_op jit(solution)/shard_map/ppermute | solution.py:21
  8.6 30.1 %collective-permute-start.4 = (bf16[192,768]{1,0:T(8,128)(2,1)}, bf16[192,768]{1,0:T(8,128)(2,1)S(1)}, u32[]{:S(2)}, u32[]{:S(2)}) collective-permute-start(bf16[192,768]{1,0:T(8,128)(2,1)} %refs_0_.1), channel_id=1, source_target_pairs={{0,4},{1,5},{2,6},{3,7},{4,8},{5,9},{6,10},{7,11},{8,12},{9,13},{1... | collective-permute-start | bytes 884744 | tf_op jit(solution)/shard_map/ppermute | solution.py:21
  11.9 24.8 %all-to-all-start = ((s32[128,1,3]{2,1,0:T(1,128)}), s32[128,1,3]{2,1,0:T(1,128)}, u32[]{:S(2)}, u32[]{:S(2)}) async-start(s32[128,1,3]{2,1,0:T(1,128)} %bitcast), calls=%async_computation | async-start | bytes 131072 | tf_op jit(solution)/shard_map/all_to_all | solution.py:285
  21.1 18.1 %collective-permute-start.11 = (bf16[192,768]{1,0:T(8,128)(2,1)}, bf16[192,768]{1,0:T(8,128)(2,1)}, u32[]{:S(2)}, u32[]{:S(2)}) collective-permute-start(bf16[192,768]{1,0:T(8,128)(2,1)} %collective-permute-done.t1.refs_1_), channel_id=1, source_target_pairs={{0,4},{1,5},{2,6},{3,7},{4,8},{5,9},{6,10},{7,11},{8,12},{9,13},{1... | collective-permute-start | bytes 884744 | tf_op jit(solution)/shard_map/ppermute | solution.py:21
  22.7 16.7 %collective-permute-start.8 = (bf16[192,768]{1,0:T(8,128)(2,1)}, bf16[192,768]{1,0:T(8,128)(2,1)}, u32[]{:S(2)}, u32[]{:S(2)}) collective-permute-start(bf16[192,768]{1,0:T(8,128)(2,1)} %collective-permute-done.t1.refs_1_), channel_id=1, source_target_pairs={{0,12},{1,13},{2,14},{3,15},{4,0},{5,1},{6,2},{7,3},{8,4},{9,5},{1... | collective-permute-start | bytes 884744 | tf_op jit(solution)/shard_map/ppermute | solution.py:21
  37.9 15.3 %collective-permute-start.12 = (bf16[192,768]{1,0:T(8,128)(2,1)}, bf16[192,768]{1,0:T(8,128)(2,1)}, u32[]{:S(2)}, u32[]{:S(2)}) collective-permute-start(bf16[192,768]{1,0:T(8,128)(2,1)} %collective-permute-done.t1.refs_1_), channel_id=1, source_target_pairs={{0,8},{1,9},{2,10},{3,11},{4,12},{5,13},{6,14},{7,15},{8,0},{9,1},... | collective-permute-start | bytes 884744 | tf_op jit(solution)/shard_map/ppermute | solution.py:21
  38.7 22.8 %collective-permute-start.9 = (bf16[192,768]{1,0:T(8,128)(2,1)S(1)}, bf16[192,768]{1,0:T(8,128)(2,1)}, u32[]{:S(2)}, u32[]{:S(2)}) collective-permute-start(bf16[192,768]{1,0:T(8,128)(2,1)S(1)} %collective-permute-done.7.t0.refs_8_), channel_id=1, source_target_pairs={{0,1},{1,0},{2,3},{3,2},{4,5},{5,4},{6,7},{7,6},{8,9},{9,8},{10,11... | collective-permute-start | bytes 884744 | tf_op jit(solution)/shard_map/ppermute | solution.py:21
  38.7 14.6 %collective-permute-start.5 = (bf16[192,768]{1,0:T(8,128)(2,1)S(1)}, bf16[192,768]{1,0:T(8,128)(2,1)}, u32[]{:S(2)}, u32[]{:S(2)}) collective-permute-start(bf16[192,768]{1,0:T(8,128)(2,1)S(1)} %collective-permute-done.3.t0.refs_4_), channel_id=1, source_target_pairs={{0,1},{1,0},{2,3},{3,2},{4,5},{5,4},{6,7},{7,6},{8,9},{9,8},{10,11... | collective-permute-start | bytes 884744 | tf_op jit(solution)/shard_map/ppermute | solution.py:21
  39.2 14.6 %collective-permute-start.6 = (bf16[192,768]{1,0:T(8,128)(2,1)S(1)}, bf16[192,768]{1,0:T(8,128)(2,1)}, u32[]{:S(2)}, u32[]{:S(2)}) collective-permute-start(bf16[192,768]{1,0:T(8,128)(2,1)S(1)} %collective-permute-done.4.t1.refs_5_), channel_id=1, source_target_pairs={{0,1},{1,0},{2,3},{3,2},{4,5},{5,4},{6,7},{7,6},{8,9},{9,8},{10,11... | collective-permute-start | bytes 884744 | tf_op jit(solution)/shard_map/ppermute | solution.py:21
  39.3 22.1 %collective-permute-start.10 = (bf16[192,768]{1,0:T(8,128)(2,1)}, bf16[192,768]{1,0:T(8,128)(2,1)}, u32[]{:S(2)}, u32[]{:S(2)}) collective-permute-start(bf16[192,768]{1,0:T(8,128)(2,1)} %collective-permute-done.8.t1.refs_9_), channel_id=1, source_target_pairs={{0,1},{1,0},{2,3},{3,2},{4,5},{5,4},{6,7},{7,6},{8,9},{9,8},{10,11... | collective-permute-start | bytes 884744 | tf_op jit(solution)/shard_map/ppermute | solution.py:21
  42.9 32.2 %all-to-all-start.1 = ((bf16[128,3,768]{2,1,0:T(4,128)(2,1)}), bf16[128,3,768]{2,1,0:T(4,128)(2,1)}, u32[]{:S(2)}, u32[]{:S(2)}) async-start(bf16[128,3,768]{2,1,0:T(4,128)(2,1)} %reshape.351), calls=%async_computation.1 | async-start | bytes 1572864 | tf_op jit(solution)/shard_map/all_to_all | solution.py:323
  53.2 14.4 %collective-permute-start.13 = (bf16[192,768]{1,0:T(8,128)(2,1)}, bf16[192,768]{1,0:T(8,128)(2,1)S(1)}, u32[]{:S(2)}, u32[]{:S(2)}) collective-permute-start(bf16[192,768]{1,0:T(8,128)(2,1)} %collective-permute-done.11.t0.refs_12_), channel_id=1, source_target_pairs={{0,1},{1,0},{2,3},{3,2},{4,5},{5,4},{6,7},{7,6},{8,9},{9,8},{10,11... | collective-permute-start | bytes 884744 | tf_op jit(solution)/shard_map/ppermute | solution.py:21
  53.3 14.3 %collective-permute-start.14 = (bf16[192,768]{1,0:T(8,128)(2,1)}, bf16[192,768]{1,0:T(8,128)(2,1)S(1)}, u32[]{:S(2)}, u32[]{:S(2)}) collective-permute-start(bf16[192,768]{1,0:T(8,128)(2,1)} %collective-permute-done.12.t1.refs_13_), channel_id=1, source_target_pairs={{0,1},{1,0},{2,3},{3,2},{4,5},{5,4},{6,7},{7,6},{8,9},{9,8},{10,11... | collective-permute-start | bytes 884744 | tf_op jit(solution)/shard_map/ppermute | solution.py:21
  59.8 17.5 %collective-permute-start.15 = (bf16[192,768]{1,0:T(8,128)(2,1)}, bf16[192,768]{1,0:T(8,128)(2,1)S(1)}, u32[]{:S(2)}, u32[]{:S(2)}) collective-permute-start(bf16[192,768]{1,0:T(8,128)(2,1)} %refs_0_.1), channel_id=1, source_target_pairs={{0,0},{1,16},{2,32},{3,48},{4,64},{5,80},{6,96},{7,112},{8,1},{9,1... | collective-permute-start | bytes 884744 | tf_op jit(solution)/shard_map/ppermute | solution.py:326
  84.2 22.9 %all-to-all-start.2 = ((f32[8,8,1536]{2,1,0:T(8,128)}), f32[8,8,1536]{2,1,0:T(8,128)S(1)}, u32[]{:S(2)}, u32[]{:S(2)}) async-start(f32[8,8,1536]{2,1,0:T(8,128)} %broadcast_in_dim.40), calls=%async_computation.2 | async-start | bytes 786432 | tf_op jit(solution)/shard_map/all_to_all | solution.py:346
  126.8 41.1 %all-to-all-start.3 = ((bf16[8,192,768]{2,1,0:T(8,128)(2,1)}), bf16[8,192,768]{2,1,0:T(8,128)(2,1)S(1)}, u32[]{:S(2)}, u32[]{:S(2)}) async-start(bf16[8,192,768]{2,1,0:T(8,128)(2,1)} %bitcast.69), calls=%async_computation.3 | async-start | bytes 4718592 | tf_op jit(solution)/shard_map/all_to_all | solution.py:350
  135.1 29.6 %collective-permute-start.18 = (bf16[384,768]{1,0:T(8,128)(2,1)}, bf16[384,768]{1,0:T(8,128)(2,1)}, u32[]{:S(2)}, u32[]{:S(2)}) collective-permute-start(bf16[384,768]{1,0:T(8,128)(2,1)} %pad_maximum_fusion), channel_id=1, source_target_pairs={{0,4},{1,5},{2,6},{3,7},{4,8},{5,9},{6,10},{7,11},{8,12},{9,13},{1... | collective-permute-start | bytes 1769480 | tf_op jit(solution)/shard_map/ppermute | solution.py:21
  136.7 28.1 %collective-permute-start.19 = (bf16[384,768]{1,0:T(8,128)(2,1)}, bf16[384,768]{1,0:T(8,128)(2,1)}, u32[]{:S(2)}, u32[]{:S(2)}) collective-permute-start(bf16[384,768]{1,0:T(8,128)(2,1)} %pad_maximum_fusion.1), channel_id=1, source_target_pairs={{0,12},{1,13},{2,14},{3,15},{4,0},{5,1},{6,2},{7,3},{8,4},{9,5},{1... | collective-permute-start | bytes 1769480 | tf_op jit(solution)/shard_map/ppermute | solution.py:21
  140.0 24.8 %collective-permute-start.20 = (bf16[384,768]{1,0:T(8,128)(2,1)}, bf16[384,768]{1,0:T(8,128)(2,1)}, u32[]{:S(2)}, u32[]{:S(2)}) collective-permute-start(bf16[384,768]{1,0:T(8,128)(2,1)} %pad_maximum_fusion.2), channel_id=1, source_target_pairs={{0,8},{1,9},{2,10},{3,11},{4,12},{5,13},{6,14},{7,15},{8,0},{9,1},... | collective-permute-start | bytes 1769480 | tf_op jit(solution)/shard_map/ppermute | solution.py:21
  172.3 21.9 %collective-permute-start.22 = (s16[96,768]{1,0:T(8,128)(2,1)}, s16[96,768]{1,0:T(8,128)(2,1)S(1)}, u32[]{:S(2)}, u32[]{:S(2)}) collective-permute-start(s16[96,768]{1,0:T(8,128)(2,1)} %get-tuple-element.50), channel_id=1, source_target_pairs={{0,96},{16,112},{32,0},{48,16},{64,32},{80,48},{96,64},{112,80},{1... | collective-permute-start | bytes 442376 | tf_op jit(solution)/shard_map/ppermute | solution.py:25
  175.1 19.2 %collective-permute-start.23 = (s16[96,768]{1,0:T(8,128)(2,1)}, s16[96,768]{1,0:T(8,128)(2,1)S(1)}, u32[]{:S(2)}, u32[]{:S(2)}) collective-permute-start(s16[96,768]{1,0:T(8,128)(2,1)} %get-tuple-element.50), channel_id=1, source_target_pairs={{0,64},{16,80},{32,96},{48,112},{64,0},{80,16},{96,32},{112,48},{1... | collective-permute-start | bytes 442376 | tf_op jit(solution)/shard_map/ppermute | solution.py:25
  175.9 18.3 %collective-permute-start.24 = (s16[96,768]{1,0:T(8,128)(2,1)}, s16[96,768]{1,0:T(8,128)(2,1)S(1)}, u32[]{:S(2)}, u32[]{:S(2)}) collective-permute-start(s16[96,768]{1,0:T(8,128)(2,1)} %get-tuple-element.50), channel_id=1, source_target_pairs={{0,32},{16,48},{32,64},{48,80},{64,96},{80,112},{96,0},{112,16},{1... | collective-permute-start | bytes 442376 | tf_op jit(solution)/shard_map/ppermute | solution.py:25
  176.8 24.4 %collective-permute-start.29 = (bf16[192,768]{1,0:T(8,128)(2,1)}, bf16[192,768]{1,0:T(8,128)(2,1)}, u32[]{:S(2)}, u32[]{:S(2)}) collective-permute-start(bf16[192,768]{1,0:T(8,128)(2,1)} %get-tuple-element.48._), channel_id=1, source_target_pairs={{0,2},{1,3},{2,0},{3,1},{4,6},{5,7},{6,4},{7,5},{8,10},{9,11},{10,... | collective-permute-start | bytes 884744 | tf_op jit(solution)/shard_map/ppermute | solution.py:21
  180.3 15.7 %collective-permute-start.21 = (s16[192,768]{1,0:T(8,128)(2,1)}, s16[192,768]{1,0:T(8,128)(2,1)S(1)}, u32[]{:S(2)}, u32[]{:S(2)}) collective-permute-start(s16[192,768]{1,0:T(8,128)(2,1)} %get-tuple-element.49.own), channel_id=1, source_target_pairs={{0,16},{16,0},{32,48},{48,32},{64,80},{80,64},{96,112},{112,96},{1... | collective-permute-start | bytes 884744 | tf_op jit(solution)/shard_map/ppermute | solution.py:25
  185.6 29.1 %all-to-all-start.4 = ((bf16[128,3,768]{2,1,0:T(4,128)(2,1)}), bf16[128,3,768]{2,1,0:T(4,128)(2,1)}, u32[]{:S(2)}, u32[]{:S(2)}) async-start(bf16[128,3,768]{2,1,0:T(4,128)(2,1)} %reshape.354), calls=%async_computation.4 | async-start | bytes 1572864 | tf_op jit(solution)/shard_map/all_to_all | solution.py:425
  195.1 24.3 %collective-permute-start.28 = (s16[3,96,768]{2,1,0:T(8,128)(2,1)}, s16[3,96,768]{2,1,0:T(8,128)(2,1)S(1)}, u32[]{:S(2)}, u32[]{:S(2)}) collective-permute-start(s16[3,96,768]{2,1,0:T(8,128)(2,1)} %pad_add_fusion), channel_id=1, source_target_pairs={{0,16},{16,0},{32,48},{48,32},{64,80},{80,64},{96,112},{112,96},{1... | collective-permute-start | bytes 1327112 | tf_op jit(solution)/shard_map/ppermute | solution.py:25
  196.8 22.6 %collective-permute-start.25 = (s16[2,96,768]{2,1,0:T(8,128)(2,1)}, s16[2,96,768]{2,1,0:T(8,128)(2,1)S(1)}, u32[]{:S(2)}, u32[]{:S(2)}) collective-permute-start(s16[2,96,768]{2,1,0:T(8,128)(2,1)} %pad_add_fusion.1), channel_id=1, source_target_pairs={{0,96},{16,112},{32,0},{48,16},{64,32},{80,48},{96,64},{112,80},{1... | collective-permute-start | bytes 884744 | tf_op jit(solution)/shard_map/ppermute | solution.py:25
  199.4 19.9 %collective-permute-start.26 = (s16[2,96,768]{2,1,0:T(8,128)(2,1)}, s16[2,96,768]{2,1,0:T(8,128)(2,1)S(1)}, u32[]{:S(2)}, u32[]{:S(2)}) collective-permute-start(s16[2,96,768]{2,1,0:T(8,128)(2,1)} %pad_add_fusion.1), channel_id=1, source_target_pairs={{0,64},{16,80},{32,96},{48,112},{64,0},{80,16},{96,32},{112,48},{1... | collective-permute-start | bytes 884744 | tf_op jit(solution)/shard_map/ppermute | solution.py:25
  200.3 19.1 %collective-permute-start.27 = (s16[2,96,768]{2,1,0:T(8,128)(2,1)}, s16[2,96,768]{2,1,0:T(8,128)(2,1)S(1)}, u32[]{:S(2)}, u32[]{:S(2)}) collective-permute-start(s16[2,96,768]{2,1,0:T(8,128)(2,1)} %pad_add_fusion.1), channel_id=1, source_target_pairs={{0,32},{16,48},{32,64},{48,80},{64,96},{80,112},{96,0},{112,16},{1... | collective-permute-start | bytes 884744 | tf_op jit(solution)/shard_map/ppermute | solution.py:25
  (21 other events, 226.9 us)

commit v4 on v3

--- a/solution.py
+++ b/solution.py
@@ -39,6 +39,7 @@
     rows = t0.shape[0]
     half = 2 * rows
     step = pl.program_id(0)
+    count = e_out.shape[1]
 
     @pl.when(step == 0)
     def _():
@@ -54,17 +55,17 @@
     column = lax.broadcasted_iota(jnp.int32, (PART, 2 * half), 1)
     line = lax.broadcasted_iota(jnp.int32, (PART, 1), 0)
     parts = []
-    for first in range(0, src.shape[0], PART):
+    for first in range(0, count, PART):
         ats = []
         for sub in range(2):
-            k = step * (src.shape[0] // rows) + first // rows + sub
+            k = step * (count // rows) + first // rows + sub
             at = jnp.int32(-(1 << 20))
             for q in range(4):
                 at = jnp.where(place[q] == k, (q - sub) * rows, at)
             ats.append(at)
         hole = line + jnp.where(line < rows, ats[0], ats[1])
         here = pl.ds(first, PART)
-        s = dot_f32(src[here, :], tgt, ((1,), (1,)))
+        s = dot_f32(src[pl.ds(pl.multiple_of(step * count + first, PART), PART), :], tgt, ((1,), (1,)))
         s = jnp.where(column == hole, NEG, s)
         top = jnp.max(s, axis=1, keepdims=True)
         e = jnp.exp(s - top)
@@ -79,7 +80,6 @@
     total = src.shape[0]
     cols = 4 * rows
     so_far = list(so_far)
-    whole = pl.BlockSpec((rows, width), lambda i, p: (0, 0))
     return pl.pallas_call(
         score_kernel,
         out_shape=(
@@ -89,8 +89,7 @@
         grid_spec=pltpu.PrefetchScalarGridSpec(
             num_scalar_prefetch=1,
             grid=(total // TILE,),
-            in_specs=[pl.BlockSpec((TILE, width), lambda i, p: (i, 0))]
-            + [whole] * 4
+            in_specs=[pl.BlockSpec(memory_space=pltpu.VMEM)] * 5
             + [pl.BlockSpec(memory_space=pl.ANY)] * len(so_far),
             out_specs=(
                 pl.BlockSpec((1, TILE, cols), lambda i, p: (n, i, 0)),
@@ -207,7 +206,7 @@
     )(place, weights, e_all, src, after)
 
 
-def code_kernel(parts, hard, tgt, col, _, out, high):
+def code_kernel(parts, hard, tgt, col, _a, _b, _c, out, high):
     total = hard[...] * col[:, 0:1] + tgt[...].astype(F32) * col[:, 1:2]
     for g in range(parts.shape[0]):
         total = total + parts[g].astype(F32) * col[:, 3 + g : 4 + g]
@@ -380,7 +379,8 @@
         here = slice(j * rows, (j + 1) * rows)
         return (keep[n, here] + got[n, here].astype(F32)).astype(BF)
 
-    moved = [hop_blk(jnp.concatenate([both(dz, 0), both(dz, 1)]), dz, 0, 0) for dz in (1, 3, 2)]
+    leave = [jnp.concatenate([both(dz, 0), both(dz, 1)]) for dz in (1, 3, 2)]
+    moved = [hop_blk(part, dz, 0, 0) for part, dz in zip(leave, (1, 3, 2))]
     whole = [pl.BlockSpec((1, 2 * rows, width), lambda i: (0, 0, 0))] * 2
     whole += [pl.BlockSpec((2 * rows, width), lambda i: (0, 0))] * 3
     mine, other = pl.pallas_call(
@@ -392,7 +392,6 @@
         cost_estimate=pl.CostEstimate(flops=10 * rows * width, bytes_accessed=30 * rows * width, transcendentals=0),
         name="lines",
     )(keep, got, *moved)
-    target_grad = mine + hop_blk(other, 0, 1, 0).astype(F32)
 
     coded, coded_high = pl.pallas_call(
         code_kernel,
@@ -403,15 +402,17 @@
             pl.BlockSpec((half, width), lambda i: (i, 0)),
             pl.BlockSpec((half, width), lambda i: (i, 0)),
             pl.BlockSpec((half, col.shape[1]), lambda i: (i, 0)),
-            pl.BlockSpec(memory_space=pl.ANY),
-        ],
+        ]
+        + [pl.BlockSpec(memory_space=pl.ANY)] * 3,
         out_specs=(pl.BlockSpec((half, width), lambda i: (i, 0)), pl.BlockSpec((half, width), lambda i: (0, 0))),
         cost_estimate=pl.CostEstimate(flops=10 * rows * width, bytes_accessed=22 * rows * width, transcendentals=0),
         name="code",
-    )(source_parts, hard_rows, own_target, col, other)
-    hard_gate = hard_prob + 0.0 * coded[0, 0].astype(F32)
+    )(source_parts, hard_rows, own_target, col, *leave)
     side = hop_grp(coded, 0, 1)
     far = [hop_grp(coded_high, -dx, 0) for dx in (1, 2, 3)]
+    other, side, far = lax.optimization_barrier((other, side, far))
+    hard_gate = hard_prob + 0.0 * side[0, 0].astype(F32)
+    target_grad = mine + hop_blk(other, 0, 1, 0).astype(F32)
     low = jnp.stack([coded[:half], side[:half]])
     pairs = [hop_grp(low, -dx, 0) for dx in (1, 2, 3)]
     far_side = hop_grp(jnp.stack(far), 0, 1)

time: 225 us -> 226 us (level)
  waiting for transfers between devices: 30.2 us -> 37.7 us
  starting transfers between devices: 75.6 us -> 70.5 us
    all_to_all x1, waiting for transfers between devices: 0.01 us -> 25.7 us  [shards(): lax.all_to_all(source_part.reshape(8, rows, width), 'grp', 0, 0, tiled=True)]
    ppermute x21, waiting for transfers between devices: 18.5 us -> 0.55 us  [hop_blk(): return lax.ppermute(value, 'blk', route)]
    all_to_all x1, waiting for transfers between devices: 11.6 us -> 6.76 us  [shards(): lax.all_to_all(outgoing, ('grp', 'blk'), 0, 0, tiled=True)]
    ppermute x8, waiting for transfers between devices: 0.02 us -> 4.76 us  [hop_grp(): lax.ppermute(value, 'grp', [(i, (i // 2 + dx) % 4 * 2 + (i % 2 ^ dy)) for...]
    ppermute x8, starting transfers between devices: 10.6 us -> 6.09 us  [hop_grp(): lax.ppermute(value, 'grp', [(i, (i // 2 + dx) % 4 * 2 + (i % 2 ^ dy)) for...]
    unnamed x37 -> x47, local copies, waits for them, and re-layouts: 7.97 us -> 7.97 us
  transfers between devices with their start and end apart: 35 -> 35, of which waited for: 5 -> 7; matrix products, arithmetic and copies ran while one was open for 17% -> 14% of each run, Pallas kernels for 18% -> 21%
where the time goes in v4:
time: 226 us; the launch traced here: 225 us
  starting transfers between devices  70.5 us (31%)
  Pallas kernels  62.8 us (28%)
  waiting for transfers between devices  37.7 us (17%)
  local copies, waits for them, and re-layouts  25 us (11%)
  other arithmetic  18.9 us (8%)
  matrix products  7.71 us (3%)
    all_to_all x1, waiting for transfers between devices, shards(): lax.all_to_all(source_part.reshape(8, rows, width), 'grp', 0, 0, tiled=True)  25.7 us
    pallas_call x4, Pallas kernels, score_call(): pl.pallas_call(score_kernel, out_shape=(pltpu.HBM((4, total, cols), BF),...  24.3 us
    ppermute x21, starting transfers between devices, hop_blk(): return lax.ppermute(value, 'blk', route)  22.3 us
    pallas_call x1, Pallas kernels, target_call(): pl.pallas_call(target_kernel, out_shape=(jax.ShapeDtypeStruct(half, F32),...  15.4 us
    pallas_call x1, Pallas kernels, source_call(): pl.pallas_call(source_kernel, out_shape=jax.ShapeDtypeStruct((total, widt...  12.6 us
    all_to_all x1, starting transfers between devices, shards(): lax.all_to_all(served, ('grp', 'blk'), 0, 0, tiled=True)  10.2 us
    all_to_all x1, starting transfers between devices, shards(): lax.all_to_all(jnp.broadcast_to(mine[None], (8, 8, total)), 'grp', 0, 0,...  9.66 us
    all_to_all x1, starting transfers between devices, shards(): lax.all_to_all(outgoing, ('grp', 'blk'), 0, 0, tiled=True)  8.79 us
  transfers between devices with their start and end apart: 35, of which 7 were waited for; matrix products, arithmetic and copies ran while one was open for 14% of the time, Pallas kernels for 21%

profile of v4, /device:TPU:0, one launch (start us, length us, event | category | flops | bytes accessed | tf_op | source)
XLA Modules:
  0.0 224.7 jit_solution(18059919911734023271)
XLA Ops:
  0.6 3.4 %collective-permute-start = (bf16[192,768]{1,0:T(8,128)(2,1)}, bf16[192,768]{1,0:T(8,128)(2,1)}, u32[]{:S(2)}, u32[]{:S(2)}) collective-permute-start(bf16[192,768]{1,0:T(8,128)(2,1)} %refs_0_.1), channel_id=1, source_target_pairs={{0,2},{1,3},{2,0},{3,1},{4,6},{5,7},{6,4},{7,5},{8,10},{9,11},{10,... | collective-permute-start | bytes 884744 | tf_op jit(solution)/shard_map/ppermute | solution.py:21
  4.0 3.9 %collective-permute-start.7 = (bf16[192,768]{1,0:T(8,128)(2,1)}, bf16[192,768]{1,0:T(8,128)(2,1)S(1)}, u32[]{:S(2)}, u32[]{:S(2)}) collective-permute-start(bf16[192,768]{1,0:T(8,128)(2,1)} %refs_0_.1), channel_id=1, source_target_pairs={{0,8},{1,9},{2,10},{3,11},{4,12},{5,13},{6,14},{7,15},{8,0},{9,1},... | collective-permute-start | bytes 884744 | tf_op jit(solution)/shard_map/ppermute | solution.py:21
  11.9 7.3 %all-to-all-start = ((s32[128,1,3]{2,1,0:T(1,128)}), s32[128,1,3]{2,1,0:T(1,128)}, u32[]{:S(2)}, u32[]{:S(2)}) async-start(s32[128,1,3]{2,1,0:T(1,128)} %bitcast), calls=%async_computation | async-start | bytes 131072 | tf_op jit(solution)/shard_map/all_to_all | solution.py:284
  22.6 2.8 %collective-permute-start.8 = (bf16[192,768]{1,0:T(8,128)(2,1)}, bf16[192,768]{1,0:T(8,128)(2,1)}, u32[]{:S(2)}, u32[]{:S(2)}) collective-permute-start(bf16[192,768]{1,0:T(8,128)(2,1)} %collective-permute-done.t1.refs_1_), channel_id=1, source_target_pairs={{0,12},{1,13},{2,14},{3,15},{4,0},{5,1},{6,2},{7,3},{8,4},{9,5},{1... | collective-permute-start | bytes 884744 | tf_op jit(solution)/shard_map/ppermute | solution.py:21
  26.8 1.7 copy-done.1
  28.5 6.0 %scores.4 = (bf16[4,1536,768]{2,1,0:T(8,128)(2,1)}, f32[8,1536]{1,0:T(8,128)S(1)}) custom-call(s32[4]{0:T(128)S(1)} %pad_add_fusion.2.place, bf16[1536,768]{1,0:T(8,128)(2,1)S(1)} %copy-done.1, bf16[192,768]{1,0:T(8,128)(2,1)} %refs_0_.1, bf16[192,768]{1,0:T(8,128)(2,1)} %collective-permute-done.t1.refs_1_, ...), custom_call_target="tpu_custom_call" | custom-call | flops 1811939328 | bytes 4718592 | tf_op jit(solution)/shard_map/scores/pallas_call | solution.py:83
  40.7 2.0 reshape.351
  42.7 10.2 %all-to-all-start.1 = ((bf16[128,3,768]{2,1,0:T(4,128)(2,1)}), bf16[128,3,768]{2,1,0:T(4,128)(2,1)}, u32[]{:S(2)}, u32[]{:S(2)}) async-start(bf16[128,3,768]{2,1,0:T(4,128)(2,1)} %reshape.351), calls=%async_computation.1 | async-start | bytes 1572864 | tf_op jit(solution)/shard_map/all_to_all | solution.py:322
  53.6 6.0 %scores.5 = (bf16[4,1536,768]{2,1,0:T(8,128)(2,1)}, f32[8,1536]{1,0:T(8,128)S(1)}) custom-call(s32[4]{0:T(128)S(1)} %pad_add_fusion.3.place, bf16[1536,768]{1,0:T(8,128)(2,1)S(1)} %copy-done.2, bf16[192,768]{1,0:T(8,128)(2,1)S(1)} %collective-permute-done.3.t0.refs_4_, ...), custom_call_target="tpu_custom_call", output_to_operand_aliasing={{0}: (6, {})} | custom-call | flops 1811939328 | bytes 4718592 | tf_op jit(solution)/shard_map/scores/pallas_call | solution.py:83
  61.3 6.1 %scores.6 = (bf16[4,1536,768]{2,1,0:T(8,128)(2,1)}, f32[8,1536]{1,0:T(8,128)S(1)}) custom-call(s32[4]{0:T(128)S(1)} %pad_add_fusion.4.place, bf16[1536,768]{1,0:T(8,128)(2,1)S(1)} %copy-done.2, bf16[192,768]{1,0:T(8,128)(2,1)S(1)} %collective-permute-done.7.t0.refs_8_, ...), custom_call_target="tpu_custom_call", output_to_operand_aliasing={{0}: (6, {})} | custom-call | flops 1811939328 | bytes 4718592 | tf_op jit(solution)/shard_map/scores/pallas_call | solution.py:83
  67.4 6.1 %scores.7 = (bf16[4,1536,768]{2,1,0:T(8,128)(2,1)}, f32[8,1536]{1,0:T(8,128)S(1)}) custom-call(s32[4]{0:T(128)S(1)} %pad_add_fusion.5.place, bf16[1536,768]{1,0:T(8,128)(2,1)S(1)} %copy-done.2, bf16[192,768]{1,0:T(8,128)(2,1)} %collective-permute-done.11.t0.refs_12_, ...), custom_call_target="tpu_custom_call", output_to_operand_aliasing={{0}: (6, {})} | custom-call | flops 1811939328 | bytes 4718592 | tf_op jit(solution)/shard_map/scores/pallas_call | solution.py:83
  75.0 2.2 reshape.352
  77.2 3.0 %fusion.3 = (f32[192]{0:T(256)S(1)}, f32[192]{0:T(256)S(1)}, f32[]{:T(128)}, f32[192,768]{1,0:T(8,128)}) fusion(bf16[1536,768]{1,0:T(8,128)(2,1)S(1)} %copy-done.2, s32[]{:T(128)S(6)} %select_n.245, bf16[192,768]{1,0:T(8,128)(2,1)S(1)} %collective-permute-done.15.tgt, bf16[384,768]{1,0:T(8,128)(2,1)} %reshape.352, s32[192]{0:T(256)S(1)} %multiply_add_fusion), kind=kOutput, calls=%fused_computation.13 | convolution fusion | flops 114499200 | bytes 1771784 | tf_op jit(solution)/shard_map/dot_general | solution.py:29
  80.2 1.7 fusion.32
  83.9 9.7 %all-to-all-start.2 = ((f32[8,8,1536]{2,1,0:T(8,128)}), f32[8,8,1536]{2,1,0:T(8,128)S(1)}, u32[]{:S(2)}, u32[]{:S(2)}) async-start(f32[8,8,1536]{2,1,0:T(8,128)} %broadcast_in_dim.40), calls=%async_computation.2 | async-start | bytes 786432 | tf_op jit(solution)/shard_map/all_to_all | solution.py:345
  94.2 12.6 %source_terms.1 = bf16[1536,768]{1,0:T(8,128)(2,1)} custom-call(f32[8,1536]{1,0:T(8,128)} %concatenate.22.w_ref, bf16[4,1536,768]{2,1,0:T(8,128)(2,1)} %get-tuple-element.48.e_ref, bf16[192,768]{1,0:T(8,128)(2,1)} %refs_0_.1, bf16[192,768]{1,0:T(8,128)(2,1)} %collective-permute-done.t1.refs_1_, bf16[192,768]{1,0:T(8,128)(2,1)} %copy-done.11, ...), custom_call_target="tpu_custom_call" | custom-call | flops 7247757312 | bytes 11796480 | tf_op jit(solution)/shard_map/source_terms/pallas_call | solution.py:130
  110.7 15.4 %target_terms.1 = (f32[4,384,768]{2,1,0:T(8,128)}, bf16[4,384,768]{2,1,0:T(8,128)(2,1)}) custom-call(s32[16]{0:T(128)} %concatenate.24.place, f32[8,1536]{1,0:T(8,128)} %maximum_maximum_fusion.w_ref, bf16[4,1536,768]{2,1,0:T(8,128)(2,1)} %get-tuple-element.48.e_ref, bf16[1536,768]{1,0:T(8,128)(2,1)} %src_ref.1, bf16[16,128]{1,0:T(8,128)(2,1)} %copy-done.22), custom_call_target="tpu_custom_call" | custom-call | flops 7247757312 | bytes 18874368 | tf_op jit(solution)/shard_map/target_terms/pallas_call | solution.py:183
  126.4 4.5 %all-to-all-start.3 = ((bf16[8,192,768]{2,1,0:T(8,128)(2,1)}), bf16[8,192,768]{2,1,0:T(8,128)(2,1)S(1)}, u32[]{:S(2)}, u32[]{:S(2)}) async-start(bf16[8,192,768]{2,1,0:T(8,128)(2,1)} %bitcast.69), calls=%async_computation.3 | async-start | bytes 4718592 | tf_op jit(solution)/shard_map/all_to_all | solution.py:349
  131.0 2.9 %fusion.10 = (bf16[192,768]{1,0:T(8,128)(2,1)S(1)}, bf16[192,768]{1,0:T(8,128)(2,1)S(1)}, bf16[192,768]{1,0:T(8,128)(2,1)S(1)}, bf16[192,768]{1,0:T(8,128)(2,1)S...) fusion(f32[4,384,768]{2,1,0:T(8,128)} %get-tuple-element.51.keep, ...), kind=kLoop, calls=%fused_computation.33 | loop fusion | flops 2654208 | bytes 7077888 | tf_op jit(solution)/shard_map/convert_element_type | solution.py:380
  136.4 2.4 %collective-permute-start.19 = (bf16[384,768]{1,0:T(8,128)(2,1)}, bf16[384,768]{1,0:T(8,128)(2,1)}, u32[]{:S(2)}, u32[]{:S(2)}) collective-permute-start(bf16[384,768]{1,0:T(8,128)(2,1)} %pad_maximum_fusion.1._b), channel_id=1, source_target_pairs={{0,12},{1,13},{2,14},{3,15},{4,0},{5,1},{6,2},{7,3},{8,4},{9,5},{1... | collective-permute-start | bytes 1769480 | tf_op jit(solution)/shard_map/ppermute | solution.py:21
  140.6 25.7 %all-to-all-done.3.parts = bf16[8,192,768]{2,1,0:T(8,128)(2,1)S(1)} async-done(((bf16[8,192,768]{2,1,0:T(8,128)(2,1)}), bf16[8,192,768]{2,1,0:T(8,128)(2,1)S(1)}, u32[]{:S(2)}, u32[]{:S(2)}) %all-to-all-start.3) | async-done | bytes 2359328 | tf_op jit(solution)/shard_map/all_to_all | solution.py:349
  167.7 3.0 %code.1 = (s16[192,768]{1,0:T(8,128)(2,1)}, s16[96,768]{1,0:T(8,128)(2,1)}) custom-call(bf16[8,192,768]{2,1,0:T(8,128)(2,1)} %copy-done.13, f32[192,768]{1,0:T(8,128)} %get-tuple-element.97.hard, bf16[192,768]{1,0:T(8,128)(2,1)} %copy-done.14, f32[192,11]{1,0:T(8,128)} %bitcast.70, bf16[384,768]{1,0:T(8,128)(2,1)} %pad_maximum_fusion._a, ...), custom_call_target="tpu_custom_call" | custom-call | flops 1474560 | bytes 3244032 | tf_op jit(solution)/shard_map/code/pallas_call | solution.py:396
  176.5 3.1 %lines.1 = (f32[192,768]{1,0:T(8,128)}, bf16[192,768]{1,0:T(8,128)(2,1)}) custom-call(f32[4,384,768]{2,1,0:T(8,128)} %get-tuple-element.51.keep, bf16[4,384,768]{2,1,0:T(8,128)(2,1)} %collective-permute-done.17.got, bf16[384,768]{1,0:T(8,128)(2,1)} %collective-permute-done.18.m1, bf16[384,768]{1,0:T(8,128)(2,1)} %collective-permute-done.19.m2, ...), custom_call_target="tpu_custom_call" | custom-call | flops 1474560 | bytes 4423680 | tf_op jit(solution)/shard_map/lines/pallas_call | solution.py:386
  180.6 2.2 collective-permute-done.23.far2
  189.4 2.7 %collective-permute-start.29 = (bf16[192,768]{1,0:T(8,128)(2,1)}, bf16[192,768]{1,0:T(8,128)(2,1)}, u32[]{:S(2)}, u32[]{:S(2)}) collective-permute-start(bf16[192,768]{1,0:T(8,128)(2,1)} %get-tuple-element.61), channel_id=1, source_target_pairs={{0,2},{1,3},{2,0},{3,1},{4,6},{5,7},{6,4},{7,5},{8,10},{9,11},{10,... | collective-permute-start | bytes 884744 | tf_op jit(solution)/shard_map/ppermute | solution.py:21
  192.9 2.3 %convolution_convert_fusion = bf16[384,768]{1,0:T(8,128)(2,1)} fusion(f32[192]{0:T(256)S(1)} %fusion.21, bf16[1536,768]{1,0:T(8,128)(2,1)} %src_ref.1, s32[]{:T(128)S(6)} %select_n.245, s32[192]{0:T(256)} %copy-done.19), kind=kOutput, calls=%fused_computation | convolution fusion | flops 114057216 | bytes 886532 | tf_op jit(solution)/shard_map/dot_general | solution.py:29
  195.1 2.0 reshape.354
  197.2 8.8 %all-to-all-start.4 = ((bf16[128,3,768]{2,1,0:T(4,128)(2,1)}), bf16[128,3,768]{2,1,0:T(4,128)(2,1)}, u32[]{:S(2)}, u32[]{:S(2)}) async-start(bf16[128,3,768]{2,1,0:T(4,128)(2,1)} %reshape.354), calls=%async_computation.4 | async-start | bytes 1572864 | tf_op jit(solution)/shard_map/all_to_all | solution.py:426
  206.0 2.8 %fusion.1.scale = f32[1536,1]{1,0:T(8,128)S(1)} fusion(f32[1536]{0:T(1024)} %copy-done.18, f32[1536,1]{1,0:T(8,128)S(1)} %copy.66, f32[1536]{0:T(1024)} %copy-done.17, f32[1536,1]{1,0:T(8,128)} %copy.63, f32[1536,1]{1,0:T(8,128)} %copy.62, f32[1536]{0:T(1024)S(1)} %slice_reduce_fusion.3), kind=kLoop, calls=%fused_computation.9 | loop fusion | flops 23040 | bytes 43008 | tf_op jit(solution)/shard_map/mul | solution.py:421
  208.8 1.8 convert_add_fusion
  210.7 4.5 %decode.1 = f32[1536,768]{1,0:T(8,128)} custom-call(s32[8]{0:T(128)S(1)} %stack.170.order, f32[1536,1]{1,0:T(8,128)S(1)} %fusion.1.scale, s16[192,768]{1,0:T(8,128)(2,1)S(1)} %copy-done.3, s16[192,768]{1,0:T(8,128)(2,1)S(1)} %collective-permute-done.21.side, s16[96,768]{1,0:T(8,128)(2,1)S(1)} %collective-permute-done.22.far1, ...), custom_call_target="tpu_custom_call" | custom-call | flops 1179648 | bytes 7077888 | tf_op jit(solution)/shard_map/decode/pallas_call | solution.py:250
  215.2 6.8 %all-to-all-done.4 = bf16[128,3,768]{2,1,0:T(4,128)(2,1)} async-done(((bf16[128,3,768]{2,1,0:T(4,128)(2,1)}), bf16[128,3,768]{2,1,0:T(4,128)(2,1)}, u32[]{:S(2)}, u32[]{:S(2)}) %all-to-all-start.4) | async-done | bytes 589856 | tf_op jit(solution)/shard_map/all_to_all | solution.py:426
  (162 shorter events, 47.3 us)
Async XLA Ops:
  0.6 20.1 %collective-permute-start = (bf16[192,768]{1,0:T(8,128)(2,1)}, bf16[192,768]{1,0:T(8,128)(2,1)}, u32[]{:S(2)}, u32[]{:S(2)}) collective-permute-start(bf16[192,768]{1,0:T(8,128)(2,1)} %refs_0_.1), channel_id=1, source_target_pairs={{0,2},{1,3},{2,0},{3,1},{4,6},{5,7},{6,4},{7,5},{8,10},{9,11},{10,... | collective-permute-start | bytes 884744 | tf_op jit(solution)/shard_map/ppermute | solution.py:21
  4.0 33.8 %collective-permute-start.7 = (bf16[192,768]{1,0:T(8,128)(2,1)}, bf16[192,768]{1,0:T(8,128)(2,1)S(1)}, u32[]{:S(2)}, u32[]{:S(2)}) collective-permute-start(bf16[192,768]{1,0:T(8,128)(2,1)} %refs_0_.1), channel_id=1, source_target_pairs={{0,8},{1,9},{2,10},{3,11},{4,12},{5,13},{6,14},{7,15},{8,0},{9,1},... | collective-permute-start | bytes 884744 | tf_op jit(solution)/shard_map/ppermute | solution.py:21
  7.9 13.1 %collective-permute-start.1 = (bf16[192,768]{1,0:T(8,128)(2,1)}, bf16[192,768]{1,0:T(8,128)(2,1)S(1)}, u32[]{:S(2)}, u32[]{:S(2)}) collective-permute-start(bf16[192,768]{1,0:T(8,128)(2,1)} %refs_0_.1), channel_id=1, source_target_pairs={{0,1},{1,0},{2,3},{3,2},{4,5},{5,4},{6,7},{7,6},{8,9},{9,8},{10,11... | collective-permute-start | bytes 884744 | tf_op jit(solution)/shard_map/ppermute | solution.py:21
  7.9 30.7 %collective-permute-start.3 = (bf16[192,768]{1,0:T(8,128)(2,1)}, bf16[192,768]{1,0:T(8,128)(2,1)S(1)}, u32[]{:S(2)}, u32[]{:S(2)}) collective-permute-start(bf16[192,768]{1,0:T(8,128)(2,1)} %refs_0_.1), channel_id=1, source_target_pairs={{0,12},{1,13},{2,14},{3,15},{4,0},{5,1},{6,2},{7,3},{8,4},{9,5},{1... | collective-permute-start | bytes 884744 | tf_op jit(solution)/shard_map/ppermute | solution.py:21
  8.6 29.9 %collective-permute-start.4 = (bf16[192,768]{1,0:T(8,128)(2,1)}, bf16[192,768]{1,0:T(8,128)(2,1)S(1)}, u32[]{:S(2)}, u32[]{:S(2)}) collective-permute-start(bf16[192,768]{1,0:T(8,128)(2,1)} %refs_0_.1), channel_id=1, source_target_pairs={{0,4},{1,5},{2,6},{3,7},{4,8},{5,9},{6,10},{7,11},{8,12},{9,13},{1... | collective-permute-start | bytes 884744 | tf_op jit(solution)/shard_map/ppermute | solution.py:21
  11.9 24.7 %all-to-all-start = ((s32[128,1,3]{2,1,0:T(1,128)}), s32[128,1,3]{2,1,0:T(1,128)}, u32[]{:S(2)}, u32[]{:S(2)}) async-start(s32[128,1,3]{2,1,0:T(1,128)} %bitcast), calls=%async_computation | async-start | bytes 131072 | tf_op jit(solution)/shard_map/all_to_all | solution.py:284
  21.0 18.0 %collective-permute-start.11 = (bf16[192,768]{1,0:T(8,128)(2,1)}, bf16[192,768]{1,0:T(8,128)(2,1)}, u32[]{:S(2)}, u32[]{:S(2)}) collective-permute-start(bf16[192,768]{1,0:T(8,128)(2,1)} %collective-permute-done.t1.refs_1_), channel_id=1, source_target_pairs={{0,4},{1,5},{2,6},{3,7},{4,8},{5,9},{6,10},{7,11},{8,12},{9,13},{1... | collective-permute-start | bytes 884744 | tf_op jit(solution)/shard_map/ppermute | solution.py:21
  22.6 16.6 %collective-permute-start.8 = (bf16[192,768]{1,0:T(8,128)(2,1)}, bf16[192,768]{1,0:T(8,128)(2,1)}, u32[]{:S(2)}, u32[]{:S(2)}) collective-permute-start(bf16[192,768]{1,0:T(8,128)(2,1)} %collective-permute-done.t1.refs_1_), channel_id=1, source_target_pairs={{0,12},{1,13},{2,14},{3,15},{4,0},{5,1},{6,2},{7,3},{8,4},{9,5},{1... | collective-permute-start | bytes 884744 | tf_op jit(solution)/shard_map/ppermute | solution.py:21
  37.8 15.3 %collective-permute-start.12 = (bf16[192,768]{1,0:T(8,128)(2,1)}, bf16[192,768]{1,0:T(8,128)(2,1)}, u32[]{:S(2)}, u32[]{:S(2)}) collective-permute-start(bf16[192,768]{1,0:T(8,128)(2,1)} %collective-permute-done.t1.refs_1_), channel_id=1, source_target_pairs={{0,8},{1,9},{2,10},{3,11},{4,12},{5,13},{6,14},{7,15},{8,0},{9,1},... | collective-permute-start | bytes 884744 | tf_op jit(solution)/shard_map/ppermute | solution.py:21
  38.5 22.7 %collective-permute-start.9 = (bf16[192,768]{1,0:T(8,128)(2,1)S(1)}, bf16[192,768]{1,0:T(8,128)(2,1)}, u32[]{:S(2)}, u32[]{:S(2)}) collective-permute-start(bf16[192,768]{1,0:T(8,128)(2,1)S(1)} %collective-permute-done.7.t0.refs_8_), channel_id=1, source_target_pairs={{0,1},{1,0},{2,3},{3,2},{4,5},{5,4},{6,7},{7,6},{8,9},{9,8},{10,11... | collective-permute-start | bytes 884744 | tf_op jit(solution)/shard_map/ppermute | solution.py:21
  38.6 14.5 %collective-permute-start.5 = (bf16[192,768]{1,0:T(8,128)(2,1)S(1)}, bf16[192,768]{1,0:T(8,128)(2,1)}, u32[]{:S(2)}, u32[]{:S(2)}) collective-permute-start(bf16[192,768]{1,0:T(8,128)(2,1)S(1)} %collective-permute-done.3.t0.refs_4_), channel_id=1, source_target_pairs={{0,1},{1,0},{2,3},{3,2},{4,5},{5,4},{6,7},{7,6},{8,9},{9,8},{10,11... | collective-permute-start | bytes 884744 | tf_op jit(solution)/shard_map/ppermute | solution.py:21
  39.1 14.6 %collective-permute-start.6 = (bf16[192,768]{1,0:T(8,128)(2,1)S(1)}, bf16[192,768]{1,0:T(8,128)(2,1)}, u32[]{:S(2)}, u32[]{:S(2)}) collective-permute-start(bf16[192,768]{1,0:T(8,128)(2,1)S(1)} %collective-permute-done.4.t1.refs_5_), channel_id=1, source_target_pairs={{0,1},{1,0},{2,3},{3,2},{4,5},{5,4},{6,7},{7,6},{8,9},{9,8},{10,11... | collective-permute-start | bytes 884744 | tf_op jit(solution)/shard_map/ppermute | solution.py:21
  39.2 22.1 %collective-permute-start.10 = (bf16[192,768]{1,0:T(8,128)(2,1)}, bf16[192,768]{1,0:T(8,128)(2,1)}, u32[]{:S(2)}, u32[]{:S(2)}) collective-permute-start(bf16[192,768]{1,0:T(8,128)(2,1)} %collective-permute-done.8.t1.refs_9_), channel_id=1, source_target_pairs={{0,1},{1,0},{2,3},{3,2},{4,5},{5,4},{6,7},{7,6},{8,9},{9,8},{10,11... | collective-permute-start | bytes 884744 | tf_op jit(solution)/shard_map/ppermute | solution.py:21
  42.7 32.2 %all-to-all-start.1 = ((bf16[128,3,768]{2,1,0:T(4,128)(2,1)}), bf16[128,3,768]{2,1,0:T(4,128)(2,1)}, u32[]{:S(2)}, u32[]{:S(2)}) async-start(bf16[128,3,768]{2,1,0:T(4,128)(2,1)} %reshape.351), calls=%async_computation.1 | async-start | bytes 1572864 | tf_op jit(solution)/shard_map/all_to_all | solution.py:322
  53.1 14.3 %collective-permute-start.13 = (bf16[192,768]{1,0:T(8,128)(2,1)}, bf16[192,768]{1,0:T(8,128)(2,1)S(1)}, u32[]{:S(2)}, u32[]{:S(2)}) collective-permute-start(bf16[192,768]{1,0:T(8,128)(2,1)} %collective-permute-done.11.t0.refs_12_), channel_id=1, source_target_pairs={{0,1},{1,0},{2,3},{3,2},{4,5},{5,4},{6,7},{7,6},{8,9},{9,8},{10,11... | collective-permute-start | bytes 884744 | tf_op jit(solution)/shard_map/ppermute | solution.py:21
  53.1 14.3 %collective-permute-start.14 = (bf16[192,768]{1,0:T(8,128)(2,1)}, bf16[192,768]{1,0:T(8,128)(2,1)S(1)}, u32[]{:S(2)}, u32[]{:S(2)}) collective-permute-start(bf16[192,768]{1,0:T(8,128)(2,1)} %collective-permute-done.12.t1.refs_13_), channel_id=1, source_target_pairs={{0,1},{1,0},{2,3},{3,2},{4,5},{5,4},{6,7},{7,6},{8,9},{9,8},{10,11... | collective-permute-start | bytes 884744 | tf_op jit(solution)/shard_map/ppermute | solution.py:21
  59.6 17.5 %collective-permute-start.15 = (bf16[192,768]{1,0:T(8,128)(2,1)}, bf16[192,768]{1,0:T(8,128)(2,1)S(1)}, u32[]{:S(2)}, u32[]{:S(2)}) collective-permute-start(bf16[192,768]{1,0:T(8,128)(2,1)} %refs_0_.1), channel_id=1, source_target_pairs={{0,0},{1,16},{2,32},{3,48},{4,64},{5,80},{6,96},{7,112},{8,1},{9,1... | collective-permute-start | bytes 884744 | tf_op jit(solution)/shard_map/ppermute | solution.py:325
  83.9 22.9 %all-to-all-start.2 = ((f32[8,8,1536]{2,1,0:T(8,128)}), f32[8,8,1536]{2,1,0:T(8,128)S(1)}, u32[]{:S(2)}, u32[]{:S(2)}) async-start(f32[8,8,1536]{2,1,0:T(8,128)} %broadcast_in_dim.40), calls=%async_computation.2 | async-start | bytes 786432 | tf_op jit(solution)/shard_map/all_to_all | solution.py:345
  126.4 39.8 %all-to-all-start.3 = ((bf16[8,192,768]{2,1,0:T(8,128)(2,1)}), bf16[8,192,768]{2,1,0:T(8,128)(2,1)S(1)}, u32[]{:S(2)}, u32[]{:S(2)}) async-start(bf16[8,192,768]{2,1,0:T(8,128)(2,1)} %bitcast.69), calls=%async_computation.3 | async-start | bytes 4718592 | tf_op jit(solution)/shard_map/all_to_all | solution.py:349
  134.7 40.5 %collective-permute-start.18 = (bf16[384,768]{1,0:T(8,128)(2,1)}, bf16[384,768]{1,0:T(8,128)(2,1)}, u32[]{:S(2)}, u32[]{:S(2)}) collective-permute-start(bf16[384,768]{1,0:T(8,128)(2,1)} %pad_maximum_fusion._a), channel_id=1, source_target_pairs={{0,4},{1,5},{2,6},{3,7},{4,8},{5,9},{6,10},{7,11},{8,12},{9,13},{1... | collective-permute-start | bytes 1769480 | tf_op jit(solution)/shard_map/ppermute | solution.py:21
  136.4 39.4 %collective-permute-start.19 = (bf16[384,768]{1,0:T(8,128)(2,1)}, bf16[384,768]{1,0:T(8,128)(2,1)}, u32[]{:S(2)}, u32[]{:S(2)}) collective-permute-start(bf16[384,768]{1,0:T(8,128)(2,1)} %pad_maximum_fusion.1._b), channel_id=1, source_target_pairs={{0,12},{1,13},{2,14},{3,15},{4,0},{5,1},{6,2},{7,3},{8,4},{9,5},{1... | collective-permute-start | bytes 1769480 | tf_op jit(solution)/shard_map/ppermute | solution.py:21
  139.7 36.9 %collective-permute-start.20 = (bf16[384,768]{1,0:T(8,128)(2,1)}, bf16[384,768]{1,0:T(8,128)(2,1)}, u32[]{:S(2)}, u32[]{:S(2)}) collective-permute-start(bf16[384,768]{1,0:T(8,128)(2,1)} %pad_maximum_fusion.2._c), channel_id=1, source_target_pairs={{0,8},{1,9},{2,10},{3,11},{4,12},{5,13},{6,14},{7,15},{8,0},{9,1},... | collective-permute-start | bytes 1769480 | tf_op jit(solution)/shard_map/ppermute | solution.py:21
  170.7 13.7 %collective-permute-start.21 = (s16[192,768]{1,0:T(8,128)(2,1)}, s16[192,768]{1,0:T(8,128)(2,1)S(1)}, u32[]{:S(2)}, u32[]{:S(2)}) collective-permute-start(s16[192,768]{1,0:T(8,128)(2,1)} %get-tuple-element.53.own), channel_id=1, source_target_pairs={{0,16},{16,0},{32,48},{48,32},{64,80},{80,64},{96,112},{112,96},{1... | collective-permute-start | bytes 884744 | tf_op jit(solution)/shard_map/ppermute | solution.py:25
  174.4 6.2 %collective-permute-start.22 = (s16[96,768]{1,0:T(8,128)(2,1)S(1)}, s16[96,768]{1,0:T(8,128)(2,1)S(1)}, u32[]{:S(2)}, u32[]{:S(2)}) collective-permute-start(s16[96,768]{1,0:T(8,128)(2,1)S(1)} %copy-done.21), channel_id=1, source_target_pairs={{0,96},{16,112},{32,0},{48,16},{64,32},{80,48},{96,64},{112,80},{1... | collective-permute-start | bytes 442376 | tf_op jit(solution)/shard_map/ppermute | solution.py:25
  175.2 7.6 %collective-permute-start.23 = (s16[96,768]{1,0:T(8,128)(2,1)S(1)}, s16[96,768]{1,0:T(8,128)(2,1)S(1)}, u32[]{:S(2)}, u32[]{:S(2)}) collective-permute-start(s16[96,768]{1,0:T(8,128)(2,1)S(1)} %copy-done.21), channel_id=1, source_target_pairs={{0,64},{16,80},{32,96},{48,112},{64,0},{80,16},{96,32},{112,48},{1... | collective-permute-start | bytes 442376 | tf_op jit(solution)/shard_map/ppermute | solution.py:25
  175.8 8.5 %collective-permute-start.24 = (s16[96,768]{1,0:T(8,128)(2,1)S(1)}, s16[96,768]{1,0:T(8,128)(2,1)S(1)}, u32[]{:S(2)}, u32[]{:S(2)}) collective-permute-start(s16[96,768]{1,0:T(8,128)(2,1)S(1)} %copy-done.21), channel_id=1, source_target_pairs={{0,32},{16,48},{32,64},{48,80},{64,96},{80,112},{96,0},{112,16},{1... | collective-permute-start | bytes 442376 | tf_op jit(solution)/shard_map/ppermute | solution.py:25
  185.1 25.5 %collective-permute-start.25 = (s16[2,96,768]{2,1,0:T(8,128)(2,1)}, s16[2,96,768]{2,1,0:T(8,128)(2,1)S(1)}, u32[]{:S(2)}, u32[]{:S(2)}) collective-permute-start(s16[2,96,768]{2,1,0:T(8,128)(2,1)} %pad_add_fusion.1), channel_id=1, source_target_pairs={{0,96},{16,112},{32,0},{48,16},{64,32},{80,48},{96,64},{112,80},{1... | collective-permute-start | bytes 884744 | tf_op jit(solution)/shard_map/ppermute | solution.py:25
  185.7 25.0 %collective-permute-start.26 = (s16[2,96,768]{2,1,0:T(8,128)(2,1)}, s16[2,96,768]{2,1,0:T(8,128)(2,1)S(1)}, u32[]{:S(2)}, u32[]{:S(2)}) collective-permute-start(s16[2,96,768]{2,1,0:T(8,128)(2,1)} %pad_add_fusion.1), channel_id=1, source_target_pairs={{0,64},{16,80},{32,96},{48,112},{64,0},{80,16},{96,32},{112,48},{1... | collective-permute-start | bytes 884744 | tf_op jit(solution)/shard_map/ppermute | solution.py:25
  186.3 24.4 %collective-permute-start.27 = (s16[2,96,768]{2,1,0:T(8,128)(2,1)}, s16[2,96,768]{2,1,0:T(8,128)(2,1)S(1)}, u32[]{:S(2)}, u32[]{:S(2)}) collective-permute-start(s16[2,96,768]{2,1,0:T(8,128)(2,1)} %pad_add_fusion.1), channel_id=1, source_target_pairs={{0,32},{16,48},{32,64},{48,80},{64,96},{80,112},{96,0},{112,16},{1... | collective-permute-start | bytes 884744 | tf_op jit(solution)/shard_map/ppermute | solution.py:25
  188.4 22.2 %collective-permute-start.28 = (s16[3,96,768]{2,1,0:T(8,128)(2,1)}, s16[3,96,768]{2,1,0:T(8,128)(2,1)S(1)}, u32[]{:S(2)}, u32[]{:S(2)}) collective-permute-start(s16[3,96,768]{2,1,0:T(8,128)(2,1)} %pad_add_fusion), channel_id=1, source_target_pairs={{0,16},{16,0},{32,48},{48,32},{64,80},{80,64},{96,112},{112,96},{1... | collective-permute-start | bytes 1327112 | tf_op jit(solution)/shard_map/ppermute | solution.py:25
  189.4 19.4 %collective-permute-start.29 = (bf16[192,768]{1,0:T(8,128)(2,1)}, bf16[192,768]{1,0:T(8,128)(2,1)}, u32[]{:S(2)}, u32[]{:S(2)}) collective-permute-start(bf16[192,768]{1,0:T(8,128)(2,1)} %get-tuple-element.61), channel_id=1, source_target_pairs={{0,2},{1,3},{2,0},{3,1},{4,6},{5,7},{6,4},{7,5},{8,10},{9,11},{10,... | collective-permute-start | bytes 884744 | tf_op jit(solution)/shard_map/ppermute | solution.py:21
  197.2 24.8 %all-to-all-start.4 = ((bf16[128,3,768]{2,1,0:T(4,128)(2,1)}), bf16[128,3,768]{2,1,0:T(4,128)(2,1)}, u32[]{:S(2)}, u32[]{:S(2)}) async-start(bf16[128,3,768]{2,1,0:T(4,128)(2,1)} %reshape.354), calls=%async_computation.4 | async-start | bytes 1572864 | tf_op jit(solution)/shard_map/all_to_all | solution.py:426
  (26 other events, 348.2 us)

commit v5 on v4

--- a/solution.py
+++ b/solution.py
@@ -206,7 +206,8 @@
     )(place, weights, e_all, src, after)
 
 
-def code_kernel(parts, hard, tgt, col, _a, _b, _c, out, high):
+def code_kernel(parts, hard, tgt, col, *refs):
+    out, high = refs[-2:]
     total = hard[...] * col[:, 0:1] + tgt[...].astype(F32) * col[:, 1:2]
     for g in range(parts.shape[0]):
         total = total + parts[g].astype(F32) * col[:, 3 + g : 4 + g]
@@ -279,9 +280,13 @@
     position = jnp.arange(rows, dtype=jnp.int32)
     same = (owner[:, None] == owner[None, :]) & (position[None, :] < position[:, None])
     slot = owner * cap + jnp.sum(same.astype(jnp.int32), axis=1)
-    at_slot = slot[:, None] == jnp.arange(slots, dtype=jnp.int32)[None, :]
-    requests = jnp.sum(jnp.where(at_slot, pool_row[:, None] + 1, 0), axis=0) - 1
-    wanted = lax.all_to_all(requests.reshape(owners, cap), ("grp", "blk"), 0, 0, tiled=True)
+    pick = (slot[:, None] == jnp.arange(slots, dtype=jnp.int32)[None, :]).astype(BF)
+    lane = jnp.arange(128, dtype=jnp.int32)[None, :]
+    note = jnp.where(lane == 0, pool_row[:, None] + 1, jnp.where(lane == 1, position[:, None], 0)).astype(BF)
+    sent = dot_f32(pick, jnp.concatenate([own_source, note], axis=1), ((0,), (0,))).astype(BF)
+    sent = sent.reshape(owners, cap, width + 128)
+    asked = lax.all_to_all(sent, ("grp", "blk"), 0, 0, tiled=True)
+
     lang_match = language[:, None] == jnp.arange(margin.shape[0], dtype=jnp.int32)[None, :]
     margin_row = jnp.sum(jnp.where(lang_match, margin[None, :], 0.0), axis=1)
 
@@ -315,22 +320,25 @@
         stats.append(stat)
 
     add_chunk(0)
-    wanted, stats[0] = lax.optimization_barrier((wanted, stats[0]))
-    serve = (wanted.reshape(slots)[:, None] == position[None, :]).astype(BF)
-    served = dot_f32(serve, hard_pool, ((1,), (0,))).astype(BF).reshape(owners, cap, width)
-    served, places[1] = lax.optimization_barrier((served, places[1]))
-    fetched = lax.all_to_all(served, ("grp", "blk"), 0, 0, tiled=True).reshape(slots, width)
     add_chunk(1)
+    asked, stats[1] = lax.optimization_barrier((asked, stats[1]))
+    asked = asked.reshape(slots, width + 128)
+    asker_rows = asked[:, :width]
+    pool_at = asked[:, width].astype(jnp.int32) - 1
+    asker_at = asked[:, width + 1].astype(jnp.int32)
+    serve = (pool_at[:, None] == position[None, :]).astype(BF)
+    served = dot_f32(serve, hard_pool, ((1,), (0,))).astype(BF)
+    served, places[2] = lax.optimization_barrier((served, places[2]))
+    fetched = lax.all_to_all(served.reshape(owners, cap, width), ("grp", "blk"), 0, 0, tiled=True)
     early_target, stats[1] = lax.optimization_barrier((target_emb, stats[1]))
     own_target = lax.ppermute(
         early_target, ("grp", "blk"), [(16 * i + j, (j % 8) * 16 + 2 * i + j // 8) for i in range(8) for j in range(16)]
     )
     add_chunk(2)
-    fetched, stats[2] = lax.optimization_barrier((fetched, stats[2]))
-    pick = at_slot.astype(BF)
-    hard_rows = dot_f32(pick, fetched, ((1,), (0,)))
+    add_chunk(3)
+    fetched, stats[3] = lax.optimization_barrier((fetched, stats[3]))
+    hard_rows = dot_f32(pick, fetched.reshape(slots, width), ((1,), (0,)))
     hard_score = jnp.sum(own_source.astype(F32) * hard_rows, axis=1)
-    add_chunk(3)
 
     tops = jnp.stack([stat[0] for stat in stats])
     sums = jnp.stack([stat[1] for stat in stats])
@@ -365,7 +373,6 @@
         [jnp.stack([jnp.exp(hard_all - log_total), less, 32767.0 / bound]), jnp.exp(everyone[:, 0] - log_total[None])]
     )
     col = lax.dynamic_slice_in_dim(col, start, rows, 1)
-    hard_prob = col[0]
     col = jnp.transpose(col)
     half = rows // 2
 
@@ -410,8 +417,7 @@
     )(source_parts, hard_rows, own_target, col, *leave)
     side = hop_grp(coded, 0, 1)
     far = [hop_grp(coded_high, -dx, 0) for dx in (1, 2, 3)]
-    other, side, far = lax.optimization_barrier((other, side, far))
-    hard_gate = hard_prob + 0.0 * side[0, 0].astype(F32)
+    other, side, far, late_logs = lax.optimization_barrier((other, side, far, log_total))
     target_grad = mine + hop_blk(other, 0, 1, 0).astype(F32)
     low = jnp.stack([coded[:half], side[:half]])
     pairs = [hop_grp(low, -dx, 0) for dx in (1, 2, 3)]
@@ -421,10 +427,15 @@
         blocks, (bound * (1.0 / 32767.0))[:, None], [coded, side, *far, *pairs, far_side]
     )
 
-    contribution = (hard_gate[:, None] * own_source.astype(F32)).astype(BF)
-    outgoing = dot_f32(pick, contribution, ((0,), (0,))).astype(BF).reshape(owners, cap, width)
-    incoming = lax.all_to_all(outgoing, ("grp", "blk"), 0, 0, tiled=True).reshape(slots, width)
-    pool_grad = dot_f32(serve, incoming, ((0,), (0,)))
+    all_logs = lax.all_to_all(jnp.broadcast_to(late_logs[None], (16, total)), "blk", 0, 0, tiled=True)
+    at_group = jnp.arange(8, dtype=jnp.int32)[:, None, None, None] * rows
+    at_row = at_group + asker_at.reshape(8, 16, cap, 1)
+    match = at_row == jnp.arange(total, dtype=jnp.int32)[None, None, None, :]
+    asked_log = jnp.sum(jnp.where(match, all_logs[None, :, None, :], 0.0), axis=3).reshape(slots)
+    asked_score = jnp.sum(asker_rows.astype(F32) * served.astype(F32), axis=1)
+    asked_prob = jnp.where(pool_at >= 0, jnp.exp(jnp.where(pool_at >= 0, asked_score - asked_log, LOW)), 0.0)
+    pool_terms = (asked_prob[:, None] * asker_rows.astype(F32)).astype(BF)
+    pool_grad = dot_f32(serve, pool_terms, ((0,), (0,)))
     return (row_loss, source_grad, target_grad, pool_grad)
 
 

time: 226 us -> 231 us (1.022)
  other arithmetic: 18.9 us -> 21.9 us
    ppermute x8, waiting for transfers between devices: 4.76 us -> 9.05 us  [hop_grp(): lax.ppermute(value, 'grp', [(i, (i // 2 + dx) % 4 * 2 + (i % 2 ^ dy)) for...]
    ppermute x21, waiting for transfers between devices: 0.55 us -> 4.6 us  [hop_blk(): return lax.ppermute(value, 'blk', route)]
    all_to_all x1, waiting for transfers between devices: 25.7 us -> 22.6 us  [shards(): lax.all_to_all(source_part.reshape(8, rows, width), 'grp', 0, 0, tiled=True)]
    all_to_all x3, waiting for transfers between devices: 6.76 us -> 3.78 us  [the longest x1 3.78 us: shards(): lax.all_to_all(jnp.broadcast_to(late_logs[None], (16, total)), 'blk', 0,...]
    reshape x4 -> x5, local copies, waits for them, and re-layouts: 7.74 us -> 9.42 us  [the longest x1 3.03 us: shards(): sent = sent.reshape(owners, cap, width + 128)]
    unnamed x47 -> x48, local copies, waits for them, and re-layouts: 7.97 us -> 6.38 us
  transfers between devices with their start and end apart: 35 -> 35, of which waited for: 7 -> 8; matrix products, arithmetic and copies ran while one was open for 14% -> 17% of each run, Pallas kernels for 21% -> 19%
where the time goes in v5:
time: 231 us; the launch traced here: 229 us
  starting transfers between devices  70 us (30%)
  Pallas kernels  62.9 us (27%)
  waiting for transfers between devices  40 us (17%)
  local copies, waits for them, and re-layouts  25.4 us (11%)
  other arithmetic  21.9 us (9%)
  matrix products  6.91 us (3%)
    pallas_call x4, Pallas kernels, score_call(): pl.pallas_call(score_kernel, out_shape=(pltpu.HBM((4, total, cols), BF),...  24.4 us
    ppermute x21, starting transfers between devices, hop_blk(): return lax.ppermute(value, 'blk', route)  24.2 us
    all_to_all x1, waiting for transfers between devices, shards(): lax.all_to_all(source_part.reshape(8, rows, width), 'grp', 0, 0, tiled=True)  22.6 us
    pallas_call x1, Pallas kernels, target_call(): pl.pallas_call(target_kernel, out_shape=(jax.ShapeDtypeStruct(half, F32),...  15.4 us
    pallas_call x1, Pallas kernels, source_call(): pl.pallas_call(source_kernel, out_shape=jax.ShapeDtypeStruct((total, widt...  12.6 us
    all_to_all x1, starting transfers between devices, shards(): lax.all_to_all(served.reshape(owners, cap, width), ('grp', 'blk'), 0, 0,...  9.32 us
    ppermute x8, waiting for transfers between devices, hop_grp(): lax.ppermute(value, 'grp', [(i, (i // 2 + dx) % 4 * 2 + (i % 2 ^ dy)) for...  9.05 us
    all_to_all x1, starting transfers between devices, shards(): lax.all_to_all(jnp.broadcast_to(mine[None], (8, 8, total)), 'grp', 0, 0,...  7.88 us
  transfers between devices with their start and end apart: 35, of which 8 were waited for; matrix products, arithmetic and copies ran while one was open for 17% of the time, Pallas kernels for 19%

profile of v5, /device:TPU:0, one launch (start us, length us, event | category | flops | bytes accessed | tf_op | source)
XLA Modules:
  0.0 228.6 jit_solution(10506566652660535176)
XLA Ops:
  0.6 3.4 %collective-permute-start = (bf16[192,768]{1,0:T(8,128)(2,1)}, bf16[192,768]{1,0:T(8,128)(2,1)}, u32[]{:S(2)}, u32[]{:S(2)}) collective-permute-start(bf16[192,768]{1,0:T(8,128)(2,1)} %refs_0_.1), channel_id=1, source_target_pairs={{0,2},{1,3},{2,0},{3,1},{4,6},{5,7},{6,4},{7,5},{8,10},{9,11},{10,... | collective-permute-start | bytes 884744 | tf_op jit(solution)/shard_map/ppermute | solution.py:21
  4.0 4.0 %collective-permute-start.3 = (bf16[192,768]{1,0:T(8,128)(2,1)}, bf16[192,768]{1,0:T(8,128)(2,1)S(1)}, u32[]{:S(2)}, u32[]{:S(2)}) collective-permute-start(bf16[192,768]{1,0:T(8,128)(2,1)} %refs_0_.1), channel_id=1, source_target_pairs={{0,12},{1,13},{2,14},{3,15},{4,0},{5,1},{6,2},{7,3},{8,4},{9,5},{1... | collective-permute-start | bytes 884744 | tf_op jit(solution)/shard_map/ppermute | solution.py:21
  14.1 3.0 %reshape.378 = bf16[128,3,896]{2,1,0:T(4,128)(2,1)} reshape(bf16[384,896]{1,0:T(8,128)(2,1)} %convolution_convert_fusion) | data formatting | bytes 1376256 | tf_op jit(solution)/shard_map/reshape | solution.py:287
  17.1 7.6 %all-to-all-start = ((bf16[128,3,896]{2,1,0:T(4,128)(2,1)}), bf16[128,3,896]{2,1,0:T(4,128)(2,1)}, u32[]{:S(2)}, u32[]{:S(2)}) async-start(bf16[128,3,896]{2,1,0:T(4,128)(2,1)} %reshape.378), calls=%async_computation | async-start | bytes 1835008 | tf_op jit(solution)/shard_map/all_to_all | solution.py:288
  25.1 2.9 %collective-permute-start.8 = (bf16[192,768]{1,0:T(8,128)(2,1)}, bf16[192,768]{1,0:T(8,128)(2,1)}, u32[]{:S(2)}, u32[]{:S(2)}) collective-permute-start(bf16[192,768]{1,0:T(8,128)(2,1)} %collective-permute-done.t1.refs_1_), channel_id=1, source_target_pairs={{0,12},{1,13},{2,14},{3,15},{4,0},{5,1},{6,2},{7,3},{8,4},{9,5},{1... | collective-permute-start | bytes 884744 | tf_op jit(solution)/shard_map/ppermute | solution.py:21
  29.7 6.1 %scores.4 = (bf16[4,1536,768]{2,1,0:T(8,128)(2,1)}, f32[8,1536]{1,0:T(8,128)S(1)}) custom-call(s32[4]{0:T(128)S(1)} %pad_add_fusion.2.place, bf16[1536,768]{1,0:T(8,128)(2,1)S(1)} %copy-done.1, bf16[192,768]{1,0:T(8,128)(2,1)S(1)} %copy-done.11, bf16[192,768]{1,0:T(8,128)(2,1)} %collective-permute-done.t1.refs_1_, ...), custom_call_target="tpu_custom_call" | custom-call | flops 1811939328 | bytes 4718592 | tf_op jit(solution)/shard_map/scores/pallas_call | solution.py:83
  36.5 2.4 %collective-permute-start.12 = (bf16[192,768]{1,0:T(8,128)(2,1)}, bf16[192,768]{1,0:T(8,128)(2,1)}, u32[]{:S(2)}, u32[]{:S(2)}) collective-permute-start(bf16[192,768]{1,0:T(8,128)(2,1)} %collective-permute-done.t1.refs_1_), channel_id=1, source_target_pairs={{0,8},{1,9},{2,10},{3,11},{4,12},{5,13},{6,14},{7,15},{8,0},{9,1},... | collective-permute-start | bytes 884744 | tf_op jit(solution)/shard_map/ppermute | solution.py:21
  38.9 4.4 %collective-permute-done.8.t1.refs_9_ = bf16[192,768]{1,0:T(8,128)(2,1)} collective-permute-done((bf16[192,768]{1,0:T(8,128)(2,1)}, bf16[192,768]{1,0:T(8,128)(2,1)}, u32[]{:S(2)}, u32[]{:S(2)}) %collective-permute-start.8) | collective-permute-done | bytes 294944 | tf_op jit(solution)/shard_map/ppermute | solution.py:21
  43.3 6.0 %scores.5 = (bf16[4,1536,768]{2,1,0:T(8,128)(2,1)}, f32[8,1536]{1,0:T(8,128)S(1)}) custom-call(s32[4]{0:T(128)S(1)} %pad_add_fusion.3.place, bf16[1536,768]{1,0:T(8,128)(2,1)S(1)} %copy-done.1, bf16[192,768]{1,0:T(8,128)(2,1)S(1)} %collective-permute-done.3.t0.refs_4_, ...), custom_call_target="tpu_custom_call", output_to_operand_aliasing={{0}: (6, {})} | custom-call | flops 1811939328 | bytes 4718592 | tf_op jit(solution)/shard_map/scores/pallas_call | solution.py:83
  50.0 3.0 %reshape.379 = bf16[384,896]{1,0:T(8,128)(2,1)} reshape(bf16[128,3,896]{2,1,0:T(4,128)(2,1)} %all-to-all-done) | data formatting | bytes 1376256 | tf_op jit(solution)/shard_map/reshape | solution.py:325
  56.3 9.3 %all-to-all-start.1 = ((bf16[128,3,768]{2,1,0:T(4,128)(2,1)}), bf16[128,3,768]{2,1,0:T(4,128)(2,1)}, u32[]{:S(2)}, u32[]{:S(2)}) async-start(bf16[128,3,768]{2,1,0:T(4,128)(2,1)} %reshape.380), calls=%async_computation.1 | async-start | bytes 1572864 | tf_op jit(solution)/shard_map/all_to_all | solution.py:332
  68.5 3.8 %collective-permute-start.15 = (bf16[192,768]{1,0:T(8,128)(2,1)}, bf16[192,768]{1,0:T(8,128)(2,1)}, u32[]{:S(2)}, u32[]{:S(2)}) collective-permute-start(bf16[192,768]{1,0:T(8,128)(2,1)} %refs_0_.1), channel_id=1, source_target_pairs={{0,0},{1,16},{2,32},{3,48},{4,64},{5,80},{6,96},{7,112},{8,1},{9,1... | collective-permute-start | bytes 884744 | tf_op jit(solution)/shard_map/ppermute | solution.py:334
  72.3 6.2 %scores.6 = (bf16[4,1536,768]{2,1,0:T(8,128)(2,1)}, f32[8,1536]{1,0:T(8,128)S(1)}) custom-call(s32[4]{0:T(128)S(1)} %pad_add_fusion.4.place, bf16[1536,768]{1,0:T(8,128)(2,1)S(1)} %copy-done.1, bf16[192,768]{1,0:T(8,128)(2,1)S(1)} %collective-permute-done.7.t0.refs_8_, ...), custom_call_target="tpu_custom_call", output_to_operand_aliasing={{0}: (6, {})} | custom-call | flops 1811939328 | bytes 4718592 | tf_op jit(solution)/shard_map/scores/pallas_call | solution.py:83
  79.1 6.1 %scores.7 = (bf16[4,1536,768]{2,1,0:T(8,128)(2,1)}, f32[8,1536]{1,0:T(8,128)S(1)}) custom-call(s32[4]{0:T(128)S(1)} %pad_add_fusion.5.place, bf16[1536,768]{1,0:T(8,128)(2,1)S(1)} %copy-done.1, bf16[192,768]{1,0:T(8,128)(2,1)} %collective-permute-done.11.t0.refs_12_, ...), custom_call_target="tpu_custom_call", output_to_operand_aliasing={{0}: (6, {})} | custom-call | flops 1811939328 | bytes 4718592 | tf_op jit(solution)/shard_map/scores/pallas_call | solution.py:83
  86.8 2.8 %abs_reduce_fusion = (f32[]{:T(128)}, f32[192]{0:T(256)S(1)}, f32[192]{0:T(256)S(1)}, f32[192,768]{1,0:T(8,128)}) fusion(bf16[192,768]{1,0:T(8,128)(2,1)} %copy-done.16, bf16[192,768]{1,0:T(8,128)(2,1)} %collective-permute-done.15.tgt, bf16[384,768]{1,0:T(8,128)(2,1)S(1)} %reshape.381, s32[192]{0:T(256)S(1)} %copy-done.19), kind=kOutput, calls=%fused_computation.31 | convolution fusion | flops 114499200 | bytes 1771780 | tf_op jit(solution)/shard_map/dot_general | solution.py:29
  92.9 7.9 %all-to-all-start.2 = ((f32[8,8,1536]{2,1,0:T(8,128)}), f32[8,8,1536]{2,1,0:T(8,128)S(1)}, u32[]{:S(2)}, u32[]{:S(2)}) async-start(f32[8,8,1536]{2,1,0:T(8,128)} %broadcast_in_dim.127), calls=%async_computation.2 | async-start | bytes 786432 | tf_op jit(solution)/shard_map/all_to_all | solution.py:353
  101.4 12.6 %source_terms.1 = bf16[1536,768]{1,0:T(8,128)(2,1)} custom-call(f32[8,1536]{1,0:T(8,128)} %concatenate.26.w_ref, bf16[4,1536,768]{2,1,0:T(8,128)(2,1)} %get-tuple-element.49.e_ref, bf16[192,768]{1,0:T(8,128)(2,1)} %refs_0_.1, bf16[192,768]{1,0:T(8,128)(2,1)} %collective-permute-done.t1.refs_1_, bf16[192,768]{1,0:T(8,128)(2,1)} %collective-permute-done.1.t2.refs_2_, ...), custom_call_target="tpu_custom_call" | custom-call | flops 7247757312 | bytes 11796480 | tf_op jit(solution)/shard_map/source_terms/pallas_call | solution.py:130
  118.5 15.4 %target_terms.1 = (f32[4,384,768]{2,1,0:T(8,128)}, bf16[4,384,768]{2,1,0:T(8,128)(2,1)}) custom-call(s32[16]{0:T(128)} %concatenate.28.place, f32[8,1536]{1,0:T(8,128)} %maximum_maximum_fusion.w_ref, bf16[4,1536,768]{2,1,0:T(8,128)(2,1)} %get-tuple-element.49.e_ref, bf16[1536,768]{1,0:T(8,128)(2,1)} %src_ref.1, bf16[16,128]{1,0:T(8,128)(2,1)} %copy-done.22), custom_call_target="tpu_custom_call" | custom-call | flops 7247757312 | bytes 18874368 | tf_op jit(solution)/shard_map/target_terms/pallas_call | solution.py:183
  135.6 4.5 %all-to-all-start.3 = ((bf16[8,192,768]{2,1,0:T(8,128)(2,1)}), bf16[8,192,768]{2,1,0:T(8,128)(2,1)S(1)}, u32[]{:S(2)}, u32[]{:S(2)}) async-start(bf16[8,192,768]{2,1,0:T(8,128)(2,1)} %bitcast.68), calls=%async_computation.3 | async-start | bytes 4718592 | tf_op jit(solution)/shard_map/all_to_all | solution.py:357
  143.7 2.9 %fusion.17 = (bf16[192,768]{1,0:T(8,128)(2,1)S(1)}, bf16[192,768]{1,0:T(8,128)(2,1)S(1)}, bf16[192,768]{1,0:T(8,128)(2,1)S(1)}, bf16[192,768]{1,0:T(8,128)(2,1)S...) fusion(f32[4,384,768]{2,1,0:T(8,128)} %get-tuple-element.52.keep, ...), kind=kLoop, calls=%fused_computation.42 | loop fusion | flops 2654208 | bytes 7077888 | tf_op jit(solution)/shard_map/convert_element_type | solution.py:387
  152.7 22.6 %all-to-all-done.3.parts = bf16[8,192,768]{2,1,0:T(8,128)(2,1)S(1)} async-done(((bf16[8,192,768]{2,1,0:T(8,128)(2,1)}), bf16[8,192,768]{2,1,0:T(8,128)(2,1)S(1)}, u32[]{:S(2)}, u32[]{:S(2)}) %all-to-all-start.3) | async-done | bytes 2359328 | tf_op jit(solution)/shard_map/all_to_all | solution.py:357
  176.8 2.9 %code.1 = (s16[192,768]{1,0:T(8,128)(2,1)}, s16[96,768]{1,0:T(8,128)(2,1)}) custom-call(bf16[8,192,768]{2,1,0:T(8,128)(2,1)} %copy-done.12, f32[192,768]{1,0:T(8,128)} %get-tuple-element.101.hard, bf16[192,768]{1,0:T(8,128)(2,1)} %collective-permute-done.15.tgt, f32[192,11]{1,0:T(8,128)} %bitcast.70, bf16[384,768]{1,0:T(8,128)(2,1)} %pad_maximum_fusion.refs_0_, ...), custom_call_target="tpu_custom_call" | custom-call | flops 1474560 | bytes 3244032 | tf_op jit(solution)/shard_map/code/pallas_call | solution.py:403
  180.6 2.3 fusion.3.scale
  185.1 3.0 %lines.1 = (f32[192,768]{1,0:T(8,128)}, bf16[192,768]{1,0:T(8,128)(2,1)}) custom-call(f32[4,384,768]{2,1,0:T(8,128)} %get-tuple-element.52.keep, bf16[4,384,768]{2,1,0:T(8,128)(2,1)} %collective-permute-done.17.got, bf16[384,768]{1,0:T(8,128)(2,1)} %collective-permute-done.18.m1, bf16[384,768]{1,0:T(8,128)(2,1)} %collective-permute-done.19.m2, ...), custom_call_target="tpu_custom_call" | custom-call | flops 1474560 | bytes 4423680 | tf_op jit(solution)/shard_map/lines/pallas_call | solution.py:393
  189.0 2.1 collective-permute-done.23.far2
  196.2 7.4 %all-to-all-start.4 = ((f32[16,1,1536]{2,1,0:T(1,128)}), f32[16,1,1536]{2,1,0:T(1,128)S(1)}, u32[]{:S(2)}, u32[]{:S(2)}) async-start(f32[16,1,1536]{2,1,0:T(1,128)} %broadcast_in_dim.129), calls=%async_computation.4 | async-start | bytes 196608 | tf_op jit(solution)/shard_map/all_to_all | solution.py:430
  203.7 3.4 %collective-permute-start.29 = (bf16[192,768]{1,0:T(8,128)(2,1)}, bf16[192,768]{1,0:T(8,128)(2,1)}, u32[]{:S(2)}, u32[]{:S(2)}) collective-permute-start(bf16[192,768]{1,0:T(8,128)(2,1)} %get-tuple-element.62), channel_id=1, source_target_pairs={{0,2},{1,3},{2,0},{3,1},{4,6},{5,7},{6,4},{7,5},{8,10},{9,11},{10,... | collective-permute-start | bytes 884744 | tf_op jit(solution)/shard_map/ppermute | solution.py:21
  208.2 3.8 %all-to-all-done.4 = f32[16,1,1536]{2,1,0:T(1,128)S(1)} async-done(((f32[16,1,1536]{2,1,0:T(1,128)}), f32[16,1,1536]{2,1,0:T(1,128)S(1)}, u32[]{:S(2)}, u32[]{:S(2)}) %all-to-all-start.4) | async-done | bytes 98336 | tf_op jit(solution)/shard_map/all_to_all | solution.py:430
  215.2 2.4 %fusion.6 = f32[192,768]{1,0:T(8,128)} fusion(f32[384]{0:T(512)S(1)} %fusion.23, bf16[384,896]{1,0:T(8,128)(2,1)} %reshape.379, s32[384]{0:T(512)S(1)} %get-tuple-element.65), kind=kOutput, calls=%fused_computation.19 | convolution fusion | flops 114204672 | bytes 1182720 | tf_op jit(solution)/shard_map/dot_general | solution.py:29
  217.6 2.0 convert_add_fusion
  219.6 4.5 %collective-permute-done.28.far_side = s16[3,96,768]{2,1,0:T(8,128)(2,1)S(1)} collective-permute-done((s16[3,96,768]{2,1,0:T(8,128)(2,1)}, s16[3,96,768]{2,1,0:T(8,128)(2,1)S(1)}, u32[]{:S(2)}, u32[]{:S(2)}) %collective-permute-start.28) | collective-permute-done | bytes 442400 | tf_op jit(solution)/shard_map/ppermute | solution.py:25
  224.1 4.5 %decode.1 = f32[1536,768]{1,0:T(8,128)} custom-call(s32[8]{0:T(128)S(1)} %stack.170.order, f32[1536,1]{1,0:T(8,128)S(1)} %fusion.3.scale, s16[192,768]{1,0:T(8,128)(2,1)S(1)} %copy-done.2, s16[192,768]{1,0:T(8,128)(2,1)S(1)} %collective-permute-done.21.side, s16[96,768]{1,0:T(8,128)(2,1)S(1)} %collective-permute-done.22.far1, ...), custom_call_target="tpu_custom_call" | custom-call | flops 1179648 | bytes 7077888 | tf_op jit(solution)/shard_map/decode/pallas_call | solution.py:251
  (172 shorter events, 52.0 us)
Async XLA Ops:
  0.6 24.3 %collective-permute-start = (bf16[192,768]{1,0:T(8,128)(2,1)}, bf16[192,768]{1,0:T(8,128)(2,1)}, u32[]{:S(2)}, u32[]{:S(2)}) collective-permute-start(bf16[192,768]{1,0:T(8,128)(2,1)} %refs_0_.1), channel_id=1, source_target_pairs={{0,2},{1,3},{2,0},{3,1},{4,6},{5,7},{6,4},{7,5},{8,10},{9,11},{10,... | collective-permute-start | bytes 884744 | tf_op jit(solution)/shard_map/ppermute | solution.py:21
  4.0 21.1 %collective-permute-start.1 = (bf16[192,768]{1,0:T(8,128)(2,1)}, bf16[192,768]{1,0:T(8,128)(2,1)}, u32[]{:S(2)}, u32[]{:S(2)}) collective-permute-start(bf16[192,768]{1,0:T(8,128)(2,1)} %refs_0_.1), channel_id=1, source_target_pairs={{0,1},{1,0},{2,3},{3,2},{4,5},{5,4},{6,7},{7,6},{8,9},{9,8},{10,11... | collective-permute-start | bytes 884744 | tf_op jit(solution)/shard_map/ppermute | solution.py:21
  4.0 24.0 %collective-permute-start.3 = (bf16[192,768]{1,0:T(8,128)(2,1)}, bf16[192,768]{1,0:T(8,128)(2,1)S(1)}, u32[]{:S(2)}, u32[]{:S(2)}) collective-permute-start(bf16[192,768]{1,0:T(8,128)(2,1)} %refs_0_.1), channel_id=1, source_target_pairs={{0,12},{1,13},{2,14},{3,15},{4,0},{5,1},{6,2},{7,3},{8,4},{9,5},{1... | collective-permute-start | bytes 884744 | tf_op jit(solution)/shard_map/ppermute | solution.py:21
  8.0 20.0 %collective-permute-start.4 = (bf16[192,768]{1,0:T(8,128)(2,1)}, bf16[192,768]{1,0:T(8,128)(2,1)S(1)}, u32[]{:S(2)}, u32[]{:S(2)}) collective-permute-start(bf16[192,768]{1,0:T(8,128)(2,1)} %refs_0_.1), channel_id=1, source_target_pairs={{0,4},{1,5},{2,6},{3,7},{4,8},{5,9},{6,10},{7,11},{8,12},{9,13},{1... | collective-permute-start | bytes 884744 | tf_op jit(solution)/shard_map/ppermute | solution.py:21
  8.0 28.4 %collective-permute-start.7 = (bf16[192,768]{1,0:T(8,128)(2,1)}, bf16[192,768]{1,0:T(8,128)(2,1)S(1)}, u32[]{:S(2)}, u32[]{:S(2)}) collective-permute-start(bf16[192,768]{1,0:T(8,128)(2,1)} %refs_0_.1), channel_id=1, source_target_pairs={{0,8},{1,9},{2,10},{3,11},{4,12},{5,13},{6,14},{7,15},{8,0},{9,1},... | collective-permute-start | bytes 884744 | tf_op jit(solution)/shard_map/ppermute | solution.py:21
  17.1 32.9 %all-to-all-start = ((bf16[128,3,896]{2,1,0:T(4,128)(2,1)}), bf16[128,3,896]{2,1,0:T(4,128)(2,1)}, u32[]{:S(2)}, u32[]{:S(2)}) async-start(bf16[128,3,896]{2,1,0:T(4,128)(2,1)} %reshape.378), calls=%async_computation | async-start | bytes 1835008 | tf_op jit(solution)/shard_map/all_to_all | solution.py:288
  25.1 18.2 %collective-permute-start.8 = (bf16[192,768]{1,0:T(8,128)(2,1)}, bf16[192,768]{1,0:T(8,128)(2,1)}, u32[]{:S(2)}, u32[]{:S(2)}) collective-permute-start(bf16[192,768]{1,0:T(8,128)(2,1)} %collective-permute-done.t1.refs_1_), channel_id=1, source_target_pairs={{0,12},{1,13},{2,14},{3,15},{4,0},{5,1},{6,2},{7,3},{8,4},{9,5},{1... | collective-permute-start | bytes 884744 | tf_op jit(solution)/shard_map/ppermute | solution.py:21
  28.0 10.8 %collective-permute-start.5 = (bf16[192,768]{1,0:T(8,128)(2,1)S(1)}, bf16[192,768]{1,0:T(8,128)(2,1)}, u32[]{:S(2)}, u32[]{:S(2)}) collective-permute-start(bf16[192,768]{1,0:T(8,128)(2,1)S(1)} %collective-permute-done.3.t0.refs_4_), channel_id=1, source_target_pairs={{0,1},{1,0},{2,3},{3,2},{4,5},{5,4},{6,7},{7,6},{8,9},{9,8},{10,11... | collective-permute-start | bytes 884744 | tf_op jit(solution)/shard_map/ppermute | solution.py:21
  28.1 15.2 %collective-permute-start.6 = (bf16[192,768]{1,0:T(8,128)(2,1)S(1)}, bf16[192,768]{1,0:T(8,128)(2,1)}, u32[]{:S(2)}, u32[]{:S(2)}) collective-permute-start(bf16[192,768]{1,0:T(8,128)(2,1)S(1)} %collective-permute-done.4.t1.refs_5_), channel_id=1, source_target_pairs={{0,1},{1,0},{2,3},{3,2},{4,5},{5,4},{6,7},{7,6},{8,9},{9,8},{10,11... | collective-permute-start | bytes 884744 | tf_op jit(solution)/shard_map/ppermute | solution.py:21
  28.7 38.4 %collective-permute-start.11 = (bf16[192,768]{1,0:T(8,128)(2,1)}, bf16[192,768]{1,0:T(8,128)(2,1)}, u32[]{:S(2)}, u32[]{:S(2)}) collective-permute-start(bf16[192,768]{1,0:T(8,128)(2,1)} %collective-permute-done.t1.refs_1_), channel_id=1, source_target_pairs={{0,4},{1,5},{2,6},{3,7},{4,8},{5,9},{6,10},{7,11},{8,12},{9,13},{1... | collective-permute-start | bytes 884744 | tf_op jit(solution)/shard_map/ppermute | solution.py:21
  36.5 30.7 %collective-permute-start.12 = (bf16[192,768]{1,0:T(8,128)(2,1)}, bf16[192,768]{1,0:T(8,128)(2,1)}, u32[]{:S(2)}, u32[]{:S(2)}) collective-permute-start(bf16[192,768]{1,0:T(8,128)(2,1)} %collective-permute-done.t1.refs_1_), channel_id=1, source_target_pairs={{0,8},{1,9},{2,10},{3,11},{4,12},{5,13},{6,14},{7,15},{8,0},{9,1},... | collective-permute-start | bytes 884744 | tf_op jit(solution)/shard_map/ppermute | solution.py:21
  38.9 33.5 %collective-permute-start.9 = (bf16[192,768]{1,0:T(8,128)(2,1)S(1)}, bf16[192,768]{1,0:T(8,128)(2,1)}, u32[]{:S(2)}, u32[]{:S(2)}) collective-permute-start(bf16[192,768]{1,0:T(8,128)(2,1)S(1)} %collective-permute-done.7.t0.refs_8_), channel_id=1, source_target_pairs={{0,1},{1,0},{2,3},{3,2},{4,5},{5,4},{6,7},{7,6},{8,9},{9,8},{10,11... | collective-permute-start | bytes 884744 | tf_op jit(solution)/shard_map/ppermute | solution.py:21
  43.3 29.0 %collective-permute-start.10 = (bf16[192,768]{1,0:T(8,128)(2,1)}, bf16[192,768]{1,0:T(8,128)(2,1)}, u32[]{:S(2)}, u32[]{:S(2)}) collective-permute-start(bf16[192,768]{1,0:T(8,128)(2,1)} %collective-permute-done.8.t1.refs_9_), channel_id=1, source_target_pairs={{0,1},{1,0},{2,3},{3,2},{4,5},{5,4},{6,7},{7,6},{8,9},{9,8},{10,11... | collective-permute-start | bytes 884744 | tf_op jit(solution)/shard_map/ppermute | solution.py:21
  56.3 29.0 %all-to-all-start.1 = ((bf16[128,3,768]{2,1,0:T(4,128)(2,1)}), bf16[128,3,768]{2,1,0:T(4,128)(2,1)}, u32[]{:S(2)}, u32[]{:S(2)}) async-start(bf16[128,3,768]{2,1,0:T(4,128)(2,1)} %reshape.380), calls=%async_computation.1 | async-start | bytes 1572864 | tf_op jit(solution)/shard_map/all_to_all | solution.py:332
  67.1 12.0 %collective-permute-start.13 = (bf16[192,768]{1,0:T(8,128)(2,1)}, bf16[192,768]{1,0:T(8,128)(2,1)S(1)}, u32[]{:S(2)}, u32[]{:S(2)}) collective-permute-start(bf16[192,768]{1,0:T(8,128)(2,1)} %collective-permute-done.11.t0.refs_12_), channel_id=1, source_target_pairs={{0,1},{1,0},{2,3},{3,2},{4,5},{5,4},{6,7},{7,6},{8,9},{9,8},{10,11... | collective-permute-start | bytes 884744 | tf_op jit(solution)/shard_map/ppermute | solution.py:21
  67.2 11.9 %collective-permute-start.14 = (bf16[192,768]{1,0:T(8,128)(2,1)}, bf16[192,768]{1,0:T(8,128)(2,1)S(1)}, u32[]{:S(2)}, u32[]{:S(2)}) collective-permute-start(bf16[192,768]{1,0:T(8,128)(2,1)} %collective-permute-done.12.t1.refs_13_), channel_id=1, source_target_pairs={{0,1},{1,0},{2,3},{3,2},{4,5},{5,4},{6,7},{7,6},{8,9},{9,8},{10,11... | collective-permute-start | bytes 884744 | tf_op jit(solution)/shard_map/ppermute | solution.py:21
  68.5 18.2 %collective-permute-start.15 = (bf16[192,768]{1,0:T(8,128)(2,1)}, bf16[192,768]{1,0:T(8,128)(2,1)}, u32[]{:S(2)}, u32[]{:S(2)}) collective-permute-start(bf16[192,768]{1,0:T(8,128)(2,1)} %refs_0_.1), channel_id=1, source_target_pairs={{0,0},{1,16},{2,32},{3,48},{4,64},{5,80},{6,96},{7,112},{8,1},{9,1... | collective-permute-start | bytes 884744 | tf_op jit(solution)/shard_map/ppermute | solution.py:334
  92.9 21.1 %all-to-all-start.2 = ((f32[8,8,1536]{2,1,0:T(8,128)}), f32[8,8,1536]{2,1,0:T(8,128)S(1)}, u32[]{:S(2)}, u32[]{:S(2)}) async-start(f32[8,8,1536]{2,1,0:T(8,128)} %broadcast_in_dim.127), calls=%async_computation.2 | async-start | bytes 786432 | tf_op jit(solution)/shard_map/all_to_all | solution.py:353
  133.9 9.8 %collective-permute-start.17 = (bf16[4,384,768]{2,1,0:T(8,128)(2,1)}, bf16[4,384,768]{2,1,0:T(8,128)(2,1)}, u32[]{:S(2)}, u32[]{:S(2)}) collective-permute-start(bf16[4,384,768]{2,1,0:T(8,128)(2,1)} %get-tuple-element.53), channel_id=1, source_target_pairs={{0,1},{1,0},{2,3},{3,2},{4,5},{5,4},{6,7},{7,6},{8,9},{9,8},{10,11... | collective-permute-start | bytes 7077896 | tf_op jit(solution)/shard_map/ppermute | solution.py:21
  135.6 39.7 %all-to-all-start.3 = ((bf16[8,192,768]{2,1,0:T(8,128)(2,1)}), bf16[8,192,768]{2,1,0:T(8,128)(2,1)S(1)}, u32[]{:S(2)}, u32[]{:S(2)}) async-start(bf16[8,192,768]{2,1,0:T(8,128)(2,1)} %bitcast.68), calls=%async_computation.3 | async-start | bytes 4718592 | tf_op jit(solution)/shard_map/all_to_all | solution.py:357
  147.5 36.3 %collective-permute-start.20 = (bf16[384,768]{1,0:T(8,128)(2,1)}, bf16[384,768]{1,0:T(8,128)(2,1)}, u32[]{:S(2)}, u32[]{:S(2)}) collective-permute-start(bf16[384,768]{1,0:T(8,128)(2,1)} %pad_maximum_fusion.2.refs_2_), channel_id=1, source_target_pairs={{0,8},{1,9},{2,10},{3,11},{4,12},{5,13},{6,14},{7,15},{8,0},{9,1},... | collective-permute-start | bytes 1769480 | tf_op jit(solution)/shard_map/ppermute | solution.py:21
  149.8 34.5 %collective-permute-start.19 = (bf16[384,768]{1,0:T(8,128)(2,1)}, bf16[384,768]{1,0:T(8,128)(2,1)}, u32[]{:S(2)}, u32[]{:S(2)}) collective-permute-start(bf16[384,768]{1,0:T(8,128)(2,1)} %pad_maximum_fusion.1.refs_1_), channel_id=1, source_target_pairs={{0,12},{1,13},{2,14},{3,15},{4,0},{5,1},{6,2},{7,3},{8,4},{9,5},{1... | collective-permute-start | bytes 1769480 | tf_op jit(solution)/shard_map/ppermute | solution.py:21
  151.7 33.4 %collective-permute-start.18 = (bf16[384,768]{1,0:T(8,128)(2,1)}, bf16[384,768]{1,0:T(8,128)(2,1)}, u32[]{:S(2)}, u32[]{:S(2)}) collective-permute-start(bf16[384,768]{1,0:T(8,128)(2,1)} %pad_maximum_fusion.refs_0_), channel_id=1, source_target_pairs={{0,4},{1,5},{2,6},{3,7},{4,8},{5,9},{6,10},{7,11},{8,12},{9,13},{1... | collective-permute-start | bytes 1769480 | tf_op jit(solution)/shard_map/ppermute | solution.py:21
  179.7 12.9 %collective-permute-start.21 = (s16[192,768]{1,0:T(8,128)(2,1)}, s16[192,768]{1,0:T(8,128)(2,1)S(1)}, u32[]{:S(2)}, u32[]{:S(2)}) collective-permute-start(s16[192,768]{1,0:T(8,128)(2,1)} %get-tuple-element.54.own), channel_id=1, source_target_pairs={{0,16},{16,0},{32,48},{48,32},{64,80},{80,64},{96,112},{112,96},{1... | collective-permute-start | bytes 884744 | tf_op jit(solution)/shard_map/ppermute | solution.py:25
  183.8 7.4 %collective-permute-start.23 = (s16[96,768]{1,0:T(8,128)(2,1)S(1)}, s16[96,768]{1,0:T(8,128)(2,1)S(1)}, u32[]{:S(2)}, u32[]{:S(2)}) collective-permute-start(s16[96,768]{1,0:T(8,128)(2,1)S(1)} %copy-done.21), channel_id=1, source_target_pairs={{0,64},{16,80},{32,96},{48,112},{64,0},{80,16},{96,32},{112,48},{1... | collective-permute-start | bytes 442376 | tf_op jit(solution)/shard_map/ppermute | solution.py:25
  184.3 8.3 %collective-permute-start.24 = (s16[96,768]{1,0:T(8,128)(2,1)S(1)}, s16[96,768]{1,0:T(8,128)(2,1)S(1)}, u32[]{:S(2)}, u32[]{:S(2)}) collective-permute-start(s16[96,768]{1,0:T(8,128)(2,1)S(1)} %copy-done.21), channel_id=1, source_target_pairs={{0,32},{16,48},{32,64},{48,80},{64,96},{80,112},{96,0},{112,16},{1... | collective-permute-start | bytes 442376 | tf_op jit(solution)/shard_map/ppermute | solution.py:25
  193.4 26.2 %collective-permute-start.25 = (s16[2,96,768]{2,1,0:T(8,128)(2,1)}, s16[2,96,768]{2,1,0:T(8,128)(2,1)S(1)}, u32[]{:S(2)}, u32[]{:S(2)}) collective-permute-start(s16[2,96,768]{2,1,0:T(8,128)(2,1)} %pad_add_fusion.1), channel_id=1, source_target_pairs={{0,96},{16,112},{32,0},{48,16},{64,32},{80,48},{96,64},{112,80},{1... | collective-permute-start | bytes 884744 | tf_op jit(solution)/shard_map/ppermute | solution.py:25
  194.0 25.6 %collective-permute-start.26 = (s16[2,96,768]{2,1,0:T(8,128)(2,1)}, s16[2,96,768]{2,1,0:T(8,128)(2,1)S(1)}, u32[]{:S(2)}, u32[]{:S(2)}) collective-permute-start(s16[2,96,768]{2,1,0:T(8,128)(2,1)} %pad_add_fusion.1), channel_id=1, source_target_pairs={{0,64},{16,80},{32,96},{48,112},{64,0},{80,16},{96,32},{112,48},{1... | collective-permute-start | bytes 884744 | tf_op jit(solution)/shard_map/ppermute | solution.py:25
  194.7 25.0 %collective-permute-start.27 = (s16[2,96,768]{2,1,0:T(8,128)(2,1)}, s16[2,96,768]{2,1,0:T(8,128)(2,1)S(1)}, u32[]{:S(2)}, u32[]{:S(2)}) collective-permute-start(s16[2,96,768]{2,1,0:T(8,128)(2,1)} %pad_add_fusion.1), channel_id=1, source_target_pairs={{0,32},{16,48},{32,64},{48,80},{64,96},{80,112},{96,0},{112,16},{1... | collective-permute-start | bytes 884744 | tf_op jit(solution)/shard_map/ppermute | solution.py:25
  196.2 15.7 %all-to-all-start.4 = ((f32[16,1,1536]{2,1,0:T(1,128)}), f32[16,1,1536]{2,1,0:T(1,128)S(1)}, u32[]{:S(2)}, u32[]{:S(2)}) async-start(f32[16,1,1536]{2,1,0:T(1,128)} %broadcast_in_dim.129), calls=%async_computation.4 | async-start | bytes 196608 | tf_op jit(solution)/shard_map/all_to_all | solution.py:430
  203.7 14.0 %collective-permute-start.29 = (bf16[192,768]{1,0:T(8,128)(2,1)}, bf16[192,768]{1,0:T(8,128)(2,1)}, u32[]{:S(2)}, u32[]{:S(2)}) collective-permute-start(bf16[192,768]{1,0:T(8,128)(2,1)} %get-tuple-element.62), channel_id=1, source_target_pairs={{0,2},{1,3},{2,0},{3,1},{4,6},{5,7},{6,4},{7,5},{8,10},{9,11},{10,... | collective-permute-start | bytes 884744 | tf_op jit(solution)/shard_map/ppermute | solution.py:21
  207.9 16.2 %collective-permute-start.28 = (s16[3,96,768]{2,1,0:T(8,128)(2,1)}, s16[3,96,768]{2,1,0:T(8,128)(2,1)S(1)}, u32[]{:S(2)}, u32[]{:S(2)}) collective-permute-start(s16[3,96,768]{2,1,0:T(8,128)(2,1)} %pad_add_fusion), channel_id=1, source_target_pairs={{0,16},{16,0},{32,48},{48,32},{64,80},{80,64},{96,112},{112,96},{1... | collective-permute-start | bytes 1327112 | tf_op jit(solution)/shard_map/ppermute | solution.py:25
  (26 other events, 262.8 us)

commit v6 on v4

--- a/solution.py
+++ b/solution.py
@@ -410,8 +410,9 @@
     )(source_parts, hard_rows, own_target, col, *leave)
     side = hop_grp(coded, 0, 1)
     far = [hop_grp(coded_high, -dx, 0) for dx in (1, 2, 3)]
-    other, side, far = lax.optimization_barrier((other, side, far))
-    hard_gate = hard_prob + 0.0 * side[0, 0].astype(F32)
+    contribution = (hard_prob[:, None] * own_source.astype(F32)).astype(BF)
+    outgoing = dot_f32(pick, contribution, ((0,), (0,))).astype(BF).reshape(owners, cap, width)
+    other, side, far, outgoing = lax.optimization_barrier((other, side, far, outgoing))
     target_grad = mine + hop_blk(other, 0, 1, 0).astype(F32)
     low = jnp.stack([coded[:half], side[:half]])
     pairs = [hop_grp(low, -dx, 0) for dx in (1, 2, 3)]
@@ -421,8 +422,6 @@
         blocks, (bound * (1.0 / 32767.0))[:, None], [coded, side, *far, *pairs, far_side]
     )
 
-    contribution = (hard_gate[:, None] * own_source.astype(F32)).astype(BF)
-    outgoing = dot_f32(pick, contribution, ((0,), (0,))).astype(BF).reshape(owners, cap, width)
     incoming = lax.all_to_all(outgoing, ("grp", "blk"), 0, 0, tiled=True).reshape(slots, width)
     pool_grad = dot_f32(serve, incoming, ((0,), (0,)))
     return (row_loss, source_grad, target_grad, pool_grad)

time: 226 us -> 226 us (level)
  waiting for transfers between devices: 37.7 us -> 40.5 us
    ppermute x21, waiting for transfers between devices: 0.55 us -> 11.8 us  [hop_blk(): return lax.ppermute(value, 'blk', route)]
    all_to_all x1, waiting for transfers between devices: 6.76 us -> 0.01 us  [shards(): lax.all_to_all(outgoing, ('grp', 'blk'), 0, 0, tiled=True)]
    unnamed x47 -> x43, local copies, waits for them, and re-layouts: 7.97 us -> 7.32 us
  transfers between devices with their start and end apart: 35 -> 35, of which waited for: 7 -> 7; matrix products, arithmetic and copies ran while one was open for 14% -> 13% of each run, Pallas kernels for 21% -> 21%
where the time goes in v6:
time: 226 us; the launch traced here: 224 us
  starting transfers between devices  70.5 us (31%)
  Pallas kernels  62.8 us (28%)
  waiting for transfers between devices  40.5 us (18%)
  local copies, waits for them, and re-layouts  23 us (10%)
  other arithmetic  18.4 us (8%)
  matrix products  7.76 us (3%)
    pallas_call x4, Pallas kernels, score_call(): pl.pallas_call(score_kernel, out_shape=(pltpu.HBM((4, total, cols), BF),...  24.3 us
    all_to_all x1, waiting for transfers between devices, shards(): lax.all_to_all(source_part.reshape(8, rows, width), 'grp', 0, 0, tiled=True)  23.9 us
    ppermute x21, starting transfers between devices, hop_blk(): return lax.ppermute(value, 'blk', route)  22.3 us
    pallas_call x1, Pallas kernels, target_call(): pl.pallas_call(target_kernel, out_shape=(jax.ShapeDtypeStruct(half, F32),...  15.4 us
    pallas_call x1, Pallas kernels, source_call(): pl.pallas_call(source_kernel, out_shape=jax.ShapeDtypeStruct((total, widt...  12.6 us
    ppermute x21, waiting for transfers between devices, hop_blk(): return lax.ppermute(value, 'blk', route)  11.8 us
    all_to_all x1, starting transfers between devices, shards(): lax.all_to_all(served, ('grp', 'blk'), 0, 0, tiled=True)  10.2 us
    all_to_all x1, starting transfers between devices, shards(): lax.all_to_all(jnp.broadcast_to(mine[None], (8, 8, total)), 'grp', 0, 0,...  9.65 us
  transfers between devices with their start and end apart: 35, of which 7 were waited for; matrix products, arithmetic and copies ran while one was open for 13% of the time, Pallas kernels for 21%

profile of v6, /device:TPU:0, one launch (start us, length us, event | category | flops | bytes accessed | tf_op | source)
XLA Modules:
  0.0 224.3 jit_solution(4589179207916479397)
XLA Ops:
  0.6 3.4 %collective-permute-start = (bf16[192,768]{1,0:T(8,128)(2,1)}, bf16[192,768]{1,0:T(8,128)(2,1)}, u32[]{:S(2)}, u32[]{:S(2)}) collective-permute-start(bf16[192,768]{1,0:T(8,128)(2,1)} %refs_0_.1), channel_id=1, source_target_pairs={{0,2},{1,3},{2,0},{3,1},{4,6},{5,7},{6,4},{7,5},{8,10},{9,11},{10,... | collective-permute-start | bytes 884744 | tf_op jit(solution)/shard_map/ppermute | solution.py:21
  4.0 3.9 %collective-permute-start.7 = (bf16[192,768]{1,0:T(8,128)(2,1)}, bf16[192,768]{1,0:T(8,128)(2,1)S(1)}, u32[]{:S(2)}, u32[]{:S(2)}) collective-permute-start(bf16[192,768]{1,0:T(8,128)(2,1)} %refs_0_.1), channel_id=1, source_target_pairs={{0,8},{1,9},{2,10},{3,11},{4,12},{5,13},{6,14},{7,15},{8,0},{9,1},... | collective-permute-start | bytes 884744 | tf_op jit(solution)/shard_map/ppermute | solution.py:21
  11.9 7.3 %all-to-all-start = ((s32[128,1,3]{2,1,0:T(1,128)}), s32[128,1,3]{2,1,0:T(1,128)}, u32[]{:S(2)}, u32[]{:S(2)}) async-start(s32[128,1,3]{2,1,0:T(1,128)} %bitcast), calls=%async_computation | async-start | bytes 131072 | tf_op jit(solution)/shard_map/all_to_all | solution.py:284
  22.6 2.8 %collective-permute-start.8 = (bf16[192,768]{1,0:T(8,128)(2,1)}, bf16[192,768]{1,0:T(8,128)(2,1)}, u32[]{:S(2)}, u32[]{:S(2)}) collective-permute-start(bf16[192,768]{1,0:T(8,128)(2,1)} %collective-permute-done.t1.refs_1_), channel_id=1, source_target_pairs={{0,12},{1,13},{2,14},{3,15},{4,0},{5,1},{6,2},{7,3},{8,4},{9,5},{1... | collective-permute-start | bytes 884744 | tf_op jit(solution)/shard_map/ppermute | solution.py:21
  26.9 1.7 copy-done.1
  28.5 6.0 %scores.4 = (bf16[4,1536,768]{2,1,0:T(8,128)(2,1)}, f32[8,1536]{1,0:T(8,128)S(1)}) custom-call(s32[4]{0:T(128)S(1)} %pad_add_fusion.2.place, bf16[1536,768]{1,0:T(8,128)(2,1)S(1)} %copy-done.1, bf16[192,768]{1,0:T(8,128)(2,1)} %refs_0_.1, bf16[192,768]{1,0:T(8,128)(2,1)} %collective-permute-done.t1.refs_1_, ...), custom_call_target="tpu_custom_call" | custom-call | flops 1811939328 | bytes 4718592 | tf_op jit(solution)/shard_map/scores/pallas_call | solution.py:83
  40.8 2.0 reshape.342
  42.8 10.2 %all-to-all-start.1 = ((bf16[128,3,768]{2,1,0:T(4,128)(2,1)}), bf16[128,3,768]{2,1,0:T(4,128)(2,1)}, u32[]{:S(2)}, u32[]{:S(2)}) async-start(bf16[128,3,768]{2,1,0:T(4,128)(2,1)} %reshape.342), calls=%async_computation.1 | async-start | bytes 1572864 | tf_op jit(solution)/shard_map/all_to_all | solution.py:322
  53.7 6.0 %scores.5 = (bf16[4,1536,768]{2,1,0:T(8,128)(2,1)}, f32[8,1536]{1,0:T(8,128)S(1)}) custom-call(s32[4]{0:T(128)S(1)} %pad_add_fusion.3.place, bf16[1536,768]{1,0:T(8,128)(2,1)S(1)} %copy-done.2, bf16[192,768]{1,0:T(8,128)(2,1)S(1)} %collective-permute-done.3.t0.refs_4_, ...), custom_call_target="tpu_custom_call", output_to_operand_aliasing={{0}: (6, {})} | custom-call | flops 1811939328 | bytes 4718592 | tf_op jit(solution)/shard_map/scores/pallas_call | solution.py:83
  59.7 1.6 collective-permute-start.15
  61.3 6.1 %scores.6 = (bf16[4,1536,768]{2,1,0:T(8,128)(2,1)}, f32[8,1536]{1,0:T(8,128)S(1)}) custom-call(s32[4]{0:T(128)S(1)} %pad_add_fusion.4.place, bf16[1536,768]{1,0:T(8,128)(2,1)S(1)} %copy-done.2, bf16[192,768]{1,0:T(8,128)(2,1)S(1)} %collective-permute-done.7.t0.refs_8_, ...), custom_call_target="tpu_custom_call", output_to_operand_aliasing={{0}: (6, {})} | custom-call | flops 1811939328 | bytes 4718592 | tf_op jit(solution)/shard_map/scores/pallas_call | solution.py:83
  67.5 6.1 %scores.7 = (bf16[4,1536,768]{2,1,0:T(8,128)(2,1)}, f32[8,1536]{1,0:T(8,128)S(1)}) custom-call(s32[4]{0:T(128)S(1)} %pad_add_fusion.5.place, bf16[1536,768]{1,0:T(8,128)(2,1)S(1)} %copy-done.2, bf16[192,768]{1,0:T(8,128)(2,1)} %collective-permute-done.11.t0.refs_12_, ...), custom_call_target="tpu_custom_call", output_to_operand_aliasing={{0}: (6, {})} | custom-call | flops 1811939328 | bytes 4718592 | tf_op jit(solution)/shard_map/scores/pallas_call | solution.py:83
  75.0 2.2 reshape.343
  77.3 3.0 %fusion.3 = (f32[192]{0:T(256)S(1)}, f32[192]{0:T(256)S(1)}, f32[]{:T(128)}, f32[192,768]{1,0:T(8,128)}) fusion(bf16[1536,768]{1,0:T(8,128)(2,1)S(1)} %copy-done.2, s32[]{:T(128)S(6)} %select_n.245, bf16[192,768]{1,0:T(8,128)(2,1)S(1)} %collective-permute-done.15.tgt, bf16[384,768]{1,0:T(8,128)(2,1)} %reshape.343, s32[192]{0:T(256)S(1)} %multiply_add_fusion), kind=kOutput, calls=%fused_computation.13 | convolution fusion | flops 114499200 | bytes 1771784 | tf_op jit(solution)/shard_map/dot_general | solution.py:29
  80.3 1.7 fusion.31
  84.0 9.7 %all-to-all-start.2 = ((f32[8,8,1536]{2,1,0:T(8,128)}), f32[8,8,1536]{2,1,0:T(8,128)S(1)}, u32[]{:S(2)}, u32[]{:S(2)}) async-start(f32[8,8,1536]{2,1,0:T(8,128)} %broadcast_in_dim.40), calls=%async_computation.2 | async-start | bytes 786432 | tf_op jit(solution)/shard_map/all_to_all | solution.py:345
  94.3 12.6 %source_terms.1 = bf16[1536,768]{1,0:T(8,128)(2,1)} custom-call(f32[8,1536]{1,0:T(8,128)} %concatenate.22.w_ref, bf16[4,1536,768]{2,1,0:T(8,128)(2,1)} %get-tuple-element.49.e_ref, bf16[192,768]{1,0:T(8,128)(2,1)} %refs_0_.1, bf16[192,768]{1,0:T(8,128)(2,1)} %collective-permute-done.t1.refs_1_, bf16[192,768]{1,0:T(8,128)(2,1)} %copy-done.11, ...), custom_call_target="tpu_custom_call" | custom-call | flops 7247757312 | bytes 11796480 | tf_op jit(solution)/shard_map/source_terms/pallas_call | solution.py:130
  110.8 15.4 %target_terms.1 = (f32[4,384,768]{2,1,0:T(8,128)}, bf16[4,384,768]{2,1,0:T(8,128)(2,1)}) custom-call(s32[16]{0:T(128)} %concatenate.24.place, f32[8,1536]{1,0:T(8,128)} %maximum_maximum_fusion.w_ref, bf16[4,1536,768]{2,1,0:T(8,128)(2,1)} %get-tuple-element.49.e_ref, bf16[1536,768]{1,0:T(8,128)(2,1)} %src_ref.1, bf16[16,128]{1,0:T(8,128)(2,1)} %copy-done.20), custom_call_target="tpu_custom_call" | custom-call | flops 7247757312 | bytes 18874368 | tf_op jit(solution)/shard_map/target_terms/pallas_call | solution.py:183
  126.5 4.4 %all-to-all-start.3 = ((bf16[8,192,768]{2,1,0:T(8,128)(2,1)}), bf16[8,192,768]{2,1,0:T(8,128)(2,1)S(1)}, u32[]{:S(2)}, u32[]{:S(2)}) async-start(bf16[8,192,768]{2,1,0:T(8,128)(2,1)} %bitcast.68), calls=%async_computation.3 | async-start | bytes 4718592 | tf_op jit(solution)/shard_map/all_to_all | solution.py:349
  131.4 2.9 %fusion.10 = (bf16[192,768]{1,0:T(8,128)(2,1)S(1)}, bf16[192,768]{1,0:T(8,128)(2,1)S(1)}, bf16[192,768]{1,0:T(8,128)(2,1)S(1)}, bf16[192,768]{1,0:T(8,128)(2,1)S...) fusion(f32[4,384,768]{2,1,0:T(8,128)} %get-tuple-element.52.keep, ...), kind=kLoop, calls=%fused_computation.33 | loop fusion | flops 2654208 | bytes 7077888 | tf_op jit(solution)/shard_map/convert_element_type | solution.py:380
  136.8 2.4 %collective-permute-start.19 = (bf16[384,768]{1,0:T(8,128)(2,1)}, bf16[384,768]{1,0:T(8,128)(2,1)}, u32[]{:S(2)}, u32[]{:S(2)}) collective-permute-start(bf16[384,768]{1,0:T(8,128)(2,1)} %pad_maximum_fusion.1._b), channel_id=1, source_target_pairs={{0,12},{1,13},{2,14},{3,15},{4,0},{5,1},{6,2},{7,3},{8,4},{9,5},{1... | collective-permute-start | bytes 1769480 | tf_op jit(solution)/shard_map/ppermute | solution.py:21
  140.1 2.3 %convolution_convert_fusion = bf16[384,768]{1,0:T(8,128)(2,1)} fusion(f32[192]{0:T(256)S(1)} %slice_reduce_fusion, bf16[1536,768]{1,0:T(8,128)(2,1)} %src_ref.1, s32[]{:T(128)S(6)} %select_n.245, s32[192]{0:T(256)S(1)} %multiply_add_fusion), kind=kOutput, calls=%fused_computation | convolution fusion | flops 114057216 | bytes 886276 | tf_op jit(solution)/shard_map/dot_general | solution.py:29
  142.4 23.9 %all-to-all-done.3.parts = bf16[8,192,768]{2,1,0:T(8,128)(2,1)S(1)} async-done(((bf16[8,192,768]{2,1,0:T(8,128)(2,1)}), bf16[8,192,768]{2,1,0:T(8,128)(2,1)S(1)}, u32[]{:S(2)}, u32[]{:S(2)}) %all-to-all-start.3) | async-done | bytes 2359328 | tf_op jit(solution)/shard_map/all_to_all | solution.py:349
  167.7 3.0 %code.1 = (s16[192,768]{1,0:T(8,128)(2,1)}, s16[96,768]{1,0:T(8,128)(2,1)}) custom-call(bf16[8,192,768]{2,1,0:T(8,128)(2,1)} %copy-done.13, f32[192,768]{1,0:T(8,128)} %get-tuple-element.99.hard, bf16[192,768]{1,0:T(8,128)(2,1)} %copy-done.15, f32[192,11]{1,0:T(8,128)} %bitcast.69, bf16[384,768]{1,0:T(8,128)(2,1)} %pad_maximum_fusion._a, ...), custom_call_target="tpu_custom_call" | custom-call | flops 1474560 | bytes 3244032 | tf_op jit(solution)/shard_map/code/pallas_call | solution.py:396
  177.7 3.0 %lines.1 = (f32[192,768]{1,0:T(8,128)}, bf16[192,768]{1,0:T(8,128)(2,1)}) custom-call(f32[4,384,768]{2,1,0:T(8,128)} %get-tuple-element.52.keep, bf16[4,384,768]{2,1,0:T(8,128)(2,1)} %collective-permute-done.17.got, bf16[384,768]{1,0:T(8,128)(2,1)} %collective-permute-done.18.m1, bf16[384,768]{1,0:T(8,128)(2,1)} %collective-permute-done.19.m2, ...), custom_call_target="tpu_custom_call" | custom-call | flops 1474560 | bytes 4423680 | tf_op jit(solution)/shard_map/lines/pallas_call | solution.py:386
  181.8 2.2 collective-permute-done.23.far2
  190.0 2.7 %collective-permute-start.29 = (bf16[192,768]{1,0:T(8,128)(2,1)}, bf16[192,768]{1,0:T(8,128)(2,1)}, u32[]{:S(2)}, u32[]{:S(2)}) collective-permute-start(bf16[192,768]{1,0:T(8,128)(2,1)} %get-tuple-element.62), channel_id=1, source_target_pairs={{0,2},{1,3},{2,0},{3,1},{4,6},{5,7},{6,4},{7,5},{8,10},{9,11},{10,... | collective-permute-start | bytes 884744 | tf_op jit(solution)/shard_map/ppermute | solution.py:21
  192.8 8.8 %all-to-all-start.4 = ((bf16[128,3,768]{2,1,0:T(4,128)(2,1)}), bf16[128,3,768]{2,1,0:T(4,128)(2,1)}, u32[]{:S(2)}, u32[]{:S(2)}) async-start(bf16[128,3,768]{2,1,0:T(4,128)(2,1)} %reshape.345), calls=%async_computation.4 | async-start | bytes 1572864 | tf_op jit(solution)/shard_map/all_to_all | solution.py:425
  201.6 2.4 %fusion.1.scale = f32[1536,1]{1,0:T(8,128)S(1)} fusion(f32[1536]{0:T(1024)S(1)} %get-tuple-element.100, f32[1536,1]{1,0:T(8,128)S(1)} %copy.66, f32[1536]{0:T(1024)S(1)} %fusion.21, f32[1536,1]{1,0:T(8,128)} %copy.63, f32[1536,1]{1,0:T(8,128)} %copy.62, f32[1536]{0:T(1024)S(1)} %slice_reduce_fusion.4), kind=kLoop, calls=%fused_computation.9 | loop fusion | flops 23040 | bytes 43008 | tf_op jit(solution)/shard_map/mul | solution.py:422
  203.9 11.2 %collective-permute-done.29 = bf16[192,768]{1,0:T(8,128)(2,1)} collective-permute-done((bf16[192,768]{1,0:T(8,128)(2,1)}, bf16[192,768]{1,0:T(8,128)(2,1)}, u32[]{:S(2)}, u32[]{:S(2)}) %collective-permute-start.29) | collective-permute-done | bytes 294944 | tf_op jit(solution)/shard_map/ppermute | solution.py:21
  215.1 1.8 convert_add_fusion
  217.0 4.5 %decode.1 = f32[1536,768]{1,0:T(8,128)} custom-call(s32[8]{0:T(128)S(1)} %stack.170.order, f32[1536,1]{1,0:T(8,128)S(1)} %fusion.1.scale, s16[192,768]{1,0:T(8,128)(2,1)S(1)} %copy-done.3, s16[192,768]{1,0:T(8,128)(2,1)S(1)} %collective-permute-done.21.side, s16[96,768]{1,0:T(8,128)(2,1)S(1)} %collective-permute-done.22.far1, ...), custom_call_target="tpu_custom_call" | custom-call | flops 1179648 | bytes 7077888 | tf_op jit(solution)/shard_map/decode/pallas_call | solution.py:250
  (157 shorter events, 45.7 us)
Async XLA Ops:
  0.6 20.2 %collective-permute-start = (bf16[192,768]{1,0:T(8,128)(2,1)}, bf16[192,768]{1,0:T(8,128)(2,1)}, u32[]{:S(2)}, u32[]{:S(2)}) collective-permute-start(bf16[192,768]{1,0:T(8,128)(2,1)} %refs_0_.1), channel_id=1, source_target_pairs={{0,2},{1,3},{2,0},{3,1},{4,6},{5,7},{6,4},{7,5},{8,10},{9,11},{10,... | collective-permute-start | bytes 884744 | tf_op jit(solution)/shard_map/ppermute | solution.py:21
  4.0 33.8 %collective-permute-start.7 = (bf16[192,768]{1,0:T(8,128)(2,1)}, bf16[192,768]{1,0:T(8,128)(2,1)S(1)}, u32[]{:S(2)}, u32[]{:S(2)}) collective-permute-start(bf16[192,768]{1,0:T(8,128)(2,1)} %refs_0_.1), channel_id=1, source_target_pairs={{0,8},{1,9},{2,10},{3,11},{4,12},{5,13},{6,14},{7,15},{8,0},{9,1},... | collective-permute-start | bytes 884744 | tf_op jit(solution)/shard_map/ppermute | solution.py:21
  7.9 13.2 %collective-permute-start.1 = (bf16[192,768]{1,0:T(8,128)(2,1)}, bf16[192,768]{1,0:T(8,128)(2,1)S(1)}, u32[]{:S(2)}, u32[]{:S(2)}) collective-permute-start(bf16[192,768]{1,0:T(8,128)(2,1)} %refs_0_.1), channel_id=1, source_target_pairs={{0,1},{1,0},{2,3},{3,2},{4,5},{5,4},{6,7},{7,6},{8,9},{9,8},{10,11... | collective-permute-start | bytes 884744 | tf_op jit(solution)/shard_map/ppermute | solution.py:21
  7.9 30.7 %collective-permute-start.3 = (bf16[192,768]{1,0:T(8,128)(2,1)}, bf16[192,768]{1,0:T(8,128)(2,1)S(1)}, u32[]{:S(2)}, u32[]{:S(2)}) collective-permute-start(bf16[192,768]{1,0:T(8,128)(2,1)} %refs_0_.1), channel_id=1, source_target_pairs={{0,12},{1,13},{2,14},{3,15},{4,0},{5,1},{6,2},{7,3},{8,4},{9,5},{1... | collective-permute-start | bytes 884744 | tf_op jit(solution)/shard_map/ppermute | solution.py:21
  8.6 30.0 %collective-permute-start.4 = (bf16[192,768]{1,0:T(8,128)(2,1)}, bf16[192,768]{1,0:T(8,128)(2,1)S(1)}, u32[]{:S(2)}, u32[]{:S(2)}) collective-permute-start(bf16[192,768]{1,0:T(8,128)(2,1)} %refs_0_.1), channel_id=1, source_target_pairs={{0,4},{1,5},{2,6},{3,7},{4,8},{5,9},{6,10},{7,11},{8,12},{9,13},{1... | collective-permute-start | bytes 884744 | tf_op jit(solution)/shard_map/ppermute | solution.py:21
  11.9 24.7 %all-to-all-start = ((s32[128,1,3]{2,1,0:T(1,128)}), s32[128,1,3]{2,1,0:T(1,128)}, u32[]{:S(2)}, u32[]{:S(2)}) async-start(s32[128,1,3]{2,1,0:T(1,128)} %bitcast), calls=%async_computation | async-start | bytes 131072 | tf_op jit(solution)/shard_map/all_to_all | solution.py:284
  21.0 18.1 %collective-permute-start.11 = (bf16[192,768]{1,0:T(8,128)(2,1)}, bf16[192,768]{1,0:T(8,128)(2,1)}, u32[]{:S(2)}, u32[]{:S(2)}) collective-permute-start(bf16[192,768]{1,0:T(8,128)(2,1)} %collective-permute-done.t1.refs_1_), channel_id=1, source_target_pairs={{0,4},{1,5},{2,6},{3,7},{4,8},{5,9},{6,10},{7,11},{8,12},{9,13},{1... | collective-permute-start | bytes 884744 | tf_op jit(solution)/shard_map/ppermute | solution.py:21
  22.6 16.6 %collective-permute-start.8 = (bf16[192,768]{1,0:T(8,128)(2,1)}, bf16[192,768]{1,0:T(8,128)(2,1)}, u32[]{:S(2)}, u32[]{:S(2)}) collective-permute-start(bf16[192,768]{1,0:T(8,128)(2,1)} %collective-permute-done.t1.refs_1_), channel_id=1, source_target_pairs={{0,12},{1,13},{2,14},{3,15},{4,0},{5,1},{6,2},{7,3},{8,4},{9,5},{1... | collective-permute-start | bytes 884744 | tf_op jit(solution)/shard_map/ppermute | solution.py:21
  37.8 15.3 %collective-permute-start.12 = (bf16[192,768]{1,0:T(8,128)(2,1)}, bf16[192,768]{1,0:T(8,128)(2,1)}, u32[]{:S(2)}, u32[]{:S(2)}) collective-permute-start(bf16[192,768]{1,0:T(8,128)(2,1)} %collective-permute-done.t1.refs_1_), channel_id=1, source_target_pairs={{0,8},{1,9},{2,10},{3,11},{4,12},{5,13},{6,14},{7,15},{8,0},{9,1},... | collective-permute-start | bytes 884744 | tf_op jit(solution)/shard_map/ppermute | solution.py:21
  38.6 22.7 %collective-permute-start.9 = (bf16[192,768]{1,0:T(8,128)(2,1)S(1)}, bf16[192,768]{1,0:T(8,128)(2,1)}, u32[]{:S(2)}, u32[]{:S(2)}) collective-permute-start(bf16[192,768]{1,0:T(8,128)(2,1)S(1)} %collective-permute-done.7.t0.refs_8_), channel_id=1, source_target_pairs={{0,1},{1,0},{2,3},{3,2},{4,5},{5,4},{6,7},{7,6},{8,9},{9,8},{10,11... | collective-permute-start | bytes 884744 | tf_op jit(solution)/shard_map/ppermute | solution.py:21
  38.6 14.6 %collective-permute-start.5 = (bf16[192,768]{1,0:T(8,128)(2,1)S(1)}, bf16[192,768]{1,0:T(8,128)(2,1)}, u32[]{:S(2)}, u32[]{:S(2)}) collective-permute-start(bf16[192,768]{1,0:T(8,128)(2,1)S(1)} %collective-permute-done.3.t0.refs_4_), channel_id=1, source_target_pairs={{0,1},{1,0},{2,3},{3,2},{4,5},{5,4},{6,7},{7,6},{8,9},{9,8},{10,11... | collective-permute-start | bytes 884744 | tf_op jit(solution)/shard_map/ppermute | solution.py:21
  39.1 14.6 %collective-permute-start.6 = (bf16[192,768]{1,0:T(8,128)(2,1)S(1)}, bf16[192,768]{1,0:T(8,128)(2,1)}, u32[]{:S(2)}, u32[]{:S(2)}) collective-permute-start(bf16[192,768]{1,0:T(8,128)(2,1)S(1)} %collective-permute-done.4.t1.refs_5_), channel_id=1, source_target_pairs={{0,1},{1,0},{2,3},{3,2},{4,5},{5,4},{6,7},{7,6},{8,9},{9,8},{10,11... | collective-permute-start | bytes 884744 | tf_op jit(solution)/shard_map/ppermute | solution.py:21
  39.2 22.1 %collective-permute-start.10 = (bf16[192,768]{1,0:T(8,128)(2,1)}, bf16[192,768]{1,0:T(8,128)(2,1)}, u32[]{:S(2)}, u32[]{:S(2)}) collective-permute-start(bf16[192,768]{1,0:T(8,128)(2,1)} %collective-permute-done.8.t1.refs_9_), channel_id=1, source_target_pairs={{0,1},{1,0},{2,3},{3,2},{4,5},{5,4},{6,7},{7,6},{8,9},{9,8},{10,11... | collective-permute-start | bytes 884744 | tf_op jit(solution)/shard_map/ppermute | solution.py:21
  42.8 32.2 %all-to-all-start.1 = ((bf16[128,3,768]{2,1,0:T(4,128)(2,1)}), bf16[128,3,768]{2,1,0:T(4,128)(2,1)}, u32[]{:S(2)}, u32[]{:S(2)}) async-start(bf16[128,3,768]{2,1,0:T(4,128)(2,1)} %reshape.342), calls=%async_computation.1 | async-start | bytes 1572864 | tf_op jit(solution)/shard_map/all_to_all | solution.py:322
  53.1 14.3 %collective-permute-start.13 = (bf16[192,768]{1,0:T(8,128)(2,1)}, bf16[192,768]{1,0:T(8,128)(2,1)S(1)}, u32[]{:S(2)}, u32[]{:S(2)}) collective-permute-start(bf16[192,768]{1,0:T(8,128)(2,1)} %collective-permute-done.11.t0.refs_12_), channel_id=1, source_target_pairs={{0,1},{1,0},{2,3},{3,2},{4,5},{5,4},{6,7},{7,6},{8,9},{9,8},{10,11... | collective-permute-start | bytes 884744 | tf_op jit(solution)/shard_map/ppermute | solution.py:21
  53.2 14.3 %collective-permute-start.14 = (bf16[192,768]{1,0:T(8,128)(2,1)}, bf16[192,768]{1,0:T(8,128)(2,1)S(1)}, u32[]{:S(2)}, u32[]{:S(2)}) collective-permute-start(bf16[192,768]{1,0:T(8,128)(2,1)} %collective-permute-done.12.t1.refs_13_), channel_id=1, source_target_pairs={{0,1},{1,0},{2,3},{3,2},{4,5},{5,4},{6,7},{7,6},{8,9},{9,8},{10,11... | collective-permute-start | bytes 884744 | tf_op jit(solution)/shard_map/ppermute | solution.py:21
  59.7 17.5 %collective-permute-start.15 = (bf16[192,768]{1,0:T(8,128)(2,1)}, bf16[192,768]{1,0:T(8,128)(2,1)S(1)}, u32[]{:S(2)}, u32[]{:S(2)}) collective-permute-start(bf16[192,768]{1,0:T(8,128)(2,1)} %refs_0_.1), channel_id=1, source_target_pairs={{0,0},{1,16},{2,32},{3,48},{4,64},{5,80},{6,96},{7,112},{8,1},{9,1... | collective-permute-start | bytes 884744 | tf_op jit(solution)/shard_map/ppermute | solution.py:325
  84.0 22.9 %all-to-all-start.2 = ((f32[8,8,1536]{2,1,0:T(8,128)}), f32[8,8,1536]{2,1,0:T(8,128)S(1)}, u32[]{:S(2)}, u32[]{:S(2)}) async-start(f32[8,8,1536]{2,1,0:T(8,128)} %broadcast_in_dim.40), calls=%async_computation.2 | async-start | bytes 786432 | tf_op jit(solution)/shard_map/all_to_all | solution.py:345
  126.5 39.8 %all-to-all-start.3 = ((bf16[8,192,768]{2,1,0:T(8,128)(2,1)}), bf16[8,192,768]{2,1,0:T(8,128)(2,1)S(1)}, u32[]{:S(2)}, u32[]{:S(2)}) async-start(bf16[8,192,768]{2,1,0:T(8,128)(2,1)} %bitcast.68), calls=%async_computation.3 | async-start | bytes 4718592 | tf_op jit(solution)/shard_map/all_to_all | solution.py:349
  135.2 41.2 %collective-permute-start.18 = (bf16[384,768]{1,0:T(8,128)(2,1)}, bf16[384,768]{1,0:T(8,128)(2,1)}, u32[]{:S(2)}, u32[]{:S(2)}) collective-permute-start(bf16[384,768]{1,0:T(8,128)(2,1)} %pad_maximum_fusion._a), channel_id=1, source_target_pairs={{0,4},{1,5},{2,6},{3,7},{4,8},{5,9},{6,10},{7,11},{8,12},{9,13},{1... | collective-permute-start | bytes 1769480 | tf_op jit(solution)/shard_map/ppermute | solution.py:21
  136.8 40.2 %collective-permute-start.19 = (bf16[384,768]{1,0:T(8,128)(2,1)}, bf16[384,768]{1,0:T(8,128)(2,1)}, u32[]{:S(2)}, u32[]{:S(2)}) collective-permute-start(bf16[384,768]{1,0:T(8,128)(2,1)} %pad_maximum_fusion.1._b), channel_id=1, source_target_pairs={{0,12},{1,13},{2,14},{3,15},{4,0},{5,1},{6,2},{7,3},{8,4},{9,5},{1... | collective-permute-start | bytes 1769480 | tf_op jit(solution)/shard_map/ppermute | solution.py:21
  140.1 37.6 %collective-permute-start.20 = (bf16[384,768]{1,0:T(8,128)(2,1)}, bf16[384,768]{1,0:T(8,128)(2,1)}, u32[]{:S(2)}, u32[]{:S(2)}) collective-permute-start(bf16[384,768]{1,0:T(8,128)(2,1)} %pad_maximum_fusion.2._c), channel_id=1, source_target_pairs={{0,8},{1,9},{2,10},{3,11},{4,12},{5,13},{6,14},{7,15},{8,0},{9,1},... | collective-permute-start | bytes 1769480 | tf_op jit(solution)/shard_map/ppermute | solution.py:21
  170.8 14.7 %collective-permute-start.21 = (s16[192,768]{1,0:T(8,128)(2,1)}, s16[192,768]{1,0:T(8,128)(2,1)S(1)}, u32[]{:S(2)}, u32[]{:S(2)}) collective-permute-start(s16[192,768]{1,0:T(8,128)(2,1)} %get-tuple-element.54.own), channel_id=1, source_target_pairs={{0,16},{16,0},{32,48},{48,32},{64,80},{80,64},{96,112},{112,96},{1... | collective-permute-start | bytes 884744 | tf_op jit(solution)/shard_map/ppermute | solution.py:25
  175.6 6.2 %collective-permute-start.22 = (s16[96,768]{1,0:T(8,128)(2,1)S(1)}, s16[96,768]{1,0:T(8,128)(2,1)S(1)}, u32[]{:S(2)}, u32[]{:S(2)}) collective-permute-start(s16[96,768]{1,0:T(8,128)(2,1)S(1)} %copy-done.19), channel_id=1, source_target_pairs={{0,96},{16,112},{32,0},{48,16},{64,32},{80,48},{96,64},{112,80},{1... | collective-permute-start | bytes 442376 | tf_op jit(solution)/shard_map/ppermute | solution.py:25
  176.4 7.6 %collective-permute-start.23 = (s16[96,768]{1,0:T(8,128)(2,1)S(1)}, s16[96,768]{1,0:T(8,128)(2,1)S(1)}, u32[]{:S(2)}, u32[]{:S(2)}) collective-permute-start(s16[96,768]{1,0:T(8,128)(2,1)S(1)} %copy-done.19), channel_id=1, source_target_pairs={{0,64},{16,80},{32,96},{48,112},{64,0},{80,16},{96,32},{112,48},{1... | collective-permute-start | bytes 442376 | tf_op jit(solution)/shard_map/ppermute | solution.py:25
  177.0 8.5 %collective-permute-start.24 = (s16[96,768]{1,0:T(8,128)(2,1)S(1)}, s16[96,768]{1,0:T(8,128)(2,1)S(1)}, u32[]{:S(2)}, u32[]{:S(2)}) collective-permute-start(s16[96,768]{1,0:T(8,128)(2,1)S(1)} %copy-done.19), channel_id=1, source_target_pairs={{0,32},{16,48},{32,64},{48,80},{64,96},{80,112},{96,0},{112,16},{1... | collective-permute-start | bytes 442376 | tf_op jit(solution)/shard_map/ppermute | solution.py:25
  186.3 30.7 %collective-permute-start.25 = (s16[2,96,768]{2,1,0:T(8,128)(2,1)}, s16[2,96,768]{2,1,0:T(8,128)(2,1)S(1)}, u32[]{:S(2)}, u32[]{:S(2)}) collective-permute-start(s16[2,96,768]{2,1,0:T(8,128)(2,1)} %pad_add_fusion.1), channel_id=1, source_target_pairs={{0,96},{16,112},{32,0},{48,16},{64,32},{80,48},{96,64},{112,80},{1... | collective-permute-start | bytes 884744 | tf_op jit(solution)/shard_map/ppermute | solution.py:25
  186.8 30.1 %collective-permute-start.26 = (s16[2,96,768]{2,1,0:T(8,128)(2,1)}, s16[2,96,768]{2,1,0:T(8,128)(2,1)S(1)}, u32[]{:S(2)}, u32[]{:S(2)}) collective-permute-start(s16[2,96,768]{2,1,0:T(8,128)(2,1)} %pad_add_fusion.1), channel_id=1, source_target_pairs={{0,64},{16,80},{32,96},{48,112},{64,0},{80,16},{96,32},{112,48},{1... | collective-permute-start | bytes 884744 | tf_op jit(solution)/shard_map/ppermute | solution.py:25
  187.4 29.5 %collective-permute-start.27 = (s16[2,96,768]{2,1,0:T(8,128)(2,1)}, s16[2,96,768]{2,1,0:T(8,128)(2,1)S(1)}, u32[]{:S(2)}, u32[]{:S(2)}) collective-permute-start(s16[2,96,768]{2,1,0:T(8,128)(2,1)} %pad_add_fusion.1), channel_id=1, source_target_pairs={{0,32},{16,48},{32,64},{48,80},{64,96},{80,112},{96,0},{112,16},{1... | collective-permute-start | bytes 884744 | tf_op jit(solution)/shard_map/ppermute | solution.py:25
  189.1 27.9 %collective-permute-start.28 = (s16[3,96,768]{2,1,0:T(8,128)(2,1)}, s16[3,96,768]{2,1,0:T(8,128)(2,1)S(1)}, u32[]{:S(2)}, u32[]{:S(2)}) collective-permute-start(s16[3,96,768]{2,1,0:T(8,128)(2,1)} %pad_add_fusion), channel_id=1, source_target_pairs={{0,16},{16,0},{32,48},{48,32},{64,80},{80,64},{96,112},{112,96},{1... | collective-permute-start | bytes 1327112 | tf_op jit(solution)/shard_map/ppermute | solution.py:25
  190.0 25.1 %collective-permute-start.29 = (bf16[192,768]{1,0:T(8,128)(2,1)}, bf16[192,768]{1,0:T(8,128)(2,1)}, u32[]{:S(2)}, u32[]{:S(2)}) collective-permute-start(bf16[192,768]{1,0:T(8,128)(2,1)} %get-tuple-element.62), channel_id=1, source_target_pairs={{0,2},{1,3},{2,0},{3,1},{4,6},{5,7},{6,4},{7,5},{8,10},{9,11},{10,... | collective-permute-start | bytes 884744 | tf_op jit(solution)/shard_map/ppermute | solution.py:21
  192.8 28.8 %all-to-all-start.4 = ((bf16[128,3,768]{2,1,0:T(4,128)(2,1)}), bf16[128,3,768]{2,1,0:T(4,128)(2,1)}, u32[]{:S(2)}, u32[]{:S(2)}) async-start(bf16[128,3,768]{2,1,0:T(4,128)(2,1)} %reshape.345), calls=%async_computation.4 | async-start | bytes 1572864 | tf_op jit(solution)/shard_map/all_to_all | solution.py:425
  (24 other events, 221.9 us)

commit v7 on v6

--- a/solution.py
+++ b/solution.py
@@ -412,8 +412,8 @@
     far = [hop_grp(coded_high, -dx, 0) for dx in (1, 2, 3)]
     contribution = (hard_prob[:, None] * own_source.astype(F32)).astype(BF)
     outgoing = dot_f32(pick, contribution, ((0,), (0,))).astype(BF).reshape(owners, cap, width)
-    other, side, far, outgoing = lax.optimization_barrier((other, side, far, outgoing))
-    target_grad = mine + hop_blk(other, 0, 1, 0).astype(F32)
+    line_far = hop_blk(other, 0, 1, 0)
+    mine, side, far, outgoing = lax.optimization_barrier((mine, side, far, outgoing))
     low = jnp.stack([coded[:half], side[:half]])
     pairs = [hop_grp(low, -dx, 0) for dx in (1, 2, 3)]
     far_side = hop_grp(jnp.stack(far), 0, 1)
@@ -422,6 +422,9 @@
         blocks, (bound * (1.0 / 32767.0))[:, None], [coded, side, *far, *pairs, far_side]
     )
 
+    line_far, source_grad = lax.optimization_barrier((line_far, source_grad))
+    target_grad = mine + line_far.astype(F32)
+
     incoming = lax.all_to_all(outgoing, ("grp", "blk"), 0, 0, tiled=True).reshape(slots, width)
     pool_grad = dot_f32(serve, incoming, ((0,), (0,)))
     return (row_loss, source_grad, target_grad, pool_grad)

time: 226 us -> 225 us (level)
  waiting for transfers between devices: 40.5 us -> 38.2 us
    ppermute x21, waiting for transfers between devices: 11.8 us -> 0.55 us  [hop_blk(): return lax.ppermute(value, 'blk', route)]
    ppermute x8, waiting for transfers between devices: 4.8 us -> 13.7 us  [hop_grp(): lax.ppermute(value, 'grp', [(i, (i // 2 + dx) % 4 * 2 + (i % 2 ^ dy)) for...]
where the time goes in v7:
time: 225 us; the launch traced here: 222 us
  starting transfers between devices  71 us (32%)
  Pallas kernels  62.8 us (28%)
  waiting for transfers between devices  38.2 us (17%)
  local copies, waits for them, and re-layouts  22.9 us (10%)
  other arithmetic  18.4 us (8%)
  matrix products  7.77 us (3%)
    pallas_call x4, Pallas kernels, score_call(): pl.pallas_call(score_kernel, out_shape=(pltpu.HBM((4, total, cols), BF),...  24.3 us
    all_to_all x1, waiting for transfers between devices, shards(): lax.all_to_all(source_part.reshape(8, rows, width), 'grp', 0, 0, tiled=True)  23.9 us
    ppermute x21, starting transfers between devices, hop_blk(): return lax.ppermute(value, 'blk', route)  22.3 us
    pallas_call x1, Pallas kernels, target_call(): pl.pallas_call(target_kernel, out_shape=(jax.ShapeDtypeStruct(half, F32),...  15.4 us
    ppermute x8, waiting for transfers between devices, hop_grp(): lax.ppermute(value, 'grp', [(i, (i // 2 + dx) % 4 * 2 + (i % 2 ^ dy)) for...  13.7 us
    pallas_call x1, Pallas kernels, source_call(): pl.pallas_call(source_kernel, out_shape=jax.ShapeDtypeStruct((total, widt...  12.6 us
    all_to_all x1, starting transfers between devices, shards(): lax.all_to_all(served, ('grp', 'blk'), 0, 0, tiled=True)  10.2 us
    all_to_all x1, starting transfers between devices, shards(): lax.all_to_all(outgoing, ('grp', 'blk'), 0, 0, tiled=True)  9.98 us
  transfers between devices with their start and end apart: 35, of which 7 were waited for; matrix products, arithmetic and copies ran while one was open for 13% of the time, Pallas kernels for 21%

profile of v7, /device:TPU:0, one launch (start us, length us, event | category | flops | bytes accessed | tf_op | source)
XLA Modules:
  0.0 222.5 jit_solution(5960159921764249723)
XLA Ops:
  0.6 3.4 %collective-permute-start = (bf16[192,768]{1,0:T(8,128)(2,1)}, bf16[192,768]{1,0:T(8,128)(2,1)}, u32[]{:S(2)}, u32[]{:S(2)}) collective-permute-start(bf16[192,768]{1,0:T(8,128)(2,1)} %refs_0_.1), channel_id=1, source_target_pairs={{0,2},{1,3},{2,0},{3,1},{4,6},{5,7},{6,4},{7,5},{8,10},{9,11},{10,... | collective-permute-start | bytes 884744 | tf_op jit(solution)/shard_map/ppermute | solution.py:21
  4.0 3.9 %collective-permute-start.7 = (bf16[192,768]{1,0:T(8,128)(2,1)}, bf16[192,768]{1,0:T(8,128)(2,1)S(1)}, u32[]{:S(2)}, u32[]{:S(2)}) collective-permute-start(bf16[192,768]{1,0:T(8,128)(2,1)} %refs_0_.1), channel_id=1, source_target_pairs={{0,8},{1,9},{2,10},{3,11},{4,12},{5,13},{6,14},{7,15},{8,0},{9,1},... | collective-permute-start | bytes 884744 | tf_op jit(solution)/shard_map/ppermute | solution.py:21
  11.9 7.3 %all-to-all-start = ((s32[128,1,3]{2,1,0:T(1,128)}), s32[128,1,3]{2,1,0:T(1,128)}, u32[]{:S(2)}, u32[]{:S(2)}) async-start(s32[128,1,3]{2,1,0:T(1,128)} %bitcast), calls=%async_computation | async-start | bytes 131072 | tf_op jit(solution)/shard_map/all_to_all | solution.py:284
  22.5 2.8 %collective-permute-start.8 = (bf16[192,768]{1,0:T(8,128)(2,1)}, bf16[192,768]{1,0:T(8,128)(2,1)}, u32[]{:S(2)}, u32[]{:S(2)}) collective-permute-start(bf16[192,768]{1,0:T(8,128)(2,1)} %collective-permute-done.t1.refs_1_), channel_id=1, source_target_pairs={{0,12},{1,13},{2,14},{3,15},{4,0},{5,1},{6,2},{7,3},{8,4},{9,5},{1... | collective-permute-start | bytes 884744 | tf_op jit(solution)/shard_map/ppermute | solution.py:21
  26.7 1.7 copy-done.1
  28.4 6.1 %scores.4 = (bf16[4,1536,768]{2,1,0:T(8,128)(2,1)}, f32[8,1536]{1,0:T(8,128)S(1)}) custom-call(s32[4]{0:T(128)S(1)} %pad_add_fusion.2.place, bf16[1536,768]{1,0:T(8,128)(2,1)S(1)} %copy-done.1, bf16[192,768]{1,0:T(8,128)(2,1)} %refs_0_.1, bf16[192,768]{1,0:T(8,128)(2,1)} %collective-permute-done.t1.refs_1_, ...), custom_call_target="tpu_custom_call" | custom-call | flops 1811939328 | bytes 4718592 | tf_op jit(solution)/shard_map/scores/pallas_call | solution.py:83
  40.7 2.0 reshape.342
  42.7 10.2 %all-to-all-start.1 = ((bf16[128,3,768]{2,1,0:T(4,128)(2,1)}), bf16[128,3,768]{2,1,0:T(4,128)(2,1)}, u32[]{:S(2)}, u32[]{:S(2)}) async-start(bf16[128,3,768]{2,1,0:T(4,128)(2,1)} %reshape.342), calls=%async_computation.1 | async-start | bytes 1572864 | tf_op jit(solution)/shard_map/all_to_all | solution.py:322
  53.6 6.0 %scores.5 = (bf16[4,1536,768]{2,1,0:T(8,128)(2,1)}, f32[8,1536]{1,0:T(8,128)S(1)}) custom-call(s32[4]{0:T(128)S(1)} %pad_add_fusion.3.place, bf16[1536,768]{1,0:T(8,128)(2,1)S(1)} %copy-done.2, bf16[192,768]{1,0:T(8,128)(2,1)S(1)} %collective-permute-done.3.t0.refs_4_, ...), custom_call_target="tpu_custom_call", output_to_operand_aliasing={{0}: (6, {})} | custom-call | flops 1811939328 | bytes 4718592 | tf_op jit(solution)/shard_map/scores/pallas_call | solution.py:83
  59.6 1.6 collective-permute-start.15
  61.2 6.1 %scores.6 = (bf16[4,1536,768]{2,1,0:T(8,128)(2,1)}, f32[8,1536]{1,0:T(8,128)S(1)}) custom-call(s32[4]{0:T(128)S(1)} %pad_add_fusion.4.place, bf16[1536,768]{1,0:T(8,128)(2,1)S(1)} %copy-done.2, bf16[192,768]{1,0:T(8,128)(2,1)S(1)} %collective-permute-done.7.t0.refs_8_, ...), custom_call_target="tpu_custom_call", output_to_operand_aliasing={{0}: (6, {})} | custom-call | flops 1811939328 | bytes 4718592 | tf_op jit(solution)/shard_map/scores/pallas_call | solution.py:83
  67.4 6.1 %scores.7 = (bf16[4,1536,768]{2,1,0:T(8,128)(2,1)}, f32[8,1536]{1,0:T(8,128)S(1)}) custom-call(s32[4]{0:T(128)S(1)} %pad_add_fusion.5.place, bf16[1536,768]{1,0:T(8,128)(2,1)S(1)} %copy-done.2, bf16[192,768]{1,0:T(8,128)(2,1)} %collective-permute-done.11.t0.refs_12_, ...), custom_call_target="tpu_custom_call", output_to_operand_aliasing={{0}: (6, {})} | custom-call | flops 1811939328 | bytes 4718592 | tf_op jit(solution)/shard_map/scores/pallas_call | solution.py:83
  74.9 2.2 reshape.343
  77.1 3.0 %fusion.3 = (f32[192]{0:T(256)S(1)}, f32[192]{0:T(256)S(1)}, f32[]{:T(128)}, f32[192,768]{1,0:T(8,128)}) fusion(bf16[1536,768]{1,0:T(8,128)(2,1)S(1)} %copy-done.2, s32[]{:T(128)S(6)} %select_n.245, bf16[192,768]{1,0:T(8,128)(2,1)S(1)} %collective-permute-done.15.tgt, bf16[384,768]{1,0:T(8,128)(2,1)} %reshape.343, s32[192]{0:T(256)S(1)} %multiply_add_fusion), kind=kOutput, calls=%fused_computation.13 | convolution fusion | flops 114499200 | bytes 1771784 | tf_op jit(solution)/shard_map/dot_general | solution.py:29
  80.1 1.7 fusion.31
  83.9 9.7 %all-to-all-start.2 = ((f32[8,8,1536]{2,1,0:T(8,128)}), f32[8,8,1536]{2,1,0:T(8,128)S(1)}, u32[]{:S(2)}, u32[]{:S(2)}) async-start(f32[8,8,1536]{2,1,0:T(8,128)} %broadcast_in_dim.40), calls=%async_computation.2 | async-start | bytes 786432 | tf_op jit(solution)/shard_map/all_to_all | solution.py:345
  94.2 12.6 %source_terms.1 = bf16[1536,768]{1,0:T(8,128)(2,1)} custom-call(f32[8,1536]{1,0:T(8,128)} %concatenate.22.w_ref, bf16[4,1536,768]{2,1,0:T(8,128)(2,1)} %get-tuple-element.51.e_ref, bf16[192,768]{1,0:T(8,128)(2,1)} %refs_0_.1, bf16[192,768]{1,0:T(8,128)(2,1)} %collective-permute-done.t1.refs_1_, bf16[192,768]{1,0:T(8,128)(2,1)} %copy-done.11, ...), custom_call_target="tpu_custom_call" | custom-call | flops 7247757312 | bytes 11796480 | tf_op jit(solution)/shard_map/source_terms/pallas_call | solution.py:130
  110.7 15.4 %target_terms.1 = (f32[4,384,768]{2,1,0:T(8,128)}, bf16[4,384,768]{2,1,0:T(8,128)(2,1)}) custom-call(s32[16]{0:T(128)} %concatenate.23.place, f32[8,1536]{1,0:T(8,128)} %maximum_maximum_fusion.w_ref, bf16[4,1536,768]{2,1,0:T(8,128)(2,1)} %get-tuple-element.51.e_ref, bf16[1536,768]{1,0:T(8,128)(2,1)} %src_ref.1, bf16[16,128]{1,0:T(8,128)(2,1)} %copy-done.20), custom_call_target="tpu_custom_call" | custom-call | flops 7247757312 | bytes 18874368 | tf_op jit(solution)/shard_map/target_terms/pallas_call | solution.py:183
  126.4 4.4 %all-to-all-start.3 = ((bf16[8,192,768]{2,1,0:T(8,128)(2,1)}), bf16[8,192,768]{2,1,0:T(8,128)(2,1)S(1)}, u32[]{:S(2)}, u32[]{:S(2)}) async-start(bf16[8,192,768]{2,1,0:T(8,128)(2,1)} %bitcast.68), calls=%async_computation.3 | async-start | bytes 4718592 | tf_op jit(solution)/shard_map/all_to_all | solution.py:349
  131.3 2.9 %fusion.10 = (bf16[192,768]{1,0:T(8,128)(2,1)S(1)}, bf16[192,768]{1,0:T(8,128)(2,1)S(1)}, bf16[192,768]{1,0:T(8,128)(2,1)S(1)}, bf16[192,768]{1,0:T(8,128)(2,1)S...) fusion(f32[4,384,768]{2,1,0:T(8,128)} %get-tuple-element.54.keep, ...), kind=kLoop, calls=%fused_computation.33 | loop fusion | flops 2654208 | bytes 7077888 | tf_op jit(solution)/shard_map/convert_element_type | solution.py:380
  136.7 2.4 %collective-permute-start.19 = (bf16[384,768]{1,0:T(8,128)(2,1)}, bf16[384,768]{1,0:T(8,128)(2,1)}, u32[]{:S(2)}, u32[]{:S(2)}) collective-permute-start(bf16[384,768]{1,0:T(8,128)(2,1)} %pad_maximum_fusion.1._b), channel_id=1, source_target_pairs={{0,12},{1,13},{2,14},{3,15},{4,0},{5,1},{6,2},{7,3},{8,4},{9,5},{1... | collective-permute-start | bytes 1769480 | tf_op jit(solution)/shard_map/ppermute | solution.py:21
  140.0 2.3 %convolution_convert_fusion = bf16[384,768]{1,0:T(8,128)(2,1)} fusion(f32[192]{0:T(256)S(1)} %slice_reduce_fusion, bf16[1536,768]{1,0:T(8,128)(2,1)} %src_ref.1, s32[]{:T(128)S(6)} %select_n.245, s32[192]{0:T(256)S(1)} %multiply_add_fusion), kind=kOutput, calls=%fused_computation | convolution fusion | flops 114057216 | bytes 886276 | tf_op jit(solution)/shard_map/dot_general | solution.py:29
  142.4 23.9 %all-to-all-done.3.parts = bf16[8,192,768]{2,1,0:T(8,128)(2,1)S(1)} async-done(((bf16[8,192,768]{2,1,0:T(8,128)(2,1)}), bf16[8,192,768]{2,1,0:T(8,128)(2,1)S(1)}, u32[]{:S(2)}, u32[]{:S(2)}) %all-to-all-start.3) | async-done | bytes 2359328 | tf_op jit(solution)/shard_map/all_to_all | solution.py:349
  167.7 3.0 %code.1 = (s16[192,768]{1,0:T(8,128)(2,1)}, s16[96,768]{1,0:T(8,128)(2,1)}) custom-call(bf16[8,192,768]{2,1,0:T(8,128)(2,1)} %copy-done.13, f32[192,768]{1,0:T(8,128)} %get-tuple-element.101.hard, bf16[192,768]{1,0:T(8,128)(2,1)} %copy-done.15, f32[192,11]{1,0:T(8,128)} %bitcast.69, bf16[384,768]{1,0:T(8,128)(2,1)} %pad_maximum_fusion._a, ...), custom_call_target="tpu_custom_call" | custom-call | flops 1474560 | bytes 3244032 | tf_op jit(solution)/shard_map/code/pallas_call | solution.py:396
  177.7 3.0 %lines.1 = (f32[192,768]{1,0:T(8,128)}, bf16[192,768]{1,0:T(8,128)(2,1)}) custom-call(f32[4,384,768]{2,1,0:T(8,128)} %get-tuple-element.54.keep, bf16[4,384,768]{2,1,0:T(8,128)(2,1)} %collective-permute-done.17.got, bf16[384,768]{1,0:T(8,128)(2,1)} %collective-permute-done.18.m1, bf16[384,768]{1,0:T(8,128)(2,1)} %collective-permute-done.19.m2, ...), custom_call_target="tpu_custom_call" | custom-call | flops 1474560 | bytes 4423680 | tf_op jit(solution)/shard_map/lines/pallas_call | solution.py:386
  181.8 2.2 collective-permute-done.24.far2
  188.3 2.7 %collective-permute-start.21 = (bf16[192,768]{1,0:T(8,128)(2,1)}, bf16[192,768]{1,0:T(8,128)(2,1)}, u32[]{:S(2)}, u32[]{:S(2)}) collective-permute-start(bf16[192,768]{1,0:T(8,128)(2,1)} %get-tuple-element.56), channel_id=1, source_target_pairs={{0,2},{1,3},{2,0},{3,1},{4,6},{5,7},{6,4},{7,5},{8,10},{9,11},{10,... | collective-permute-start | bytes 884744 | tf_op jit(solution)/shard_map/ppermute | solution.py:21
  192.1 10.0 %all-to-all-start.4 = ((bf16[128,3,768]{2,1,0:T(4,128)(2,1)}), bf16[128,3,768]{2,1,0:T(4,128)(2,1)}, u32[]{:S(2)}, u32[]{:S(2)}) async-start(bf16[128,3,768]{2,1,0:T(4,128)(2,1)} %reshape.345), calls=%async_computation.4 | async-start | bytes 1572864 | tf_op jit(solution)/shard_map/all_to_all | solution.py:428
  202.1 2.3 %fusion.1.scale = f32[1536,1]{1,0:T(8,128)S(1)} fusion(f32[1536]{0:T(1024)S(1)} %broadcast_multiply_fusion, f32[1536,1]{1,0:T(8,128)S(1)} %copy.66, f32[1536]{0:T(1024)S(1)} %fusion.21, f32[1536,1]{1,0:T(8,128)} %copy.63, f32[1536,1]{1,0:T(8,128)} %copy.62, f32[1536]{0:T(1024)S(1)} %slice_reduce_fusion.4), kind=kLoop, calls=%fused_computation.9 | loop fusion | flops 23040 | bytes 43008 | tf_op jit(solution)/shard_map/mul | solution.py:422
  204.4 8.9 %collective-permute-done.29.far_side = s16[3,96,768]{2,1,0:T(8,128)(2,1)S(1)} collective-permute-done((s16[3,96,768]{2,1,0:T(8,128)(2,1)}, s16[3,96,768]{2,1,0:T(8,128)(2,1)S(1)}, u32[]{:S(2)}, u32[]{:S(2)}) %collective-permute-start.29) | collective-permute-done | bytes 442400 | tf_op jit(solution)/shard_map/ppermute | solution.py:25
  213.3 4.5 %decode.1 = f32[1536,768]{1,0:T(8,128)} custom-call(s32[8]{0:T(128)S(1)} %stack.170.order, f32[1536,1]{1,0:T(8,128)S(1)} %fusion.1.scale, s16[192,768]{1,0:T(8,128)(2,1)S(1)} %copy-done.3, s16[192,768]{1,0:T(8,128)(2,1)S(1)} %collective-permute-done.22.side, s16[96,768]{1,0:T(8,128)(2,1)S(1)} %collective-permute-done.23.far1, ...), custom_call_target="tpu_custom_call" | custom-call | flops 1179648 | bytes 7077888 | tf_op jit(solution)/shard_map/decode/pallas_call | solution.py:250
  217.8 1.8 convert_add_fusion
  (159 shorter events, 44.9 us)
Async XLA Ops:
  0.6 20.1 %collective-permute-start = (bf16[192,768]{1,0:T(8,128)(2,1)}, bf16[192,768]{1,0:T(8,128)(2,1)}, u32[]{:S(2)}, u32[]{:S(2)}) collective-permute-start(bf16[192,768]{1,0:T(8,128)(2,1)} %refs_0_.1), channel_id=1, source_target_pairs={{0,2},{1,3},{2,0},{3,1},{4,6},{5,7},{6,4},{7,5},{8,10},{9,11},{10,... | collective-permute-start | bytes 884744 | tf_op jit(solution)/shard_map/ppermute | solution.py:21
  4.0 33.7 %collective-permute-start.7 = (bf16[192,768]{1,0:T(8,128)(2,1)}, bf16[192,768]{1,0:T(8,128)(2,1)S(1)}, u32[]{:S(2)}, u32[]{:S(2)}) collective-permute-start(bf16[192,768]{1,0:T(8,128)(2,1)} %refs_0_.1), channel_id=1, source_target_pairs={{0,8},{1,9},{2,10},{3,11},{4,12},{5,13},{6,14},{7,15},{8,0},{9,1},... | collective-permute-start | bytes 884744 | tf_op jit(solution)/shard_map/ppermute | solution.py:21
  7.9 13.1 %collective-permute-start.1 = (bf16[192,768]{1,0:T(8,128)(2,1)}, bf16[192,768]{1,0:T(8,128)(2,1)S(1)}, u32[]{:S(2)}, u32[]{:S(2)}) collective-permute-start(bf16[192,768]{1,0:T(8,128)(2,1)} %refs_0_.1), channel_id=1, source_target_pairs={{0,1},{1,0},{2,3},{3,2},{4,5},{5,4},{6,7},{7,6},{8,9},{9,8},{10,11... | collective-permute-start | bytes 884744 | tf_op jit(solution)/shard_map/ppermute | solution.py:21
  7.9 30.6 %collective-permute-start.3 = (bf16[192,768]{1,0:T(8,128)(2,1)}, bf16[192,768]{1,0:T(8,128)(2,1)S(1)}, u32[]{:S(2)}, u32[]{:S(2)}) collective-permute-start(bf16[192,768]{1,0:T(8,128)(2,1)} %refs_0_.1), channel_id=1, source_target_pairs={{0,12},{1,13},{2,14},{3,15},{4,0},{5,1},{6,2},{7,3},{8,4},{9,5},{1... | collective-permute-start | bytes 884744 | tf_op jit(solution)/shard_map/ppermute | solution.py:21
  8.6 29.9 %collective-permute-start.4 = (bf16[192,768]{1,0:T(8,128)(2,1)}, bf16[192,768]{1,0:T(8,128)(2,1)S(1)}, u32[]{:S(2)}, u32[]{:S(2)}) collective-permute-start(bf16[192,768]{1,0:T(8,128)(2,1)} %refs_0_.1), channel_id=1, source_target_pairs={{0,4},{1,5},{2,6},{3,7},{4,8},{5,9},{6,10},{7,11},{8,12},{9,13},{1... | collective-permute-start | bytes 884744 | tf_op jit(solution)/shard_map/ppermute | solution.py:21
  11.9 24.6 %all-to-all-start = ((s32[128,1,3]{2,1,0:T(1,128)}), s32[128,1,3]{2,1,0:T(1,128)}, u32[]{:S(2)}, u32[]{:S(2)}) async-start(s32[128,1,3]{2,1,0:T(1,128)} %bitcast), calls=%async_computation | async-start | bytes 131072 | tf_op jit(solution)/shard_map/all_to_all | solution.py:284
  20.9 18.1 %collective-permute-start.11 = (bf16[192,768]{1,0:T(8,128)(2,1)}, bf16[192,768]{1,0:T(8,128)(2,1)}, u32[]{:S(2)}, u32[]{:S(2)}) collective-permute-start(bf16[192,768]{1,0:T(8,128)(2,1)} %collective-permute-done.t1.refs_1_), channel_id=1, source_target_pairs={{0,4},{1,5},{2,6},{3,7},{4,8},{5,9},{6,10},{7,11},{8,12},{9,13},{1... | collective-permute-start | bytes 884744 | tf_op jit(solution)/shard_map/ppermute | solution.py:21
  22.5 16.6 %collective-permute-start.8 = (bf16[192,768]{1,0:T(8,128)(2,1)}, bf16[192,768]{1,0:T(8,128)(2,1)}, u32[]{:S(2)}, u32[]{:S(2)}) collective-permute-start(bf16[192,768]{1,0:T(8,128)(2,1)} %collective-permute-done.t1.refs_1_), channel_id=1, source_target_pairs={{0,12},{1,13},{2,14},{3,15},{4,0},{5,1},{6,2},{7,3},{8,4},{9,5},{1... | collective-permute-start | bytes 884744 | tf_op jit(solution)/shard_map/ppermute | solution.py:21
  37.7 15.3 %collective-permute-start.12 = (bf16[192,768]{1,0:T(8,128)(2,1)}, bf16[192,768]{1,0:T(8,128)(2,1)}, u32[]{:S(2)}, u32[]{:S(2)}) collective-permute-start(bf16[192,768]{1,0:T(8,128)(2,1)} %collective-permute-done.t1.refs_1_), channel_id=1, source_target_pairs={{0,8},{1,9},{2,10},{3,11},{4,12},{5,13},{6,14},{7,15},{8,0},{9,1},... | collective-permute-start | bytes 884744 | tf_op jit(solution)/shard_map/ppermute | solution.py:21
  38.5 22.7 %collective-permute-start.9 = (bf16[192,768]{1,0:T(8,128)(2,1)S(1)}, bf16[192,768]{1,0:T(8,128)(2,1)}, u32[]{:S(2)}, u32[]{:S(2)}) collective-permute-start(bf16[192,768]{1,0:T(8,128)(2,1)S(1)} %collective-permute-done.7.t0.refs_8_), channel_id=1, source_target_pairs={{0,1},{1,0},{2,3},{3,2},{4,5},{5,4},{6,7},{7,6},{8,9},{9,8},{10,11... | collective-permute-start | bytes 884744 | tf_op jit(solution)/shard_map/ppermute | solution.py:21
  38.5 14.5 %collective-permute-start.5 = (bf16[192,768]{1,0:T(8,128)(2,1)S(1)}, bf16[192,768]{1,0:T(8,128)(2,1)}, u32[]{:S(2)}, u32[]{:S(2)}) collective-permute-start(bf16[192,768]{1,0:T(8,128)(2,1)S(1)} %collective-permute-done.3.t0.refs_4_), channel_id=1, source_target_pairs={{0,1},{1,0},{2,3},{3,2},{4,5},{5,4},{6,7},{7,6},{8,9},{9,8},{10,11... | collective-permute-start | bytes 884744 | tf_op jit(solution)/shard_map/ppermute | solution.py:21
  39.0 14.6 %collective-permute-start.6 = (bf16[192,768]{1,0:T(8,128)(2,1)S(1)}, bf16[192,768]{1,0:T(8,128)(2,1)}, u32[]{:S(2)}, u32[]{:S(2)}) collective-permute-start(bf16[192,768]{1,0:T(8,128)(2,1)S(1)} %collective-permute-done.4.t1.refs_5_), channel_id=1, source_target_pairs={{0,1},{1,0},{2,3},{3,2},{4,5},{5,4},{6,7},{7,6},{8,9},{9,8},{10,11... | collective-permute-start | bytes 884744 | tf_op jit(solution)/shard_map/ppermute | solution.py:21
  39.1 22.1 %collective-permute-start.10 = (bf16[192,768]{1,0:T(8,128)(2,1)}, bf16[192,768]{1,0:T(8,128)(2,1)}, u32[]{:S(2)}, u32[]{:S(2)}) collective-permute-start(bf16[192,768]{1,0:T(8,128)(2,1)} %collective-permute-done.8.t1.refs_9_), channel_id=1, source_target_pairs={{0,1},{1,0},{2,3},{3,2},{4,5},{5,4},{6,7},{7,6},{8,9},{9,8},{10,11... | collective-permute-start | bytes 884744 | tf_op jit(solution)/shard_map/ppermute | solution.py:21
  42.7 32.2 %all-to-all-start.1 = ((bf16[128,3,768]{2,1,0:T(4,128)(2,1)}), bf16[128,3,768]{2,1,0:T(4,128)(2,1)}, u32[]{:S(2)}, u32[]{:S(2)}) async-start(bf16[128,3,768]{2,1,0:T(4,128)(2,1)} %reshape.342), calls=%async_computation.1 | async-start | bytes 1572864 | tf_op jit(solution)/shard_map/all_to_all | solution.py:322
  53.0 14.3 %collective-permute-start.13 = (bf16[192,768]{1,0:T(8,128)(2,1)}, bf16[192,768]{1,0:T(8,128)(2,1)S(1)}, u32[]{:S(2)}, u32[]{:S(2)}) collective-permute-start(bf16[192,768]{1,0:T(8,128)(2,1)} %collective-permute-done.11.t0.refs_12_), channel_id=1, source_target_pairs={{0,1},{1,0},{2,3},{3,2},{4,5},{5,4},{6,7},{7,6},{8,9},{9,8},{10,11... | collective-permute-start | bytes 884744 | tf_op jit(solution)/shard_map/ppermute | solution.py:21
  53.1 14.3 %collective-permute-start.14 = (bf16[192,768]{1,0:T(8,128)(2,1)}, bf16[192,768]{1,0:T(8,128)(2,1)S(1)}, u32[]{:S(2)}, u32[]{:S(2)}) collective-permute-start(bf16[192,768]{1,0:T(8,128)(2,1)} %collective-permute-done.12.t1.refs_13_), channel_id=1, source_target_pairs={{0,1},{1,0},{2,3},{3,2},{4,5},{5,4},{6,7},{7,6},{8,9},{9,8},{10,11... | collective-permute-start | bytes 884744 | tf_op jit(solution)/shard_map/ppermute | solution.py:21
  59.6 17.6 %collective-permute-start.15 = (bf16[192,768]{1,0:T(8,128)(2,1)}, bf16[192,768]{1,0:T(8,128)(2,1)S(1)}, u32[]{:S(2)}, u32[]{:S(2)}) collective-permute-start(bf16[192,768]{1,0:T(8,128)(2,1)} %refs_0_.1), channel_id=1, source_target_pairs={{0,0},{1,16},{2,32},{3,48},{4,64},{5,80},{6,96},{7,112},{8,1},{9,1... | collective-permute-start | bytes 884744 | tf_op jit(solution)/shard_map/ppermute | solution.py:325
  83.9 22.9 %all-to-all-start.2 = ((f32[8,8,1536]{2,1,0:T(8,128)}), f32[8,8,1536]{2,1,0:T(8,128)S(1)}, u32[]{:S(2)}, u32[]{:S(2)}) async-start(f32[8,8,1536]{2,1,0:T(8,128)} %broadcast_in_dim.40), calls=%async_computation.2 | async-start | bytes 786432 | tf_op jit(solution)/shard_map/all_to_all | solution.py:345
  126.4 39.8 %all-to-all-start.3 = ((bf16[8,192,768]{2,1,0:T(8,128)(2,1)}), bf16[8,192,768]{2,1,0:T(8,128)(2,1)S(1)}, u32[]{:S(2)}, u32[]{:S(2)}) async-start(bf16[8,192,768]{2,1,0:T(8,128)(2,1)} %bitcast.68), calls=%async_computation.3 | async-start | bytes 4718592 | tf_op jit(solution)/shard_map/all_to_all | solution.py:349
  135.1 41.3 %collective-permute-start.18 = (bf16[384,768]{1,0:T(8,128)(2,1)}, bf16[384,768]{1,0:T(8,128)(2,1)}, u32[]{:S(2)}, u32[]{:S(2)}) collective-permute-start(bf16[384,768]{1,0:T(8,128)(2,1)} %pad_maximum_fusion._a), channel_id=1, source_target_pairs={{0,4},{1,5},{2,6},{3,7},{4,8},{5,9},{6,10},{7,11},{8,12},{9,13},{1... | collective-permute-start | bytes 1769480 | tf_op jit(solution)/shard_map/ppermute | solution.py:21
  136.7 40.3 %collective-permute-start.19 = (bf16[384,768]{1,0:T(8,128)(2,1)}, bf16[384,768]{1,0:T(8,128)(2,1)}, u32[]{:S(2)}, u32[]{:S(2)}) collective-permute-start(bf16[384,768]{1,0:T(8,128)(2,1)} %pad_maximum_fusion.1._b), channel_id=1, source_target_pairs={{0,12},{1,13},{2,14},{3,15},{4,0},{5,1},{6,2},{7,3},{8,4},{9,5},{1... | collective-permute-start | bytes 1769480 | tf_op jit(solution)/shard_map/ppermute | solution.py:21
  140.0 37.7 %collective-permute-start.20 = (bf16[384,768]{1,0:T(8,128)(2,1)}, bf16[384,768]{1,0:T(8,128)(2,1)}, u32[]{:S(2)}, u32[]{:S(2)}) collective-permute-start(bf16[384,768]{1,0:T(8,128)(2,1)} %pad_maximum_fusion.2._c), channel_id=1, source_target_pairs={{0,8},{1,9},{2,10},{3,11},{4,12},{5,13},{6,14},{7,15},{8,0},{9,1},... | collective-permute-start | bytes 1769480 | tf_op jit(solution)/shard_map/ppermute | solution.py:21
  170.7 14.8 %collective-permute-start.22 = (s16[192,768]{1,0:T(8,128)(2,1)}, s16[192,768]{1,0:T(8,128)(2,1)S(1)}, u32[]{:S(2)}, u32[]{:S(2)}) collective-permute-start(s16[192,768]{1,0:T(8,128)(2,1)} %get-tuple-element.57.own), channel_id=1, source_target_pairs={{0,16},{16,0},{32,48},{48,32},{64,80},{80,64},{96,112},{112,96},{1... | collective-permute-start | bytes 884744 | tf_op jit(solution)/shard_map/ppermute | solution.py:25
  175.6 6.2 %collective-permute-start.23 = (s16[96,768]{1,0:T(8,128)(2,1)S(1)}, s16[96,768]{1,0:T(8,128)(2,1)S(1)}, u32[]{:S(2)}, u32[]{:S(2)}) collective-permute-start(s16[96,768]{1,0:T(8,128)(2,1)S(1)} %copy-done.19), channel_id=1, source_target_pairs={{0,96},{16,112},{32,0},{48,16},{64,32},{80,48},{96,64},{112,80},{1... | collective-permute-start | bytes 442376 | tf_op jit(solution)/shard_map/ppermute | solution.py:25
  176.4 7.6 %collective-permute-start.24 = (s16[96,768]{1,0:T(8,128)(2,1)S(1)}, s16[96,768]{1,0:T(8,128)(2,1)S(1)}, u32[]{:S(2)}, u32[]{:S(2)}) collective-permute-start(s16[96,768]{1,0:T(8,128)(2,1)S(1)} %copy-done.19), channel_id=1, source_target_pairs={{0,64},{16,80},{32,96},{48,112},{64,0},{80,16},{96,32},{112,48},{1... | collective-permute-start | bytes 442376 | tf_op jit(solution)/shard_map/ppermute | solution.py:25
  177.0 8.5 %collective-permute-start.25 = (s16[96,768]{1,0:T(8,128)(2,1)S(1)}, s16[96,768]{1,0:T(8,128)(2,1)S(1)}, u32[]{:S(2)}, u32[]{:S(2)}) collective-permute-start(s16[96,768]{1,0:T(8,128)(2,1)S(1)} %copy-done.19), channel_id=1, source_target_pairs={{0,32},{16,48},{32,64},{48,80},{64,96},{80,112},{96,0},{112,16},{1... | collective-permute-start | bytes 442376 | tf_op jit(solution)/shard_map/ppermute | solution.py:25
  186.3 18.1 %collective-permute-start.26 = (s16[2,96,768]{2,1,0:T(8,128)(2,1)}, s16[2,96,768]{2,1,0:T(8,128)(2,1)S(1)}, u32[]{:S(2)}, u32[]{:S(2)}) collective-permute-start(s16[2,96,768]{2,1,0:T(8,128)(2,1)} %pad_add_fusion.1), channel_id=1, source_target_pairs={{0,96},{16,112},{32,0},{48,16},{64,32},{80,48},{96,64},{112,80},{1... | collective-permute-start | bytes 884744 | tf_op jit(solution)/shard_map/ppermute | solution.py:25
  186.9 17.6 %collective-permute-start.27 = (s16[2,96,768]{2,1,0:T(8,128)(2,1)}, s16[2,96,768]{2,1,0:T(8,128)(2,1)S(1)}, u32[]{:S(2)}, u32[]{:S(2)}) collective-permute-start(s16[2,96,768]{2,1,0:T(8,128)(2,1)} %pad_add_fusion.1), channel_id=1, source_target_pairs={{0,64},{16,80},{32,96},{48,112},{64,0},{80,16},{96,32},{112,48},{1... | collective-permute-start | bytes 884744 | tf_op jit(solution)/shard_map/ppermute | solution.py:25
  187.5 17.0 %collective-permute-start.28 = (s16[2,96,768]{2,1,0:T(8,128)(2,1)}, s16[2,96,768]{2,1,0:T(8,128)(2,1)S(1)}, u32[]{:S(2)}, u32[]{:S(2)}) collective-permute-start(s16[2,96,768]{2,1,0:T(8,128)(2,1)} %pad_add_fusion.1), channel_id=1, source_target_pairs={{0,32},{16,48},{32,64},{48,80},{64,96},{80,112},{96,0},{112,16},{1... | collective-permute-start | bytes 884744 | tf_op jit(solution)/shard_map/ppermute | solution.py:25
  188.3 29.5 %collective-permute-start.21 = (bf16[192,768]{1,0:T(8,128)(2,1)}, bf16[192,768]{1,0:T(8,128)(2,1)}, u32[]{:S(2)}, u32[]{:S(2)}) collective-permute-start(bf16[192,768]{1,0:T(8,128)(2,1)} %get-tuple-element.56), channel_id=1, source_target_pairs={{0,2},{1,3},{2,0},{3,1},{4,6},{5,7},{6,4},{7,5},{8,10},{9,11},{10,... | collective-permute-start | bytes 884744 | tf_op jit(solution)/shard_map/ppermute | solution.py:21
  191.8 21.5 %collective-permute-start.29 = (s16[3,96,768]{2,1,0:T(8,128)(2,1)}, s16[3,96,768]{2,1,0:T(8,128)(2,1)S(1)}, u32[]{:S(2)}, u32[]{:S(2)}) collective-permute-start(s16[3,96,768]{2,1,0:T(8,128)(2,1)} %pad_add_fusion), channel_id=1, source_target_pairs={{0,16},{16,0},{32,48},{48,32},{64,80},{80,64},{96,112},{112,96},{1... | collective-permute-start | bytes 1327112 | tf_op jit(solution)/shard_map/ppermute | solution.py:25
  192.1 27.6 %all-to-all-start.4 = ((bf16[128,3,768]{2,1,0:T(4,128)(2,1)}), bf16[128,3,768]{2,1,0:T(4,128)(2,1)}, u32[]{:S(2)}, u32[]{:S(2)}) async-start(bf16[128,3,768]{2,1,0:T(4,128)(2,1)} %reshape.345), calls=%async_computation.4 | async-start | bytes 1572864 | tf_op jit(solution)/shard_map/all_to_all | solution.py:428
  (24 other events, 221.8 us)

commit v8 on v3

--- a/solution.py
+++ b/solution.py
@@ -409,7 +409,9 @@
         cost_estimate=pl.CostEstimate(flops=10 * rows * width, bytes_accessed=22 * rows * width, transcendentals=0),
         name="code",
     )(source_parts, hard_rows, own_target, col, other)
-    hard_gate = hard_prob + 0.0 * coded[0, 0].astype(F32)
+    contribution = (hard_prob[:, None] * own_source.astype(F32)).astype(BF)
+    outgoing = dot_f32(pick, contribution, ((0,), (0,))).astype(BF).reshape(owners, cap, width)
+    outgoing, coded, coded_high = lax.optimization_barrier((outgoing, coded, coded_high))
     side = hop_grp(coded, 0, 1)
     far = [hop_grp(coded_high, -dx, 0) for dx in (1, 2, 3)]
     low = jnp.stack([coded[:half], side[:half]])
@@ -420,8 +422,6 @@
         blocks, (bound * (1.0 / 32767.0))[:, None], [coded, side, *far, *pairs, far_side]
     )
 
-    contribution = (hard_gate[:, None] * own_source.astype(F32)).astype(BF)
-    outgoing = dot_f32(pick, contribution, ((0,), (0,))).astype(BF).reshape(owners, cap, width)
     incoming = lax.all_to_all(outgoing, ("grp", "blk"), 0, 0, tiled=True).reshape(slots, width)
     pool_grad = dot_f32(serve, incoming, ((0,), (0,)))
     return (row_loss, source_grad, target_grad, pool_grad)

time: 225 us -> 223 us (level)
    all_to_all x1, waiting for transfers between devices: 11.6 us -> 2.56 us  [shards(): lax.all_to_all(outgoing, ('grp', 'blk'), 0, 0, tiled=True)]
    ppermute x8, waiting for transfers between devices: 0.02 us -> 8.39 us  [hop_grp(): lax.ppermute(value, 'grp', [(i, (i // 2 + dx) % 4 * 2 + (i % 2 ^ dy)) for...]
    unnamed x37 -> x57, local copies, waits for them, and re-layouts: 7.97 us -> 7.33 us
  transfers between devices with their start and end apart: 35 -> 35, of which waited for: 5 -> 7; matrix products, arithmetic and copies ran while one was open for 17% -> 16% of each run, Pallas kernels for 18% -> 18%
where the time goes in v8:
time: 223 us; the launch traced here: 221 us
  starting transfers between devices  76.3 us (34%)
  Pallas kernels  62.7 us (28%)
  waiting for transfers between devices  28.9 us (13%)
  local copies, waits for them, and re-layouts  25.6 us (11%)
  other arithmetic  18.6 us (8%)
  matrix products  7.96 us (4%)
    pallas_call x4, Pallas kernels, score_call(): pl.pallas_call(score_kernel, out_shape=(pltpu.HBM((4, total, cols), BF),...  24.2 us
    ppermute x21, starting transfers between devices, hop_blk(): return lax.ppermute(value, 'blk', route)  23.1 us
    ppermute x21, waiting for transfers between devices, hop_blk(): return lax.ppermute(value, 'blk', route)  18 us
    pallas_call x1, Pallas kernels, target_call(): pl.pallas_call(target_kernel, out_shape=(jax.ShapeDtypeStruct(half, F32),...  15.4 us
    pallas_call x1, Pallas kernels, source_call(): pl.pallas_call(source_kernel, out_shape=jax.ShapeDtypeStruct((total, widt...  12.6 us
    ppermute x8, starting transfers between devices, hop_grp(): lax.ppermute(value, 'grp', [(i, (i // 2 + dx) % 4 * 2 + (i % 2 ^ dy)) for...  11.3 us
    all_to_all x1, starting transfers between devices, shards(): lax.all_to_all(served, ('grp', 'blk'), 0, 0, tiled=True)  10.2 us
    all_to_all x1, starting transfers between devices, shards(): lax.all_to_all(jnp.broadcast_to(mine[None], (8, 8, total)), 'grp', 0, 0,...  9.66 us
  transfers between devices with their start and end apart: 35, of which 7 were waited for; matrix products, arithmetic and copies ran while one was open for 16% of the time, Pallas kernels for 18%

profile of v8, /device:TPU:0, one launch (start us, length us, event | category | flops | bytes accessed | tf_op | source)
XLA Modules:
  0.0 221.5 jit_solution(11249229274252919541)
XLA Ops:
  0.6 3.4 %collective-permute-start = (bf16[192,768]{1,0:T(8,128)(2,1)}, bf16[192,768]{1,0:T(8,128)(2,1)}, u32[]{:S(2)}, u32[]{:S(2)}) collective-permute-start(bf16[192,768]{1,0:T(8,128)(2,1)} %refs_0_.1), channel_id=1, source_target_pairs={{0,2},{1,3},{2,0},{3,1},{4,6},{5,7},{6,4},{7,5},{8,10},{9,11},{10,... | collective-permute-start | bytes 884744 | tf_op jit(solution)/shard_map/ppermute | solution.py:21
  4.0 3.9 %collective-permute-start.7 = (bf16[192,768]{1,0:T(8,128)(2,1)}, bf16[192,768]{1,0:T(8,128)(2,1)S(1)}, u32[]{:S(2)}, u32[]{:S(2)}) collective-permute-start(bf16[192,768]{1,0:T(8,128)(2,1)} %refs_0_.1), channel_id=1, source_target_pairs={{0,8},{1,9},{2,10},{3,11},{4,12},{5,13},{6,14},{7,15},{8,0},{9,1},... | collective-permute-start | bytes 884744 | tf_op jit(solution)/shard_map/ppermute | solution.py:21
  11.9 7.3 %all-to-all-start = ((s32[128,1,3]{2,1,0:T(1,128)}), s32[128,1,3]{2,1,0:T(1,128)}, u32[]{:S(2)}, u32[]{:S(2)}) async-start(s32[128,1,3]{2,1,0:T(1,128)} %bitcast), calls=%async_computation | async-start | bytes 131072 | tf_op jit(solution)/shard_map/all_to_all | solution.py:285
  22.6 2.8 %collective-permute-start.8 = (bf16[192,768]{1,0:T(8,128)(2,1)}, bf16[192,768]{1,0:T(8,128)(2,1)}, u32[]{:S(2)}, u32[]{:S(2)}) collective-permute-start(bf16[192,768]{1,0:T(8,128)(2,1)} %collective-permute-done.t1.refs_1_), channel_id=1, source_target_pairs={{0,12},{1,13},{2,14},{3,15},{4,0},{5,1},{6,2},{7,3},{8,4},{9,5},{1... | collective-permute-start | bytes 884744 | tf_op jit(solution)/shard_map/ppermute | solution.py:21
  28.5 6.0 %scores.4 = (bf16[4,1536,768]{2,1,0:T(8,128)(2,1)}, f32[8,1536]{1,0:T(8,128)S(1)}) custom-call(s32[4]{0:T(128)S(1)} %pad_add_fusion.2.place, bf16[1536,768]{1,0:T(8,128)(2,1)S(1)} %copy-done.1, bf16[192,768]{1,0:T(8,128)(2,1)} %refs_0_.1, bf16[192,768]{1,0:T(8,128)(2,1)} %collective-permute-done.t1.refs_1_, ...), custom_call_target="tpu_custom_call" | custom-call | flops 1811939328 | bytes 4718592 | tf_op jit(solution)/shard_map/scores/pallas_call | solution.py:83
  42.8 10.2 %all-to-all-start.1 = ((bf16[128,3,768]{2,1,0:T(4,128)(2,1)}), bf16[128,3,768]{2,1,0:T(4,128)(2,1)}, u32[]{:S(2)}, u32[]{:S(2)}) async-start(bf16[128,3,768]{2,1,0:T(4,128)(2,1)} %reshape.342), calls=%async_computation.1 | async-start | bytes 1572864 | tf_op jit(solution)/shard_map/all_to_all | solution.py:323
  53.6 6.0 %scores.5 = (bf16[4,1536,768]{2,1,0:T(8,128)(2,1)}, f32[8,1536]{1,0:T(8,128)S(1)}) custom-call(s32[4]{0:T(128)S(1)} %pad_add_fusion.3.place, bf16[1536,768]{1,0:T(8,128)(2,1)S(1)} %copy-done.2, bf16[192,768]{1,0:T(8,128)(2,1)S(1)} %collective-permute-done.3.t0.refs_4_, ...), custom_call_target="tpu_custom_call", output_to_operand_aliasing={{0}: (6, {})} | custom-call | flops 1811939328 | bytes 4718592 | tf_op jit(solution)/shard_map/scores/pallas_call | solution.py:83
  61.3 6.1 %scores.6 = (bf16[4,1536,768]{2,1,0:T(8,128)(2,1)}, f32[8,1536]{1,0:T(8,128)S(1)}) custom-call(s32[4]{0:T(128)S(1)} %pad_add_fusion.4.place, bf16[1536,768]{1,0:T(8,128)(2,1)S(1)} %copy-done.2, bf16[192,768]{1,0:T(8,128)(2,1)S(1)} %collective-permute-done.7.t0.refs_8_, ...), custom_call_target="tpu_custom_call", output_to_operand_aliasing={{0}: (6, {})} | custom-call | flops 1811939328 | bytes 4718592 | tf_op jit(solution)/shard_map/scores/pallas_call | solution.py:83
  67.4 6.0 %scores.7 = (bf16[4,1536,768]{2,1,0:T(8,128)(2,1)}, f32[8,1536]{1,0:T(8,128)S(1)}) custom-call(s32[4]{0:T(128)S(1)} %pad_add_fusion.5.place, bf16[1536,768]{1,0:T(8,128)(2,1)S(1)} %copy-done.2, bf16[192,768]{1,0:T(8,128)(2,1)} %collective-permute-done.11.t0.refs_12_, ...), custom_call_target="tpu_custom_call", output_to_operand_aliasing={{0}: (6, {})} | custom-call | flops 1811939328 | bytes 4718592 | tf_op jit(solution)/shard_map/scores/pallas_call | solution.py:83
  74.9 2.2 %reshape.343 = bf16[384,768]{1,0:T(8,128)(2,1)} reshape(bf16[128,3,768]{2,1,0:T(4,128)(2,1)} %all-to-all-done.1) | data formatting | bytes 1179648 | tf_op jit(solution)/shard_map/reshape | solution.py:323
  77.1 3.0 %fusion.3 = (f32[192]{0:T(256)S(1)}, f32[192]{0:T(256)S(1)}, f32[]{:T(128)}, f32[192,768]{1,0:T(8,128)}) fusion(bf16[1536,768]{1,0:T(8,128)(2,1)S(1)} %copy-done.2, s32[]{:T(128)S(6)} %select_n.245, bf16[192,768]{1,0:T(8,128)(2,1)S(1)} %collective-permute-done.15.tgt, bf16[384,768]{1,0:T(8,128)(2,1)} %reshape.343, s32[192]{0:T(256)S(1)} %multiply_add_fusion), kind=kOutput, calls=%fused_computation.13 | convolution fusion | flops 114499200 | bytes 1771784 | tf_op jit(solution)/shard_map/dot_general | solution.py:29
  83.9 9.7 %all-to-all-start.2 = ((f32[8,8,1536]{2,1,0:T(8,128)}), f32[8,8,1536]{2,1,0:T(8,128)S(1)}, u32[]{:S(2)}, u32[]{:S(2)}) async-start(f32[8,8,1536]{2,1,0:T(8,128)} %broadcast_in_dim.40), calls=%async_computation.2 | async-start | bytes 786432 | tf_op jit(solution)/shard_map/all_to_all | solution.py:346
  94.2 12.6 %source_terms.1 = bf16[1536,768]{1,0:T(8,128)(2,1)} custom-call(f32[8,1536]{1,0:T(8,128)} %concatenate.22.w_ref, bf16[4,1536,768]{2,1,0:T(8,128)(2,1)} %get-tuple-element.46.e_ref, bf16[192,768]{1,0:T(8,128)(2,1)} %refs_0_.1, bf16[192,768]{1,0:T(8,128)(2,1)} %collective-permute-done.t1.refs_1_, bf16[192,768]{1,0:T(8,128)(2,1)} %copy-done.11, ...), custom_call_target="tpu_custom_call" | custom-call | flops 7247757312 | bytes 11796480 | tf_op jit(solution)/shard_map/source_terms/pallas_call | solution.py:131
  110.7 15.4 %target_terms.1 = (f32[4,384,768]{2,1,0:T(8,128)}, bf16[4,384,768]{2,1,0:T(8,128)(2,1)}) custom-call(s32[16]{0:T(128)} %concatenate.24.place, f32[8,1536]{1,0:T(8,128)} %maximum_maximum_fusion.w_ref, bf16[4,1536,768]{2,1,0:T(8,128)(2,1)} %get-tuple-element.46.e_ref, bf16[1536,768]{1,0:T(8,128)(2,1)} %src_ref.1, bf16[16,128]{1,0:T(8,128)(2,1)} %copy-done.27), custom_call_target="tpu_custom_call" | custom-call | flops 7247757312 | bytes 18874368 | tf_op jit(solution)/shard_map/target_terms/pallas_call | solution.py:184
  126.5 4.5 %all-to-all-start.3 = ((bf16[8,192,768]{2,1,0:T(8,128)(2,1)}), bf16[8,192,768]{2,1,0:T(8,128)(2,1)S(1)}, u32[]{:S(2)}, u32[]{:S(2)}) async-start(bf16[8,192,768]{2,1,0:T(8,128)(2,1)} %bitcast.68), calls=%async_computation.3 | async-start | bytes 4718592 | tf_op jit(solution)/shard_map/all_to_all | solution.py:350
  132.9 2.9 %fusion.10 = (bf16[192,768]{1,0:T(8,128)(2,1)S(1)}, bf16[192,768]{1,0:T(8,128)(2,1)S(1)}, bf16[192,768]{1,0:T(8,128)(2,1)S(1)}, bf16[192,768]{1,0:T(8,128)(2,1)S...) fusion(f32[4,384,768]{2,1,0:T(8,128)} %get-tuple-element.49.keep, ...), kind=kLoop, calls=%fused_computation.33 | loop fusion | flops 2654208 | bytes 7077888 | tf_op jit(solution)/shard_map/convert_element_type | solution.py:381
  138.3 2.4 %collective-permute-start.19 = (bf16[384,768]{1,0:T(8,128)(2,1)}, bf16[384,768]{1,0:T(8,128)(2,1)}, u32[]{:S(2)}, u32[]{:S(2)}) collective-permute-start(bf16[384,768]{1,0:T(8,128)(2,1)} %pad_maximum_fusion.1), channel_id=1, source_target_pairs={{0,12},{1,13},{2,14},{3,15},{4,0},{5,1},{6,2},{7,3},{8,4},{9,5},{1... | collective-permute-start | bytes 1769480 | tf_op jit(solution)/shard_map/ppermute | solution.py:21
  146.4 2.4 %fusion.1.scale = f32[1536,1]{1,0:T(8,128)S(1)} fusion(f32[1536]{0:T(1024)S(1)} %copy-done.24, f32[1536,1]{1,0:T(8,128)} %copy.66, f32[1536]{0:T(1024)S(1)} %copy-done.22, f32[1536,1]{1,0:T(8,128)} %copy.63, f32[1536,1]{1,0:T(8,128)} %copy.62, f32[1536]{0:T(1024)S(1)} %copy-done.20), kind=kLoop, calls=%fused_computation.9 | loop fusion | flops 23040 | bytes 43008 | tf_op jit(solution)/shard_map/mul | solution.py:422
  148.8 5.5 %collective-permute-done.18.m1 = bf16[384,768]{1,0:T(8,128)(2,1)} collective-permute-done((bf16[384,768]{1,0:T(8,128)(2,1)}, bf16[384,768]{1,0:T(8,128)(2,1)}, u32[]{:S(2)}, u32[]{:S(2)}) %collective-permute-start.18) | collective-permute-done | bytes 589856 | tf_op jit(solution)/shard_map/ppermute | solution.py:21
  154.3 12.0 %collective-permute-done.19.m2 = bf16[384,768]{1,0:T(8,128)(2,1)} collective-permute-done((bf16[384,768]{1,0:T(8,128)(2,1)}, bf16[384,768]{1,0:T(8,128)(2,1)}, u32[]{:S(2)}, u32[]{:S(2)}) %collective-permute-start.19) | collective-permute-done | bytes 589856 | tf_op jit(solution)/shard_map/ppermute | solution.py:21
  166.2 3.0 %lines.1 = (f32[192,768]{1,0:T(8,128)}, bf16[192,768]{1,0:T(8,128)(2,1)}) custom-call(f32[4,384,768]{2,1,0:T(8,128)} %get-tuple-element.49.keep, bf16[4,384,768]{2,1,0:T(8,128)(2,1)} %collective-permute-done.17.got, bf16[384,768]{1,0:T(8,128)(2,1)} %collective-permute-done.18.m1, bf16[384,768]{1,0:T(8,128)(2,1)} %collective-permute-done.19.m2, ...), custom_call_target="tpu_custom_call" | custom-call | flops 1474560 | bytes 4423680 | tf_op jit(solution)/shard_map/lines/pallas_call | solution.py:386
  170.7 3.0 %code.1 = (s16[192,768]{1,0:T(8,128)(2,1)}, s16[96,768]{1,0:T(8,128)(2,1)}) custom-call(bf16[8,192,768]{2,1,0:T(8,128)(2,1)} %copy-done.13, f32[192,768]{1,0:T(8,128)} %get-tuple-element.93.hard, bf16[192,768]{1,0:T(8,128)(2,1)} %copy-done.14, f32[192,11]{1,0:T(8,128)} %bitcast.69, bf16[192,768]{1,0:T(8,128)(2,1)} %get-tuple-element.51._), custom_call_target="tpu_custom_call" | custom-call | flops 1474560 | bytes 3244032 | tf_op jit(solution)/shard_map/code/pallas_call | solution.py:397
  173.6 3.0 %collective-permute-start.22 = (s16[96,768]{1,0:T(8,128)(2,1)}, s16[96,768]{1,0:T(8,128)(2,1)S(1)}, u32[]{:S(2)}, u32[]{:S(2)}) collective-permute-start(s16[96,768]{1,0:T(8,128)(2,1)} %get-tuple-element.55), channel_id=1, source_target_pairs={{0,96},{16,112},{32,0},{48,16},{64,32},{80,48},{96,64},{112,80},{1... | collective-permute-start | bytes 442376 | tf_op jit(solution)/shard_map/ppermute | solution.py:25
  178.3 3.5 %collective-permute-start.29 = (bf16[192,768]{1,0:T(8,128)(2,1)}, bf16[192,768]{1,0:T(8,128)(2,1)}, u32[]{:S(2)}, u32[]{:S(2)}) collective-permute-start(bf16[192,768]{1,0:T(8,128)(2,1)} %get-tuple-element.51._), channel_id=1, source_target_pairs={{0,2},{1,3},{2,0},{3,1},{4,6},{5,7},{6,4},{7,5},{8,10},{9,11},{10,... | collective-permute-start | bytes 884744 | tf_op jit(solution)/shard_map/ppermute | solution.py:21
  182.6 8.5 %all-to-all-start.4 = ((bf16[128,3,768]{2,1,0:T(4,128)(2,1)}), bf16[128,3,768]{2,1,0:T(4,128)(2,1)}, u32[]{:S(2)}, u32[]{:S(2)}) async-start(bf16[128,3,768]{2,1,0:T(4,128)(2,1)} %reshape.344), calls=%async_computation.4 | async-start | bytes 1572864 | tf_op jit(solution)/shard_map/all_to_all | solution.py:425
  193.9 7.8 %collective-permute-done.21.side = s16[192,768]{1,0:T(8,128)(2,1)S(1)} collective-permute-done((s16[192,768]{1,0:T(8,128)(2,1)}, s16[192,768]{1,0:T(8,128)(2,1)S(1)}, u32[]{:S(2)}, u32[]{:S(2)}) %collective-permute-start.21) | collective-permute-done | bytes 294944 | tf_op jit(solution)/shard_map/ppermute | solution.py:25
  202.5 2.8 %collective-permute-start.25 = (s16[2,96,768]{2,1,0:T(8,128)(2,1)}, s16[2,96,768]{2,1,0:T(8,128)(2,1)S(1)}, u32[]{:S(2)}, u32[]{:S(2)}) collective-permute-start(s16[2,96,768]{2,1,0:T(8,128)(2,1)} %pad_add_fusion.1), channel_id=1, source_target_pairs={{0,96},{16,112},{32,0},{48,16},{64,32},{80,48},{96,64},{112,80},{1... | collective-permute-start | bytes 884744 | tf_op jit(solution)/shard_map/ppermute | solution.py:25
  205.3 2.1 collective-permute-start.26
  209.2 2.6 %all-to-all-done.4 = bf16[128,3,768]{2,1,0:T(4,128)(2,1)} async-done(((bf16[128,3,768]{2,1,0:T(4,128)(2,1)}), bf16[128,3,768]{2,1,0:T(4,128)(2,1)}, u32[]{:S(2)}, u32[]{:S(2)}) %all-to-all-start.4) | async-done | bytes 589856 | tf_op jit(solution)/shard_map/all_to_all | solution.py:425
  211.8 2.2 %reshape.346 = bf16[384,768]{1,0:T(8,128)(2,1)} reshape(bf16[128,3,768]{2,1,0:T(4,128)(2,1)} %all-to-all-done.4) | data formatting | bytes 1179648 | tf_op jit(solution)/shard_map/reshape | solution.py:425
  214.0 2.3 %fusion.5 = f32[192,768]{1,0:T(8,128)} fusion(bf16[384,768]{1,0:T(8,128)(2,1)} %reshape.346, s32[384]{0:T(512)S(1)} %eq.135), kind=kOutput, calls=%fused_computation.28 | convolution fusion | flops 113319936 | bytes 1181184 | tf_op jit(solution)/shard_map/dot_general | solution.py:29
  216.9 4.5 %decode.1 = f32[1536,768]{1,0:T(8,128)} custom-call(s32[8]{0:T(128)S(1)} %stack.170.order, f32[1536,1]{1,0:T(8,128)S(1)} %fusion.1.scale, s16[192,768]{1,0:T(8,128)(2,1)S(1)} %copy-done.3, s16[192,768]{1,0:T(8,128)(2,1)S(1)} %collective-permute-done.21.side, s16[96,768]{1,0:T(8,128)(2,1)S(1)} %collective-permute-done.22.far1, ...), custom_call_target="tpu_custom_call" | custom-call | flops 1179648 | bytes 7077888 | tf_op jit(solution)/shard_map/decode/pallas_call | solution.py:251
  (171 shorter events, 50.5 us)
Async XLA Ops:
  0.6 20.1 %collective-permute-start = (bf16[192,768]{1,0:T(8,128)(2,1)}, bf16[192,768]{1,0:T(8,128)(2,1)}, u32[]{:S(2)}, u32[]{:S(2)}) collective-permute-start(bf16[192,768]{1,0:T(8,128)(2,1)} %refs_0_.1), channel_id=1, source_target_pairs={{0,2},{1,3},{2,0},{3,1},{4,6},{5,7},{6,4},{7,5},{8,10},{9,11},{10,... | collective-permute-start | bytes 884744 | tf_op jit(solution)/shard_map/ppermute | solution.py:21
  4.0 33.8 %collective-permute-start.7 = (bf16[192,768]{1,0:T(8,128)(2,1)}, bf16[192,768]{1,0:T(8,128)(2,1)S(1)}, u32[]{:S(2)}, u32[]{:S(2)}) collective-permute-start(bf16[192,768]{1,0:T(8,128)(2,1)} %refs_0_.1), channel_id=1, source_target_pairs={{0,8},{1,9},{2,10},{3,11},{4,12},{5,13},{6,14},{7,15},{8,0},{9,1},... | collective-permute-start | bytes 884744 | tf_op jit(solution)/shard_map/ppermute | solution.py:21
  7.9 13.1 %collective-permute-start.1 = (bf16[192,768]{1,0:T(8,128)(2,1)}, bf16[192,768]{1,0:T(8,128)(2,1)S(1)}, u32[]{:S(2)}, u32[]{:S(2)}) collective-permute-start(bf16[192,768]{1,0:T(8,128)(2,1)} %refs_0_.1), channel_id=1, source_target_pairs={{0,1},{1,0},{2,3},{3,2},{4,5},{5,4},{6,7},{7,6},{8,9},{9,8},{10,11... | collective-permute-start | bytes 884744 | tf_op jit(solution)/shard_map/ppermute | solution.py:21
  7.9 30.7 %collective-permute-start.3 = (bf16[192,768]{1,0:T(8,128)(2,1)}, bf16[192,768]{1,0:T(8,128)(2,1)S(1)}, u32[]{:S(2)}, u32[]{:S(2)}) collective-permute-start(bf16[192,768]{1,0:T(8,128)(2,1)} %refs_0_.1), channel_id=1, source_target_pairs={{0,12},{1,13},{2,14},{3,15},{4,0},{5,1},{6,2},{7,3},{8,4},{9,5},{1... | collective-permute-start | bytes 884744 | tf_op jit(solution)/shard_map/ppermute | solution.py:21
  8.6 30.0 %collective-permute-start.4 = (bf16[192,768]{1,0:T(8,128)(2,1)}, bf16[192,768]{1,0:T(8,128)(2,1)S(1)}, u32[]{:S(2)}, u32[]{:S(2)}) collective-permute-start(bf16[192,768]{1,0:T(8,128)(2,1)} %refs_0_.1), channel_id=1, source_target_pairs={{0,4},{1,5},{2,6},{3,7},{4,8},{5,9},{6,10},{7,11},{8,12},{9,13},{1... | collective-permute-start | bytes 884744 | tf_op jit(solution)/shard_map/ppermute | solution.py:21
  11.9 24.7 %all-to-all-start = ((s32[128,1,3]{2,1,0:T(1,128)}), s32[128,1,3]{2,1,0:T(1,128)}, u32[]{:S(2)}, u32[]{:S(2)}) async-start(s32[128,1,3]{2,1,0:T(1,128)} %bitcast), calls=%async_computation | async-start | bytes 131072 | tf_op jit(solution)/shard_map/all_to_all | solution.py:285
  21.0 18.0 %collective-permute-start.11 = (bf16[192,768]{1,0:T(8,128)(2,1)}, bf16[192,768]{1,0:T(8,128)(2,1)}, u32[]{:S(2)}, u32[]{:S(2)}) collective-permute-start(bf16[192,768]{1,0:T(8,128)(2,1)} %collective-permute-done.t1.refs_1_), channel_id=1, source_target_pairs={{0,4},{1,5},{2,6},{3,7},{4,8},{5,9},{6,10},{7,11},{8,12},{9,13},{1... | collective-permute-start | bytes 884744 | tf_op jit(solution)/shard_map/ppermute | solution.py:21
  22.6 16.6 %collective-permute-start.8 = (bf16[192,768]{1,0:T(8,128)(2,1)}, bf16[192,768]{1,0:T(8,128)(2,1)}, u32[]{:S(2)}, u32[]{:S(2)}) collective-permute-start(bf16[192,768]{1,0:T(8,128)(2,1)} %collective-permute-done.t1.refs_1_), channel_id=1, source_target_pairs={{0,12},{1,13},{2,14},{3,15},{4,0},{5,1},{6,2},{7,3},{8,4},{9,5},{1... | collective-permute-start | bytes 884744 | tf_op jit(solution)/shard_map/ppermute | solution.py:21
  37.8 15.3 %collective-permute-start.12 = (bf16[192,768]{1,0:T(8,128)(2,1)}, bf16[192,768]{1,0:T(8,128)(2,1)}, u32[]{:S(2)}, u32[]{:S(2)}) collective-permute-start(bf16[192,768]{1,0:T(8,128)(2,1)} %collective-permute-done.t1.refs_1_), channel_id=1, source_target_pairs={{0,8},{1,9},{2,10},{3,11},{4,12},{5,13},{6,14},{7,15},{8,0},{9,1},... | collective-permute-start | bytes 884744 | tf_op jit(solution)/shard_map/ppermute | solution.py:21
  38.5 22.7 %collective-permute-start.9 = (bf16[192,768]{1,0:T(8,128)(2,1)S(1)}, bf16[192,768]{1,0:T(8,128)(2,1)}, u32[]{:S(2)}, u32[]{:S(2)}) collective-permute-start(bf16[192,768]{1,0:T(8,128)(2,1)S(1)} %collective-permute-done.7.t0.refs_8_), channel_id=1, source_target_pairs={{0,1},{1,0},{2,3},{3,2},{4,5},{5,4},{6,7},{7,6},{8,9},{9,8},{10,11... | collective-permute-start | bytes 884744 | tf_op jit(solution)/shard_map/ppermute | solution.py:21
  38.6 14.6 %collective-permute-start.5 = (bf16[192,768]{1,0:T(8,128)(2,1)S(1)}, bf16[192,768]{1,0:T(8,128)(2,1)}, u32[]{:S(2)}, u32[]{:S(2)}) collective-permute-start(bf16[192,768]{1,0:T(8,128)(2,1)S(1)} %collective-permute-done.3.t0.refs_4_), channel_id=1, source_target_pairs={{0,1},{1,0},{2,3},{3,2},{4,5},{5,4},{6,7},{7,6},{8,9},{9,8},{10,11... | collective-permute-start | bytes 884744 | tf_op jit(solution)/shard_map/ppermute | solution.py:21
  39.1 14.6 %collective-permute-start.6 = (bf16[192,768]{1,0:T(8,128)(2,1)S(1)}, bf16[192,768]{1,0:T(8,128)(2,1)}, u32[]{:S(2)}, u32[]{:S(2)}) collective-permute-start(bf16[192,768]{1,0:T(8,128)(2,1)S(1)} %collective-permute-done.4.t1.refs_5_), channel_id=1, source_target_pairs={{0,1},{1,0},{2,3},{3,2},{4,5},{5,4},{6,7},{7,6},{8,9},{9,8},{10,11... | collective-permute-start | bytes 884744 | tf_op jit(solution)/shard_map/ppermute | solution.py:21
  39.2 22.1 %collective-permute-start.10 = (bf16[192,768]{1,0:T(8,128)(2,1)}, bf16[192,768]{1,0:T(8,128)(2,1)}, u32[]{:S(2)}, u32[]{:S(2)}) collective-permute-start(bf16[192,768]{1,0:T(8,128)(2,1)} %collective-permute-done.8.t1.refs_9_), channel_id=1, source_target_pairs={{0,1},{1,0},{2,3},{3,2},{4,5},{5,4},{6,7},{7,6},{8,9},{9,8},{10,11... | collective-permute-start | bytes 884744 | tf_op jit(solution)/shard_map/ppermute | solution.py:21
  42.8 32.1 %all-to-all-start.1 = ((bf16[128,3,768]{2,1,0:T(4,128)(2,1)}), bf16[128,3,768]{2,1,0:T(4,128)(2,1)}, u32[]{:S(2)}, u32[]{:S(2)}) async-start(bf16[128,3,768]{2,1,0:T(4,128)(2,1)} %reshape.342), calls=%async_computation.1 | async-start | bytes 1572864 | tf_op jit(solution)/shard_map/all_to_all | solution.py:323
  53.1 14.3 %collective-permute-start.13 = (bf16[192,768]{1,0:T(8,128)(2,1)}, bf16[192,768]{1,0:T(8,128)(2,1)S(1)}, u32[]{:S(2)}, u32[]{:S(2)}) collective-permute-start(bf16[192,768]{1,0:T(8,128)(2,1)} %collective-permute-done.11.t0.refs_12_), channel_id=1, source_target_pairs={{0,1},{1,0},{2,3},{3,2},{4,5},{5,4},{6,7},{7,6},{8,9},{9,8},{10,11... | collective-permute-start | bytes 884744 | tf_op jit(solution)/shard_map/ppermute | solution.py:21
  53.1 14.3 %collective-permute-start.14 = (bf16[192,768]{1,0:T(8,128)(2,1)}, bf16[192,768]{1,0:T(8,128)(2,1)S(1)}, u32[]{:S(2)}, u32[]{:S(2)}) collective-permute-start(bf16[192,768]{1,0:T(8,128)(2,1)} %collective-permute-done.12.t1.refs_13_), channel_id=1, source_target_pairs={{0,1},{1,0},{2,3},{3,2},{4,5},{5,4},{6,7},{7,6},{8,9},{9,8},{10,11... | collective-permute-start | bytes 884744 | tf_op jit(solution)/shard_map/ppermute | solution.py:21
  59.6 17.5 %collective-permute-start.15 = (bf16[192,768]{1,0:T(8,128)(2,1)}, bf16[192,768]{1,0:T(8,128)(2,1)S(1)}, u32[]{:S(2)}, u32[]{:S(2)}) collective-permute-start(bf16[192,768]{1,0:T(8,128)(2,1)} %refs_0_.1), channel_id=1, source_target_pairs={{0,0},{1,16},{2,32},{3,48},{4,64},{5,80},{6,96},{7,112},{8,1},{9,1... | collective-permute-start | bytes 884744 | tf_op jit(solution)/shard_map/ppermute | solution.py:326
  83.9 22.9 %all-to-all-start.2 = ((f32[8,8,1536]{2,1,0:T(8,128)}), f32[8,8,1536]{2,1,0:T(8,128)S(1)}, u32[]{:S(2)}, u32[]{:S(2)}) async-start(f32[8,8,1536]{2,1,0:T(8,128)} %broadcast_in_dim.40), calls=%async_computation.2 | async-start | bytes 786432 | tf_op jit(solution)/shard_map/all_to_all | solution.py:346
  126.5 42.7 %all-to-all-start.3 = ((bf16[8,192,768]{2,1,0:T(8,128)(2,1)}), bf16[8,192,768]{2,1,0:T(8,128)(2,1)S(1)}, u32[]{:S(2)}, u32[]{:S(2)}) async-start(bf16[8,192,768]{2,1,0:T(8,128)(2,1)} %bitcast.68), calls=%async_computation.3 | async-start | bytes 4718592 | tf_op jit(solution)/shard_map/all_to_all | solution.py:350
  136.6 17.7 %collective-permute-start.18 = (bf16[384,768]{1,0:T(8,128)(2,1)}, bf16[384,768]{1,0:T(8,128)(2,1)}, u32[]{:S(2)}, u32[]{:S(2)}) collective-permute-start(bf16[384,768]{1,0:T(8,128)(2,1)} %pad_maximum_fusion), channel_id=1, source_target_pairs={{0,4},{1,5},{2,6},{3,7},{4,8},{5,9},{6,10},{7,11},{8,12},{9,13},{1... | collective-permute-start | bytes 1769480 | tf_op jit(solution)/shard_map/ppermute | solution.py:21
  138.3 27.9 %collective-permute-start.19 = (bf16[384,768]{1,0:T(8,128)(2,1)}, bf16[384,768]{1,0:T(8,128)(2,1)}, u32[]{:S(2)}, u32[]{:S(2)}) collective-permute-start(bf16[384,768]{1,0:T(8,128)(2,1)} %pad_maximum_fusion.1), channel_id=1, source_target_pairs={{0,12},{1,13},{2,14},{3,15},{4,0},{5,1},{6,2},{7,3},{8,4},{9,5},{1... | collective-permute-start | bytes 1769480 | tf_op jit(solution)/shard_map/ppermute | solution.py:21
  141.7 24.6 %collective-permute-start.20 = (bf16[384,768]{1,0:T(8,128)(2,1)}, bf16[384,768]{1,0:T(8,128)(2,1)}, u32[]{:S(2)}, u32[]{:S(2)}) collective-permute-start(bf16[384,768]{1,0:T(8,128)(2,1)} %pad_maximum_fusion.2), channel_id=1, source_target_pairs={{0,8},{1,9},{2,10},{3,11},{4,12},{5,13},{6,14},{7,15},{8,0},{9,1},... | collective-permute-start | bytes 1769480 | tf_op jit(solution)/shard_map/ppermute | solution.py:21
  173.6 18.6 %collective-permute-start.22 = (s16[96,768]{1,0:T(8,128)(2,1)}, s16[96,768]{1,0:T(8,128)(2,1)S(1)}, u32[]{:S(2)}, u32[]{:S(2)}) collective-permute-start(s16[96,768]{1,0:T(8,128)(2,1)} %get-tuple-element.55), channel_id=1, source_target_pairs={{0,96},{16,112},{32,0},{48,16},{64,32},{80,48},{96,64},{112,80},{1... | collective-permute-start | bytes 442376 | tf_op jit(solution)/shard_map/ppermute | solution.py:25
  176.6 15.6 %collective-permute-start.23 = (s16[96,768]{1,0:T(8,128)(2,1)}, s16[96,768]{1,0:T(8,128)(2,1)S(1)}, u32[]{:S(2)}, u32[]{:S(2)}) collective-permute-start(s16[96,768]{1,0:T(8,128)(2,1)} %get-tuple-element.55), channel_id=1, source_target_pairs={{0,64},{16,80},{32,96},{48,112},{64,0},{80,16},{96,32},{112,48},{1... | collective-permute-start | bytes 442376 | tf_op jit(solution)/shard_map/ppermute | solution.py:25
  177.4 14.8 %collective-permute-start.24 = (s16[96,768]{1,0:T(8,128)(2,1)}, s16[96,768]{1,0:T(8,128)(2,1)S(1)}, u32[]{:S(2)}, u32[]{:S(2)}) collective-permute-start(s16[96,768]{1,0:T(8,128)(2,1)} %get-tuple-element.55), channel_id=1, source_target_pairs={{0,32},{16,48},{32,64},{48,80},{64,96},{80,112},{96,0},{112,16},{1... | collective-permute-start | bytes 442376 | tf_op jit(solution)/shard_map/ppermute | solution.py:25
  178.3 29.1 %collective-permute-start.29 = (bf16[192,768]{1,0:T(8,128)(2,1)}, bf16[192,768]{1,0:T(8,128)(2,1)}, u32[]{:S(2)}, u32[]{:S(2)}) collective-permute-start(bf16[192,768]{1,0:T(8,128)(2,1)} %get-tuple-element.51._), channel_id=1, source_target_pairs={{0,2},{1,3},{2,0},{3,1},{4,6},{5,7},{6,4},{7,5},{8,10},{9,11},{10,... | collective-permute-start | bytes 884744 | tf_op jit(solution)/shard_map/ppermute | solution.py:21
  181.8 19.9 %collective-permute-start.21 = (s16[192,768]{1,0:T(8,128)(2,1)}, s16[192,768]{1,0:T(8,128)(2,1)S(1)}, u32[]{:S(2)}, u32[]{:S(2)}) collective-permute-start(s16[192,768]{1,0:T(8,128)(2,1)} %get-tuple-element.54.own), channel_id=1, source_target_pairs={{0,16},{16,0},{32,48},{48,32},{64,80},{80,64},{96,112},{112,96},{1... | collective-permute-start | bytes 884744 | tf_op jit(solution)/shard_map/ppermute | solution.py:25
  182.6 29.2 %all-to-all-start.4 = ((bf16[128,3,768]{2,1,0:T(4,128)(2,1)}), bf16[128,3,768]{2,1,0:T(4,128)(2,1)}, u32[]{:S(2)}, u32[]{:S(2)}) async-start(bf16[128,3,768]{2,1,0:T(4,128)(2,1)} %reshape.344), calls=%async_computation.4 | async-start | bytes 1572864 | tf_op jit(solution)/shard_map/all_to_all | solution.py:425
  193.0 23.3 %collective-permute-start.28 = (s16[3,96,768]{2,1,0:T(8,128)(2,1)}, s16[3,96,768]{2,1,0:T(8,128)(2,1)S(1)}, u32[]{:S(2)}, u32[]{:S(2)}) collective-permute-start(s16[3,96,768]{2,1,0:T(8,128)(2,1)} %pad_add_fusion), channel_id=1, source_target_pairs={{0,16},{16,0},{32,48},{48,32},{64,80},{80,64},{96,112},{112,96},{1... | collective-permute-start | bytes 1327112 | tf_op jit(solution)/shard_map/ppermute | solution.py:25
  202.5 13.9 %collective-permute-start.25 = (s16[2,96,768]{2,1,0:T(8,128)(2,1)}, s16[2,96,768]{2,1,0:T(8,128)(2,1)S(1)}, u32[]{:S(2)}, u32[]{:S(2)}) collective-permute-start(s16[2,96,768]{2,1,0:T(8,128)(2,1)} %pad_add_fusion.1), channel_id=1, source_target_pairs={{0,96},{16,112},{32,0},{48,16},{64,32},{80,48},{96,64},{112,80},{1... | collective-permute-start | bytes 884744 | tf_op jit(solution)/shard_map/ppermute | solution.py:25
  205.3 11.0 %collective-permute-start.26 = (s16[2,96,768]{2,1,0:T(8,128)(2,1)}, s16[2,96,768]{2,1,0:T(8,128)(2,1)S(1)}, u32[]{:S(2)}, u32[]{:S(2)}) collective-permute-start(s16[2,96,768]{2,1,0:T(8,128)(2,1)} %pad_add_fusion.1), channel_id=1, source_target_pairs={{0,64},{16,80},{32,96},{48,112},{64,0},{80,16},{96,32},{112,48},{1... | collective-permute-start | bytes 884744 | tf_op jit(solution)/shard_map/ppermute | solution.py:25
  207.4 9.5 %collective-permute-start.27 = (s16[2,96,768]{2,1,0:T(8,128)(2,1)}, s16[2,96,768]{2,1,0:T(8,128)(2,1)S(1)}, u32[]{:S(2)}, u32[]{:S(2)}) collective-permute-start(s16[2,96,768]{2,1,0:T(8,128)(2,1)} %pad_add_fusion.1), channel_id=1, source_target_pairs={{0,32},{16,48},{32,64},{48,80},{64,96},{80,112},{96,0},{112,16},{1... | collective-permute-start | bytes 884744 | tf_op jit(solution)/shard_map/ppermute | solution.py:25
  (31 other events, 411.1 us)

commit v9 on v8

--- a/solution.py
+++ b/solution.py
@@ -422,8 +422,9 @@
         blocks, (bound * (1.0 / 32767.0))[:, None], [coded, side, *far, *pairs, far_side]
     )
 
-    incoming = lax.all_to_all(outgoing, ("grp", "blk"), 0, 0, tiled=True).reshape(slots, width)
-    pool_grad = dot_f32(serve, incoming, ((0,), (0,)))
+    incoming = lax.all_to_all(outgoing, ("grp", "blk"), 0, 0, tiled=True)
+    incoming, source_grad = lax.optimization_barrier((incoming, source_grad))
+    pool_grad = dot_f32(serve, incoming.reshape(slots, width), ((0,), (0,)))
     return (row_loss, source_grad, target_grad, pool_grad)
 
 

time: 223 us -> 232 us (1.040)
  waiting for transfers between devices: 28.9 us -> 41 us
  other arithmetic: 18.6 us -> 15.9 us
    ppermute x8, waiting for transfers between devices: 8.39 us -> 23.9 us  [hop_grp(): lax.ppermute(value, 'grp', [(i, (i // 2 + dx) % 4 * 2 + (i % 2 ^ dy)) for...]
    all_to_all x1, waiting for transfers between devices: 2.56 us -> 0.01 us  [shards(): incoming = lax.all_to_all(outgoing, ('grp', 'blk'), 0, 0, tiled=True)]
    unnamed x57 -> x47, local copies, waits for them, and re-layouts: 7.33 us -> 7.34 us
  transfers between devices with their start and end apart: 35 -> 35, of which waited for: 7 -> 8; matrix products, arithmetic and copies ran while one was open for 16% -> 13% of each run, Pallas kernels for 18% -> 19%
where the time goes in v9:
time: 232 us; the launch traced here: 230 us
  starting transfers between devices  75.2 us (32%)
  Pallas kernels  62.7 us (27%)
  waiting for transfers between devices  41 us (18%)
  local copies, waits for them, and re-layouts  25.8 us (11%)
  other arithmetic  15.9 us (7%)
  matrix products  7.76 us (3%)
    pallas_call x4, Pallas kernels, score_call(): pl.pallas_call(score_kernel, out_shape=(pltpu.HBM((4, total, cols), BF),...  24.3 us
    ppermute x8, waiting for transfers between devices, hop_grp(): lax.ppermute(value, 'grp', [(i, (i // 2 + dx) % 4 * 2 + (i % 2 ^ dy)) for...  23.9 us
    ppermute x21, starting transfers between devices, hop_blk(): return lax.ppermute(value, 'blk', route)  23 us
    ppermute x21, waiting for transfers between devices, hop_blk(): return lax.ppermute(value, 'blk', route)  17.1 us
    pallas_call x1, Pallas kernels, target_call(): pl.pallas_call(target_kernel, out_shape=(jax.ShapeDtypeStruct(half, F32),...  15.4 us
    pallas_call x1, Pallas kernels, source_call(): pl.pallas_call(source_kernel, out_shape=jax.ShapeDtypeStruct((total, widt...  12.6 us
    ppermute x8, starting transfers between devices, hop_grp(): lax.ppermute(value, 'grp', [(i, (i // 2 + dx) % 4 * 2 + (i % 2 ^ dy)) for...  10.9 us
    all_to_all x1, starting transfers between devices, shards(): lax.all_to_all(served, ('grp', 'blk'), 0, 0, tiled=True)  10.2 us
  transfers between devices with their start and end apart: 35, of which 8 were waited for; matrix products, arithmetic and copies ran while one was open for 13% of the time, Pallas kernels for 19%

profile of v9, /device:TPU:0, one launch (start us, length us, event | category | flops | bytes accessed | tf_op | source)
XLA Modules:
  0.0 229.8 jit_solution(7836065674996839100)
XLA Ops:
  0.6 3.4 %collective-permute-start = (bf16[192,768]{1,0:T(8,128)(2,1)}, bf16[192,768]{1,0:T(8,128)(2,1)}, u32[]{:S(2)}, u32[]{:S(2)}) collective-permute-start(bf16[192,768]{1,0:T(8,128)(2,1)} %refs_0_.1), channel_id=1, source_target_pairs={{0,2},{1,3},{2,0},{3,1},{4,6},{5,7},{6,4},{7,5},{8,10},{9,11},{10,... | collective-permute-start | bytes 884744 | tf_op jit(solution)/shard_map/ppermute | solution.py:21
  4.0 3.9 %collective-permute-start.7 = (bf16[192,768]{1,0:T(8,128)(2,1)}, bf16[192,768]{1,0:T(8,128)(2,1)S(1)}, u32[]{:S(2)}, u32[]{:S(2)}) collective-permute-start(bf16[192,768]{1,0:T(8,128)(2,1)} %refs_0_.1), channel_id=1, source_target_pairs={{0,8},{1,9},{2,10},{3,11},{4,12},{5,13},{6,14},{7,15},{8,0},{9,1},... | collective-permute-start | bytes 884744 | tf_op jit(solution)/shard_map/ppermute | solution.py:21
  11.9 7.3 %all-to-all-start = ((s32[128,1,3]{2,1,0:T(1,128)}), s32[128,1,3]{2,1,0:T(1,128)}, u32[]{:S(2)}, u32[]{:S(2)}) async-start(s32[128,1,3]{2,1,0:T(1,128)} %bitcast), calls=%async_computation | async-start | bytes 131072 | tf_op jit(solution)/shard_map/all_to_all | solution.py:285
  22.6 2.8 %collective-permute-start.8 = (bf16[192,768]{1,0:T(8,128)(2,1)}, bf16[192,768]{1,0:T(8,128)(2,1)}, u32[]{:S(2)}, u32[]{:S(2)}) collective-permute-start(bf16[192,768]{1,0:T(8,128)(2,1)} %collective-permute-done.t1.refs_1_), channel_id=1, source_target_pairs={{0,12},{1,13},{2,14},{3,15},{4,0},{5,1},{6,2},{7,3},{8,4},{9,5},{1... | collective-permute-start | bytes 884744 | tf_op jit(solution)/shard_map/ppermute | solution.py:21
  28.5 6.0 %scores.4 = (bf16[4,1536,768]{2,1,0:T(8,128)(2,1)}, f32[8,1536]{1,0:T(8,128)S(1)}) custom-call(s32[4]{0:T(128)S(1)} %pad_add_fusion.2.place, bf16[1536,768]{1,0:T(8,128)(2,1)S(1)} %copy-done.1, bf16[192,768]{1,0:T(8,128)(2,1)} %refs_0_.1, bf16[192,768]{1,0:T(8,128)(2,1)} %collective-permute-done.t1.refs_1_, ...), custom_call_target="tpu_custom_call" | custom-call | flops 1811939328 | bytes 4718592 | tf_op jit(solution)/shard_map/scores/pallas_call | solution.py:83
  40.8 2.0 reshape.342
  42.8 10.2 %all-to-all-start.1 = ((bf16[128,3,768]{2,1,0:T(4,128)(2,1)}), bf16[128,3,768]{2,1,0:T(4,128)(2,1)}, u32[]{:S(2)}, u32[]{:S(2)}) async-start(bf16[128,3,768]{2,1,0:T(4,128)(2,1)} %reshape.342), calls=%async_computation.1 | async-start | bytes 1572864 | tf_op jit(solution)/shard_map/all_to_all | solution.py:323
  53.6 6.0 %scores.5 = (bf16[4,1536,768]{2,1,0:T(8,128)(2,1)}, f32[8,1536]{1,0:T(8,128)S(1)}) custom-call(s32[4]{0:T(128)S(1)} %pad_add_fusion.3.place, bf16[1536,768]{1,0:T(8,128)(2,1)S(1)} %copy-done.2, bf16[192,768]{1,0:T(8,128)(2,1)S(1)} %collective-permute-done.3.t0.refs_4_, ...), custom_call_target="tpu_custom_call", output_to_operand_aliasing={{0}: (6, {})} | custom-call | flops 1811939328 | bytes 4718592 | tf_op jit(solution)/shard_map/scores/pallas_call | solution.py:83
  61.3 6.1 %scores.6 = (bf16[4,1536,768]{2,1,0:T(8,128)(2,1)}, f32[8,1536]{1,0:T(8,128)S(1)}) custom-call(s32[4]{0:T(128)S(1)} %pad_add_fusion.4.place, bf16[1536,768]{1,0:T(8,128)(2,1)S(1)} %copy-done.2, bf16[192,768]{1,0:T(8,128)(2,1)S(1)} %collective-permute-done.7.t0.refs_8_, ...), custom_call_target="tpu_custom_call", output_to_operand_aliasing={{0}: (6, {})} | custom-call | flops 1811939328 | bytes 4718592 | tf_op jit(solution)/shard_map/scores/pallas_call | solution.py:83
  67.4 6.1 %scores.7 = (bf16[4,1536,768]{2,1,0:T(8,128)(2,1)}, f32[8,1536]{1,0:T(8,128)S(1)}) custom-call(s32[4]{0:T(128)S(1)} %pad_add_fusion.5.place, bf16[1536,768]{1,0:T(8,128)(2,1)S(1)} %copy-done.2, bf16[192,768]{1,0:T(8,128)(2,1)} %collective-permute-done.11.t0.refs_12_, ...), custom_call_target="tpu_custom_call", output_to_operand_aliasing={{0}: (6, {})} | custom-call | flops 1811939328 | bytes 4718592 | tf_op jit(solution)/shard_map/scores/pallas_call | solution.py:83
  75.0 2.2 reshape.343
  77.2 3.0 %fusion.3 = (f32[192]{0:T(256)S(1)}, f32[192]{0:T(256)S(1)}, f32[]{:T(128)}, f32[192,768]{1,0:T(8,128)}) fusion(bf16[1536,768]{1,0:T(8,128)(2,1)S(1)} %copy-done.2, s32[]{:T(128)S(6)} %select_n.245, bf16[192,768]{1,0:T(8,128)(2,1)S(1)} %collective-permute-done.15.tgt, bf16[384,768]{1,0:T(8,128)(2,1)} %reshape.343, s32[192]{0:T(256)S(1)} %multiply_add_fusion), kind=kOutput, calls=%fused_computation.13 | convolution fusion | flops 114499200 | bytes 1771784 | tf_op jit(solution)/shard_map/dot_general | solution.py:29
  84.0 9.7 %all-to-all-start.2 = ((f32[8,8,1536]{2,1,0:T(8,128)}), f32[8,8,1536]{2,1,0:T(8,128)S(1)}, u32[]{:S(2)}, u32[]{:S(2)}) async-start(f32[8,8,1536]{2,1,0:T(8,128)} %broadcast_in_dim.40), calls=%async_computation.2 | async-start | bytes 786432 | tf_op jit(solution)/shard_map/all_to_all | solution.py:346
  94.3 12.6 %source_terms.1 = bf16[1536,768]{1,0:T(8,128)(2,1)} custom-call(f32[8,1536]{1,0:T(8,128)} %concatenate.22.w_ref, bf16[4,1536,768]{2,1,0:T(8,128)(2,1)} %get-tuple-element.48.e_ref, bf16[192,768]{1,0:T(8,128)(2,1)} %refs_0_.1, bf16[192,768]{1,0:T(8,128)(2,1)} %collective-permute-done.t1.refs_1_, bf16[192,768]{1,0:T(8,128)(2,1)} %copy-done.11, ...), custom_call_target="tpu_custom_call" | custom-call | flops 7247757312 | bytes 11796480 | tf_op jit(solution)/shard_map/source_terms/pallas_call | solution.py:131
  110.8 15.4 %target_terms.1 = (f32[4,384,768]{2,1,0:T(8,128)}, bf16[4,384,768]{2,1,0:T(8,128)(2,1)}) custom-call(s32[16]{0:T(128)} %concatenate.24.place, f32[8,1536]{1,0:T(8,128)} %maximum_maximum_fusion.w_ref, bf16[4,1536,768]{2,1,0:T(8,128)(2,1)} %get-tuple-element.48.e_ref, bf16[1536,768]{1,0:T(8,128)(2,1)} %src_ref.1, bf16[16,128]{1,0:T(8,128)(2,1)} %copy-done.22), custom_call_target="tpu_custom_call" | custom-call | flops 7247757312 | bytes 18874368 | tf_op jit(solution)/shard_map/target_terms/pallas_call | solution.py:184
  126.5 4.5 %all-to-all-start.3 = ((bf16[8,192,768]{2,1,0:T(8,128)(2,1)}), bf16[8,192,768]{2,1,0:T(8,128)(2,1)S(1)}, u32[]{:S(2)}, u32[]{:S(2)}) async-start(bf16[8,192,768]{2,1,0:T(8,128)(2,1)} %bitcast.68), calls=%async_computation.3 | async-start | bytes 4718592 | tf_op jit(solution)/shard_map/all_to_all | solution.py:350
  131.1 2.9 %fusion.10 = (bf16[192,768]{1,0:T(8,128)(2,1)S(1)}, bf16[192,768]{1,0:T(8,128)(2,1)S(1)}, bf16[192,768]{1,0:T(8,128)(2,1)S(1)}, bf16[192,768]{1,0:T(8,128)(2,1)S...) fusion(f32[4,384,768]{2,1,0:T(8,128)} %get-tuple-element.51.keep, ...), kind=kLoop, calls=%fused_computation.33 | loop fusion | flops 2654208 | bytes 7077888 | tf_op jit(solution)/shard_map/convert_element_type | solution.py:381
  136.5 2.4 %collective-permute-start.19 = (bf16[384,768]{1,0:T(8,128)(2,1)}, bf16[384,768]{1,0:T(8,128)(2,1)}, u32[]{:S(2)}, u32[]{:S(2)}) collective-permute-start(bf16[384,768]{1,0:T(8,128)(2,1)} %pad_maximum_fusion.1), channel_id=1, source_target_pairs={{0,12},{1,13},{2,14},{3,15},{4,0},{5,1},{6,2},{7,3},{8,4},{9,5},{1... | collective-permute-start | bytes 1769480 | tf_op jit(solution)/shard_map/ppermute | solution.py:21
  140.2 2.3 %convolution_convert_fusion = bf16[384,768]{1,0:T(8,128)(2,1)} fusion(f32[192]{0:T(256)S(1)} %slice_reduce_fusion, bf16[1536,768]{1,0:T(8,128)(2,1)} %src_ref.1, s32[]{:T(128)S(6)} %select_n.245, s32[192]{0:T(256)S(1)} %multiply_add_fusion), kind=kOutput, calls=%fused_computation | convolution fusion | flops 114057216 | bytes 886276 | tf_op jit(solution)/shard_map/dot_general | solution.py:29
  142.5 2.0 reshape.344
  148.2 16.3 %collective-permute-done.18.m1 = bf16[384,768]{1,0:T(8,128)(2,1)} collective-permute-done((bf16[384,768]{1,0:T(8,128)(2,1)}, bf16[384,768]{1,0:T(8,128)(2,1)}, u32[]{:S(2)}, u32[]{:S(2)}) %collective-permute-start.18) | collective-permute-done | bytes 589856 | tf_op jit(solution)/shard_map/ppermute | solution.py:21
  164.7 3.0 %lines.1 = (f32[192,768]{1,0:T(8,128)}, bf16[192,768]{1,0:T(8,128)(2,1)}) custom-call(f32[4,384,768]{2,1,0:T(8,128)} %get-tuple-element.51.keep, bf16[4,384,768]{2,1,0:T(8,128)(2,1)} %collective-permute-done.17.got, bf16[384,768]{1,0:T(8,128)(2,1)} %collective-permute-done.18.m1, bf16[384,768]{1,0:T(8,128)(2,1)} %collective-permute-done.19.m2, ...), custom_call_target="tpu_custom_call" | custom-call | flops 1474560 | bytes 4423680 | tf_op jit(solution)/shard_map/lines/pallas_call | solution.py:386
  169.1 3.0 %code.1 = (s16[192,768]{1,0:T(8,128)(2,1)}, s16[96,768]{1,0:T(8,128)(2,1)}) custom-call(bf16[8,192,768]{2,1,0:T(8,128)(2,1)} %copy-done.13, f32[192,768]{1,0:T(8,128)} %get-tuple-element.97.hard, bf16[192,768]{1,0:T(8,128)(2,1)} %copy-done.17, f32[192,11]{1,0:T(8,128)} %bitcast.69, bf16[192,768]{1,0:T(8,128)(2,1)} %get-tuple-element.53._), custom_call_target="tpu_custom_call" | custom-call | flops 1474560 | bytes 3244032 | tf_op jit(solution)/shard_map/code/pallas_call | solution.py:397
  172.1 2.8 %collective-permute-start.22 = (s16[96,768]{1,0:T(8,128)(2,1)}, s16[96,768]{1,0:T(8,128)(2,1)S(1)}, u32[]{:S(2)}, u32[]{:S(2)}) collective-permute-start(s16[96,768]{1,0:T(8,128)(2,1)} %get-tuple-element.58), channel_id=1, source_target_pairs={{0,96},{16,112},{32,0},{48,16},{64,32},{80,48},{96,64},{112,80},{1... | collective-permute-start | bytes 442376 | tf_op jit(solution)/shard_map/ppermute | solution.py:25
  176.6 3.5 %collective-permute-start.29 = (bf16[192,768]{1,0:T(8,128)(2,1)S(1)}, bf16[192,768]{1,0:T(8,128)(2,1)}, u32[]{:S(2)}, u32[]{:S(2)}) collective-permute-start(bf16[192,768]{1,0:T(8,128)(2,1)S(1)} %copy-done.20), channel_id=1, source_target_pairs={{0,2},{1,3},{2,0},{3,1},{4,6},{5,7},{6,4},{7,5},{8,10},{9,11},{10,... | collective-permute-start | bytes 884744 | tf_op jit(solution)/shard_map/ppermute | solution.py:21
  180.0 8.0 %all-to-all-start.4 = ((bf16[128,3,768]{2,1,0:T(4,128)(2,1)}), bf16[128,3,768]{2,1,0:T(4,128)(2,1)}, u32[]{:S(2)}, u32[]{:S(2)}) async-start(bf16[128,3,768]{2,1,0:T(4,128)(2,1)} %reshape.344), calls=%async_computation.4 | async-start | bytes 1572864 | tf_op jit(solution)/shard_map/all_to_all | solution.py:425
  191.2 12.9 %collective-permute-done.21.side = s16[192,768]{1,0:T(8,128)(2,1)S(1)} collective-permute-done((s16[192,768]{1,0:T(8,128)(2,1)}, s16[192,768]{1,0:T(8,128)(2,1)S(1)}, u32[]{:S(2)}, u32[]{:S(2)}) %collective-permute-start.21) | collective-permute-done | bytes 294944 | tf_op jit(solution)/shard_map/ppermute | solution.py:25
  204.2 2.7 %collective-permute-start.25 = (s16[2,96,768]{2,1,0:T(8,128)(2,1)S(1)}, s16[2,96,768]{2,1,0:T(8,128)(2,1)S(1)}, u32[]{:S(2)}, u32[]{:S(2)}) collective-permute-start(s16[2,96,768]{2,1,0:T(8,128)(2,1)S(1)} %pad_add_fusion.1), channel_id=1, source_target_pairs={{0,96},{16,112},{32,0},{48,16},{64,32},{80,48},{96,64},{112,80},{1... | collective-permute-start | bytes 884744 | tf_op jit(solution)/shard_map/ppermute | solution.py:25
  209.7 1.8 convert_add_fusion
  213.2 5.7 %collective-permute-done.25.pairs1 = s16[2,96,768]{2,1,0:T(8,128)(2,1)S(1)} collective-permute-done((s16[2,96,768]{2,1,0:T(8,128)(2,1)S(1)}, s16[2,96,768]{2,1,0:T(8,128)(2,1)S(1)}, u32[]{:S(2)}, u32[]{:S(2)}) %collective-permute-start.25) | collective-permute-done | bytes 294944 | tf_op jit(solution)/shard_map/ppermute | solution.py:25
  218.9 3.7 %collective-permute-done.27.pairs3 = s16[2,96,768]{2,1,0:T(8,128)(2,1)S(1)} collective-permute-done((s16[2,96,768]{2,1,0:T(8,128)(2,1)S(1)}, s16[2,96,768]{2,1,0:T(8,128)(2,1)S(1)}, u32[]{:S(2)}, u32[]{:S(2)}) %collective-permute-start.27) | collective-permute-done | bytes 294944 | tf_op jit(solution)/shard_map/ppermute | solution.py:25
  222.5 4.5 %decode.1 = f32[1536,768]{1,0:T(8,128)} custom-call(s32[8]{0:T(128)S(1)} %stack.170.order, f32[1536,1]{1,0:T(8,128)S(1)} %fusion.1.scale, s16[192,768]{1,0:T(8,128)(2,1)S(1)} %copy-done.3, s16[192,768]{1,0:T(8,128)(2,1)S(1)} %collective-permute-done.21.side, s16[96,768]{1,0:T(8,128)(2,1)S(1)} %collective-permute-done.22.far1, ...), custom_call_target="tpu_custom_call" | custom-call | flops 1179648 | bytes 7077888 | tf_op jit(solution)/shard_map/decode/pallas_call | solution.py:251
  (161 shorter events, 49.9 us)
Async XLA Ops:
  0.6 20.1 %collective-permute-start = (bf16[192,768]{1,0:T(8,128)(2,1)}, bf16[192,768]{1,0:T(8,128)(2,1)}, u32[]{:S(2)}, u32[]{:S(2)}) collective-permute-start(bf16[192,768]{1,0:T(8,128)(2,1)} %refs_0_.1), channel_id=1, source_target_pairs={{0,2},{1,3},{2,0},{3,1},{4,6},{5,7},{6,4},{7,5},{8,10},{9,11},{10,... | collective-permute-start | bytes 884744 | tf_op jit(solution)/shard_map/ppermute | solution.py:21
  4.0 33.8 %collective-permute-start.7 = (bf16[192,768]{1,0:T(8,128)(2,1)}, bf16[192,768]{1,0:T(8,128)(2,1)S(1)}, u32[]{:S(2)}, u32[]{:S(2)}) collective-permute-start(bf16[192,768]{1,0:T(8,128)(2,1)} %refs_0_.1), channel_id=1, source_target_pairs={{0,8},{1,9},{2,10},{3,11},{4,12},{5,13},{6,14},{7,15},{8,0},{9,1},... | collective-permute-start | bytes 884744 | tf_op jit(solution)/shard_map/ppermute | solution.py:21
  7.9 13.1 %collective-permute-start.1 = (bf16[192,768]{1,0:T(8,128)(2,1)}, bf16[192,768]{1,0:T(8,128)(2,1)S(1)}, u32[]{:S(2)}, u32[]{:S(2)}) collective-permute-start(bf16[192,768]{1,0:T(8,128)(2,1)} %refs_0_.1), channel_id=1, source_target_pairs={{0,1},{1,0},{2,3},{3,2},{4,5},{5,4},{6,7},{7,6},{8,9},{9,8},{10,11... | collective-permute-start | bytes 884744 | tf_op jit(solution)/shard_map/ppermute | solution.py:21
  7.9 30.7 %collective-permute-start.3 = (bf16[192,768]{1,0:T(8,128)(2,1)}, bf16[192,768]{1,0:T(8,128)(2,1)S(1)}, u32[]{:S(2)}, u32[]{:S(2)}) collective-permute-start(bf16[192,768]{1,0:T(8,128)(2,1)} %refs_0_.1), channel_id=1, source_target_pairs={{0,12},{1,13},{2,14},{3,15},{4,0},{5,1},{6,2},{7,3},{8,4},{9,5},{1... | collective-permute-start | bytes 884744 | tf_op jit(solution)/shard_map/ppermute | solution.py:21
  8.6 30.0 %collective-permute-start.4 = (bf16[192,768]{1,0:T(8,128)(2,1)}, bf16[192,768]{1,0:T(8,128)(2,1)S(1)}, u32[]{:S(2)}, u32[]{:S(2)}) collective-permute-start(bf16[192,768]{1,0:T(8,128)(2,1)} %refs_0_.1), channel_id=1, source_target_pairs={{0,4},{1,5},{2,6},{3,7},{4,8},{5,9},{6,10},{7,11},{8,12},{9,13},{1... | collective-permute-start | bytes 884744 | tf_op jit(solution)/shard_map/ppermute | solution.py:21
  11.9 24.7 %all-to-all-start = ((s32[128,1,3]{2,1,0:T(1,128)}), s32[128,1,3]{2,1,0:T(1,128)}, u32[]{:S(2)}, u32[]{:S(2)}) async-start(s32[128,1,3]{2,1,0:T(1,128)} %bitcast), calls=%async_computation | async-start | bytes 131072 | tf_op jit(solution)/shard_map/all_to_all | solution.py:285
  21.0 18.1 %collective-permute-start.11 = (bf16[192,768]{1,0:T(8,128)(2,1)}, bf16[192,768]{1,0:T(8,128)(2,1)}, u32[]{:S(2)}, u32[]{:S(2)}) collective-permute-start(bf16[192,768]{1,0:T(8,128)(2,1)} %collective-permute-done.t1.refs_1_), channel_id=1, source_target_pairs={{0,4},{1,5},{2,6},{3,7},{4,8},{5,9},{6,10},{7,11},{8,12},{9,13},{1... | collective-permute-start | bytes 884744 | tf_op jit(solution)/shard_map/ppermute | solution.py:21
  22.6 16.6 %collective-permute-start.8 = (bf16[192,768]{1,0:T(8,128)(2,1)}, bf16[192,768]{1,0:T(8,128)(2,1)}, u32[]{:S(2)}, u32[]{:S(2)}) collective-permute-start(bf16[192,768]{1,0:T(8,128)(2,1)} %collective-permute-done.t1.refs_1_), channel_id=1, source_target_pairs={{0,12},{1,13},{2,14},{3,15},{4,0},{5,1},{6,2},{7,3},{8,4},{9,5},{1... | collective-permute-start | bytes 884744 | tf_op jit(solution)/shard_map/ppermute | solution.py:21
  37.8 15.3 %collective-permute-start.12 = (bf16[192,768]{1,0:T(8,128)(2,1)}, bf16[192,768]{1,0:T(8,128)(2,1)}, u32[]{:S(2)}, u32[]{:S(2)}) collective-permute-start(bf16[192,768]{1,0:T(8,128)(2,1)} %collective-permute-done.t1.refs_1_), channel_id=1, source_target_pairs={{0,8},{1,9},{2,10},{3,11},{4,12},{5,13},{6,14},{7,15},{8,0},{9,1},... | collective-permute-start | bytes 884744 | tf_op jit(solution)/shard_map/ppermute | solution.py:21
  38.6 22.7 %collective-permute-start.9 = (bf16[192,768]{1,0:T(8,128)(2,1)S(1)}, bf16[192,768]{1,0:T(8,128)(2,1)}, u32[]{:S(2)}, u32[]{:S(2)}) collective-permute-start(bf16[192,768]{1,0:T(8,128)(2,1)S(1)} %collective-permute-done.7.t0.refs_8_), channel_id=1, source_target_pairs={{0,1},{1,0},{2,3},{3,2},{4,5},{5,4},{6,7},{7,6},{8,9},{9,8},{10,11... | collective-permute-start | bytes 884744 | tf_op jit(solution)/shard_map/ppermute | solution.py:21
  38.6 14.6 %collective-permute-start.5 = (bf16[192,768]{1,0:T(8,128)(2,1)S(1)}, bf16[192,768]{1,0:T(8,128)(2,1)}, u32[]{:S(2)}, u32[]{:S(2)}) collective-permute-start(bf16[192,768]{1,0:T(8,128)(2,1)S(1)} %collective-permute-done.3.t0.refs_4_), channel_id=1, source_target_pairs={{0,1},{1,0},{2,3},{3,2},{4,5},{5,4},{6,7},{7,6},{8,9},{9,8},{10,11... | collective-permute-start | bytes 884744 | tf_op jit(solution)/shard_map/ppermute | solution.py:21
  39.1 14.6 %collective-permute-start.6 = (bf16[192,768]{1,0:T(8,128)(2,1)S(1)}, bf16[192,768]{1,0:T(8,128)(2,1)}, u32[]{:S(2)}, u32[]{:S(2)}) collective-permute-start(bf16[192,768]{1,0:T(8,128)(2,1)S(1)} %collective-permute-done.4.t1.refs_5_), channel_id=1, source_target_pairs={{0,1},{1,0},{2,3},{3,2},{4,5},{5,4},{6,7},{7,6},{8,9},{9,8},{10,11... | collective-permute-start | bytes 884744 | tf_op jit(solution)/shard_map/ppermute | solution.py:21
  39.2 22.1 %collective-permute-start.10 = (bf16[192,768]{1,0:T(8,128)(2,1)}, bf16[192,768]{1,0:T(8,128)(2,1)}, u32[]{:S(2)}, u32[]{:S(2)}) collective-permute-start(bf16[192,768]{1,0:T(8,128)(2,1)} %collective-permute-done.8.t1.refs_9_), channel_id=1, source_target_pairs={{0,1},{1,0},{2,3},{3,2},{4,5},{5,4},{6,7},{7,6},{8,9},{9,8},{10,11... | collective-permute-start | bytes 884744 | tf_op jit(solution)/shard_map/ppermute | solution.py:21
  42.8 32.2 %all-to-all-start.1 = ((bf16[128,3,768]{2,1,0:T(4,128)(2,1)}), bf16[128,3,768]{2,1,0:T(4,128)(2,1)}, u32[]{:S(2)}, u32[]{:S(2)}) async-start(bf16[128,3,768]{2,1,0:T(4,128)(2,1)} %reshape.342), calls=%async_computation.1 | async-start | bytes 1572864 | tf_op jit(solution)/shard_map/all_to_all | solution.py:323
  53.1 14.3 %collective-permute-start.13 = (bf16[192,768]{1,0:T(8,128)(2,1)}, bf16[192,768]{1,0:T(8,128)(2,1)S(1)}, u32[]{:S(2)}, u32[]{:S(2)}) collective-permute-start(bf16[192,768]{1,0:T(8,128)(2,1)} %collective-permute-done.11.t0.refs_12_), channel_id=1, source_target_pairs={{0,1},{1,0},{2,3},{3,2},{4,5},{5,4},{6,7},{7,6},{8,9},{9,8},{10,11... | collective-permute-start | bytes 884744 | tf_op jit(solution)/shard_map/ppermute | solution.py:21
  53.1 14.3 %collective-permute-start.14 = (bf16[192,768]{1,0:T(8,128)(2,1)}, bf16[192,768]{1,0:T(8,128)(2,1)S(1)}, u32[]{:S(2)}, u32[]{:S(2)}) collective-permute-start(bf16[192,768]{1,0:T(8,128)(2,1)} %collective-permute-done.12.t1.refs_13_), channel_id=1, source_target_pairs={{0,1},{1,0},{2,3},{3,2},{4,5},{5,4},{6,7},{7,6},{8,9},{9,8},{10,11... | collective-permute-start | bytes 884744 | tf_op jit(solution)/shard_map/ppermute | solution.py:21
  59.7 17.5 %collective-permute-start.15 = (bf16[192,768]{1,0:T(8,128)(2,1)}, bf16[192,768]{1,0:T(8,128)(2,1)S(1)}, u32[]{:S(2)}, u32[]{:S(2)}) collective-permute-start(bf16[192,768]{1,0:T(8,128)(2,1)} %refs_0_.1), channel_id=1, source_target_pairs={{0,0},{1,16},{2,32},{3,48},{4,64},{5,80},{6,96},{7,112},{8,1},{9,1... | collective-permute-start | bytes 884744 | tf_op jit(solution)/shard_map/ppermute | solution.py:326
  84.0 22.9 %all-to-all-start.2 = ((f32[8,8,1536]{2,1,0:T(8,128)}), f32[8,8,1536]{2,1,0:T(8,128)S(1)}, u32[]{:S(2)}, u32[]{:S(2)}) async-start(f32[8,8,1536]{2,1,0:T(8,128)} %broadcast_in_dim.40), calls=%async_computation.2 | async-start | bytes 786432 | tf_op jit(solution)/shard_map/all_to_all | solution.py:346
  126.5 41.2 %all-to-all-start.3 = ((bf16[8,192,768]{2,1,0:T(8,128)(2,1)}), bf16[8,192,768]{2,1,0:T(8,128)(2,1)S(1)}, u32[]{:S(2)}, u32[]{:S(2)}) async-start(bf16[8,192,768]{2,1,0:T(8,128)(2,1)} %bitcast.68), calls=%async_computation.3 | async-start | bytes 4718592 | tf_op jit(solution)/shard_map/all_to_all | solution.py:350
  134.8 29.6 %collective-permute-start.18 = (bf16[384,768]{1,0:T(8,128)(2,1)}, bf16[384,768]{1,0:T(8,128)(2,1)}, u32[]{:S(2)}, u32[]{:S(2)}) collective-permute-start(bf16[384,768]{1,0:T(8,128)(2,1)} %pad_maximum_fusion), channel_id=1, source_target_pairs={{0,4},{1,5},{2,6},{3,7},{4,8},{5,9},{6,10},{7,11},{8,12},{9,13},{1... | collective-permute-start | bytes 1769480 | tf_op jit(solution)/shard_map/ppermute | solution.py:21
  136.5 28.1 %collective-permute-start.19 = (bf16[384,768]{1,0:T(8,128)(2,1)}, bf16[384,768]{1,0:T(8,128)(2,1)}, u32[]{:S(2)}, u32[]{:S(2)}) collective-permute-start(bf16[384,768]{1,0:T(8,128)(2,1)} %pad_maximum_fusion.1), channel_id=1, source_target_pairs={{0,12},{1,13},{2,14},{3,15},{4,0},{5,1},{6,2},{7,3},{8,4},{9,5},{1... | collective-permute-start | bytes 1769480 | tf_op jit(solution)/shard_map/ppermute | solution.py:21
  139.9 24.8 %collective-permute-start.20 = (bf16[384,768]{1,0:T(8,128)(2,1)}, bf16[384,768]{1,0:T(8,128)(2,1)}, u32[]{:S(2)}, u32[]{:S(2)}) collective-permute-start(bf16[384,768]{1,0:T(8,128)(2,1)} %pad_maximum_fusion.2), channel_id=1, source_target_pairs={{0,8},{1,9},{2,10},{3,11},{4,12},{5,13},{6,14},{7,15},{8,0},{9,1},... | collective-permute-start | bytes 1769480 | tf_op jit(solution)/shard_map/ppermute | solution.py:21
  172.1 17.9 %collective-permute-start.22 = (s16[96,768]{1,0:T(8,128)(2,1)}, s16[96,768]{1,0:T(8,128)(2,1)S(1)}, u32[]{:S(2)}, u32[]{:S(2)}) collective-permute-start(s16[96,768]{1,0:T(8,128)(2,1)} %get-tuple-element.58), channel_id=1, source_target_pairs={{0,96},{16,112},{32,0},{48,16},{64,32},{80,48},{96,64},{112,80},{1... | collective-permute-start | bytes 442376 | tf_op jit(solution)/shard_map/ppermute | solution.py:25
  174.8 15.1 %collective-permute-start.23 = (s16[96,768]{1,0:T(8,128)(2,1)}, s16[96,768]{1,0:T(8,128)(2,1)S(1)}, u32[]{:S(2)}, u32[]{:S(2)}) collective-permute-start(s16[96,768]{1,0:T(8,128)(2,1)} %get-tuple-element.58), channel_id=1, source_target_pairs={{0,64},{16,80},{32,96},{48,112},{64,0},{80,16},{96,32},{112,48},{1... | collective-permute-start | bytes 442376 | tf_op jit(solution)/shard_map/ppermute | solution.py:25
  175.7 14.3 %collective-permute-start.24 = (s16[96,768]{1,0:T(8,128)(2,1)}, s16[96,768]{1,0:T(8,128)(2,1)S(1)}, u32[]{:S(2)}, u32[]{:S(2)}) collective-permute-start(s16[96,768]{1,0:T(8,128)(2,1)} %get-tuple-element.58), channel_id=1, source_target_pairs={{0,32},{16,48},{32,64},{48,80},{64,96},{80,112},{96,0},{112,16},{1... | collective-permute-start | bytes 442376 | tf_op jit(solution)/shard_map/ppermute | solution.py:25
  176.6 33.1 %collective-permute-start.29 = (bf16[192,768]{1,0:T(8,128)(2,1)S(1)}, bf16[192,768]{1,0:T(8,128)(2,1)}, u32[]{:S(2)}, u32[]{:S(2)}) collective-permute-start(bf16[192,768]{1,0:T(8,128)(2,1)S(1)} %copy-done.20), channel_id=1, source_target_pairs={{0,2},{1,3},{2,0},{3,1},{4,6},{5,7},{6,4},{7,5},{8,10},{9,11},{10,... | collective-permute-start | bytes 884744 | tf_op jit(solution)/shard_map/ppermute | solution.py:21
  180.0 47.0 %all-to-all-start.4 = ((bf16[128,3,768]{2,1,0:T(4,128)(2,1)}), bf16[128,3,768]{2,1,0:T(4,128)(2,1)}, u32[]{:S(2)}, u32[]{:S(2)}) async-start(bf16[128,3,768]{2,1,0:T(4,128)(2,1)} %reshape.344), calls=%async_computation.4 | async-start | bytes 1572864 | tf_op jit(solution)/shard_map/all_to_all | solution.py:425
  188.0 16.1 %collective-permute-start.21 = (s16[192,768]{1,0:T(8,128)(2,1)}, s16[192,768]{1,0:T(8,128)(2,1)S(1)}, u32[]{:S(2)}, u32[]{:S(2)}) collective-permute-start(s16[192,768]{1,0:T(8,128)(2,1)} %get-tuple-element.57.own), channel_id=1, source_target_pairs={{0,16},{16,0},{32,48},{48,32},{64,80},{80,64},{96,112},{112,96},{1... | collective-permute-start | bytes 884744 | tf_op jit(solution)/shard_map/ppermute | solution.py:25
  190.0 23.1 %collective-permute-start.28 = (s16[3,96,768]{2,1,0:T(8,128)(2,1)S(1)}, s16[3,96,768]{2,1,0:T(8,128)(2,1)S(1)}, u32[]{:S(2)}, u32[]{:S(2)}) collective-permute-start(s16[3,96,768]{2,1,0:T(8,128)(2,1)S(1)} %pad_add_fusion), channel_id=1, source_target_pairs={{0,16},{16,0},{32,48},{48,32},{64,80},{80,64},{96,112},{112,96},{1... | collective-permute-start | bytes 1327112 | tf_op jit(solution)/shard_map/ppermute | solution.py:25
  204.2 14.7 %collective-permute-start.25 = (s16[2,96,768]{2,1,0:T(8,128)(2,1)S(1)}, s16[2,96,768]{2,1,0:T(8,128)(2,1)S(1)}, u32[]{:S(2)}, u32[]{:S(2)}) collective-permute-start(s16[2,96,768]{2,1,0:T(8,128)(2,1)S(1)} %pad_add_fusion.1), channel_id=1, source_target_pairs={{0,96},{16,112},{32,0},{48,16},{64,32},{80,48},{96,64},{112,80},{1... | collective-permute-start | bytes 884744 | tf_op jit(solution)/shard_map/ppermute | solution.py:25
  206.8 12.0 %collective-permute-start.26 = (s16[2,96,768]{2,1,0:T(8,128)(2,1)S(1)}, s16[2,96,768]{2,1,0:T(8,128)(2,1)S(1)}, u32[]{:S(2)}, u32[]{:S(2)}) collective-permute-start(s16[2,96,768]{2,1,0:T(8,128)(2,1)S(1)} %pad_add_fusion.1), channel_id=1, source_target_pairs={{0,64},{16,80},{32,96},{48,112},{64,0},{80,16},{96,32},{112,48},{1... | collective-permute-start | bytes 884744 | tf_op jit(solution)/shard_map/ppermute | solution.py:25
  207.8 14.7 %collective-permute-start.27 = (s16[2,96,768]{2,1,0:T(8,128)(2,1)S(1)}, s16[2,96,768]{2,1,0:T(8,128)(2,1)S(1)}, u32[]{:S(2)}, u32[]{:S(2)}) collective-permute-start(s16[2,96,768]{2,1,0:T(8,128)(2,1)S(1)} %pad_add_fusion.1), channel_id=1, source_target_pairs={{0,32},{16,48},{32,64},{48,80},{64,96},{80,112},{96,0},{112,16},{1... | collective-permute-start | bytes 884744 | tf_op jit(solution)/shard_map/ppermute | solution.py:25
  (26 other events, 353.6 us)
